TPU v7x, 32 devices: a whole 2x2x4 slice. The times are simulated.
32 devices in a mesh: fsdp: 8 (over y, x, core), ctx: 4 (over z).
Axes of the slice: x: 2, y: 2, z: 4, core: 2. Of those that a mesh axis runs over, the one named last changes fastest.
Arguments:
- inputs: bfloat16 [8, 4096, 1024], P('fsdp', 'ctx'), may hold values from -6 to 6
- cotangent: bfloat16 [8, 4096, 1024], P('fsdp', 'ctx'), may hold values from -6 to 6
- positions: int32 [8, 4096], P('fsdp', 'ctx'), may hold values from 0 to 2303, as said below
- segments: int32 [8, 4096], P('fsdp', 'ctx'), may hold values from 0 to 8, as said below
- ln1_gain: bfloat16 [1024], P('fsdp'), may hold values from 0.5 to 1.5
- ln1_bias: bfloat16 [1024], P('fsdp'), may hold values from -2.5 to 2.5
- w_qkv: bfloat16 [1024, 3072], P('fsdp'), may hold values from -0.1875 to 0.1875
- b_qkv: bfloat16 [3072], P('fsdp'), may hold values from -3 to 3
- w_attn_out: bfloat16 [1024, 1024], P('fsdp'), may hold values from -1.5 to 1.5
- b_out: bfloat16 [1024], P('fsdp'), may hold values from -2.5 to 2.5
- ln2_gain: bfloat16 [1024], P('fsdp'), may hold values from 0.5 to 1.5
- ln2_bias: bfloat16 [1024], P('fsdp'), may hold values from -2.5 to 2.5
- w_in: bfloat16 [1024, 4096], P('fsdp'), may hold values from -0.1875 to 0.1875
- b_in: bfloat16 [4096], P('fsdp'), may hold values from -2.5 to 2.5
- w_out: bfloat16 [4096, 1024], P('fsdp'), may hold values from -0.09375 to 0.09375
Outputs:
- output: bfloat16 [8, 4096, 1024], P('fsdp', 'ctx')
- grad_inputs: float32 [8, 4096, 1024], P('fsdp', 'ctx')
- grad_ln1_gain: float32 [1024], P(('fsdp', 'ctx'))
- grad_ln1_bias: float32 [1024], P(('fsdp', 'ctx'))
- grad_w_qkv: float32 [1024, 3072], P(('fsdp', 'ctx'))
- grad_b_qkv: float32 [3072], P(('fsdp', 'ctx'))
- grad_w_attn_out: float32 [1024, 1024], P(('fsdp', 'ctx'))
- grad_b_out: float32 [1024], P(('fsdp', 'ctx'))
- grad_ln2_gain: float32 [1024], P(('fsdp', 'ctx'))
- grad_ln2_bias: float32 [1024], P(('fsdp', 'ctx'))
- grad_w_in: float32 [1024, 4096], P(('fsdp', 'ctx'))
- grad_b_in: float32 [4096], P(('fsdp', 'ctx'))
- grad_w_out: float32 [4096, 1024], P(('fsdp', 'ctx'))
Inputs may be any that keep to these rules, and one draw needn't show every extreme that they name: `positions`: in a group, token t of the natural order (the prompt, then the continuations one after another) has position t and segment 0 if t < 2048, else position 2048 + (t - 2048) % 256 and segment 1 + (t - 2048) // 256. The natural order is cut into 8 blocks of 512 tokens; index j of ctx holds block p_j followed by block 7 - p_j, where p is a permutation of 0 to 3 drawn for each group. `segments`: laid out with positions as stated there.
All inputs are finite; a program needn't handle non-finite values.
Results may differ from a plain program's by a relative error of at most 0.014.
Values may be sent and summed in bfloat16 or wider, within the bound.
No kernel may reach another device: no remote copies, remote signals or barrier semaphores. Data moves between devices by JAX's collectives and lax.ppermute only.
A program may use at most 256 MiB of HBM per device.

v0:
```python
from functools import partial
import math

import jax
import jax.numpy as jnp
from jax import lax
from jax.sharding import PartitionSpec as P

HEADS = 16
HD = 64
ROT = 16


NORM_EPS = 1e-05
MASKED = -1e30


def layer_norm(values, scaling, offset):
    average = jnp.mean(values, axis=-1, keepdims=True)
    centered = values - average
    variance = jnp.mean(centered * centered, axis=-1, keepdims=True)
    return centered * lax.rsqrt(variance + NORM_EPS) * scaling + offset


def rotary_tables(positions):
    halfway = ROT // 2
    spacing = jnp.arange(halfway, dtype=jnp.float32) * (2.0 / ROT)
    inverse = jnp.exp(-math.log(10000.0) * spacing)
    angles = positions.astype(jnp.float32)[..., None] * inverse
    return (jnp.cos(angles), jnp.sin(angles))


def rotate(heads_in, cosine, sine):
    halfway = ROT // 2
    cosine = cosine[..., None, :]
    sine = sine[..., None, :]
    first = heads_in[..., :halfway]
    second = heads_in[..., halfway:ROT]
    return jnp.concatenate(
        [first * cosine - second * sine, second * cosine + first * sine, heads_in[..., ROT:]],
        axis=-1,
    )


def unrotate(grads_in, cosine, sine):
    halfway = ROT // 2
    cosine = cosine[..., None, :]
    sine = sine[..., None, :]
    first = grads_in[..., :halfway]
    second = grads_in[..., halfway:ROT]
    return jnp.concatenate(
        [first * cosine + second * sine, second * cosine - first * sine, grads_in[..., ROT:]],
        axis=-1,
    )


def allowed_mask(query_pos, query_seg, key_pos, key_seg):
    same_doc = (key_seg[:, None, :] == 0) | (key_seg[:, None, :] == query_seg[:, :, None])
    causal = key_pos[:, None, :] <= query_pos[:, :, None]
    return (same_doc & causal)[:, None]


def scores_of(queries, keys_blk):
    return jnp.einsum("gqhd,gkhd->ghqk", queries, keys_blk, preferred_element_type=jnp.float32)


def block_grads(queries, grad_att, log_total, delta, mask, keys_blk, values_blk):
    probs = jnp.where(mask, jnp.exp(scores_of(queries, keys_blk) - log_total[..., None]), 0.0)
    dprobs = jnp.einsum("gqhd,gkhd->ghqk", grad_att, values_blk, preferred_element_type=jnp.float32)
    grad_scores = (probs * (dprobs - delta[..., None])).astype(jnp.bfloat16)
    return (probs.astype(jnp.bfloat16), grad_scores)


def local(
    inputs,
    cotangent,
    positions,
    segments,
    ln1_gain,
    ln1_bias,
    w_qkv,
    b_qkv,
    w_attn_out,
    b_out,
    ln2_gain,
    ln2_bias,
    w_in,
    b_in,
    w_out,
):
    shards = (
        ln1_gain,
        ln1_bias,
        w_qkv,
        b_qkv,
        w_attn_out,
        b_out,
        ln2_gain,
        ln2_bias,
        w_in,
        b_in,
        w_out,
    )
    params = (
        lax.all_gather(shards[0], "fsdp", axis=0, tiled=True),
        lax.all_gather(shards[1], "fsdp", axis=0, tiled=True),
        lax.all_gather(shards[2], "fsdp", axis=0, tiled=True),
        lax.all_gather(shards[3], "fsdp", axis=0, tiled=True),
        lax.all_gather(shards[4], "fsdp", axis=0, tiled=True),
        lax.all_gather(shards[5], "fsdp", axis=0, tiled=True),
        lax.all_gather(shards[6], "fsdp", axis=0, tiled=True),
        lax.all_gather(shards[7], "fsdp", axis=0, tiled=True),
        lax.all_gather(shards[8], "fsdp", axis=0, tiled=True),
        lax.all_gather(shards[9], "fsdp", axis=0, tiled=True),
        lax.all_gather(shards[10], "fsdp", axis=0, tiled=True),
    )
    groups, local_len, width = inputs.shape
    rows_total = groups * local_len
    block = math.gcd(local_len, 256)
    label_pos, label_seg = (
        lax.all_gather(positions, "ctx", axis=1, tiled=True),
        lax.all_gather(segments, "ctx", axis=1, tiled=True),
    )
    count = label_pos.shape[1] // block
    f32 = jnp.float32
    bf16 = jnp.bfloat16
    (
        gain_attn,
        shift_attn,
        weight_qkv,
        bias_qkv,
        weight_attn,
        bias_out,
        gain_mlp,
        shift_mlp,
        weight_in,
        bias_in,
        weight_out,
    ) = params
    flat_in = inputs.reshape(rows_total, width).astype(f32)
    normed_attn = layer_norm(flat_in, gain_attn.astype(f32), shift_attn.astype(f32)).astype(bf16)
    normed_mlp = layer_norm(flat_in, gain_mlp.astype(f32), shift_mlp.astype(f32)).astype(bf16)
    projected = jnp.dot(normed_attn, weight_qkv, preferred_element_type=f32) + bias_qkv.astype(f32)
    cosine, sine = rotary_tables(positions)

    def split_heads(columns):
        return columns.reshape(groups, local_len, HEADS, HD)

    scale = HD ** (-0.5)
    queries = (rotate(split_heads(projected[:, :width]), cosine, sine) * scale).astype(bf16)
    keys_own = rotate(split_heads(projected[:, width : 2 * width]), cosine, sine).astype(bf16)
    values_own = split_heads(projected[:, 2 * width :]).astype(bf16)
    keys_all, values_all = (
        lax.all_gather(keys_own, "ctx", axis=1, tiled=True),
        lax.all_gather(values_own, "ctx", axis=1, tiled=True),
    )

    def key_block(index):
        start = index * block
        keys_blk = lax.dynamic_slice_in_dim(keys_all, start, block, 1)
        values_blk = lax.dynamic_slice_in_dim(values_all, start, block, 1)
        mask = allowed_mask(
            positions,
            segments,
            lax.dynamic_slice_in_dim(label_pos, start, block, 1),
            lax.dynamic_slice_in_dim(label_seg, start, block, 1),
        )
        return (keys_blk, values_blk, mask)

    def total_step(carry, index):
        peak, total = carry
        keys_blk, values_blk, mask = key_block(index)
        scores = jnp.where(mask, scores_of(queries, keys_blk), MASKED)
        fresh = jnp.maximum(peak, jnp.max(scores, axis=-1))
        added = jnp.sum(jnp.where(mask, jnp.exp(scores - fresh[..., None]), 0.0), axis=-1)
        return ((fresh, total * jnp.exp(peak - fresh) + added), None)

    stat_shape = (groups, HEADS, local_len)
    (peak, total), unused = lax.scan(
        total_step,
        (jnp.full(stat_shape, MASKED, f32), jnp.zeros(stat_shape, f32)),
        jnp.arange(count),
    )
    log_total = peak + jnp.log(total)

    def attend_step(rounded_sum, index):
        keys_blk, values_blk, mask = key_block(index)
        probs = jnp.where(mask, jnp.exp(scores_of(queries, keys_blk) - log_total[..., None]), 0.0)
        rounded_sum = rounded_sum + jnp.einsum(
            "ghqk,gkhd->gqhd", probs.astype(bf16), values_blk, preferred_element_type=f32
        )
        return (rounded_sum, None)

    head_shape = (groups, local_len, HEADS, HD)
    rounded_sum, unused = lax.scan(attend_step, jnp.zeros(head_shape, f32), jnp.arange(count))
    attended = rounded_sum.reshape(rows_total, width).astype(bf16)
    pre_act = jnp.dot(normed_mlp, weight_in, preferred_element_type=f32) + bias_in.astype(f32)
    activated = jax.nn.gelu(pre_act, approximate=False).astype(bf16)
    output = (
        flat_in
        + jnp.dot(attended, weight_attn, preferred_element_type=f32)
        + jnp.dot(activated, weight_out, preferred_element_type=f32)
        + bias_out.astype(f32)
    )
    (
        gain_attn,
        shift_attn,
        weight_qkv,
        bias_qkv,
        weight_attn,
        bias_out,
        gain_mlp,
        shift_mlp,
        weight_in,
        bias_in,
        weight_out,
    ) = params
    grad_out = cotangent.reshape(rows_total, width)
    grad_bias_out = jnp.sum(grad_out.astype(f32), axis=0)
    grad_weight_out = jnp.einsum("rf,rd->fd", activated, grad_out, preferred_element_type=f32)
    grad_act = jnp.einsum("rd,fd->rf", grad_out, weight_out, preferred_element_type=f32)
    unused, gelu_back = jax.vjp(partial(jax.nn.gelu, approximate=False), pre_act)
    grad_pre = gelu_back(grad_act)[0].astype(bf16)
    grad_weight_in = jnp.einsum("rd,rf->df", normed_mlp, grad_pre, preferred_element_type=f32)
    grad_bias_in = jnp.sum(grad_pre.astype(f32), axis=0)
    grad_normed_mlp = jnp.einsum("rf,df->rd", grad_pre, weight_in, preferred_element_type=f32)
    grad_weight_attn = jnp.einsum("ra,rd->ad", attended, grad_out, preferred_element_type=f32)
    grad_att = (
        jnp.einsum("rd,ad->ra", grad_out, weight_attn, preferred_element_type=f32)
        .astype(bf16)
        .reshape(head_shape)
    )
    delta = jnp.einsum(
        "gqhd,gqhd->ghq", grad_att.astype(f32), rounded_sum, precision=lax.Precision.HIGHEST
    )

    def back_step(carry, index):
        keys_blk, values_blk, mask = key_block(index)
        rounded, grad_scores = block_grads(
            queries, grad_att, log_total, delta, mask, keys_blk, values_blk
        )
        carry = carry + jnp.einsum(
            "ghqk,gkhd->gqhd", grad_scores, keys_blk, preferred_element_type=f32
        )
        key_term = jnp.einsum("ghqk,gqhd->gkhd", grad_scores, queries, preferred_element_type=f32)
        value_term = jnp.einsum("ghqk,gqhd->gkhd", rounded, grad_att, preferred_element_type=f32)
        return (carry, (key_term, value_term))

    grad_queries, (key_terms, value_terms) = lax.scan(
        back_step, jnp.zeros(head_shape, f32), jnp.arange(count)
    )
    key_sums, value_sums = (
        lax.psum_scatter(
            key_terms.astype(jnp.bfloat16), "ctx", scatter_dimension=0, tiled=True
        ).astype(jnp.float32),
        lax.psum_scatter(
            value_terms.astype(jnp.bfloat16), "ctx", scatter_dimension=0, tiled=True
        ).astype(jnp.float32),
    )
    grad_keys = jnp.transpose(key_sums, (1, 0, 2, 3, 4)).reshape(head_shape)
    grad_values = jnp.transpose(value_sums, (1, 0, 2, 3, 4)).reshape(head_shape)
    grad_q_pre = unrotate(grad_queries * scale, cosine, sine).reshape(rows_total, width)
    grad_k_pre = unrotate(grad_keys, cosine, sine).reshape(rows_total, width)
    grad_projected = jnp.concatenate(
        [grad_q_pre, grad_k_pre, grad_values.reshape(rows_total, width)], axis=1
    ).astype(bf16)
    grad_weight_qkv = jnp.einsum(
        "rd,re->de", normed_attn, grad_projected, preferred_element_type=f32
    )
    grad_bias_qkv = jnp.sum(grad_projected.astype(f32), axis=0)
    grad_normed_attn = jnp.einsum(
        "re,de->rd", grad_projected, weight_qkv, preferred_element_type=f32
    )
    unused, norm_back_attn = jax.vjp(
        layer_norm, flat_in, gain_attn.astype(f32), shift_attn.astype(f32)
    )
    grad_in_attn, grad_gain_attn, grad_shift_attn = norm_back_attn(grad_normed_attn)
    unused, norm_back_mlp = jax.vjp(
        layer_norm, flat_in, gain_mlp.astype(f32), shift_mlp.astype(f32)
    )
    grad_in_mlp, grad_gain_mlp, grad_shift_mlp = norm_back_mlp(grad_normed_mlp)
    grad_inputs = (grad_out.astype(f32) + grad_in_attn + grad_in_mlp).reshape(
        groups, local_len, width
    )
    sums = (
        lax.psum_scatter(grad_gain_attn, ("fsdp", "ctx"), scatter_dimension=0, tiled=True),
        lax.psum_scatter(grad_shift_attn, ("fsdp", "ctx"), scatter_dimension=0, tiled=True),
        lax.psum_scatter(grad_weight_qkv, ("fsdp", "ctx"), scatter_dimension=0, tiled=True),
        lax.psum_scatter(grad_bias_qkv, ("fsdp", "ctx"), scatter_dimension=0, tiled=True),
        lax.psum_scatter(grad_weight_attn, ("fsdp", "ctx"), scatter_dimension=0, tiled=True),
        lax.psum_scatter(grad_bias_out, ("fsdp", "ctx"), scatter_dimension=0, tiled=True),
        lax.psum_scatter(grad_gain_mlp, ("fsdp", "ctx"), scatter_dimension=0, tiled=True),
        lax.psum_scatter(grad_shift_mlp, ("fsdp", "ctx"), scatter_dimension=0, tiled=True),
        lax.psum_scatter(grad_weight_in, ("fsdp", "ctx"), scatter_dimension=0, tiled=True),
        lax.psum_scatter(grad_bias_in, ("fsdp", "ctx"), scatter_dimension=0, tiled=True),
        lax.psum_scatter(grad_weight_out, ("fsdp", "ctx"), scatter_dimension=0, tiled=True),
    )
    result = output.reshape(groups, local_len, width).astype(bf16)
    return (
        result,
        grad_inputs,
        sums[0],
        sums[1],
        sums[2],
        sums[3],
        sums[4],
        sums[5],
        sums[6],
        sums[7],
        sums[8],
        sums[9],
        sums[10],
    )


def solution(mesh):
    in_specs = (
        P("fsdp", "ctx", None),
        P("fsdp", "ctx", None),
        P("fsdp", "ctx"),
        P("fsdp", "ctx"),
        P("fsdp"),
        P("fsdp"),
        P("fsdp", None),
        P("fsdp"),
        P("fsdp", None),
        P("fsdp"),
        P("fsdp"),
        P("fsdp"),
        P("fsdp", None),
        P("fsdp"),
        P("fsdp", None),
    )
    out_specs = (
        P("fsdp", "ctx", None),
        P("fsdp", "ctx", None),
        P(("fsdp", "ctx")),
        P(("fsdp", "ctx")),
        P(("fsdp", "ctx"), None),
        P(("fsdp", "ctx")),
        P(("fsdp", "ctx"), None),
        P(("fsdp", "ctx")),
        P(("fsdp", "ctx")),
        P(("fsdp", "ctx")),
        P(("fsdp", "ctx"), None),
        P(("fsdp", "ctx")),
        P(("fsdp", "ctx"), None),
    )
    return jax.shard_map(local, mesh=mesh, in_specs=in_specs, out_specs=out_specs, check_vma=False)
```

profile of v0, /device:TPU:0, one launch (start us, length us, event | category | flops | bytes accessed | tf_op | source)
XLA Modules:
  0.0 2799.0 jit_solution(5648398646766879114)
XLA Ops:
  8.0 10.3 all-gather
  40.2 18.0 all-gather.14.cloned.1.call-done
  98.3 13.3 all_gather.51
  111.5 18.1 all_gather.50
  133.6 107.9 %all-gather.18.cloned.1.call-done = bf16[1,4096,16,64]{1,3,2,0:T(8,128)(2,1)} async-done(((bf16[1,1024,16,64]{1,3,2,0:T(8,128)(2,1)}), bf16[1,4096,16,64]{1,3,2,0:T(8,128)(2,1)}) %all-gather.18.cloned.1.call-update) | async-done | bytes 8388624 | tf_op jit(solution)/shard_map/all_gather | solution.py:154
  241.4 326.4 %while.39 = (s32[]{:T(128)}, f32[1,16,1024]{2,1,0:T(8,128)S(1)}, f32[1,16,1024]{2,1,0:T(8,128)S(1)}, s32[16]{0:T(128)S(1)}, s32[1,4096]{1,0:T(1,128)S(1)}, /*ind...) while((s32[]{:T(128)}, f32[1,16,1024]{2,1,0:T(8,128)S(1)}, ...), condition=%wide.region_5.6_spmd.clone, body=%wide.region_2.5_spmd.clone.sunk | while | flops 563167488 | bytes 37830352 | solution.py:179
  243.1 11.0 fusion.159
  567.9 167.2 %while.40 = (s32[]{:T(128)}, f32[1,1024,16,64]{1,3,2,0:T(8,128)}, s32[16]{0:T(128)S(1)}, bf16[1,4096,16,64]{1,3,2,0:T(8,128)(2,1)}, s32[1,4096]{1,0:T(1,128)S(1)...) while((s32[]{:T(128)}, f32[1,1024,16,64]{1,3,2,0:T(8,128)}, ...), condition=%wide.region_7.8_spmd.clone, body=%wide.region_6.7_spmd.clone.sunk | while | flops 1089470720 | bytes 12141780 | solution.py:195
  742.4 715.6 %while.41 = (s32[]{:T(128)}, f32[1,1024,16,64]{1,3,2,0:T(8,128)}, bf16[16,1,256,16,64]{2,4,3,1,0:T(8,128)(2,1)}, bf16[16,1,256,16,64]{2,4,3,1,0:T(8,128)(2,1)}, ...) while((s32[]{:T(128)}, f32[1,1024,16,64]{1,3,2,0:T(8,128)}, ...), condition=%wide.region_9.10_spmd.clone, body=%wide.region_8.9_spmd.clone.sunk | while | flops 2721054976 | bytes 138887984 | solution.py:249
  776.0 10.0 fusion.176
  865.7 9.9 fusion.176
  910.5 9.9 fusion.176
  955.3 9.9 fusion.176
  1134.5 9.9 fusion.176
  1179.3 9.9 fusion.176
  1224.1 9.9 fusion.176
  1268.9 9.9 fusion.176
  1313.7 9.9 fusion.176
  1494.4 50.9 %multiply_convert_fusion = (bf16[1024,4096]{1,0:T(8,128)(2,1)}, f32[1024,4096]{1,0:T(8,128)}, f32[1024,4096]{1,0:T(8,128)}) fusion(f32[4096]{0:T(1024)S(1)} %bitcast.419, bf16[1024,4096]{1,0:T(8,128)(2,1)} %all-gather.22.cloned.1.call-done, bf16[1,1024,1024]{2,1,0:T(8,128)(2,1)S(1)} %copy-done.3, f32[1024]{0:T(1024)S(1)} %bitcast.424, ...), kind=kOutput, calls=%fused_computation.67 | convolution fusion | flops 8873050112 | bytes 52461568 | tf_op jit(solution)/shard_map/dot_general | solution.py:197
  1545.3 24.3 convert_reduce_fusion
  1569.6 15.1 fusion.109
  1584.7 16.6 fusion.95
  1613.3 136.2 %reduce-scatter.9.cloned.1.call-done = bf16[4,1,256,16,64]{2,4,3,1,0:T(8,128)(2,1)} async-done(((bf16[16,1,256,16,64]{2,4,3,1,0:T(8,128)(2,1)}), bf16[4,1,256,16,64]{2,4,3,1,0:T(8,128)(2,1)}) %reduce-scatter.9.cloned.1.call-update) | async-done | bytes 2097168 | tf_op jit(solution)/shard_map/reduce_scatter | solution.py:256
  1759.0 11.7 fusion.113
  1780.0 13.1 fusion.124
  1795.5 14.9 fusion.94
  1810.4 13.5 fusion.120
  1838.5 41.4 %all-reduce.7 = (f32[1024]{0:T(1024)S(1)}, f32[1024]{0:T(1024)S(1)}, f32[3072]{0:T(1024)S(1)}, f32[1024]{0:T(1024)S(1)}, f32[1024]{0:T(1024)S(1)}, /*index=5*/f32[1024]{0:T(1024)S(1)}, f32[4096]{0:T(1024)S(1)}) all-reduce(f32[1024]{0:T(1024)S(1)} %get-tuple-element.356, ...), channel_id=4, replica_groups=mesh['fsdp'=8,'ctx'=4] {'fsdp','ctx'}, use_global_device_ids=true, to_apply=%region_17.18.clone | all-reduce | flops 12288 | bytes 98304
  1884.0 17.0 reduce-scatter.13.cloned.1.call-done
  1901.0 366.0 %reduce-scatter.15.cloned.1.call-done = f32[32,4096]{1,0:T(8,128)} async-done(((f32[1024,4096]{1,0:T(8,128)}), f32[32,4096]{1,0:T(8,128)}) %reduce-scatter.15.cloned.1.call-update) | async-done | bytes 524304 | tf_op jit(solution)/shard_map/reduce_scatter | solution.py:294
  2267.0 365.1 %reduce-scatter.17.cloned.1.call-done = f32[128,1024]{1,0:T(8,128)} async-done(((f32[4096,1024]{1,0:T(8,128)}), f32[128,1024]{1,0:T(8,128)}) %reduce-scatter.17.cloned.1.call-update) | async-done | bytes 524304 | tf_op jit(solution)/shard_map/reduce_scatter | solution.py:296
  2632.0 159.8 %reduce-scatter.11.cloned.1.call-done = f32[32,3072]{1,0:T(8,128)} async-done(((f32[1024,3072]{1,0:T(8,128)}), f32[32,3072]{1,0:T(8,128)}) %reduce-scatter.11.cloned.1.call-update) | async-done | bytes 393232 | tf_op jit(solution)/shard_map/reduce_scatter | solution.py:288
  (596 shorter events, 1236.7 us)
Async XLA Ops:
  7.2 31.5 %copy-start.2 = (bf16[1,1024,1024]{2,1,0:T(8,128)(2,1)S(1)}, bf16[1,1024,1024]{2,1,0:T(8,128)(2,1)}, u32[]{:S(2)}) copy-start(bf16[1,1024,1024]{2,1,0:T(8,128)(2,1)} %param.21) | copy-start | bytes 6291460
  7.2 51.0 %all-gather.14.cloned.1.call-start = ((), (), s32[]{:S(2)}) async-start(), calls=%async_computation.6 | async-start | bytes 7077888 | tf_op jit(solution)/shard_map/all_gather | solution.py:107
  7.9 233.5 %all-gather.18.cloned.1.call-start = ((), (), s32[]{:S(2)}) async-start(), calls=%async_computation.8 | async-start | bytes 10485760 | tf_op jit(solution)/shard_map/all_gather | solution.py:154
  18.3 48.9 %copy-start.27 = (f32[8,1,128]{2,1,0:T(1,128)}, f32[8,1,128]{2,1,0:T(1,128)S(1)}, u32[]{:S(2)}) copy-start(f32[8,1,128]{2,1,0:T(1,128)S(1)} %convert_element_type.150) | copy-start | bytes 12292
  26.9 40.3 %copy-start.33 = (f32[8,1,128]{2,1,0:T(1,128)}, f32[8,1,128]{2,1,0:T(1,128)S(1)}, u32[]{:S(2)}) copy-start(f32[8,1,128]{2,1,0:T(1,128)S(1)} %convert_element_type.151) | copy-start | bytes 12292
  38.7 28.5 %copy-start.25 = (f32[1024]{0:T(1024)}, f32[1024]{0:T(1024)S(1)}, u32[]{:S(2)}) copy-start(f32[1024]{0:T(1024)S(1)} %broadcast_multiply_fusion.1) | copy-start | bytes 12292
  40.0 27.3 copy-start.29
  40.2 46.9 %copy-start.21 = (f32[1024,8]{0,1:T(8,128)}, f32[1024,8]{0,1:T(8,128)S(1)}, u32[]{:S(2)}) copy-start(f32[1024,8]{0,1:T(8,128)S(1)} %get-tuple-element.464) | copy-start | bytes 98308
  40.2 46.9 %copy-start.23 = (f32[1024,8]{0,1:T(8,128)}, f32[1024,8]{0,1:T(8,128)S(1)}, u32[]{:S(2)}) copy-start(f32[1024,8]{0,1:T(8,128)S(1)} %get-tuple-element.465) | copy-start | bytes 98308
  91.3 476.6 %all-gather.16.cloned.1.call-start = ((), (), s32[]{:S(2)}) async-start(), calls=%async_computation.7 | async-start | bytes 10485760 | tf_op jit(solution)/shard_map/all_gather | solution.py:155
  93.9 17.7 copy-start.20
  96.5 638.7 %all-gather.20.cloned.1.call-start = ((), (), s32[]{:S(2)}) async-start(), calls=%async_computation.9 | async-start | bytes 2359296 | tf_op jit(solution)/shard_map/all_gather | solution.py:109
  97.0 1395.9 %all-gather.22.cloned.1.call-start = ((), (), s32[]{:S(2)}) async-start(), calls=%async_computation.10 | async-start | bytes 9437184 | tf_op jit(solution)/shard_map/all_gather | solution.py:113
  97.6 1447.7 %all-gather.24.cloned.1.call-start = ((), (), s32[]{:S(2)}) async-start(), calls=%async_computation.11 | async-start | bytes 9437184 | tf_op jit(solution)/shard_map/all_gather | solution.py:115
  98.2 1509.3 %reduce-scatter.7.cloned.1.call-start = ((), (), s32[]{:S(2)}) async-start(), calls=%async_computation.12 | async-start | bytes 10485760 | tf_op jit(solution)/shard_map/reduce_scatter | solution.py:253
  877.2 9.3 copy-start.1
  922.1 9.3 copy-start.1
  966.9 9.3 copy-start.1
  1458.0 291.5 %reduce-scatter.9.cloned.1.call-start = ((), (), s32[]{:S(2)}) async-start(), calls=%async_computation.13 | async-start | bytes 10485760 | tf_op jit(solution)/shard_map/reduce_scatter | solution.py:256
  1458.0 9.6 copy-start.35
  1458.0 18.4 copy-start.37
  1458.7 29.7 %copy-start.15 = (bf16[1,1024,1024]{2,1,0:T(8,128)(2,1)S(1)}, bf16[1,1024,1024]{2,1,0:T(8,128)(2,1)}, u32[]{:S(2)}) copy-start(bf16[1,1024,1024]{2,1,0:T(8,128)(2,1)} %param.22) | copy-start | bytes 6291460
  1458.7 442.3 %reduce-scatter.13.cloned.1.call-start = ((), (), s32[]{:S(2)}) async-start(), calls=%async_computation.15 | async-start | bytes 4325376 | tf_op jit(solution)/shard_map/reduce_scatter | solution.py:290
  1492.8 774.1 %reduce-scatter.15.cloned.1.call-start = ((), (), s32[]{:S(2)}) async-start(), calls=%async_computation.16 | async-start | bytes 17301504 | tf_op jit(solution)/shard_map/reduce_scatter | solution.py:294
  1584.6 1047.4 %reduce-scatter.17.cloned.1.call-start = ((), (), s32[]{:S(2)}) async-start(), calls=%async_computation.17 | async-start | bytes 17301504 | tf_op jit(solution)/shard_map/reduce_scatter | solution.py:296
  1601.3 1190.5 %reduce-scatter.11.cloned.1.call-start = ((), (), s32[]{:S(2)}) async-start(), calls=%async_computation.14 | async-start | bytes 12976128 | tf_op jit(solution)/shard_map/reduce_scatter | solution.py:288
  1613.3 140.1 %copy-start.22 = (f32[1024,8]{0,1:T(8,128)S(1)}, f32[1024,8]{0,1:T(8,128)}, u32[]{:S(2)}) copy-start(f32[1024,8]{0,1:T(8,128)} %copy-done.21) | copy-start | bytes 98308
  1613.3 140.1 %copy-start.24 = (f32[1024,8]{0,1:T(8,128)S(1)}, f32[1024,8]{0,1:T(8,128)}, u32[]{:S(2)}) copy-start(f32[1024,8]{0,1:T(8,128)} %copy-done.23) | copy-start | bytes 98308
  1780.0 13.1 copy-start.18
  1780.0 13.1 copy-start.39
  1795.5 14.9 copy-start.8
  1810.4 13.5 copy-start.32
  (50 other events, 233.5 us)
Sparse Core Ops, SparseCore 0:
  9.9 48.2 all-gather.13
  91.4 149.9 all-gather.17
  243.6 147.9 all-gather.15
  393.3 26.0 all-gather.19
  421.1 54.3 all-gather.21
  477.3 54.3 all-gather.23
  1458.1 143.7 reduce-scatter.6
  1604.2 145.1 reduce-scatter.8
  1752.3 148.6 reduce-scatter.12
  1903.7 363.2 reduce-scatter.14
  2269.8 362.1 reduce-scatter.16
  2638.5 153.3 reduce-scatter.10
where the time goes:
time: 2810 us; the launch traced here: 2800 us
  waiting for transfers between devices  1170 us (42%)
  matrix products  1110 us (40%)
  other arithmetic  202 us (7%)
  blocking collectives  134 us (5%)
  local copies, waits for them, and re-layouts  129 us (5%)
  loops' own time  34 us (1%)
    reduce_scatter x1, waiting for transfers between devices, local(): lax.psum_scatter(grad_weight_in, ('fsdp', 'ctx'), scatter_dimension=0, ti...  366 us
    reduce_scatter x1, waiting for transfers between devices, local(): lax.psum_scatter(grad_weight_out, ('fsdp', 'ctx'), scatter_dimension=0, t...  365 us
    dot_general x32, matrix products, scores_of(): jnp.einsum('gqhd,gkhd->ghqk', queries, keys_blk, preferred_element_type=j...  299 us
    reduce_scatter x1, waiting for transfers between devices, local(): lax.psum_scatter(grad_weight_qkv, ('fsdp', 'ctx'), scatter_dimension=0, t...  160 us
    dot_general x16, matrix products, back_step(): jnp.einsum('ghqk,gqhd->gkhd', rounded, grad_att, preferred_element_type=f32)  158 us
    reduce_sum x16, other arithmetic, total_step(): jnp.sum(jnp.where(mask, jnp.exp(scores - fresh[..., None]), 0.0), axis=-1)  149 us
    dot_general x16, matrix products, block_grads(): jnp.einsum('gqhd,gkhd->ghqk', grad_att, values_blk, preferred_element_typ...  144 us
    dot_general x16, matrix products, attend_step(): jnp.einsum('ghqk,gkhd->gqhd', probs.astype(bf16), values_blk, preferred_e...  141 us
  transfers between devices with their start and end apart: 12, of which 7 were waited for; matrix products, arithmetic and copies ran while one was open for 48% of the time, Pallas kernels for 0%

commit v1 on v0

--- a/solution.py
+++ b/solution.py
@@ -4,11 +4,18 @@
 import jax
 import jax.numpy as jnp
 from jax import lax
+from jax.experimental import pallas as pl
+from jax.experimental.pallas import tpu as pltpu
 from jax.sharding import PartitionSpec as P
 
 HEADS = 16
 HD = 64
 ROT = 16
+CLEN = 256
+QB = 256
+PAIR = 2 * HD
+bf16 = jnp.bfloat16
+f32 = jnp.float32
 
 
 NORM_EPS = 1e-05
@@ -71,7 +78,274 @@
     return (probs.astype(jnp.bfloat16), grad_scores)
 
 
-def local(
+def attn_kernel(half, nctx, kind_ref, q_ref, do_ref, k_ref, v_ref, o_ref, dq_ref, dk_ref, dv_ref,
+                kt_ref, vt_ref, s_ref, p_ref, ds_ref, dka_ref, dva_ref):
+    qb = pl.program_id(1)
+    nqb = pl.num_programs(1)
+    keys = k_ref.shape[0]
+    wide0 = half
+    starts = [i for i in range(0, half, QB)] + [i for i in range(2*half, keys, QB)]
+    nch = len(starts)
+    @pl.when(qb == 0)
+    def _():
+        kt_ref[...] = k_ref[...].T
+        vt_ref[...] = v_ref[...].T
+        dka_ref[...] = jnp.zeros_like(dka_ref)
+        dva_ref[...] = jnp.zeros_like(dva_ref)
+    diag0 = pl.multiple_of(qb * QB, QB)
+    lane = lax.broadcasted_iota(jnp.int32, (PAIR, QB), 0)
+    qT = q_ref[...].T
+    doT = do_ref[...].T.astype(f32)
+    zero = jnp.zeros((), bf16)
+    row = lax.broadcasted_iota(jnp.int32, (QB, QB), 0)
+    col = lax.broadcasted_iota(jnp.int32, (QB, QB), 1)
+    causal = row <= col
+    lanes = lax.broadcasted_iota(jnp.int32, (QB, PAIR), 1)
+    def red8(x, op):
+        return op(x.reshape(x.shape[0] // 8, 8, x.shape[1]), axis=0)
+    def kload(ref, c):
+        return ref[pl.ds(diag0, QB), :] if c == nch else ref[starts[c]:starts[c]+QB, :]
+    outs = []
+    ots = []; dots_ = []; dqts = []
+    ms = []
+    for h in range(2):
+        keep = (lane < HD) if h == 0 else (lane >= HD)
+        qh = jnp.where(keep, qT, zero)
+        mx = jnp.full((8, QB), MASKED, f32)
+        for c in range(nch + 1):
+            s = jnp.dot(kload(k_ref, c), qh, preferred_element_type=f32)
+            if c == nch:
+                s = jnp.where(causal, s, MASKED)
+                mc = red8(s, jnp.max)
+            else:
+                mc = red8(s, jnp.max) + kind_ref[qb, c]
+            s_ref[h, c] = s
+            mx = jnp.maximum(mx, mc)
+        m = jnp.max(mx, axis=0, keepdims=True)
+        ms.append(m)
+    for h in range(2):
+        m = ms[h]
+        l8 = jnp.zeros((8, QB), f32)
+        ot = jnp.zeros((HD, QB), f32)
+        for c in range(nch + 1):
+            t = -m if c == nch else kind_ref[qb, c] - m
+            e = jnp.exp2(s_ref[h, c] + t)
+            l8 = l8 + red8(e, jnp.sum)
+            p = e.astype(bf16)
+            p_ref[h, c] = p
+            if c == nch:
+                vt = vt_ref[h*HD:(h+1)*HD, pl.ds(diag0, QB)]
+            else:
+                vt = vt_ref[h*HD:(h+1)*HD, starts[c]:starts[c]+QB]
+            ot = ot + jnp.dot(vt, p, preferred_element_type=f32)
+        l = jnp.sum(l8, axis=0, keepdims=True)
+        r = 1.0 / l
+        oth = ot * r
+        ots.append(oth)
+        doh = doT[h*HD:(h+1)*HD]
+        delta = jnp.sum(oth * doh, axis=0, keepdims=True) * r
+        dos = (doh * r).astype(bf16)
+        z = jnp.zeros_like(dos)
+        dop = jnp.concatenate([dos, z] if h == 0 else [z, dos], axis=0)
+        dots_.append((dop, delta))
+    for h in range(2):
+        dop, delta = dots_[h]
+        dqt = jnp.zeros((HD, QB), f32)
+        for c in range(nch + 1):
+            dp = jnp.dot(kload(v_ref, c), dop, preferred_element_type=f32)
+            ds = (p_ref[h, c].astype(f32) * (dp - delta)).astype(bf16)
+            ds_ref[h, c] = ds
+            if c == nch:
+                kt = kt_ref[h*HD:(h+1)*HD, pl.ds(diag0, QB)]
+            else:
+                kt = kt_ref[h*HD:(h+1)*HD, starts[c]:starts[c]+QB]
+            dqt = dqt + jnp.dot(kt, ds, preferred_element_type=f32)
+        dqts.append(dqt)
+    qv = q_ref[...]
+    qm = [jnp.where(lanes < HD, qv, zero), jnp.where(lanes >= HD, qv, zero)]
+    dom = [dots_[h][0].T for h in range(2)]
+    for c in range(nch + 1):
+        dva = jnp.dot(p_ref[0, c], dom[0], preferred_element_type=f32) + jnp.dot(p_ref[1, c], dom[1], preferred_element_type=f32)
+        dka = jnp.dot(ds_ref[0, c], qm[0], preferred_element_type=f32) + jnp.dot(ds_ref[1, c], qm[1], preferred_element_type=f32)
+        if c == nch:
+            sl = pl.ds(diag0, QB)
+        else:
+            sl = pl.ds(starts[c], QB)
+        dva_ref[sl, :] += dva
+        dka_ref[sl, :] += dka
+    o_ref[...] = jnp.concatenate(ots, axis=0).T.astype(o_ref.dtype)
+    dq_ref[...] = jnp.concatenate(dqts, axis=0).T.astype(dq_ref.dtype)
+    @pl.when(qb == nqb - 1)
+    def _():
+        dk_ref[...] = (dka_ref[...] * math.log(2.0)).astype(dk_ref.dtype)
+        dv_ref[...] = dva_ref[...].astype(dv_ref.dtype)
+
+def attention(q, do, k, v, kind, half, nctx):
+    rows, width = q.shape
+    keys = k.shape[0]
+    nqb = rows // QB
+    nch = kind.shape[1]
+    pairs = width // PAIR
+    qspec = pl.BlockSpec((QB, PAIR), lambda p, b: (b, p))
+    kspec = pl.BlockSpec((keys, PAIR), lambda p, b: (0, p))
+    return pl.pallas_call(
+        partial(attn_kernel, half, nctx),
+        grid=(pairs, nqb),
+        in_specs=[pl.BlockSpec(memory_space=pltpu.SMEM), qspec, qspec, kspec, kspec],
+        out_specs=[qspec, qspec, kspec, kspec],
+        out_shape=[jax.ShapeDtypeStruct((rows, width), bf16), jax.ShapeDtypeStruct((rows, width), f32),
+                   jax.ShapeDtypeStruct((keys, width), bf16), jax.ShapeDtypeStruct((keys, width), bf16)],
+        scratch_shapes=[pltpu.VMEM((PAIR, keys), bf16), pltpu.VMEM((PAIR, keys), bf16),
+                        pltpu.VMEM((2, nch + 1, QB, QB), f32), pltpu.VMEM((2, nch + 1, QB, QB), bf16),
+                        pltpu.VMEM((2, nch + 1, QB, QB), bf16),
+                        pltpu.VMEM((keys, PAIR), f32), pltpu.VMEM((keys, PAIR), f32)],
+        compiler_params=pltpu.CompilerParams(vmem_limit_bytes=60 << 20),
+        name="attention",
+    )(kind, q, do, k, v)
+
+
+def turn_tables(positions):
+    halfway = ROT // 2
+    lane = jnp.arange(HEADS * HD) % HD
+    inverse = jnp.exp(-math.log(10000.0) * (2.0 / ROT) * (lane % halfway).astype(f32))
+    angles = positions.astype(f32)[:, None] * inverse[None, :]
+    cosine = jnp.where(lane < ROT, jnp.cos(angles), 1.0)
+    sine = jnp.sin(angles)
+    return cosine, jnp.where(lane < halfway, sine, 0.0), jnp.where((lane >= halfway) & (lane < ROT), sine, 0.0)
+
+
+def turn(u, tables):
+    cosine, low, high = tables
+    return u * cosine - jnp.roll(u, -(ROT // 2), 1) * low + jnp.roll(u, ROT // 2, 1) * high
+
+
+def turn_back(g, tables):
+    cosine, low, high = tables
+    return g * cosine + jnp.roll(g, -(ROT // 2), 1) * low - jnp.roll(g, ROT // 2, 1) * high
+
+
+def scatter_sum(terms):
+    part = lax.psum_scatter(terms, "fsdp", scatter_dimension=0, tiled=True)
+    return lax.psum_scatter(part, "ctx", scatter_dimension=0, tiled=True)
+
+
+def fast(inputs, cotangent, positions, segments, ln1_gain, ln1_bias, w_qkv, b_qkv, w_attn_out, b_out,
+         ln2_gain, ln2_bias, w_in, b_in, w_out):
+    x, grad_out, pos = inputs[0], cotangent[0], positions[0]
+    rows, width = x.shape
+    half = rows // 2
+    n = lax.axis_size("ctx")
+    f = lax.axis_size("fsdp")
+    ring = [(i, (i + 1) % n) for i in range(n)]
+    back = [(i, (i - 1) % n) for i in range(n)]
+    xs, poss = [x[:half]], [pos[:half]]
+    for _ in range(n - 1):
+        xs.append(lax.ppermute(xs[-1], "ctx", ring))
+        poss.append(lax.ppermute(poss[-1], "ctx", ring))
+    small = jnp.concatenate([ln1_gain, ln1_bias, b_qkv, b_out, ln2_gain, ln2_bias, b_in])
+    small = lax.all_gather(small.reshape(1, -1), "fsdp", axis=0, tiled=True)
+    sizes = [a.shape[0] for a in (ln1_gain, ln1_bias, b_qkv, b_out, ln2_gain, ln2_bias, b_in)]
+    full, at = [], 0
+    for size in sizes:
+        full.append(small[:, at:at + size].reshape(-1).astype(f32))
+        at += size
+    gain_attn, shift_attn, bias_qkv, bias_out, gain_mlp, shift_mlp, bias_in = full
+    weight_qkv = lax.all_gather(w_qkv, "fsdp", axis=0, tiled=True)
+    weight_in = lax.all_gather(w_in, "fsdp", axis=0, tiled=True)
+    weight_out = lax.all_gather(w_out, "fsdp", axis=0, tiled=True)
+    weight_attn = lax.all_gather(w_attn_out, "fsdp", axis=0, tiled=True)
+
+    x_all = jnp.concatenate([x] + xs[1:], axis=0)
+    pos_all = jnp.concatenate([pos] + poss[1:], axis=0)
+    normed_all = layer_norm(x_all.astype(f32), gain_attn, shift_attn).astype(bf16)
+    normed_attn = normed_all[:rows]
+    tables = turn_tables(pos_all)
+    own = tuple(t[:rows] for t in tables)
+    scale = HD ** (-0.5)
+    q_part = jnp.dot(normed_attn, weight_qkv[:, :width], preferred_element_type=f32) + bias_qkv[:width]
+    queries = (turn(q_part, own) * (scale / math.log(2.0))).astype(bf16)
+    k_part = jnp.dot(normed_all, weight_qkv[:, width:2 * width], preferred_element_type=f32) + bias_qkv[width:2 * width]
+    keys = turn(k_part, tables).astype(bf16)
+    v_part = jnp.dot(normed_all, weight_qkv[:, 2 * width:], preferred_element_type=f32) + bias_qkv[2 * width:]
+    values = v_part.astype(bf16)
+    grad_att = jnp.einsum("rd,ad->ra", grad_out, weight_attn, preferred_element_type=f32).astype(bf16)
+
+    flat_in = x.astype(f32)
+    normed_mlp = layer_norm(flat_in, gain_mlp, shift_mlp).astype(bf16)
+    pre_act = jnp.dot(normed_mlp, weight_in, preferred_element_type=f32) + bias_in
+    activated = jax.nn.gelu(pre_act, approximate=False).astype(bf16)
+    partial_out = jnp.dot(activated, weight_out, preferred_element_type=f32)
+    grad_bias_out = jnp.sum(grad_out.astype(f32), axis=0)
+    grad_weight_out = jnp.einsum("rf,rd->fd", activated, grad_out, preferred_element_type=f32).astype(bf16)
+    grad_act = jnp.einsum("rd,fd->rf", grad_out, weight_out, preferred_element_type=f32)
+    unused, gelu_back = jax.vjp(partial(jax.nn.gelu, approximate=False), pre_act)
+    grad_pre = gelu_back(grad_act)[0].astype(bf16)
+    grad_weight_in = jnp.einsum("rd,rf->df", normed_mlp, grad_pre, preferred_element_type=f32).astype(bf16)
+    grad_bias_in = jnp.sum(grad_pre.astype(f32), axis=0)
+    grad_normed_mlp = jnp.einsum("rf,df->rd", grad_pre, weight_in, preferred_element_type=f32)
+    sum_out = scatter_sum(grad_weight_out)
+    sum_in = scatter_sum(grad_weight_in)
+
+    first = pos[0]
+    free, shut = jnp.zeros((), f32), jnp.full((), MASKED, f32)
+    per = half // QB
+    table = []
+    for qb in range(2 * per):
+        line = [free if qb > c else shut for c in range(per)]
+        for s in range(1, n):
+            flag = free if qb >= per else jnp.where(poss[s][0] < first, free, shut)
+            line += [flag] * per
+        table.append(jnp.stack(line))
+    kind = jnp.stack(table)
+    attended, grad_q, grad_k, grad_v = attention(queries, grad_att, keys, values, kind, half, n)
+
+    def piece(a, s):
+        return a[:half] if s == 0 else a[(s + 1) * half:(s + 2) * half]
+
+    run_k, run_v = piece(grad_k, n - 1), piece(grad_v, n - 1)
+    for s in range(n - 2, -1, -1):
+        run_k = lax.ppermute(run_k, "ctx", back).astype(f32) + piece(grad_k, s).astype(f32)
+        run_v = lax.ppermute(run_v, "ctx", back).astype(f32) + piece(grad_v, s).astype(f32)
+        if s:
+            run_k, run_v = run_k.astype(bf16), run_v.astype(bf16)
+    full_k = jnp.concatenate([run_k, grad_k[half:2 * half].astype(f32)], axis=0)
+    full_v = jnp.concatenate([run_v, grad_v[half:2 * half].astype(f32)], axis=0)
+
+    output = (flat_in + jnp.dot(attended, weight_attn, preferred_element_type=f32) + partial_out + bias_out).astype(bf16)
+    grad_weight_attn = jnp.einsum("ra,rd->ad", attended, grad_out, preferred_element_type=f32).astype(bf16)
+    sum_attn = scatter_sum(grad_weight_attn)
+    grad_projected = jnp.concatenate(
+        [turn_back(grad_q * scale, own), turn_back(full_k, own), full_v], axis=1).astype(bf16)
+    grad_weight_qkv = jnp.einsum("rd,re->de", normed_attn, grad_projected, preferred_element_type=f32).astype(bf16)
+    sum_qkv = scatter_sum(grad_weight_qkv)
+    grad_bias_qkv = jnp.sum(grad_projected.astype(f32), axis=0)
+    grad_normed_attn = jnp.einsum("re,de->rd", grad_projected, weight_qkv, preferred_element_type=f32)
+    unused, norm_back_attn = jax.vjp(layer_norm, flat_in, gain_attn, shift_attn)
+    grad_in_attn, grad_gain_attn, grad_shift_attn = norm_back_attn(grad_normed_attn)
+    unused, norm_back_mlp = jax.vjp(layer_norm, flat_in, gain_mlp, shift_mlp)
+    grad_in_mlp, grad_gain_mlp, grad_shift_mlp = norm_back_mlp(grad_normed_mlp)
+    grad_inputs = grad_out.astype(f32) + grad_in_attn + grad_in_mlp
+    parts = n * f
+    smalls = (grad_gain_attn, grad_shift_attn, grad_bias_qkv, grad_bias_out, grad_gain_mlp, grad_shift_mlp, grad_bias_in)
+    packed = jnp.concatenate([a.reshape(parts, -1) for a in smalls], axis=1)
+    packed = lax.psum_scatter(packed, ("fsdp", "ctx"), scatter_dimension=0, tiled=True)[0]
+    done, at = [], 0
+    for a in smalls:
+        size = a.shape[0] // parts
+        done.append(packed[at:at + size])
+        at += size
+    return (output[None], grad_inputs[None], done[0], done[1], sum_qkv.astype(f32), done[2], sum_attn.astype(f32),
+            done[3], done[4], done[5], sum_in.astype(f32), done[6], sum_out.astype(f32))
+
+
+def local(*args):
+    half = args[0].shape[1] // 2
+    if args[0].shape[0] == 1 and half % CLEN == 0 and half % QB == 0:
+        return fast(*args)
+    return generic(*args)
+
+
+def generic(
     inputs,
     cotangent,
     positions,

time: 2810 us -> 922 us (0.33)
  waiting for transfers between devices: 1170 us -> 258 us
  matrix products: 1110 us -> 210 us
  Pallas kernels: 0 us -> 164 us
  local copies, waits for them, and re-layouts: 129 us -> 31 us
  blocking collectives: 134 us -> 48.2 us
  other arithmetic: 202 us -> 158 us
  loops' own time: 34 us -> 0 us
    reduce_scatter x6 -> x8, waiting for transfers between devices: 1040 us -> 118 us  [the longest x4 74 us: scatter_sum(): return lax.psum_scatter(part, 'ctx', scatter_dimension=0, tiled=True)]
    dot_general x124 -> x14, matrix products: 1110 us -> 210 us  [the longest x1 51.1 us: fast(): jnp.dot(normed_mlp, weight_in, preferred_element_type=f32) + bias_in]
    pallas_call x0 -> x1, Pallas kernels: none -> 164 us  [attention(): pl.pallas_call(partial(attn_kernel, half, nctx), grid=(pairs, nqb), in_sp...]
    ppermute x0 -> x12, waiting for transfers between devices: none -> 137 us  [the longest x3 51.9 us: fast(): lax.ppermute(run_k, 'ctx', back).astype(f32) + piece(grad_k, s).astype(f32)]
    reduce_sum x18 -> x2, other arithmetic: 158 us -> 25 us  [the longest x1 20.6 us: fast(): grad_bias_qkv = jnp.sum(grad_projected.astype(f32), axis=0)]
    all_gather x6 -> x4, waiting for transfers between devices: 126 us -> 0.04 us  [the longest x1 0.02 us: fast(): weight_attn = lax.all_gather(w_attn_out, 'fsdp', axis=0, tiled=True)]
    all_gather x9 -> x1, blocking collectives: 92.7 us -> 9.16 us  [fast(): small = lax.all_gather(small.reshape(1, -1), 'fsdp', axis=0, tiled=True)]
    convert_element_type x10 -> x14, other arithmetic: 4.87 us -> 79.7 us  [the longest x1 45.9 us: fast(): keys = turn(k_part, tables).astype(bf16)]
  transfers between devices with their start and end apart: 12 -> 24, of which waited for: 7 -> 15; matrix products, arithmetic and copies ran while one was open for 48% -> 43% of each run, Pallas kernels for 0% -> 18%
where the time goes in v1:
time: 922 us; the launch traced here: 914 us
  waiting for transfers between devices  258 us (28%)
  matrix products  210 us (23%)
  Pallas kernels  164 us (18%)
  other arithmetic  158 us (17%)
  blocking collectives  48.2 us (5%)
  local copies, waits for them, and re-layouts  31 us (3%)
  starting transfers between devices  25.5 us (3%)
  between operations  19.2 us (2%)
    pallas_call x1, Pallas kernels, attention(): pl.pallas_call(partial(attn_kernel, half, nctx), grid=(pairs, nqb), in_sp...  164 us
    reduce_scatter x4, waiting for transfers between devices, scatter_sum(): return lax.psum_scatter(part, 'ctx', scatter_dimension=0, tiled=True)  74 us
    ppermute x3, waiting for transfers between devices, fast(): lax.ppermute(run_k, 'ctx', back).astype(f32) + piece(grad_k, s).astype(f32)  51.9 us
    dot_general x1, matrix products, fast(): jnp.dot(normed_mlp, weight_in, preferred_element_type=f32) + bias_in  51.1 us
    convert_element_type x1, other arithmetic, fast(): keys = turn(k_part, tables).astype(bf16)  45.9 us
    reduce_scatter x4, waiting for transfers between devices, scatter_sum(): part = lax.psum_scatter(terms, 'fsdp', scatter_dimension=0, tiled=True)  44.4 us
    unnamed x1, blocking collectives  39.1 us
    ppermute x3, waiting for transfers between devices, fast(): xs.append(lax.ppermute(xs[-1], 'ctx', ring))  38.8 us
  transfers between devices with their start and end apart: 24, of which 15 were waited for; matrix products, arithmetic and copies ran while one was open for 43% of the time, Pallas kernels for 18%

profile of v1, /device:TPU:0, one launch (start us, length us, event | category | flops | bytes accessed | tf_op | source)
XLA Modules:
  0.0 914.1 jit_solution(16058595817760260583)
XLA Ops:
  13.9 25.2 %collective-permute-done.3 = bf16[512,1024]{1,0:T(8,128)(2,1)S(1)} collective-permute-done((bf16[512,1024]{1,0:T(8,128)(2,1)S(1)}, bf16[512,1024]{1,0:T(8,128)(2,1)S(1)}, u32[]{:S(2)}, u32[]{:S(2)}) %collective-permute-start.3) | collective-permute-done | bytes 1048608 | tf_op jit(solution)/shard_map/ppermute | solution.py:243
  42.5 9.2 %all-gather.1 = bf16[8,1,1536]{2,1,0:T(2,128)(2,1)S(1)} all-gather(bf16[1,1,1536]{2,1,0:T(2,128)(2,1)S(1)} %reshape.246), channel_id=2, replica_groups=mesh['fsdp'=8,'ctx'=4] {'fsdp'}, dimensions={0}, use_global_device_ids=true | all-gather | bytes 27648 | tf_op jit(solution)/shard_map/all_gather | solution.py:246
  51.7 13.6 %collective-permute-done.4 = bf16[512,1024]{1,0:T(8,128)(2,1)} collective-permute-done((bf16[512,1024]{1,0:T(8,128)(2,1)S(1)}, bf16[512,1024]{1,0:T(8,128)(2,1)}, u32[]{:S(2)}, u32[]{:S(2)}) %collective-permute-start.4) | collective-permute-done | bytes 1048608 | tf_op jit(solution)/shard_map/ppermute | solution.py:243
  66.1 24.8 %collective-permute-done.1 = s32[512]{0:T(512)S(1)} collective-permute-done((s32[512]{0:T(512)S(1)}, s32[512]{0:T(512)S(1)}, u32[]{:S(2)}, u32[]{:S(2)}) %collective-permute-start.1) | collective-permute-done | bytes 2080 | tf_op jit(solution)/shard_map/ppermute | solution.py:244
  104.5 9.5 %fusion.10 = f32[2560]{0:T(1024)S(1)} fusion(f32[2560]{0:T(1024)S(1)} %broadcast_multiply_fusion.1, bf16[512,1024]{1,0:T(8,128)(2,1)} %collective-permute-done.5, bf16[512,1024]{1,0:T(8,128)(2,1)} %collective-permute-done.4, bf16[512,1024]{1,0:T(8,128)(2,1)S(1)} %collective-permute-done.3, bf16[1024,1024]{1,0:T(8,128)(2,1)S(1)} %bitcast.121), kind=kLoop, calls=%fused_computation.27 | loop fusion | flops 28833280 | bytes 5263360 | tf_op jit(solution)/shard_map/reduce_sum | solution.py:28
  114.0 7.5 fusion.13
  153.7 45.9 %fusion.17 = (bf16[2560,1024]{1,0:T(8,128)(2,1)}, f32[2560,1024]{1,0:T(8,128)}, f32[2560,1024]{1,0:T(8,128)}, f32[2560,1024]{1,0:T(8,128)}) fusion(f32[2560,8]{1,0:T(8,128)} %get-tuple-element.37, f32[2560,1016]{1,0:T(8,128)} %get-tuple-element.39, f32[2560,1016]{1,0:T(8,128)S(1)} %get-tuple-element.38, f32[2560,8]{1,0:T(8,128)S(1)} %get-tuple-element.36, ...), kind=kLoop, calls=%fused_computation.35 | loop fusion | flops 31457280 | bytes 68174848 | tf_op jit(solution)/shard_map/convert_element_type | solution.py:268
  199.6 10.2 %fusion.48.q_ref = bf16[1024,1024]{1,0:T(8,128)(2,1)} fusion(f32[1024,8]{1,0:T(8,128)} %get-tuple-element.53, f32[1024,1016]{1,0:T(8,128)} %get-tuple-element.55, f32[1024,1016]{1,0:T(8,128)} %get-tuple-element.54, f32[1024,8]{1,0:T(8,128)} %get-tuple-element.52, f32[1024,1024]{1,0:T(8,128)S(1)} %broadcast_add_fusion, f32[2560,1024]{1,0:T(8,128)} %get-tuple-element.70, ...), kind=kLoop, calls=%fused_computation.91 | loop fusion | flops 9437184 | bytes 27262976 | tf_op jit(solution)/shard_map/convert_element_type | solution.py:266
  209.8 10.3 %add_convert_fusion.1.v_ref = bf16[2560,1024]{1,0:T(8,128)(2,1)} fusion(bf16[2560,1024]{1,0:T(8,128)(2,1)} %fusion.13, f32[1024]{0:T(1024)S(1)} %get-tuple-element.72, bf16[1024,3072]{1,0:T(8,128)(2,1)} %all-gather.7.cloned.1.call-done), kind=kOutput, calls=%fused_computation.37 | convolution fusion | flops 5373952000 | bytes 12587008 | tf_op jit(solution)/shard_map/dot_general | solution.py:269
  220.1 163.9 %attention.1 = (bf16[1024,1024]{1,0:T(8,128)(2,1)}, f32[1024,1024]{1,0:T(8,128)}, bf16[2560,1024]{1,0:T(8,128)(2,1)}, bf16[2560,1024]{1,0:T(8,128)(2,1)}) custom-call(f32[4,8]{1,0:T(4,128)} %maximum_maximum_fusion.1.kind_ref, bf16[1024,1024]{1,0:T(8,128)(2,1)} %fusion.48.q_ref, bf16[1024,1024]{1,0:T(8,128)(2,1)} %fusion.68.do_ref, ...), custom_call_target="tpu_custom_call" | custom-call | tf_op jit(solution)/shard_map/attention/pallas_call | solution.py:191
  393.9 19.9 %collective-permute-done.6 = bf16[512,1024]{1,0:T(8,128)(2,1)S(1)} collective-permute-done((bf16[512,1024]{1,0:T(8,128)(2,1)S(1)}, bf16[512,1024]{1,0:T(8,128)(2,1)S(1)}, u32[]{:S(2)}, u32[]{:S(2)}) %collective-permute-start.6) | collective-permute-done | bytes 1048608 | tf_op jit(solution)/shard_map/ppermute | solution.py:307
  427.2 9.2 %collective-permute-done.9 = bf16[512,1024]{1,0:T(8,128)(2,1)S(1)} collective-permute-done((bf16[512,1024]{1,0:T(8,128)(2,1)}, bf16[512,1024]{1,0:T(8,128)(2,1)S(1)}, u32[]{:S(2)}, u32[]{:S(2)}) %collective-permute-start.9) | collective-permute-done | bytes 1048608 | tf_op jit(solution)/shard_map/ppermute | solution.py:308
  442.2 16.6 %collective-permute-done.7 = bf16[512,1024]{1,0:T(8,128)(2,1)} collective-permute-done((bf16[512,1024]{1,0:T(8,128)(2,1)}, bf16[512,1024]{1,0:T(8,128)(2,1)}, u32[]{:S(2)}, u32[]{:S(2)}) %collective-permute-start.7) | collective-permute-done | bytes 1048608 | tf_op jit(solution)/shard_map/ppermute | solution.py:307
  470.0 11.2 %collective-permute-done.10 = bf16[512,1024]{1,0:T(8,128)(2,1)S(1)} collective-permute-done((bf16[512,1024]{1,0:T(8,128)(2,1)S(1)}, bf16[512,1024]{1,0:T(8,128)(2,1)S(1)}, u32[]{:S(2)}, u32[]{:S(2)}) %collective-permute-start.10) | collective-permute-done | bytes 1048608 | tf_op jit(solution)/shard_map/ppermute | solution.py:308
  488.2 15.4 %collective-permute-done.8 = bf16[512,1024]{1,0:T(8,128)(2,1)S(1)} collective-permute-done((bf16[512,1024]{1,0:T(8,128)(2,1)S(1)}, bf16[512,1024]{1,0:T(8,128)(2,1)S(1)}, u32[]{:S(2)}, u32[]{:S(2)}) %collective-permute-start.8) | collective-permute-done | bytes 1048608 | tf_op jit(solution)/shard_map/ppermute | solution.py:307
  509.8 17.0 %fusion.51 = (bf16[1024,1024]{1,0:T(8,128)(2,1)}, bf16[1024,1024]{1,0:T(8,128)(2,1)}) fusion(f32[1024,8]{1,0:T(8,128)S(1)} %get-tuple-element.45, f32[1024,1016]{1,0:T(8,128)} %get-tuple-element.47, f32[1024,1016]{1,0:T(8,128)} %get-tuple-element.46, f32[1024,8]{1,0:T(8,128)S(1)} %get-tuple-element.44, f32[2560,1024]{1,0:T(8,128)} %get-tuple-element.70, ...), kind=kLoop, calls=%fused_computation.96 | loop fusion | flops 18874368 | bytes 41943040 | tf_op jit(solution)/shard_map/convert.7
  528.8 19.5 %fusion.102 = (f32[1024]{0:T(1024)}, f32[1024]{0:T(1024)}, f32[1024]{0:T(1024)S(1)}, f32[1024,1024]{1,0:T(8,128)}) fusion(f32[1024]{0:T(1024)S(1)} %get-tuple-element.67, f32[1024]{0:T(1024)S(1)} %broadcast_multiply_fusion.2, bf16[1,1024,1024]{2,1,0:T(8,128)(2,1)S(1)} %copy-done, bf16[1024,3072]{1,0:T(8,128)(2,1)} %all-gather.7.cloned.1.call-done, ...), kind=kOutput, calls=%fused_computation.182 | convolution fusion | flops 6476002304 | bytes 18894848 | tf_op jit(solution)/shard_map/re,de->rd/dot_general | solution.py:322
  548.3 15.3 %convolution_convert_fusion.2 = bf16[1024,3072]{1,0:T(8,128)(2,1)} fusion(bf16[2560,1024]{1,0:T(8,128)(2,1)} %fusion.13, bf16[512,1024]{1,0:T(8,128)(2,1)} %get-tuple-element.43, bf16[512,1024]{1,0:T(8,128)(2,1)S(1)} %add_convert_fusion.2, bf16[1024,1024]{1,0:T(8,128)(2,1)S(1)} %copy-done.7, bf16[1024,1024]{1,0:T(8,128)(2,1)S(1)} %copy-done.5), kind=kOutput, calls=%fused_computation.62 | convolution fusion | flops 6470762496 | bytes 14680064 | tf_op jit(solution)/shard_map/rd,re->de/dot_general | solution.py:319
  564.3 51.1 %multiply_convert_fusion = (bf16[1024,4096]{1,0:T(8,128)(2,1)}, f32[1024,4096]{1,0:T(8,128)}, f32[1024,4096]{1,0:T(8,128)}) fusion(f32[4096]{0:T(1024)S(1)} %bitcast.129, bf16[1024,4096]{1,0:T(8,128)(2,1)} %all-gather.11.cloned.1.call-done, f32[1024]{0:T(1024)S(1)} %copy-done.21, f32[1024]{0:T(1024)S(1)} %copy-done.16, f32[1024]{0:T(1024)S(1)} %fusion.89, ...), kind=kOutput, calls=%fused_computation.4 | convolution fusion | flops 8873050112 | bytes 52461568 | tf_op jit(solution)/shard_map/dot_general | solution.py:275
  615.4 24.1 %convert_reduce_fusion = (f32[4096]{0:T(1024)S(1)}, bf16[1024,4096]{1,0:T(8,128)(2,1)}) fusion(f32[1024,4096]{1,0:T(8,128)} %get-tuple-element.33, bf16[4096,1024]{1,0:T(8,128)(2,1)} %all-gather.13.cloned.1.call-done, bf16[1,1024,1024]{2,1,0:T(8,128)(2,1)} %param.16, f32[1024,4096]{1,0:T(8,128)} %get-tuple-element.78, f32[4096]{0:T(1024)S(1)} %bitcast.130), kind=kOutput, calls=%fused_computation.2 | convolution fusion | flops 8661233664 | bytes 52461568 | tf_op jit(solution)/shard_map/rd,fd->rf/dot_general | solution.py:280
  639.5 14.9 %convolution_convert_fusion.1 = bf16[1024,4096]{1,0:T(8,128)(2,1)} fusion(bf16[1024,4096]{1,0:T(8,128)(2,1)} %get-tuple-element.81, f32[1024]{0:T(1024)S(1)} %copy-done.21, f32[1024]{0:T(1024)S(1)} %copy-done.16, f32[1024]{0:T(1024)S(1)} %fusion.89, f32[1024]{0:T(1024)S(1)} %broadcast_multiply_fusion.2, bf16[1,1024,1024]{2,1,0:T(8,128)(2,1)S(1)} %copy-done), kind=kOutput, calls=%fused_computation.39 | convolution fusion | flops 8600420352 | bytes 18890752 | tf_op jit(solution)/shard_map/rd,rf->df/dot_general | solution.py:283
  655.2 15.2 %convolution_convert_fusion = bf16[4096,1024]{1,0:T(8,128)(2,1)} fusion(bf16[1024,4096]{1,0:T(8,128)(2,1)} %get-tuple-element.32, bf16[1,1024,1024]{2,1,0:T(8,128)(2,1)} %param.16), kind=kOutput, calls=%fused_computation.38 | convolution fusion | flops 8594128896 | bytes 18874368 | tf_op jit(solution)/shard_map/rf,rd->fd/dot_general | solution.py:279
  677.5 20.6 %convert_reduce_fusion.2 = f32[3072]{0:T(1024)S(1)} fusion(bf16[512,1024]{1,0:T(8,128)(2,1)S(1)} %copy-done.11, bf16[512,1024]{1,0:T(8,128)(2,1)S(1)} %copy-done.10, bf16[1024,1024]{1,0:T(8,128)(2,1)S(1)} %copy-done.8, bf16[1024,1024]{1,0:T(8,128)(2,1)S(1)} %copy-done.6), kind=kLoop, calls=%fused_computation.24 | loop fusion | flops 28308480 | bytes 6303744 | tf_op jit(solution)/shard_map/reduce_sum | solution.py:321
  698.4 15.6 %fusion.101 = (f32[1024]{0:T(1024)S(1)}, f32[1024]{0:T(1024)S(1)}, f32[1024,1024]{1,0:T(8,128)}) fusion(f32[1024]{0:T(1024)S(1)} %copy-done.16, f32[1024]{0:T(1024)S(1)} %broadcast_multiply_fusion.2, bf16[1,1024,1024]{2,1,0:T(8,128)(2,1)S(1)} %copy-done, bf16[1024,4096]{1,0:T(8,128)(2,1)} %get-tuple-element.81, ...), kind=kOutput, calls=%fused_computation.181 | convolution fusion | flops 8596224000 | bytes 23085056 | tf_op jit(solution)/shard_map/rf,df->rd/dot_general | solution.py:285
  713.9 13.1 %reduce-scatter.17.cloned.1.call-done = bf16[128,4096]{1,0:T(8,128)(2,1)} async-done(((bf16[1024,4096]{1,0:T(8,128)(2,1)}), bf16[128,4096]{1,0:T(8,128)(2,1)}) %reduce-scatter.17.cloned.1.call-update) | async-done | bytes 1048592 | tf_op jit(solution)/shard_map/reduce_scatter | solution.py:228
  738.6 10.4 %reduce-scatter.15.cloned.1.call-done = bf16[32,1024]{1,0:T(8,128)(2,1)} async-done(((bf16[128,1024]{1,0:T(8,128)(2,1)}), bf16[32,1024]{1,0:T(8,128)(2,1)}) %reduce-scatter.15.cloned.1.call-update) | async-done | bytes 65552 | tf_op jit(solution)/shard_map/reduce_scatter | solution.py:229
  750.5 39.1 %all-reduce = f32[32,384]{1,0:T(8,128)S(1)} all-reduce(f32[32,384]{1,0:T(8,128)S(1)} %concatenate.72), channel_id=3, replica_groups=mesh['fsdp'=8,'ctx'=4] {'fsdp','ctx'}, use_global_device_ids=true, to_apply=%region_15.16.clone | all-reduce | flops 12288 | bytes 98304
  791.4 31.3 %reduce-scatter.21.cloned.1.call-done = bf16[512,1024]{1,0:T(8,128)(2,1)} async-done(((bf16[4096,1024]{1,0:T(8,128)(2,1)}), bf16[512,1024]{1,0:T(8,128)(2,1)}) %reduce-scatter.21.cloned.1.call-update) | async-done | bytes 1048592 | tf_op jit(solution)/shard_map/reduce_scatter | solution.py:228
  822.7 15.4 %fusion.52 = bf16[1,1024,1024]{2,1,0:T(8,128)(2,1)} fusion(f32[1024,1024]{1,0:T(8,128)} %fusion.113, f32[1024]{0:T(1024)S(1)} %copy-done.20, bf16[1024,4096]{1,0:T(8,128)(2,1)} %get-tuple-element.32, bf16[4096,1024]{1,0:T(8,128)(2,1)} %all-gather.13.cloned.1.call-done, bf16[1,1024,1024]{2,1,0:T(8,128)(2,1)S(1)} %copy-done), kind=kOutput, calls=%fused_computation.100 | convolution fusion | flops 8595177472 | bytes 25169920 | tf_op jit(solution)/shard_map/dot_general | solution.py:277
  838.0 10.2 %reduce-scatter.11.cloned.1.call-done = bf16[32,3072]{1,0:T(8,128)(2,1)} async-done(((bf16[128,3072]{1,0:T(8,128)(2,1)}), bf16[32,3072]{1,0:T(8,128)(2,1)}) %reduce-scatter.11.cloned.1.call-update) | async-done | bytes 196624 | tf_op jit(solution)/shard_map/reduce_scatter | solution.py:229
  849.9 27.1 %reduce-scatter.19.cloned.1.call-done = bf16[32,4096]{1,0:T(8,128)(2,1)} async-done(((bf16[128,4096]{1,0:T(8,128)(2,1)}), bf16[32,4096]{1,0:T(8,128)(2,1)}) %reduce-scatter.19.cloned.1.call-update) | async-done | bytes 262160 | tf_op jit(solution)/shard_map/reduce_scatter | solution.py:229
  878.9 26.2 %reduce-scatter.23.cloned.1.call-done = bf16[128,1024]{1,0:T(8,128)(2,1)} async-done(((bf16[512,1024]{1,0:T(8,128)(2,1)}), bf16[128,1024]{1,0:T(8,128)(2,1)}) %reduce-scatter.23.cloned.1.call-update) | async-done | bytes 262160 | tf_op jit(solution)/shard_map/reduce_scatter | solution.py:229
  (194 shorter events, 136.6 us)
Async XLA Ops:
  7.2 91.8 %copy-start = (bf16[1,1024,1024]{2,1,0:T(8,128)(2,1)S(1)}, bf16[1,1024,1024]{2,1,0:T(8,128)(2,1)}, u32[]{:S(2)}) copy-start(bf16[1,1024,1024]{2,1,0:T(8,128)(2,1)} %param.15) | copy-start | bytes 6291460
  7.2 83.7 %copy-start.19 = (s32[1,1024]{1,0:T(1,128)S(1)}, s32[1,1024]{1,0:T(1,128)}, u32[]{:S(2)}) copy-start(s32[1,1024]{1,0:T(1,128)} %param.17) | copy-start | bytes 12292
  7.2 34.8 %copy-start.29 = (bf16[128]{0:T(256)(128)(2,1)S(1)}, bf16[128]{0:T(256)(128)(2,1)}, u32[]{:S(2)}) copy-start(bf16[128]{0:T(256)(128)(2,1)} %param.24) | copy-start | bytes 772
  7.3 35.0 %copy-start.30 = (bf16[128]{0:T(256)(128)(2,1)S(1)}, bf16[128]{0:T(256)(128)(2,1)}, u32[]{:S(2)}) copy-start(bf16[128]{0:T(256)(128)(2,1)} %param.25) | copy-start | bytes 772
  7.3 35.3 %copy-start.24 = (bf16[512]{0:T(512)(128)(2,1)S(1)}, bf16[512]{0:T(512)(128)(2,1)}, u32[]{:S(2)}) copy-start(bf16[512]{0:T(512)(128)(2,1)} %param.27) | copy-start | bytes 3076
  7.3 114.3 %all-gather.9.cloned.1.call-start = ((), (), s32[]{:S(2)}) async-start(), calls=%async_computation.9 | async-start | bytes 2359296 | tf_op jit(solution)/shard_map/all_gather | solution.py:256
  8.0 119.5 %all-gather.7.cloned.1.call-start = ((), (), s32[]{:S(2)}) async-start(), calls=%async_computation.8 | async-start | bytes 7077888 | tf_op jit(solution)/shard_map/all_gather | solution.py:253
  8.8 554.9 %all-gather.11.cloned.1.call-start = ((), (), s32[]{:S(2)}) async-start(), calls=%async_computation.10 | async-start | bytes 9437184 | tf_op jit(solution)/shard_map/all_gather | solution.py:254
  9.5 605.9 %all-gather.13.cloned.1.call-start = ((), (), s32[]{:S(2)}) async-start(), calls=%async_computation.11 | async-start | bytes 9437184 | tf_op jit(solution)/shard_map/all_gather | solution.py:255
  10.8 28.3 %collective-permute-start.3 = (bf16[512,1024]{1,0:T(8,128)(2,1)S(1)}, bf16[512,1024]{1,0:T(8,128)(2,1)S(1)}, u32[]{:S(2)}, u32[]{:S(2)}) collective-permute-start(bf16[512,1024]{1,0:T(8,128)(2,1)S(1)} %slice_bitcast_fusion), channel_id=1, source_target_pairs={{0,1},{1,2},{2,3},{3,0},{4,5},{5,6},{6,7},{7,4},{8,9},{9,10},{10,1... | collective-permute-start | bytes 3145736 | tf_op jit(solution)/shard_map/ppermute | solution.py:243
  39.1 26.3 %collective-permute-start.4 = (bf16[512,1024]{1,0:T(8,128)(2,1)S(1)}, bf16[512,1024]{1,0:T(8,128)(2,1)}, u32[]{:S(2)}, u32[]{:S(2)}) collective-permute-start(bf16[512,1024]{1,0:T(8,128)(2,1)S(1)} %collective-permute-done.3), channel_id=1, source_target_pairs={{0,1},{1,2},{2,3},{3,0},{4,5},{5,6},{6,7},{7,4},{8,9},{9,10},{10,1... | collective-permute-start | bytes 3145736 | tf_op jit(solution)/shard_map/ppermute | solution.py:243
  39.8 26.2 %collective-permute-start = (s32[512]{0:T(512)S(1)}, s32[512]{0:T(512)S(1)}, u32[]{:S(2)}, u32[]{:S(2)}) collective-permute-start(s32[512]{0:T(512)S(1)} %bitcast.133), channel_id=1, source_target_pairs={{0,1},{1,2},{2,3},{3,0},{4,5},{5,6},{6,7},{7,4},{8,9},{9,10},{10,1... | collective-permute-start | bytes 6152 | tf_op jit(solution)/shard_map/ppermute | solution.py:244
  41.1 613.4 %reduce-scatter.13.cloned.1.call-start = ((), (), s32[]{:S(2)}) async-start(), calls=%async_computation.14 | async-start | bytes 2359296 | tf_op jit(solution)/shard_map/reduce_scatter | solution.py:228
  65.4 33.6 %collective-permute-start.5 = (bf16[512,1024]{1,0:T(8,128)(2,1)}, bf16[512,1024]{1,0:T(8,128)(2,1)}, u32[]{:S(2)}, u32[]{:S(2)}) collective-permute-start(bf16[512,1024]{1,0:T(8,128)(2,1)} %collective-permute-done.4), channel_id=1, source_target_pairs={{0,1},{1,2},{2,3},{3,0},{4,5},{5,6},{6,7},{7,4},{8,9},{9,10},{10,1... | collective-permute-start | bytes 3145736 | tf_op jit(solution)/shard_map/ppermute | solution.py:243
  66.0 462.8 %copy-start.14 = (f32[1024]{0:T(1024)}, f32[1024]{0:T(1024)S(1)}, u32[]{:S(2)}) copy-start(f32[1024]{0:T(1024)S(1)} %get-tuple-element.67) | copy-start | bytes 12292
  66.0 24.9 %collective-permute-start.1 = (s32[512]{0:T(512)S(1)}, s32[512]{0:T(512)S(1)}, u32[]{:S(2)}, u32[]{:S(2)}) collective-permute-start(s32[512]{0:T(512)S(1)} %collective-permute-done), channel_id=1, source_target_pairs={{0,1},{1,2},{2,3},{3,0},{4,5},{5,6},{6,7},{7,4},{8,9},{9,10},{10,1... | collective-permute-start | bytes 6152 | tf_op jit(solution)/shard_map/ppermute | solution.py:244
  90.9 5.4 collective-permute-start.2
  387.1 26.6 %collective-permute-start.6 = (bf16[512,1024]{1,0:T(8,128)(2,1)S(1)}, bf16[512,1024]{1,0:T(8,128)(2,1)S(1)}, u32[]{:S(2)}, u32[]{:S(2)}) collective-permute-start(bf16[512,1024]{1,0:T(8,128)(2,1)S(1)} %get-tuple-element.40), channel_id=1, source_target_pairs={{0,3},{1,0},{2,1},{3,2},{4,7},{5,4},{6,5},{7,6},{8,11},{9,8},{10,9... | collective-permute-start | bytes 3145736 | tf_op jit(solution)/shard_map/ppermute | solution.py:307
  393.6 42.8 %collective-permute-start.9 = (bf16[512,1024]{1,0:T(8,128)(2,1)}, bf16[512,1024]{1,0:T(8,128)(2,1)S(1)}, u32[]{:S(2)}, u32[]{:S(2)}) collective-permute-start(bf16[512,1024]{1,0:T(8,128)(2,1)} %get-tuple-element.42), channel_id=1, source_target_pairs={{0,3},{1,0},{2,1},{3,2},{4,7},{5,4},{6,5},{7,6},{8,11},{9,8},{10,9... | collective-permute-start | bytes 3145736 | tf_op jit(solution)/shard_map/ppermute | solution.py:308
  416.3 42.4 %collective-permute-start.7 = (bf16[512,1024]{1,0:T(8,128)(2,1)}, bf16[512,1024]{1,0:T(8,128)(2,1)}, u32[]{:S(2)}, u32[]{:S(2)}) collective-permute-start(bf16[512,1024]{1,0:T(8,128)(2,1)} %add_convert_fusion.6), channel_id=1, source_target_pairs={{0,3},{1,0},{2,1},{3,2},{4,7},{5,4},{6,5},{7,6},{8,11},{9,8},{10,9... | collective-permute-start | bytes 3145736 | tf_op jit(solution)/shard_map/ppermute | solution.py:307
  424.5 273.8 %reduce-scatter.9.cloned.1.call-start = ((), (), s32[]{:S(2)}) async-start(), calls=%async_computation.12 | async-start | bytes 7077888 | tf_op jit(solution)/shard_map/reduce_scatter | solution.py:228
  437.9 43.2 %collective-permute-start.10 = (bf16[512,1024]{1,0:T(8,128)(2,1)S(1)}, bf16[512,1024]{1,0:T(8,128)(2,1)S(1)}, u32[]{:S(2)}, u32[]{:S(2)}) collective-permute-start(bf16[512,1024]{1,0:T(8,128)(2,1)S(1)} %add_convert_fusion.4), channel_id=1, source_target_pairs={{0,3},{1,0},{2,1},{3,2},{4,7},{5,4},{6,5},{7,6},{8,11},{9,8},{10,9... | collective-permute-start | bytes 3145736 | tf_op jit(solution)/shard_map/ppermute | solution.py:308
  460.7 42.9 %collective-permute-start.8 = (bf16[512,1024]{1,0:T(8,128)(2,1)S(1)}, bf16[512,1024]{1,0:T(8,128)(2,1)S(1)}, u32[]{:S(2)}, u32[]{:S(2)}) collective-permute-start(bf16[512,1024]{1,0:T(8,128)(2,1)S(1)} %add_convert_fusion.5), channel_id=1, source_target_pairs={{0,3},{1,0},{2,1},{3,2},{4,7},{5,4},{6,5},{7,6},{8,11},{9,8},{10,9... | collective-permute-start | bytes 3145736 | tf_op jit(solution)/shard_map/ppermute | solution.py:307
  470.0 35.3 %copy-start.1 = (f32[512,1024]{1,0:T(8,128)S(1)}, f32[512,1024]{1,0:T(8,128)}, u32[]{:S(2)}) copy-start(f32[512,1024]{1,0:T(8,128)} %get-tuple-element.41) | copy-start | bytes 6291460
  483.7 43.1 %collective-permute-start.11 = (bf16[512,1024]{1,0:T(8,128)(2,1)}, bf16[512,1024]{1,0:T(8,128)(2,1)}, u32[]{:S(2)}, u32[]{:S(2)}) collective-permute-start(bf16[512,1024]{1,0:T(8,128)(2,1)} %add_convert_fusion.3), channel_id=1, source_target_pairs={{0,3},{1,0},{2,1},{3,2},{4,7},{5,4},{6,5},{7,6},{8,11},{9,8},{10,9... | collective-permute-start | bytes 3145736 | tf_op jit(solution)/shard_map/ppermute | solution.py:308
  563.6 163.4 %reduce-scatter.17.cloned.1.call-start = ((), (), s32[]{:S(2)}) async-start(), calls=%async_computation.16 | async-start | bytes 9437184 | tf_op jit(solution)/shard_map/reduce_scatter | solution.py:228
  654.4 94.6 %reduce-scatter.15.cloned.1.call-start = ((), (), s32[]{:S(2)}) async-start(), calls=%async_computation.15 | async-start | bytes 327680 | tf_op jit(solution)/shard_map/reduce_scatter | solution.py:229
  655.2 167.5 %reduce-scatter.21.cloned.1.call-start = ((), (), s32[]{:S(2)}) async-start(), calls=%async_computation.18 | async-start | bytes 9437184 | tf_op jit(solution)/shard_map/reduce_scatter | solution.py:228
  670.5 177.8 %reduce-scatter.11.cloned.1.call-start = ((), (), s32[]{:S(2)}) async-start(), calls=%async_computation.13 | async-start | bytes 983040 | tf_op jit(solution)/shard_map/reduce_scatter | solution.py:229
  698.3 178.8 %reduce-scatter.19.cloned.1.call-start = ((), (), s32[]{:S(2)}) async-start(), calls=%async_computation.17 | async-start | bytes 1310720 | tf_op jit(solution)/shard_map/reduce_scatter | solution.py:229
  727.1 178.0 %reduce-scatter.23.cloned.1.call-start = ((), (), s32[]{:S(2)}) async-start(), calls=%async_computation.19 | async-start | bytes 1310720 | tf_op jit(solution)/shard_map/reduce_scatter | solution.py:229
  733.8 88.9 %copy-start.20 = (f32[1024]{0:T(1024)S(1)}, f32[1024]{0:T(1024)}, u32[]{:S(2)}) copy-start(f32[1024]{0:T(1024)} %get-tuple-element.64) | copy-start | bytes 12292
  (26 other events, 423.2 us)
Sparse Core Ops, SparseCore 0:
  10.0 30.5 all-gather.8
  42.5 45.5 all-gather.6
  90.0 54.3 all-gather.10
  146.2 54.3 all-gather.12
  424.6 38.6 reduce-scatter.12
  563.8 62.9 reduce-scatter.8
  654.5 72.4 reduce-scatter.16
  729.4 19.5 reduce-scatter.14
  752.5 70.1 reduce-scatter.20
  824.9 23.2 reduce-scatter.10
  850.6 26.3 reduce-scatter.18
  879.2 25.7 reduce-scatter.22

commit v2 on v0

--- a/solution.py
+++ b/solution.py
@@ -4,11 +4,22 @@
 import jax
 import jax.numpy as jnp
 from jax import lax
+from jax.experimental import pallas as pl
+from jax.experimental.pallas import tpu as pltpu
 from jax.sharding import PartitionSpec as P
 
 HEADS = 16
 HD = 64
 ROT = 16
+CLEN = 256
+QB = 256
+RB = 256
+PAIR = 2 * HD
+bf16 = jnp.bfloat16
+f32 = jnp.float32
+NN = (((1,), (0,)), ((), ()))
+NT = (((1,), (1,)), ((), ()))
+TN = (((0,), (0,)), ((), ()))
 
 
 NORM_EPS = 1e-05
@@ -71,7 +82,576 @@
     return (probs.astype(jnp.bfloat16), grad_scores)
 
 
-def local(
+def mm(a, b, dims):
+    return lax.dot_general(a, b, dims, preferred_element_type=f32)
+
+
+def row_stats(x):
+    average = jnp.mean(x, axis=1, keepdims=True)
+    centered = x - average
+    return centered, lax.rsqrt(jnp.mean(centered * centered, axis=1, keepdims=True) + NORM_EPS)
+
+
+def norm_rows(x, scaling, offset):
+    centered, inverse = row_stats(x)
+    return (centered * inverse * scaling + offset).astype(bf16)
+
+
+def norm_back(x, grad, scaling):
+    centered, inverse = row_stats(x)
+    unit = centered * inverse
+    e = grad * scaling
+    inner = e - jnp.mean(e, axis=1, keepdims=True) - unit * jnp.mean(e * unit, axis=1, keepdims=True)
+    return inverse * inner, grad * unit
+
+
+def col_sum(a):
+    return jnp.sum(a, axis=0, keepdims=True)
+
+
+def vmem(*shape, dtype=f32):
+    return pltpu.VMEM(shape, dtype)
+
+
+def params():
+    return pltpu.CompilerParams(vmem_limit_bytes=60 << 20)
+
+
+FC = 512
+ROOT = math.sqrt(0.5)
+DENS = 1.0 / math.sqrt(2.0 * math.pi)
+
+
+def mlp_kernel(x_ref, c_ref, gain_ref, shift_ref, win_ref, bin_ref, wout_ref,
+               out_ref, gin_ref, dwin_ref, dwout_ref, dbin_ref, dbout_ref, dgain_ref, dshift_ref,
+               h_ref, act_ref, gp_ref, gh_ref):
+    step = pl.program_id(0)
+    rows = x_ref.shape[0]
+    blocks = [slice(r, r + RB) for r in range(0, rows, RB)]
+
+    @pl.when(step == 0)
+    def _():
+        for r in blocks:
+            h_ref[r, :] = norm_rows(x_ref[r, :].astype(f32), gain_ref[...], shift_ref[...])
+            out_ref[r, :] = jnp.zeros((RB, out_ref.shape[1]), f32)
+            gh_ref[r, :] = jnp.zeros((RB, gh_ref.shape[1]), f32)
+
+    dbin = jnp.zeros((1, FC), f32)
+    for r in blocks:
+        pre = mm(h_ref[r, :], win_ref[...], NN) + bin_ref[...]
+        phi = 0.5 + 0.5 * lax.erf(pre * ROOT)
+        act_ref[r, :] = (pre * phi).astype(bf16)
+        gp = phi + pre * (DENS * jnp.exp(-0.5 * (pre * pre)))
+        gact = mm(c_ref[r, :], wout_ref[...], NT)
+        gpre = (gact * gp).astype(bf16)
+        gp_ref[r, :] = gpre
+        dbin = dbin + col_sum(gpre.astype(f32))
+    for r in blocks:
+        out_ref[r, :] += mm(act_ref[r, :], wout_ref[...], NN)
+        gh_ref[r, :] += mm(gp_ref[r, :], win_ref[...], NT)
+    dwout_ref[...] = mm(act_ref[...], c_ref[...], TN).astype(bf16)
+    dwin_ref[...] = mm(h_ref[...], gp_ref[...], TN).astype(bf16)
+    dbin_ref[...] = dbin
+
+    @pl.when(step == pl.num_programs(0) - 1)
+    def _():
+        dgain = jnp.zeros(dgain_ref.shape, f32)
+        dshift = jnp.zeros(dshift_ref.shape, f32)
+        dbout = jnp.zeros(dbout_ref.shape, f32)
+        for r in blocks:
+            grad = gh_ref[r, :]
+            back, scaled = norm_back(x_ref[r, :].astype(f32), grad, gain_ref[...])
+            c = c_ref[r, :].astype(f32)
+            gin_ref[r, :] = back + c
+            dgain += col_sum(scaled)
+            dshift += col_sum(grad)
+            dbout += col_sum(c)
+        dgain_ref[...] = dgain
+        dshift_ref[...] = dshift
+        dbout_ref[...] = dbout
+
+
+def mlp(x, c, gain, shift, weight_in, bias_in, weight_out):
+    rows, width = x.shape
+    ff = weight_in.shape[1]
+    whole = pl.BlockSpec((rows, width), lambda j: (0, 0))
+    line = pl.BlockSpec((1, width), lambda j: (0, 0))
+    s = jax.ShapeDtypeStruct
+    return pl.pallas_call(
+        mlp_kernel,
+        grid=(ff // FC,),
+        in_specs=[whole, whole, line, line, pl.BlockSpec((width, FC), lambda j: (0, j)),
+                  pl.BlockSpec((1, FC), lambda j: (0, j)), pl.BlockSpec((FC, width), lambda j: (j, 0))],
+        out_specs=[whole, whole, pl.BlockSpec((width, FC), lambda j: (0, j)), pl.BlockSpec((FC, width), lambda j: (j, 0)),
+                   pl.BlockSpec((1, FC), lambda j: (0, j)), line, line, line],
+        out_shape=[s((rows, width), f32), s((rows, width), f32), s((width, ff), bf16), s((ff, width), bf16),
+                   s((1, ff), f32), s((1, width), f32), s((1, width), f32), s((1, width), f32)],
+        scratch_shapes=[vmem(rows, width, dtype=bf16), vmem(rows, FC, dtype=bf16), vmem(rows, FC, dtype=bf16),
+                        vmem(rows, width)],
+        compiler_params=params(),
+        cost_estimate=pl.CostEstimate(flops=12 * rows * width * ff, bytes_accessed=48 << 20, transcendentals=2 * rows * ff),
+        name="mlp",
+    )(x, c, gain.reshape(1, -1), shift.reshape(1, -1), weight_in, bias_in.reshape(1, -1), weight_out)
+
+
+def turn_lanes(u, cosine, low, high, sign):
+    half = ROT // 2
+    parts = []
+    for at in range(0, u.shape[1], PAIR):
+        g = u[:, at:at + PAIR]
+        parts.append(g * cosine + sign * (pltpu.roll(g, half, 1) * high - pltpu.roll(g, PAIR - half, 1) * low))
+    return jnp.concatenate(parts, axis=1)
+
+
+def qkv_kernel(with_q, spot_ref, x_ref, gain_ref, shift_ref, w_ref, b_ref, cos_ref, low_ref, high_ref, *outs):
+    width = x_ref.shape[1]
+    h = norm_rows(x_ref[...].astype(f32), gain_ref[...], shift_ref[...])
+    tables = (cos_ref[...], low_ref[...], high_ref[...])
+    if with_q:
+        h_ref, q_ref, k_ref, v_ref = outs
+        h_ref[...] = h
+        q = mm(h, w_ref[:, :width], NN) + b_ref[:, :width]
+        q_ref[...] = (turn_lanes(q, *tables, 1.0) * (HD ** (-0.5) / math.log(2.0))).astype(bf16)
+    else:
+        k_ref, v_ref = outs
+    k = mm(h, w_ref[:, width:2 * width], NN) + b_ref[:, width:2 * width]
+    k_ref[...] = turn_lanes(k, *tables, 1.0).astype(bf16)
+    v_ref[...] = (mm(h, w_ref[:, 2 * width:], NN) + b_ref[:, 2 * width:]).astype(bf16)
+
+
+def qkv(spots, x, gain, shift, weight, bias, tables, with_q):
+    rows, width = x.shape
+    s = jax.ShapeDtypeStruct((rows, width), bf16)
+    block = pl.BlockSpec((RB, width), lambda j, spot: (j, 0))
+    line = pl.BlockSpec((1, width), lambda j, spot: (0, 0))
+    table = pl.BlockSpec((RB, PAIR), lambda j, spot: (spot[j], 0))
+    count = 4 if with_q else 2
+    return pl.pallas_call(
+        partial(qkv_kernel, with_q),
+        grid_spec=pltpu.PrefetchScalarGridSpec(
+            num_scalar_prefetch=1,
+            grid=(rows // RB,),
+            in_specs=[block, line, line, pl.BlockSpec((width, 3 * width), lambda j, spot: (0, 0)),
+                      pl.BlockSpec((1, 3 * width), lambda j, spot: (0, 0)), table, table, table],
+            out_specs=[block] * count,
+        ),
+        out_shape=[s] * count,
+        compiler_params=params(),
+        cost_estimate=pl.CostEstimate(flops=2 * rows * width * width * (3 if with_q else 2), bytes_accessed=16 << 20,
+                                      transcendentals=0),
+        name="qkv_own" if with_q else "kv_remote",
+    )(spots, x, gain.reshape(1, -1), shift.reshape(1, -1), weight, bias.reshape(1, -1), *tables)
+
+
+def tail_kernel(groups, spot_ref, x_ref, h_ref, gain_ref, w_ref, cos_ref, low_ref, high_ref, gin_ref, *refs):
+    dq_refs, own_refs, come_refs = refs[:groups], refs[groups:2 * groups], refs[2 * groups:3 * groups]
+    grad_ref, dw_ref, db_ref, dgain_ref, dshift_ref, p_ref, gh_ref = refs[3 * groups:]
+    step = pl.program_id(0)
+    rows = x_ref.shape[0]
+    half = rows // 2
+    blocks = [slice(r, r + RB) for r in range(0, rows, RB)]
+    part = dq_refs[0].shape[1]
+
+    def put(shift):
+        for r in blocks:
+            spot = pl.ds(pl.multiple_of(spot_ref[r.start // RB] * RB, RB), RB)
+            for g in range(groups):
+                for at in range(0, part, PAIR):
+                    if shift is None:
+                        p_ref[r, g * part + at:g * part + at + PAIR] = dq_refs[g][r, at:at + PAIR]
+                        continue
+                    lanes = slice(2 * at + shift, 2 * at + shift + PAIR)
+                    t = own_refs[g][r, lanes].astype(f32)
+                    if r.start < half:
+                        t = t + come_refs[g][r, lanes].astype(f32)
+                    if shift == 0:
+                        t = turn_lanes(t, cos_ref[spot, :], low_ref[spot, :], high_ref[spot, :], -1.0)
+                    p_ref[r, g * part + at:g * part + at + PAIR] = t.astype(bf16)
+
+    @pl.when(step == 0)
+    def _():
+        put(None)
+        for r in blocks:
+            gh_ref[r, :] = mm(p_ref[r, :], w_ref[...], NT)
+
+    @pl.when(step == 1)
+    def _():
+        put(0)
+
+    @pl.when(step == 2)
+    def _():
+        put(PAIR)
+
+    @pl.when(step > 0)
+    def _():
+        for r in blocks:
+            gh_ref[r, :] += mm(p_ref[r, :], w_ref[...], NT)
+
+    dw_ref[...] = mm(h_ref[...], p_ref[...], TN).astype(bf16)
+    db = jnp.zeros(db_ref.shape, f32)
+    for r in blocks:
+        db += col_sum(p_ref[r, :].astype(f32))
+    db_ref[...] = db
+
+    @pl.when(step == 2)
+    def _():
+        dgain = jnp.zeros(dgain_ref.shape, f32)
+        dshift = jnp.zeros(dshift_ref.shape, f32)
+        for r in blocks:
+            grad = gh_ref[r, :]
+            back, scaled = norm_back(x_ref[r, :].astype(f32), grad, gain_ref[...])
+            grad_ref[r, :] = back + gin_ref[r, :]
+            dgain += col_sum(scaled)
+            dshift += col_sum(grad)
+        dgain_ref[...] = dgain
+        dshift_ref[...] = dshift
+
+
+def tail(spots, x, h, gain, weight, tables, gin, dqs, owns, comes):
+    rows, width = x.shape
+    groups = len(dqs)
+    s = jax.ShapeDtypeStruct
+
+    def full(a):
+        return pl.BlockSpec(a.shape, lambda j, spot: (0, 0))
+
+    line = pl.BlockSpec((1, width), lambda j, spot: (0, 0))
+    arrays = [*tables, gin, *dqs, *owns, *comes]
+    return pl.pallas_call(
+        partial(tail_kernel, groups),
+        grid_spec=pltpu.PrefetchScalarGridSpec(
+            num_scalar_prefetch=1,
+            grid=(3,),
+            in_specs=[full(x), full(h), line, pl.BlockSpec((width, width), lambda j, spot: (0, j))] + [full(a) for a in arrays],
+            out_specs=[full(x), pl.BlockSpec((width, width), lambda j, spot: (0, j)),
+                       pl.BlockSpec((1, width), lambda j, spot: (0, j)), line, line],
+            scratch_shapes=[vmem(rows, width, dtype=bf16), vmem(rows, width)],
+        ),
+        out_shape=[s((rows, width), f32), s((width, 3 * width), bf16), s((1, 3 * width), f32), s((1, width), f32),
+                   s((1, width), f32)],
+        compiler_params=params(),
+        cost_estimate=pl.CostEstimate(flops=12 * rows * width * width, bytes_accessed=32 << 20, transcendentals=0),
+        name="tail",
+    )(spots, x, h, gain.reshape(1, -1), weight, *arrays)
+
+
+def join_kernel(x_ref, c_ref, att_ref, w_ref, mlp_ref, b_ref, out_ref, dw_ref, acc_ref):
+    step = pl.program_id(0)
+    out = x_ref[...].astype(f32) + mm(att_ref[...], w_ref[...], NN) + mlp_ref[...] + b_ref[...]
+    out_ref[...] = out.astype(bf16)
+
+    @pl.when(step == 0)
+    def _():
+        acc_ref[...] = mm(att_ref[...], c_ref[...], TN)
+
+    @pl.when(step > 0)
+    def _():
+        acc_ref[...] += mm(att_ref[...], c_ref[...], TN)
+
+    @pl.when(step == pl.num_programs(0) - 1)
+    def _():
+        dw_ref[...] = acc_ref[...].astype(bf16)
+
+
+def join(x, c, attended, weight, mlp_out, bias):
+    rows, width = x.shape
+    s = jax.ShapeDtypeStruct
+    block = pl.BlockSpec((RB, width), lambda j: (j, 0))
+    square = pl.BlockSpec((width, width), lambda j: (0, 0))
+    return pl.pallas_call(
+        join_kernel,
+        grid=(rows // RB,),
+        in_specs=[block, block, block, square, block, pl.BlockSpec((1, width), lambda j: (0, 0))],
+        out_specs=[block, square],
+        out_shape=[s((rows, width), bf16), s((width, width), bf16)],
+        scratch_shapes=[vmem(width, width)],
+        compiler_params=params(),
+        cost_estimate=pl.CostEstimate(flops=4 * rows * width * width, bytes_accessed=16 << 20, transcendentals=0),
+        name="join",
+    )(x, c, attended, weight, mlp_out, bias.reshape(1, -1))
+
+
+def fold(x, op):
+    return op(x.reshape(x.shape[0] // 8, 8, x.shape[1]), axis=0)
+
+
+def eye(size):
+    return (lax.broadcasted_iota(jnp.int32, (size, size), 0) == lax.broadcasted_iota(jnp.int32, (size, size), 1)).astype(bf16)
+
+
+def attention_kernel(half, n, kind_ref, cos_ref, sin_ref, q_ref, do_ref, *refs):
+    k_refs, v_refs = refs[:n], refs[n:2 * n]
+    o_ref, dq_ref = refs[2 * n:2 * n + 2]
+    g_refs = refs[2 * n + 2:3 * n + 2]
+    kt_ref, vt_ref, s_ref, p_ref, ds_ref, dka_ref, dva_ref = refs[3 * n + 2:]
+    per = half // QB
+    wide = n * half
+    count = wide // QB
+    spots = [(0, c * QB) for c in range(per)] + [(s, c * QB) for s in range(1, n) for c in range(per)]
+
+    ident = eye(PAIR)
+    for refs_in, out in ((k_refs, kt_ref), (v_refs, vt_ref)):
+        for c, (s, at) in enumerate(spots):
+            out[:, c * QB:(c + 1) * QB] = refs_in[s][at:at + QB, :].T
+        for c in range(per):
+            out[:, wide + c * QB:wide + (c + 1) * QB] = refs_in[0][half + c * QB:half + (c + 1) * QB, :].T
+    dka_ref[...] = jnp.zeros_like(dka_ref)
+    dva_ref[...] = jnp.zeros_like(dva_ref)
+
+
+    def block(qb, carry):
+        own = pl.ds(pl.multiple_of(qb * QB, QB), QB)
+        slot = pl.ds(pl.multiple_of(jnp.where(qb < per, qb * QB, wide + (qb - per) * QB), QB), QB)
+        zero = jnp.zeros((), bf16)
+        causal = lax.broadcasted_iota(jnp.int32, (QB, QB), 0) <= lax.broadcasted_iota(jnp.int32, (QB, QB), 1)
+        left = lax.broadcasted_iota(jnp.int32, (QB, PAIR), 1) < HD
+
+        def by_head(a):
+            return jnp.where(left, a, zero), jnp.where(left, zero, a)
+
+        def keys_of(some, c):
+            if c == count:
+                return some[0][own, :]
+            s, at = spots[c]
+            return some[s][at:at + QB, :]
+
+        def cut(c):
+            return slice(c * QB, (c + 1) * QB)
+
+        ident = eye(QB)
+        q_heads = by_head(q_ref[own, :])
+        do_t = mm(eye(PAIR), do_ref[own, :], NT)
+        upper = lax.broadcasted_iota(jnp.int32, (PAIR, QB), 0) < HD
+        q_t = mm(eye(PAIR), q_ref[own, :], NT).astype(bf16)
+        q_cols = jnp.where(upper, q_t, zero), jnp.where(upper, zero, q_t)
+        peaks, norms, outs, deltas, scaled = [None, None], [None, None], [None, None], [None, None], [None, None]
+
+        def scores(h):
+            peak = jnp.full((8, QB), MASKED, f32)
+            for c in range(count + 1):
+                s = mm(keys_of(k_refs, c), q_cols[h], NN)
+                if c == count:
+                    s = jnp.where(causal, s, MASKED)
+                    top = fold(s, jnp.max)
+                else:
+                    top = fold(s, jnp.max) + kind_ref[qb, c]
+                s_ref[h, cut(c)] = s
+                peak = jnp.maximum(peak, top)
+            peaks[h] = jnp.max(peak, axis=0, keepdims=True)
+
+        def weigh(h):
+            total = jnp.zeros((8, QB), f32)
+            for c in range(count + 1):
+                bias = -peaks[h] if c == count else kind_ref[qb, c] - peaks[h]
+                e = jnp.exp2(s_ref[h, cut(c)] + bias)
+                total = total + fold(e, jnp.sum)
+                p_ref[h, cut(c)] = e.astype(bf16)
+            norms[h] = 1.0 / jnp.sum(total, axis=0, keepdims=True)
+
+        def attend(h):
+            lines = slice(h * HD, (h + 1) * HD)
+            out = mm(vt_ref[lines, 0:wide], p_ref[h, 0:wide], NN) + mm(vt_ref[lines, slot], p_ref[h, wide:], NN)
+            outs[h] = out * norms[h]
+            deltas[h] = jnp.sum(outs[h] * do_t[lines], axis=0, keepdims=True) * norms[h]
+            scaled[h] = do_t[lines] * norms[h]
+
+        scores(0)
+        scores(1)
+        weigh(0)
+        attend(0)
+        weigh(1)
+        attend(1)
+        d_t = jnp.concatenate(scaled, axis=0).astype(bf16)
+        d_cols = jnp.where(upper, d_t, zero), jnp.where(upper, zero, d_t)
+        do_heads = by_head(mm(ident, d_t, NT).astype(bf16))
+        grads = []
+        for h in range(2):
+            lines = slice(h * HD, (h + 1) * HD)
+            for c in range(count + 1):
+                dp = mm(keys_of(v_refs, c), d_cols[h], NN)
+                ds_ref[h, cut(c)] = (p_ref[h, cut(c)].astype(f32) * (dp - deltas[h])).astype(bf16)
+            dq = mm(kt_ref[lines, 0:wide], ds_ref[h, 0:wide], NN) + mm(kt_ref[lines, slot], ds_ref[h, wide:], NN)
+            a, b = dq[:ROT // 2], dq[ROT // 2:ROT]
+            cosine, sine = cos_ref[:, own], sin_ref[:, own]
+            grads.append(jnp.concatenate([a * cosine + b * sine, b * cosine - a * sine, dq[ROT:]], axis=0))
+        for c in range(count + 1):
+            at = slot if c == count else cut(c)
+            dva_ref[at, :] += mm(p_ref[0, cut(c)], do_heads[0], NN) + mm(p_ref[1, cut(c)], do_heads[1], NN)
+            dka_ref[at, :] += mm(ds_ref[0, cut(c)], q_heads[0], NN) + mm(ds_ref[1, cut(c)], q_heads[1], NN)
+        o_ref[own, :] = mm(ident, jnp.concatenate(outs, axis=0).astype(bf16), NT).astype(bf16)
+        dq_ref[own, :] = mm(ident, (jnp.concatenate(grads, axis=0) * (HD ** (-0.5))).astype(bf16), NT).astype(bf16)
+
+        return carry
+
+    lax.fori_loop(0, 2 * per, block, 0)
+
+    def flush(out, to, frm, size):
+        out[to:to + size, :PAIR] = (dka_ref[frm:frm + size, :] * math.log(2.0)).astype(bf16)
+        out[to:to + size, PAIR:] = dva_ref[frm:frm + size, :].astype(bf16)
+
+    flush(g_refs[0], 0, 0, half)
+    flush(g_refs[0], half, wide, half)
+    for s in range(1, n):
+        flush(g_refs[s], 0, s * half, half)
+
+
+def attention(kind, cos_t, sin_t, q, do, ks, vs, first, pairs):
+    rows = q.shape[0]
+    half = rows // 2
+    n = len(ks)
+    wide = n * half
+    keys = wide + half
+    total = wide + QB
+    qspec = pl.BlockSpec((rows, PAIR), lambda p: (0, p + first))
+    ospec = pl.BlockSpec((rows, PAIR), lambda p: (0, p))
+    table = pl.BlockSpec((ROT // 2, rows), lambda p: (0, 0))
+    kspecs = [pl.BlockSpec((k.shape[0], PAIR), lambda p: (0, p + first)) for k in ks]
+    gspecs = [pl.BlockSpec((k.shape[0], 2 * PAIR), lambda p: (0, p)) for k in ks]
+    s = jax.ShapeDtypeStruct
+    pieces = pairs * rows // QB
+    return pl.pallas_call(
+        partial(attention_kernel, half, n),
+        grid=(pairs,),
+        in_specs=[pl.BlockSpec(memory_space=pltpu.SMEM), table, table, qspec, qspec] + kspecs + kspecs,
+        out_specs=[ospec, ospec] + gspecs,
+        out_shape=[s((rows, pairs * PAIR), bf16), s((rows, pairs * PAIR), bf16)]
+        + [s((k.shape[0], 2 * pairs * PAIR), bf16) for k in ks],
+        scratch_shapes=[pltpu.VMEM((PAIR, keys), bf16), pltpu.VMEM((PAIR, keys), bf16),
+                        pltpu.VMEM((2, total, QB), f32), pltpu.VMEM((2, total, QB), bf16),
+                        pltpu.VMEM((2, total, QB), bf16),
+                        pltpu.VMEM((keys, PAIR), f32), pltpu.VMEM((keys, PAIR), f32)],
+        compiler_params=pltpu.CompilerParams(vmem_limit_bytes=60 << 20),
+        cost_estimate=pl.CostEstimate(flops=pieces * 24 * total * QB * HD * 4, bytes_accessed=16 << 20,
+                                      transcendentals=pieces * 2 * total * QB),
+        name="attention",
+    )(kind, cos_t, sin_t, q, do, *ks, *vs)
+
+
+def pairs_of(bit, size):
+    return [(a, a ^ bit) for a in range(size)]
+
+
+def pick(a, axis, i):
+    return lax.dynamic_index_in_dim(a, i, axis, keepdims=False)
+
+
+def plus(a, b):
+    return (a.astype(f32) + b.astype(f32)).astype(bf16)
+
+
+def scatter_sum(terms):
+    me = lax.axis_index("fsdp")
+    y, x, core = me // 4, (me // 2) % 2, me % 2
+    rows, cols = terms.shape
+    t = terms.reshape(2, 2, 2, rows // 8, cols)
+    t = plus(pick(t, 2, core), lax.ppermute(pick(t, 2, 1 - core), "fsdp", pairs_of(1, 8)))
+    a, b = t[..., :cols // 2], t[..., cols // 2:]
+    a = plus(pick(a, 1, x), lax.ppermute(pick(a, 1, 1 - x), "fsdp", pairs_of(2, 8)))
+    b = plus(pick(b, 0, y), lax.ppermute(pick(b, 0, 1 - y), "fsdp", pairs_of(4, 8)))
+    a = plus(pick(a, 0, y), lax.ppermute(pick(a, 0, 1 - y), "fsdp", pairs_of(4, 8)))
+    b = plus(pick(b, 0, x), lax.ppermute(pick(b, 0, 1 - x), "fsdp", pairs_of(2, 8)))
+    part = jnp.concatenate([a, b], axis=-1)
+    return lax.psum_scatter(part, "ctx", scatter_dimension=0, tiled=True)
+
+
+def after(value, *others):
+    return lax.optimization_barrier((value, *others))[0]
+
+
+def fast(inputs, cotangent, positions, segments, ln1_gain, ln1_bias, w_qkv, b_qkv, w_attn_out, b_out,
+         ln2_gain, ln2_bias, w_in, b_in, w_out):
+    x, grad_out, pos = inputs[0], cotangent[0], positions[0]
+    rows, width = x.shape
+    half = rows // 2
+    n = lax.axis_size("ctx")
+    ring = [(i, (i + 1) % n) for i in range(n)]
+    back = [(i, (i - 1) % n) for i in range(n)]
+    xs, spots = [x], [pos[::RB] // RB]
+    run = x[:half]
+    for s in range(1, n):
+        run = lax.ppermute(run, "ctx", ring)
+        xs.append(run)
+        spots.append(lax.ppermute(spots[0][:half // RB], "ctx", [(i, (i + s) % n) for i in range(n)]))
+    mine = (ln1_gain, ln1_bias, b_qkv, b_out, ln2_gain, ln2_bias, b_in)
+    small = lax.all_gather(jnp.concatenate(mine).reshape(1, -1), "fsdp", axis=0, tiled=True)
+    full, at = [], 0
+    for a in mine:
+        full.append(small[:, at:at + a.shape[0]].reshape(-1).astype(f32))
+        at += a.shape[0]
+    gain_attn, shift_attn, bias_qkv, bias_out, gain_mlp, shift_mlp, bias_in = full
+    weight_qkv = lax.all_gather(w_qkv, "fsdp", axis=0, tiled=True)
+    weight_attn = lax.all_gather(w_attn_out, "fsdp", axis=0, tiled=True)
+    weight_in = lax.all_gather(w_in, "fsdp", axis=0, tiled=True)
+    weight_out = lax.all_gather(w_out, "fsdp", axis=0, tiled=True)
+
+    lane = jnp.arange(PAIR) % HD
+    inverse = jnp.exp(-math.log(10000.0) * (2.0 / ROT) * (lane % (ROT // 2)).astype(f32))
+    angles = jnp.arange(n * half + CLEN).astype(f32)[:, None] * inverse[None, :]
+    sine = jnp.sin(angles)
+    tables = (jnp.where(lane < ROT, jnp.cos(angles), 1.0), jnp.where(lane < ROT // 2, sine, 0.0),
+              jnp.where((lane >= ROT // 2) & (lane < ROT), sine, 0.0))
+    angles_t = pos.astype(f32)[None, :] * inverse[:ROT // 2, None]
+    cos_t, sin_t = jnp.cos(angles_t), jnp.sin(angles_t)
+
+    normed, queries, key, value = qkv(spots[0], x, gain_attn, shift_attn, weight_qkv, bias_qkv, tables, True)
+    keys, values = [key], [value]
+    for s in range(1, n):
+        key, value = qkv(spots[s], xs[s], gain_attn, shift_attn, weight_qkv, bias_qkv, tables, False)
+        keys.append(key)
+        values.append(value)
+    grad_att = mm(grad_out, weight_attn, NT).astype(bf16)
+
+    per = half // QB
+    earlier = jnp.stack([spots[s][0] < spots[0][0] for s in range(1, n)])
+    local_row = jnp.arange(2 * per)[:, None]
+    seen_own = local_row > jnp.arange(per)[None, :]
+    seen_far = jnp.repeat(earlier[None, :] | (local_row >= per), per, axis=1)
+    kind = jnp.where(jnp.concatenate([seen_own, seen_far], axis=1), 0.0, MASKED).astype(f32)
+
+    groups = 2
+    count = HEADS // 2 // groups
+    attended, grad_q, own_kv, come_kv = [], [], [], []
+    for g in range(groups):
+        out = attention(kind, cos_t, sin_t, queries, grad_att, keys, values, g * count, count)
+        attended.append(out[0])
+        grad_q.append(out[1])
+        own_kv.append(out[2])
+        run = out[2 + n - 1]
+        for s in range(n - 2, 0, -1):
+            run = plus(lax.ppermute(run, "ctx", back), out[2 + s])
+        come_kv.append(lax.ppermute(run, "ctx", back))
+    attended = jnp.concatenate(attended, axis=1)
+
+    x_late, attended = lax.optimization_barrier((x, attended))
+    mlp_out, grad_mlp, dw_in, dw_out, db_in, db_out, dgain_mlp, dshift_mlp = mlp(
+        x_late, grad_out, gain_mlp, shift_mlp, weight_in, bias_in, weight_out)
+    output, dw_attn = join(x, grad_out, attended, weight_attn, mlp_out, bias_out)
+    sum_out = scatter_sum(dw_out)
+    sum_in = scatter_sum(dw_in)
+    sum_attn = scatter_sum(dw_attn)
+    grad_inputs, dw_qkv, db_qkv, dgain_attn, dshift_attn = tail(
+        spots[0], x, normed, gain_attn, weight_qkv, tables, grad_mlp, grad_q, own_kv, come_kv)
+    sum_qkv = scatter_sum(dw_qkv)
+    smalls = [a.reshape(width, -1) for a in (dgain_attn, dshift_attn, db_qkv, db_out, dgain_mlp, dshift_mlp, db_in)]
+    used = sum(a.shape[1] for a in smalls)
+    packed = jnp.concatenate(smalls + [jnp.zeros((width, PAIR - used), f32)], axis=1).astype(bf16)
+    packed = scatter_sum(packed).astype(f32)
+    done, at = [], 0
+    for a in smalls:
+        done.append(packed[:, at:at + a.shape[1]].reshape(-1))
+        at += a.shape[1]
+    return (output[None], grad_inputs[None], done[0], done[1], sum_qkv.astype(f32), done[2], sum_attn.astype(f32),
+            done[3], done[4], done[5], sum_in.astype(f32), done[6], sum_out.astype(f32))
+
+
+def local(*args):
+    half = args[0].shape[1] // 2
+    if args[0].shape[0] == 1 and half % CLEN == 0 and lax.axis_size("fsdp") == 8:
+        return fast(*args)
+    return generic(*args)
+
+
+def generic(
     inputs,
     cotangent,
     positions,

time: 2810 us -> 686 us (0.24)
  matrix products: 1110 us -> 5.94 us
  waiting for transfers between devices: 1170 us -> 204 us
  Pallas kernels: 0 us -> 306 us
  other arithmetic: 202 us -> 56.5 us
  blocking collectives: 134 us -> 9.16 us
  local copies, waits for them, and re-layouts: 129 us -> 37.3 us
  starting transfers between devices: 0.48 us -> 45.8 us
  loops' own time: 34 us -> 0 us
    dot_general x124 -> x1, matrix products: 1110 us -> 5.94 us  [mm(): return lax.dot_general(a, b, dims, preferred_element_type=f32)]
    reduce_scatter x6 -> x5, waiting for transfers between devices: 1040 us -> 31.4 us  [scatter_sum(): return lax.psum_scatter(part, 'ctx', scatter_dimension=0, tiled=True)]
    pallas_call x0 -> x9, Pallas kernels: none -> 306 us  [the longest x2 154 us: attention(): pl.pallas_call(partial(attention_kernel, half, n), grid=(pairs,), in_spec...]
    reduce_sum x21 -> x0, other arithmetic: 166 us -> none  [the longest x16 149 us: total_step(): jnp.sum(jnp.where(mask, jnp.exp(scores - fresh[..., None]), 0.0), axis=-1)]
    ppermute x0 -> x37, waiting for transfers between devices: none -> 157 us  [the longest x4 60.3 us: fast(): run = plus(lax.ppermute(run, 'ctx', back), out[2 + s])]
    all_gather x6 -> x4, waiting for transfers between devices: 126 us -> 13.5 us  [the longest x1 13.5 us: fast(): weight_qkv = lax.all_gather(w_qkv, 'fsdp', axis=0, tiled=True)]
    all_gather x9 -> x1, blocking collectives: 92.7 us -> 9.16 us  [fast(): lax.all_gather(jnp.concatenate(mine).reshape(1, -1), 'fsdp', axis=0, tile...]
    while x80 -> x0, local copies, waits for them, and re-layouts: 51.8 us -> none
  transfers between devices with their start and end apart: 12 -> 46, of which waited for: 7 -> 19; matrix products, arithmetic and copies ran while one was open for 48% -> 13% of each run, Pallas kernels for 0% -> 40%
where the time goes in v2:
time: 686 us; the launch traced here: 680 us
  Pallas kernels  306 us (45%)
  waiting for transfers between devices  204 us (30%)
  other arithmetic  56.5 us (8%)
  starting transfers between devices  45.8 us (7%)
  local copies, waits for them, and re-layouts  37.3 us (5%)
  between operations  15 us (2%)
  blocking collectives  9.16 us (1%)
    pallas_call x2, Pallas kernels, attention(): pl.pallas_call(partial(attention_kernel, half, n), grid=(pairs,), in_spec...  154 us
    pallas_call x1, Pallas kernels, mlp(): pl.pallas_call(mlp_kernel, grid=(ff // FC,), in_specs=[whole, whole, line...  70.1 us
    ppermute x4, waiting for transfers between devices, fast(): run = plus(lax.ppermute(run, 'ctx', back), out[2 + s])  60.3 us
    ppermute x5, waiting for transfers between devices, scatter_sum(): lax.ppermute(pick(b, 0, 1 - y), 'fsdp', pairs_of(4, 8))  47.4 us
    pallas_call x4, Pallas kernels, qkv(): pl.pallas_call(partial(qkv_kernel, with_q), grid_spec=pltpu.PrefetchScala...  37.9 us
    pallas_call x1, Pallas kernels, tail(): pl.pallas_call(partial(tail_kernel, groups), grid_spec=pltpu.PrefetchScal...  32.7 us
    reduce_scatter x5, waiting for transfers between devices, scatter_sum(): return lax.psum_scatter(part, 'ctx', scatter_dimension=0, tiled=True)  31.4 us
    convert_element_type x29, other arithmetic, plus(): return (a.astype(f32) + b.astype(f32)).astype(bf16)  30 us
  transfers between devices with their start and end apart: 46, of which 19 were waited for; matrix products, arithmetic and copies ran while one was open for 13% of the time, Pallas kernels for 40%

profile of v2, /device:TPU:0, one launch (start us, length us, event | category | flops | bytes accessed | tf_op | source)
XLA Modules:
  0.0 680.0 jit_solution(6246504337596178508)
XLA Ops:
  9.6 5.1 collective-permute-start.2
  21.0 9.2 %all-gather.1 = bf16[8,1,1536]{2,1,0:T(2,128)(2,1)S(1)} all-gather(bf16[1,1,1536]{2,1,0:T(2,128)(2,1)S(1)} %reshape.340), channel_id=2, replica_groups=mesh['fsdp'=8,'ctx'=4] {'fsdp'}, dimensions={0}, use_global_device_ids=true | all-gather | bytes 27648 | tf_op jit(solution)/shard_map/all_gather | solution.py:576
  32.3 10.6 %collective-permute-done.3.x_ref = bf16[512,1024]{1,0:T(8,128)(2,1)S(1)} collective-permute-done((bf16[512,1024]{1,0:T(8,128)(2,1)S(1)}, bf16[512,1024]{1,0:T(8,128)(2,1)S(1)}, u32[]{:S(2)}, u32[]{:S(2)}) %collective-permute-start.3) | collective-permute-done | bytes 1048608 | tf_op jit(solution)/shard_map/ppermute | solution.py:572
  43.6 6.5 fusion.8
  50.6 17.3 %collective-permute-done.4.x_ref = bf16[512,1024]{1,0:T(8,128)(2,1)S(1)} collective-permute-done((bf16[512,1024]{1,0:T(8,128)(2,1)S(1)}, bf16[512,1024]{1,0:T(8,128)(2,1)S(1)}, u32[]{:S(2)}, u32[]{:S(2)}) %collective-permute-start.4) | collective-permute-done | bytes 1048608 | tf_op jit(solution)/shard_map/ppermute | solution.py:572
  68.7 5.9 convolution_convert_fusion.do_ref
  74.6 13.5 %all-gather.7.cloned.1.call-done.w_ref = bf16[1024,3072]{1,0:T(8,128)(2,1)} async-done(((bf16[128,3072]{1,0:T(8,128)(2,1)}), bf16[1024,3072]{1,0:T(8,128)(2,1)}) %all-gather.7.cloned.1.call-update) | async-done | bytes 6291472 | tf_op jit(solution)/shard_map/all_gather | solution.py:582
  88.1 8.1 %kv_remote.4 = (bf16[512,1024]{1,0:T(8,128)(2,1)}, bf16[512,1024]{1,0:T(8,128)(2,1)}) custom-call(s32[2]{0:T(128)} %copy-done.22, bf16[512,1024]{1,0:T(8,128)(2,1)} %copy-done.10, f32[1,1024]{1,0:T(1,128)} %bitcast.200, f32[1,1024]{1,0:T(1,128)} %bitcast.205, bf16[1024,3072]{1,0:T(8,128)(2,1)} %all-gather.7.cloned.1.call-done.w_ref, f32[1,3072]{1,0:T(1,128)} %bitcast.193, ...), custom_call_target="tpu_custom_call" | custom-call | flops 2147483648 | bytes 16777216 | tf_op jit(solution)/shard_map/kv_remote/pallas_call | solution.py:229
  96.2 8.5 %kv_remote.3 = (bf16[512,1024]{1,0:T(8,128)(2,1)}, bf16[512,1024]{1,0:T(8,128)(2,1)}) custom-call(s32[2]{0:T(128)} %copy-done.23, bf16[512,1024]{1,0:T(8,128)(2,1)} %copy-done.9, f32[1,1024]{1,0:T(1,128)} %bitcast.201, f32[1,1024]{1,0:T(1,128)} %bitcast.206, bf16[1024,3072]{1,0:T(8,128)(2,1)} %all-gather.7.cloned.1.call-done.w_ref, f32[1,3072]{1,0:T(1,128)} %bitcast.194, ...), custom_call_target="tpu_custom_call" | custom-call | flops 2147483648 | bytes 16777216 | tf_op jit(solution)/shard_map/kv_remote/pallas_call | solution.py:229
  105.7 7.8 %kv_remote.5 = (bf16[512,1024]{1,0:T(8,128)(2,1)}, bf16[512,1024]{1,0:T(8,128)(2,1)}) custom-call(s32[2]{0:T(128)} %copy-done.21, bf16[512,1024]{1,0:T(8,128)(2,1)} %copy-done.13, f32[1,1024]{1,0:T(1,128)} %bitcast.202, f32[1,1024]{1,0:T(1,128)} %bitcast.207, bf16[1024,3072]{1,0:T(8,128)(2,1)} %all-gather.7.cloned.1.call-done.w_ref, f32[1,3072]{1,0:T(1,128)} %bitcast.195, ...), custom_call_target="tpu_custom_call" | custom-call | flops 2147483648 | bytes 16777216 | tf_op jit(solution)/shard_map/kv_remote/pallas_call | solution.py:229
  113.5 13.5 %qkv_own.1 = (bf16[1024,1024]{1,0:T(8,128)(2,1)}, bf16[1024,1024]{1,0:T(8,128)(2,1)}, bf16[1024,1024]{1,0:T(8,128)(2,1)}, bf16[1024,1024]{1,0:T(8,128)(2,1)}) custom-call(s32[4]{0:T(128)} %copy-done.30, bf16[1024,1024]{1,0:T(8,128)(2,1)} %bitcast.189, f32[1,1024]{1,0:T(1,128)} %bitcast.203, f32[1,1024]{1,0:T(1,128)} %bitcast.208, ...), custom_call_target="tpu_custom_call" | custom-call | flops 6442450944 | bytes 16777216 | tf_op jit(solution)/shard_map/qkv_own/pallas_call | solution.py:229
  127.0 76.7 %attention.3 = (bf16[1024,512]{1,0:T(8,128)(2,1)}, bf16[1024,512]{1,0:T(8,128)(2,1)}, bf16[1024,1024]{1,0:T(8,128)(2,1)}, bf16[512,1024]{1,0:T(8,128)(2,1)}, bf1...) custom-call(f32[4,8]{1,0:T(4,128)} %add_select_fusion.kind_ref, f32[8,1024]{1,0:T(8,128)} %get-tuple-element.115.cos_ref, ...), custom_call_target="tpu_custom_call" | custom-call | flops 57982058496 | bytes 16777216 | tf_op jit(solution)/shard_map/attention/pallas_call | solution.py:512
  203.7 3.5 collective-permute-start.9
  207.2 77.5 %attention.2 = (bf16[1024,512]{1,0:T(8,128)(2,1)}, bf16[1024,512]{1,0:T(8,128)(2,1)}, bf16[1024,1024]{1,0:T(8,128)(2,1)}, bf16[512,1024]{1,0:T(8,128)(2,1)}, bf1...) custom-call(f32[4,8]{1,0:T(4,128)} %add_select_fusion.kind_ref, f32[8,1024]{1,0:T(8,128)} %get-tuple-element.115.cos_ref, ...), custom_call_target="tpu_custom_call" | custom-call | flops 57982058496 | bytes 16777216 | tf_op jit(solution)/shard_map/attention/pallas_call | solution.py:512
  286.3 24.7 %collective-permute-done.6 = bf16[512,1024]{1,0:T(8,128)(2,1)S(1)} collective-permute-done((bf16[512,1024]{1,0:T(8,128)(2,1)}, bf16[512,1024]{1,0:T(8,128)(2,1)S(1)}, u32[]{:S(2)}, u32[]{:S(2)}) %collective-permute-start.6) | collective-permute-done | bytes 1048608 | tf_op jit(solution)/shard_map/ppermute | solution.py:621
  317.7 15.8 %collective-permute-done.10 = bf16[512,1024]{1,0:T(8,128)(2,1)S(1)} collective-permute-done((bf16[512,1024]{1,0:T(8,128)(2,1)S(1)}, bf16[512,1024]{1,0:T(8,128)(2,1)S(1)}, u32[]{:S(2)}, u32[]{:S(2)}) %collective-permute-start.10) | collective-permute-done | bytes 1048608 | tf_op jit(solution)/shard_map/ppermute | solution.py:621
  336.3 19.8 %collective-permute-done.7 = bf16[512,1024]{1,0:T(8,128)(2,1)} collective-permute-done((bf16[512,1024]{1,0:T(8,128)(2,1)S(1)}, bf16[512,1024]{1,0:T(8,128)(2,1)}, u32[]{:S(2)}, u32[]{:S(2)}) %collective-permute-start.7) | collective-permute-done | bytes 1048608 | tf_op jit(solution)/shard_map/ppermute | solution.py:621
  360.1 70.1 %mlp.1 = (f32[1024,1024]{1,0:T(8,128)}, f32[1024,1024]{1,0:T(8,128)}, bf16[1024,4096]{1,0:T(8,128)(2,1)}, bf16[4096,1024]{1,0:T(8,128)(2,1)}, f32[1,4096]{1,0:T(...) custom-call(bf16[1024,1024]{1,0:T(8,128)(2,1)} %bitcast.190, bf16[1024,1024]{1,0:T(8,128)(2,1)} %bitcast.224, ...), custom_call_target="tpu_custom_call" | custom-call | flops 51539607552 | bytes 50331648 | tf_op jit(solution)/shard_map/mlp/pallas_call | solution.py:180
  431.3 32.7 %tail.1 = (f32[1024,1024]{1,0:T(8,128)}, bf16[1024,3072]{1,0:T(8,128)(2,1)}, f32[1,3072]{1,0:T(1,128)}, f32[1,1024]{1,0:T(1,128)}, f32[1,1024]{1,0:T(1,128)}) custom-call(s32[4]{0:T(128)} %copy-done.30, bf16[1024,1024]{1,0:T(8,128)(2,1)} %bitcast.191, bf16[1024,1024]{1,0:T(8,128)(2,1)} %get-tuple-element.67.h_ref, f32[1,1024]{1,0:T(1,128)} %bitcast.204, ...), custom_call_target="tpu_custom_call" | custom-call | flops 12884901888 | bytes 33554432 | tf_op jit(solution)/shard_map/tail/pallas_call | solution.py:320
  468.5 3.6 concatenate.53
  472.2 10.8 %join.1 = (bf16[1024,1024]{1,0:T(8,128)(2,1)}, bf16[1024,1024]{1,0:T(8,128)(2,1)}) custom-call(bf16[1024,1024]{1,0:T(8,128)(2,1)} %bitcast.192, bf16[1024,1024]{1,0:T(8,128)(2,1)} %bitcast.225, bf16[1024,1024]{1,0:T(8,128)(2,1)} %pad_maximum_fusion.att_ref, bf16[1024,1024]{1,0:T(8,128)(2,1)} %all-gather.9.cloned.1.call-done.w_ref, ...), custom_call_target="tpu_custom_call" | custom-call | flops 4294967296 | bytes 16777216 | tf_op jit(solution)/shard_map/join/pallas_call | solution.py:361
  487.2 4.9 dynamic-slice_bitcast_fusion.1
  524.3 4.0 fusion.2
  533.5 11.4 %collective-permute-done.20 = bf16[2,128,1536]{2,1,0:T(8,128)(2,1)} collective-permute-done((bf16[2,128,1536]{2,1,0:T(8,128)(2,1)}, bf16[2,128,1536]{2,1,0:T(8,128)(2,1)}, u32[]{:S(2)}, u32[]{:S(2)}) %collective-permute-start.20) | collective-permute-done | bytes 786464 | tf_op jit(solution)/shard_map/ppermute | solution.py:550
  549.8 5.7 fusion
  559.7 3.7 fusion.1
  569.7 13.8 %collective-permute-done.35 = bf16[2,512,512]{2,1,0:T(8,128)(2,1)} collective-permute-done((bf16[2,512,512]{2,1,0:T(8,128)(2,1)}, bf16[2,512,512]{2,1,0:T(8,128)(2,1)}, u32[]{:S(2)}, u32[]{:S(2)}) %collective-permute-start.35) | collective-permute-done | bytes 1048608 | tf_op jit(solution)/shard_map/ppermute | solution.py:550
  589.4 16.5 %collective-permute-done.30 = bf16[2,128,2048]{2,1,0:T(8,128)(2,1)} collective-permute-done((bf16[2,128,2048]{2,1,0:T(8,128)(2,1)}, bf16[2,128,2048]{2,1,0:T(8,128)(2,1)}, u32[]{:S(2)}, u32[]{:S(2)}) %collective-permute-start.30) | collective-permute-done | bytes 1048608 | tf_op jit(solution)/shard_map/ppermute | solution.py:550
  609.5 7.7 %collective-permute-done.36 = bf16[512,512]{1,0:T(8,128)(2,1)S(1)} collective-permute-done((bf16[512,512]{1,0:T(8,128)(2,1)S(1)}, bf16[512,512]{1,0:T(8,128)(2,1)S(1)}, u32[]{:S(2)}, u32[]{:S(2)}) %collective-permute-start.36) | collective-permute-done | bytes 524320 | tf_op jit(solution)/shard_map/ppermute | solution.py:552
  624.1 5.6 collective-permute-done.29
  638.4 4.9 reduce-scatter.14.cloned.1.call-done
  645.1 26.4 %reduce-scatter.12.cloned.1.call-done = bf16[32,4096]{1,0:T(8,128)(2,1)} async-done(((bf16[128,4096]{1,0:T(8,128)(2,1)}), bf16[32,4096]{1,0:T(8,128)(2,1)}) %reduce-scatter.12.cloned.1.call-update) | async-done | bytes 262160 | tf_op jit(solution)/shard_map/reduce_scatter | solution.py:554
  (278 shorter events, 119.1 us)
Async XLA Ops:
  7.2 61.5 %all-gather.9.cloned.1.call-start = ((), (), s32[]{:S(2)}) async-start(), calls=%async_computation.6 | async-start | bytes 2359296 | tf_op jit(solution)/shard_map/all_gather | solution.py:583
  7.9 80.2 %all-gather.7.cloned.1.call-start = ((), (), s32[]{:S(2)}) async-start(), calls=%async_computation.5 | async-start | bytes 7077888 | tf_op jit(solution)/shard_map/all_gather | solution.py:582
  8.7 351.3 %all-gather.11.cloned.1.call-start = ((), (), s32[]{:S(2)}) async-start(), calls=%async_computation.7 | async-start | bytes 9437184 | tf_op jit(solution)/shard_map/all_gather | solution.py:584
  9.5 350.6 %all-gather.13.cloned.1.call-start = ((), (), s32[]{:S(2)}) async-start(), calls=%async_computation.8 | async-start | bytes 9437184 | tf_op jit(solution)/shard_map/all_gather | solution.py:585
  9.6 40.5 %collective-permute-start.2 = (s32[2]{0:T(128)S(1)}, s32[2]{0:T(128)S(1)}, u32[]{:S(2)}, u32[]{:S(2)}) collective-permute-start(s32[2]{0:T(128)S(1)} %bitcast.226), channel_id=1, source_target_pairs={{0,3},{1,0},{2,1},{3,2},{4,7},{5,4},{6,5},{7,6},{8,11},{9,8},{10,9... | collective-permute-start | bytes 32 | tf_op jit(solution)/shard_map/ppermute | solution.py:574
  14.7 35.5 %collective-permute-start.1 = (s32[2]{0:T(128)S(1)}, s32[2]{0:T(128)S(1)}, u32[]{:S(2)}, u32[]{:S(2)}) collective-permute-start(s32[2]{0:T(128)S(1)} %bitcast.227), channel_id=1, source_target_pairs={{0,2},{1,3},{2,0},{3,1},{4,6},{5,7},{6,4},{7,5},{8,10},{9,11},{10,... | collective-permute-start | bytes 32 | tf_op jit(solution)/shard_map/ppermute | solution.py:574
  14.7 35.5 %collective-permute-start = (s32[2]{0:T(128)S(1)}, s32[2]{0:T(128)S(1)}, u32[]{:S(2)}, u32[]{:S(2)}) collective-permute-start(s32[2]{0:T(128)S(1)} %bitcast.228), channel_id=1, source_target_pairs={{0,1},{1,2},{2,3},{3,0},{4,5},{5,6},{6,7},{7,4},{8,9},{9,10},{10,1... | collective-permute-start | bytes 32 | tf_op jit(solution)/shard_map/ppermute | solution.py:574
  17.1 25.9 %collective-permute-start.3 = (bf16[512,1024]{1,0:T(8,128)(2,1)S(1)}, bf16[512,1024]{1,0:T(8,128)(2,1)S(1)}, u32[]{:S(2)}, u32[]{:S(2)}) collective-permute-start(bf16[512,1024]{1,0:T(8,128)(2,1)S(1)} %slice_bitcast_fusion), channel_id=1, source_target_pairs={{0,1},{1,2},{2,3},{3,0},{4,5},{5,6},{6,7},{7,4},{8,9},{9,10},{10,1... | collective-permute-start | bytes 3145736 | tf_op jit(solution)/shard_map/ppermute | solution.py:572
  19.6 611.3 %reduce-scatter.6.cloned.1.call-start = ((), (), s32[]{:S(2)}) async-start(), calls=%async_computation.9 | async-start | bytes 40960 | tf_op jit(solution)/shard_map/reduce_scatter | solution.py:554
  43.0 24.9 %collective-permute-start.4 = (bf16[512,1024]{1,0:T(8,128)(2,1)S(1)}, bf16[512,1024]{1,0:T(8,128)(2,1)S(1)}, u32[]{:S(2)}, u32[]{:S(2)}) collective-permute-start(bf16[512,1024]{1,0:T(8,128)(2,1)S(1)} %collective-permute-done.3.x_ref), channel_id=1, source_target_pairs={{0,1},{1,2},{2,3},{3,0},{4,5},{5,6},{6,7},{7,4},{8,9},{9,10},{10,1... | collective-permute-start | bytes 3145736 | tf_op jit(solution)/shard_map/ppermute | solution.py:572
  67.9 36.8 %collective-permute-start.5 = (bf16[512,1024]{1,0:T(8,128)(2,1)S(1)}, bf16[512,1024]{1,0:T(8,128)(2,1)S(1)}, u32[]{:S(2)}, u32[]{:S(2)}) collective-permute-start(bf16[512,1024]{1,0:T(8,128)(2,1)S(1)} %collective-permute-done.4.x_ref), channel_id=1, source_target_pairs={{0,1},{1,2},{2,3},{3,0},{4,5},{5,6},{6,7},{7,4},{8,9},{9,10},{10,1... | collective-permute-start | bytes 3145736 | tf_op jit(solution)/shard_map/ppermute | solution.py:572
  203.7 81.6 %collective-permute-start.9 = (bf16[512,1024]{1,0:T(8,128)(2,1)}, bf16[512,1024]{1,0:T(8,128)(2,1)S(1)}, u32[]{:S(2)}, u32[]{:S(2)}) collective-permute-start(bf16[512,1024]{1,0:T(8,128)(2,1)} %get-tuple-element.76), channel_id=1, source_target_pairs={{0,3},{1,0},{2,1},{3,2},{4,7},{5,4},{6,5},{7,6},{8,11},{9,8},{10,9... | collective-permute-start | bytes 3145736 | tf_op jit(solution)/shard_map/ppermute | solution.py:621
  284.7 26.3 %collective-permute-start.6 = (bf16[512,1024]{1,0:T(8,128)(2,1)}, bf16[512,1024]{1,0:T(8,128)(2,1)S(1)}, u32[]{:S(2)}, u32[]{:S(2)}) collective-permute-start(bf16[512,1024]{1,0:T(8,128)(2,1)} %get-tuple-element.73), channel_id=1, source_target_pairs={{0,3},{1,0},{2,1},{3,2},{4,7},{5,4},{6,5},{7,6},{8,11},{9,8},{10,9... | collective-permute-start | bytes 3145736 | tf_op jit(solution)/shard_map/ppermute | solution.py:621
  285.7 47.8 %collective-permute-start.10 = (bf16[512,1024]{1,0:T(8,128)(2,1)S(1)}, bf16[512,1024]{1,0:T(8,128)(2,1)S(1)}, u32[]{:S(2)}, u32[]{:S(2)}) collective-permute-start(bf16[512,1024]{1,0:T(8,128)(2,1)S(1)} %add_convert_fusion.1), channel_id=1, source_target_pairs={{0,3},{1,0},{2,1},{3,2},{4,7},{5,4},{6,5},{7,6},{8,11},{9,8},{10,9... | collective-permute-start | bytes 3145736 | tf_op jit(solution)/shard_map/ppermute | solution.py:621
  311.4 44.6 %collective-permute-start.7 = (bf16[512,1024]{1,0:T(8,128)(2,1)S(1)}, bf16[512,1024]{1,0:T(8,128)(2,1)}, u32[]{:S(2)}, u32[]{:S(2)}) collective-permute-start(bf16[512,1024]{1,0:T(8,128)(2,1)S(1)} %add_convert_fusion.3), channel_id=1, source_target_pairs={{0,3},{1,0},{2,1},{3,2},{4,7},{5,4},{6,5},{7,6},{8,11},{9,8},{10,9... | collective-permute-start | bytes 3145736 | tf_op jit(solution)/shard_map/ppermute | solution.py:621
  333.9 96.3 %collective-permute-start.11 = (bf16[512,1024]{1,0:T(8,128)(2,1)S(1)}, bf16[512,1024]{1,0:T(8,128)(2,1)}, u32[]{:S(2)}, u32[]{:S(2)}) collective-permute-start(bf16[512,1024]{1,0:T(8,128)(2,1)S(1)} %add_convert_fusion), channel_id=1, source_target_pairs={{0,3},{1,0},{2,1},{3,2},{4,7},{5,4},{6,5},{7,6},{8,11},{9,8},{10,9... | collective-permute-start | bytes 3145736 | tf_op jit(solution)/shard_map/ppermute | solution.py:622
  357.7 72.6 %collective-permute-start.8 = (bf16[512,1024]{1,0:T(8,128)(2,1)S(1)}, bf16[512,1024]{1,0:T(8,128)(2,1)S(1)}, u32[]{:S(2)}, u32[]{:S(2)}) collective-permute-start(bf16[512,1024]{1,0:T(8,128)(2,1)S(1)} %add_convert_fusion.2), channel_id=1, source_target_pairs={{0,3},{1,0},{2,1},{3,2},{4,7},{5,4},{6,5},{7,6},{8,11},{9,8},{10,9... | collective-permute-start | bytes 3145736 | tf_op jit(solution)/shard_map/ppermute | solution.py:622
  472.1 23.0 %collective-permute-start.12 = (bf16[2,2,128,128]{3,2,1,0:T(8,128)(2,1)S(1)}, bf16[2,2,128,128]{3,2,1,0:T(8,128)(2,1)S(1)}, u32[]{:S(2)}, u32[]{:S(2)}) collective-permute-start(bf16[2,2,128,128]{3,2,1,0:T(8,128)(2,1)S(1)} %dynamic-slice_bitcast_fusion.20), channel_id=1, source_target_pairs={{0,4},{4,0},{8,12},{12,8},{16,20},{20,16},{24,28},{28,24},{1,5},{5... | collective-permute-start | bytes 393224 | tf_op jit(solution)/shard_map/ppermute | solution.py:547
  484.4 24.9 %collective-permute-start.22 = (bf16[2,2,128,1024]{3,2,1,0:T(8,128)(2,1)S(1)}, bf16[2,2,128,1024]{3,2,1,0:T(8,128)(2,1)S(1)}, u32[]{:S(2)}, u32[]{:S(2)}) collective-permute-start(bf16[2,2,128,1024]{3,2,1,0:T(8,128)(2,1)S(1)} %dynamic-slice_bitcast_fusion.7), channel_id=1, source_target_pairs={{0,4},{4,0},{8,12},{12,8},{16,20},{20,16},{24,28},{28,24},{1,5},{5... | collective-permute-start | bytes 3145736 | tf_op jit(solution)/shard_map/ppermute | solution.py:547
  487.1 37.2 %collective-permute-start.17 = (bf16[2,2,128,3072]{3,2,1,0:T(8,128)(2,1)S(1)}, bf16[2,2,128,3072]{3,2,1,0:T(8,128)(2,1)}, u32[]{:S(2)}, u32[]{:S(2)}) collective-permute-start(bf16[2,2,128,3072]{3,2,1,0:T(8,128)(2,1)S(1)} %dynamic-slice_bitcast_fusion.2), channel_id=1, source_target_pairs={{0,4},{4,0},{8,12},{12,8},{16,20},{20,16},{24,28},{28,24},{1,5},{5... | collective-permute-start | bytes 9437192 | tf_op jit(solution)/shard_map/ppermute | solution.py:547
  494.5 55.3 %collective-permute-start.32 = (bf16[2,2,512,1024]{3,2,1,0:T(8,128)(2,1)}, bf16[2,2,512,1024]{3,2,1,0:T(8,128)(2,1)}, u32[]{:S(2)}, u32[]{:S(2)}) collective-permute-start(bf16[2,2,512,1024]{3,2,1,0:T(8,128)(2,1)} %dynamic-slice_bitcast_fusion), channel_id=1, source_target_pairs={{0,4},{4,0},{8,12},{12,8},{16,20},{20,16},{24,28},{28,24},{1,5},{5... | collective-permute-start | bytes 12582920 | tf_op jit(solution)/shard_map/ppermute | solution.py:547
  495.1 64.5 %collective-permute-start.27 = (bf16[2,2,128,4096]{3,2,1,0:T(8,128)(2,1)}, bf16[2,2,128,4096]{3,2,1,0:T(8,128)(2,1)}, u32[]{:S(2)}, u32[]{:S(2)}) collective-permute-start(bf16[2,2,128,4096]{3,2,1,0:T(8,128)(2,1)} %dynamic-slice_bitcast_fusion.1), channel_id=1, source_target_pairs={{0,4},{4,0},{8,12},{12,8},{16,20},{20,16},{24,28},{28,24},{1,5},{5... | collective-permute-start | bytes 12582920 | tf_op jit(solution)/shard_map/ppermute | solution.py:547
  513.1 122.1 %reduce-scatter.10.cloned.1.call-start = ((), (), s32[]{:S(2)}) async-start(), calls=%async_computation.11 | async-start | bytes 327680 | tf_op jit(solution)/shard_map/reduce_scatter | solution.py:554
  533.3 103.4 %reduce-scatter.8.cloned.1.call-start = ((), (), s32[]{:S(2)}) async-start(), calls=%async_computation.10 | async-start | bytes 983040 | tf_op jit(solution)/shard_map/reduce_scatter | solution.py:554
  557.1 26.4 %collective-permute-start.35 = (bf16[2,512,512]{2,1,0:T(8,128)(2,1)}, bf16[2,512,512]{2,1,0:T(8,128)(2,1)}, u32[]{:S(2)}, u32[]{:S(2)}) collective-permute-start(bf16[2,512,512]{2,1,0:T(8,128)(2,1)} %dynamic-slice_bitcast_fusion.3), channel_id=1, source_target_pairs={{0,16},{4,20},{8,24},{12,28},{16,0},{20,4},{24,8},{28,12},{1,17},{... | collective-permute-start | bytes 3145736 | tf_op jit(solution)/shard_map/ppermute | solution.py:550
  558.6 27.9 %collective-permute-start.33 = (bf16[2,512,512]{2,1,0:T(8,128)(2,1)S(1)}, bf16[2,512,512]{2,1,0:T(8,128)(2,1)}, u32[]{:S(2)}, u32[]{:S(2)}) collective-permute-start(bf16[2,512,512]{2,1,0:T(8,128)(2,1)S(1)} %dynamic-slice_bitcast_fusion.4), channel_id=1, source_target_pairs={{0,8},{4,12},{8,0},{12,4},{16,24},{20,28},{24,16},{28,20},{1,9},{5... | collective-permute-start | bytes 3145736 | tf_op jit(solution)/shard_map/ppermute | solution.py:549
  565.1 40.8 %collective-permute-start.30 = (bf16[2,128,2048]{2,1,0:T(8,128)(2,1)}, bf16[2,128,2048]{2,1,0:T(8,128)(2,1)}, u32[]{:S(2)}, u32[]{:S(2)}) collective-permute-start(bf16[2,128,2048]{2,1,0:T(8,128)(2,1)} %dynamic-slice_bitcast_fusion.5), channel_id=1, source_target_pairs={{0,16},{4,20},{8,24},{12,28},{16,0},{20,4},{24,8},{28,12},{1,17},{... | collective-permute-start | bytes 3145736 | tf_op jit(solution)/shard_map/ppermute | solution.py:550
  567.5 51.3 %collective-permute-start.28 = (bf16[2,128,2048]{2,1,0:T(8,128)(2,1)}, bf16[2,128,2048]{2,1,0:T(8,128)(2,1)}, u32[]{:S(2)}, u32[]{:S(2)}) collective-permute-start(bf16[2,128,2048]{2,1,0:T(8,128)(2,1)} %dynamic-slice_bitcast_fusion.6), channel_id=1, source_target_pairs={{0,8},{4,12},{8,0},{12,4},{16,24},{20,28},{24,16},{28,20},{1,9},{5... | collective-permute-start | bytes 3145736 | tf_op jit(solution)/shard_map/ppermute | solution.py:549
  569.7 73.7 %reduce-scatter.14.cloned.1.call-start = ((), (), s32[]{:S(2)}) async-start(), calls=%async_computation.13 | async-start | bytes 1310720 | tf_op jit(solution)/shard_map/reduce_scatter | solution.py:554
  585.4 31.8 %collective-permute-start.36 = (bf16[512,512]{1,0:T(8,128)(2,1)S(1)}, bf16[512,512]{1,0:T(8,128)(2,1)S(1)}, u32[]{:S(2)}, u32[]{:S(2)}) collective-permute-start(bf16[512,512]{1,0:T(8,128)(2,1)S(1)} %dynamic-slice_bitcast_fusion.10), channel_id=1, source_target_pairs={{0,8},{4,12},{8,0},{12,4},{16,24},{20,28},{24,16},{28,20},{1,9},{5... | collective-permute-start | bytes 1572872 | tf_op jit(solution)/shard_map/ppermute | solution.py:552
  588.1 29.3 %collective-permute-start.34 = (bf16[512,512]{1,0:T(8,128)(2,1)S(1)}, bf16[512,512]{1,0:T(8,128)(2,1)S(1)}, u32[]{:S(2)}, u32[]{:S(2)}) collective-permute-start(bf16[512,512]{1,0:T(8,128)(2,1)S(1)} %dynamic-slice_bitcast_fusion.11), channel_id=1, source_target_pairs={{0,16},{4,20},{8,24},{12,28},{16,0},{20,4},{24,8},{28,12},{1,17},{... | collective-permute-start | bytes 1572872 | tf_op jit(solution)/shard_map/ppermute | solution.py:551
  618.7 52.8 %reduce-scatter.12.cloned.1.call-start = ((), (), s32[]{:S(2)}) async-start(), calls=%async_computation.12 | async-start | bytes 1310720 | tf_op jit(solution)/shard_map/reduce_scatter | solution.py:554
  (49 other events, 779.1 us)
Sparse Core Ops, SparseCore 0:
  9.9 30.7 all-gather.8
  42.6 45.5 all-gather.6
  90.0 54.4 all-gather.10
  146.3 54.4 all-gather.12
  513.2 16.1 reduce-scatter.5
  533.4 16.9 reduce-scatter.9
  569.8 20.3 reduce-scatter.7
  618.8 24.4 reduce-scatter.13
  645.7 25.7 reduce-scatter.11

commit v3 on v2

--- a/solution.py
+++ b/solution.py
@@ -117,14 +117,20 @@
     return pltpu.CompilerParams(vmem_limit_bytes=60 << 20)
 
 
-FC = 512
 ROOT = math.sqrt(0.5)
 DENS = 1.0 / math.sqrt(2.0 * math.pi)
 
 
-def mlp_kernel(x_ref, c_ref, gain_ref, shift_ref, win_ref, bin_ref, wout_ref,
-               out_ref, gin_ref, dwin_ref, dwout_ref, dbin_ref, dbout_ref, dgain_ref, dshift_ref,
-               h_ref, act_ref, gp_ref, gh_ref):
+def reorder(order_ref, source, target):
+    size = source.shape[1] // order_ref.shape[0]
+    for i in range(order_ref.shape[0]):
+        at = pl.multiple_of(order_ref[i] * size, size)
+        target[:, i * size:(i + 1) * size] = source[:, pl.ds(at, size)]
+
+
+def mlp_kernel(order_ref, x_ref, c_ref, gain_ref, shift_ref, win_ref, bin_ref, wout_ref,
+               out_ref, gin_ref, dwin_send, dwin_keep, dwout_send, dwout_keep, dbin_ref, dbout_ref, dgain_ref, dshift_ref,
+               h_ref, turned_ref, act_ref, gp_ref, gh_ref):
     step = pl.program_id(0)
     rows = x_ref.shape[0]
     blocks = [slice(r, r + RB) for r in range(0, rows, RB)]
@@ -135,8 +141,9 @@
             h_ref[r, :] = norm_rows(x_ref[r, :].astype(f32), gain_ref[...], shift_ref[...])
             out_ref[r, :] = jnp.zeros((RB, out_ref.shape[1]), f32)
             gh_ref[r, :] = jnp.zeros((RB, gh_ref.shape[1]), f32)
-
-    dbin = jnp.zeros((1, FC), f32)
+        reorder(order_ref, h_ref, turned_ref)
+
+    dbin = jnp.zeros(dbin_ref.shape, f32)
     for r in blocks:
         pre = mm(h_ref[r, :], win_ref[...], NN) + bin_ref[...]
         phi = 0.5 + 0.5 * lax.erf(pre * ROOT)
@@ -149,8 +156,20 @@
     for r in blocks:
         out_ref[r, :] += mm(act_ref[r, :], wout_ref[...], NN)
         gh_ref[r, :] += mm(gp_ref[r, :], win_ref[...], NT)
-    dwout_ref[...] = mm(act_ref[...], c_ref[...], TN).astype(bf16)
-    dwin_ref[...] = mm(h_ref[...], gp_ref[...], TN).astype(bf16)
+    dwout = mm(act_ref[...], c_ref[...], TN).astype(bf16)
+    middle = pl.num_programs(0) // 2
+
+    @pl.when(step < middle)
+    def _():
+        dwout_send[...] = dwout
+
+    @pl.when(step >= middle)
+    def _():
+        dwout_keep[...] = dwout
+
+    dwin = mm(turned_ref[...], gp_ref[...], TN).astype(bf16)
+    dwin_send[...] = dwin[:dwin_send.shape[0]]
+    dwin_keep[...] = dwin[dwin_send.shape[0]:]
     dbin_ref[...] = dbin
 
     @pl.when(step == pl.num_programs(0) - 1)
@@ -171,27 +190,36 @@
         dbout_ref[...] = dbout
 
 
-def mlp(x, c, gain, shift, weight_in, bias_in, weight_out):
+def mlp(order, x, c, gain, shift, weight_in, bias_in, weight_out):
     rows, width = x.shape
     ff = weight_in.shape[1]
-    whole = pl.BlockSpec((rows, width), lambda j: (0, 0))
-    line = pl.BlockSpec((1, width), lambda j: (0, 0))
+    steps = order.shape[0]
+    fc = ff // steps
+    whole = pl.BlockSpec((rows, width), lambda j, o: (0, 0))
+    line = pl.BlockSpec((1, width), lambda j, o: (0, 0))
+    down = pl.BlockSpec((width // 2, fc), lambda j, o: (0, o[j]))
     s = jax.ShapeDtypeStruct
     return pl.pallas_call(
         mlp_kernel,
-        grid=(ff // FC,),
-        in_specs=[whole, whole, line, line, pl.BlockSpec((width, FC), lambda j: (0, j)),
-                  pl.BlockSpec((1, FC), lambda j: (0, j)), pl.BlockSpec((FC, width), lambda j: (j, 0))],
-        out_specs=[whole, whole, pl.BlockSpec((width, FC), lambda j: (0, j)), pl.BlockSpec((FC, width), lambda j: (j, 0)),
-                   pl.BlockSpec((1, FC), lambda j: (0, j)), line, line, line],
-        out_shape=[s((rows, width), f32), s((rows, width), f32), s((width, ff), bf16), s((ff, width), bf16),
-                   s((1, ff), f32), s((1, width), f32), s((1, width), f32), s((1, width), f32)],
-        scratch_shapes=[vmem(rows, width, dtype=bf16), vmem(rows, FC, dtype=bf16), vmem(rows, FC, dtype=bf16),
-                        vmem(rows, width)],
+        grid_spec=pltpu.PrefetchScalarGridSpec(
+            num_scalar_prefetch=1,
+            grid=(steps,),
+            in_specs=[whole, whole, line, line, pl.BlockSpec((width, fc), lambda j, o: (0, o[j])),
+                      pl.BlockSpec((1, fc), lambda j, o: (0, o[j])), pl.BlockSpec((fc, width), lambda j, o: (o[j], 0))],
+            out_specs=[whole, whole, down, down,
+                       pl.BlockSpec((fc, width), lambda j, o: (jnp.minimum(j, steps // 2 - 1), 0)),
+                       pl.BlockSpec((fc, width), lambda j, o: (jnp.maximum(j - steps // 2, 0), 0)),
+                       pl.BlockSpec((1, fc), lambda j, o: (0, o[j])), line, line, line],
+            scratch_shapes=[vmem(rows, width, dtype=bf16), vmem(rows, width, dtype=bf16), vmem(rows, fc, dtype=bf16),
+                            vmem(rows, fc, dtype=bf16), vmem(rows, width)],
+        ),
+        out_shape=[s((rows, width), f32), s((rows, width), f32), s((width // 2, ff), bf16), s((width // 2, ff), bf16),
+                   s((ff // 2, width), bf16), s((ff // 2, width), bf16), s((1, ff), f32), s((1, width), f32),
+                   s((1, width), f32), s((1, width), f32)],
         compiler_params=params(),
         cost_estimate=pl.CostEstimate(flops=12 * rows * width * ff, bytes_accessed=48 << 20, transcendentals=2 * rows * ff),
         name="mlp",
-    )(x, c, gain.reshape(1, -1), shift.reshape(1, -1), weight_in, bias_in.reshape(1, -1), weight_out)
+    )(order, x, c, gain.reshape(1, -1), shift.reshape(1, -1), weight_in, bias_in.reshape(1, -1), weight_out)
 
 
 def turn_lanes(u, cosine, low, high, sign):
@@ -243,9 +271,9 @@
     )(spots, x, gain.reshape(1, -1), shift.reshape(1, -1), weight, bias.reshape(1, -1), *tables)
 
 
-def tail_kernel(groups, spot_ref, x_ref, h_ref, gain_ref, w_ref, cos_ref, low_ref, high_ref, gin_ref, *refs):
+def tail_kernel(groups, spot_ref, order_ref, x_ref, h_ref, gain_ref, w_ref, cos_ref, low_ref, high_ref, gin_ref, *refs):
     dq_refs, own_refs, come_refs = refs[:groups], refs[groups:2 * groups], refs[2 * groups:3 * groups]
-    grad_ref, dw_ref, db_ref, dgain_ref, dshift_ref, p_ref, gh_ref = refs[3 * groups:]
+    grad_ref, send_ref, keep_ref, db_ref, dgain_ref, dshift_ref, p_ref, turned_ref, gh_ref = refs[3 * groups:]
     step = pl.program_id(0)
     rows = x_ref.shape[0]
     half = rows // 2
@@ -261,15 +289,17 @@
                         p_ref[r, g * part + at:g * part + at + PAIR] = dq_refs[g][r, at:at + PAIR]
                         continue
                     lanes = slice(2 * at + shift, 2 * at + shift + PAIR)
-                    t = own_refs[g][r, lanes].astype(f32)
                     if r.start < half:
-                        t = t + come_refs[g][r, lanes].astype(f32)
+                        t = come_refs[g][r, lanes].astype(f32)
+                    else:
+                        t = own_refs[g][r.start - half:r.stop - half, lanes].astype(f32)
                     if shift == 0:
                         t = turn_lanes(t, cos_ref[spot, :], low_ref[spot, :], high_ref[spot, :], -1.0)
                     p_ref[r, g * part + at:g * part + at + PAIR] = t.astype(bf16)
 
     @pl.when(step == 0)
     def _():
+        reorder(order_ref, h_ref, turned_ref)
         put(None)
         for r in blocks:
             gh_ref[r, :] = mm(p_ref[r, :], w_ref[...], NT)
@@ -287,7 +317,9 @@
         for r in blocks:
             gh_ref[r, :] += mm(p_ref[r, :], w_ref[...], NT)
 
-    dw_ref[...] = mm(h_ref[...], p_ref[...], TN).astype(bf16)
+    dw = mm(turned_ref[...], p_ref[...], TN).astype(bf16)
+    send_ref[...] = dw[:send_ref.shape[0]]
+    keep_ref[...] = dw[send_ref.shape[0]:]
     db = jnp.zeros(db_ref.shape, f32)
     for r in blocks:
         db += col_sum(p_ref[r, :].astype(f32))
@@ -307,68 +339,81 @@
         dshift_ref[...] = dshift
 
 
-def tail(spots, x, h, gain, weight, tables, gin, dqs, owns, comes):
+def tail(spots, order, x, h, gain, weight, tables, gin, dqs, owns, comes):
     rows, width = x.shape
     groups = len(dqs)
     s = jax.ShapeDtypeStruct
 
     def full(a):
-        return pl.BlockSpec(a.shape, lambda j, spot: (0, 0))
-
-    line = pl.BlockSpec((1, width), lambda j, spot: (0, 0))
+        return pl.BlockSpec(a.shape, lambda j, spot, o: (0, 0))
+
+    line = pl.BlockSpec((1, width), lambda j, spot, o: (0, 0))
+    down = pl.BlockSpec((width // 2, width), lambda j, spot, o: (0, j))
     arrays = [*tables, gin, *dqs, *owns, *comes]
     return pl.pallas_call(
         partial(tail_kernel, groups),
         grid_spec=pltpu.PrefetchScalarGridSpec(
-            num_scalar_prefetch=1,
+            num_scalar_prefetch=2,
             grid=(3,),
-            in_specs=[full(x), full(h), line, pl.BlockSpec((width, width), lambda j, spot: (0, j))] + [full(a) for a in arrays],
-            out_specs=[full(x), pl.BlockSpec((width, width), lambda j, spot: (0, j)),
-                       pl.BlockSpec((1, width), lambda j, spot: (0, j)), line, line],
-            scratch_shapes=[vmem(rows, width, dtype=bf16), vmem(rows, width)],
+            in_specs=[full(x), full(h), line, pl.BlockSpec((width, width), lambda j, spot, o: (0, j))] + [full(a) for a in arrays],
+            out_specs=[full(x), down, down,
+                       pl.BlockSpec((1, width), lambda j, spot, o: (0, j)), line, line],
+            scratch_shapes=[vmem(rows, width, dtype=bf16), vmem(rows, width, dtype=bf16), vmem(rows, width)],
         ),
-        out_shape=[s((rows, width), f32), s((width, 3 * width), bf16), s((1, 3 * width), f32), s((1, width), f32),
+        out_shape=[s((rows, width), f32), s((width // 2, 3 * width), bf16), s((width // 2, 3 * width), bf16), s((1, 3 * width), f32), s((1, width), f32),
                    s((1, width), f32)],
         compiler_params=params(),
         cost_estimate=pl.CostEstimate(flops=12 * rows * width * width, bytes_accessed=32 << 20, transcendentals=0),
         name="tail",
-    )(spots, x, h, gain.reshape(1, -1), weight, *arrays)
-
-
-def join_kernel(x_ref, c_ref, att_ref, w_ref, mlp_ref, b_ref, out_ref, dw_ref, acc_ref):
+    )(spots, order, x, h, gain.reshape(1, -1), weight, *arrays)
+
+
+def join_kernel(groups, order_ref, x_ref, c_ref, w_ref, mlp_ref, b_ref, *refs):
+    att_refs, (out_ref, send_ref, keep_ref, att_ref, turned_ref, acc_ref) = refs[:groups], refs[groups:]
     step = pl.program_id(0)
+    part = att_refs[0].shape[1]
+    for g in range(groups):
+        att_ref[:, g * part:(g + 1) * part] = att_refs[g][...]
     out = x_ref[...].astype(f32) + mm(att_ref[...], w_ref[...], NN) + mlp_ref[...] + b_ref[...]
     out_ref[...] = out.astype(bf16)
+    reorder(order_ref, att_ref, turned_ref)
 
     @pl.when(step == 0)
     def _():
-        acc_ref[...] = mm(att_ref[...], c_ref[...], TN)
+        acc_ref[...] = mm(turned_ref[...], c_ref[...], TN)
 
     @pl.when(step > 0)
     def _():
-        acc_ref[...] += mm(att_ref[...], c_ref[...], TN)
+        acc_ref[...] += mm(turned_ref[...], c_ref[...], TN)
 
     @pl.when(step == pl.num_programs(0) - 1)
     def _():
-        dw_ref[...] = acc_ref[...].astype(bf16)
-
-
-def join(x, c, attended, weight, mlp_out, bias):
+        half = send_ref.shape[0]
+        send_ref[...] = acc_ref[:half, :].astype(bf16)
+        keep_ref[...] = acc_ref[half:, :].astype(bf16)
+
+
+def join(order, x, c, attended, weight, mlp_out, bias):
     rows, width = x.shape
     s = jax.ShapeDtypeStruct
-    block = pl.BlockSpec((RB, width), lambda j: (j, 0))
-    square = pl.BlockSpec((width, width), lambda j: (0, 0))
+    block = pl.BlockSpec((RB, width), lambda j, o: (j, 0))
+    half = pl.BlockSpec((width // 2, width), lambda j, o: (0, 0))
     return pl.pallas_call(
-        join_kernel,
-        grid=(rows // RB,),
-        in_specs=[block, block, block, square, block, pl.BlockSpec((1, width), lambda j: (0, 0))],
-        out_specs=[block, square],
-        out_shape=[s((rows, width), bf16), s((width, width), bf16)],
-        scratch_shapes=[vmem(width, width)],
+        partial(join_kernel, len(attended)),
+        grid_spec=pltpu.PrefetchScalarGridSpec(
+            num_scalar_prefetch=1,
+            grid=(rows // RB,),
+            in_specs=[block, block, pl.BlockSpec((width, width), lambda j, o: (0, 0)), block,
+                      pl.BlockSpec((1, width), lambda j, o: (0, 0))]
+            + [pl.BlockSpec((RB, a.shape[1]), lambda j, o: (j, 0)) for a in attended],
+            out_specs=[block, half, half],
+            scratch_shapes=[vmem(RB, width, dtype=bf16), vmem(RB, width, dtype=bf16), vmem(width, width)],
+        ),
+        out_shape=[s((rows, width), bf16), s((width // 2, width), bf16), s((width // 2, width), bf16)],
         compiler_params=params(),
         cost_estimate=pl.CostEstimate(flops=4 * rows * width * width, bytes_accessed=16 << 20, transcendentals=0),
         name="join",
-    )(x, c, attended, weight, mlp_out, bias.reshape(1, -1))
+    )(order, x, c, weight, mlp_out, bias.reshape(1, -1), *attended)
 
 
 def fold(x, op):
@@ -379,11 +424,11 @@
     return (lax.broadcasted_iota(jnp.int32, (size, size), 0) == lax.broadcasted_iota(jnp.int32, (size, size), 1)).astype(bf16)
 
 
-def attention_kernel(half, n, kind_ref, cos_ref, sin_ref, q_ref, do_ref, *refs):
+def attention_kernel(half, n, kind_ref, owner_ref, cos_ref, sin_ref, q_ref, do_ref, *refs):
     k_refs, v_refs = refs[:n], refs[n:2 * n]
     o_ref, dq_ref = refs[2 * n:2 * n + 2]
-    g_refs = refs[2 * n + 2:3 * n + 2]
-    kt_ref, vt_ref, s_ref, p_ref, ds_ref, dka_ref, dva_ref = refs[3 * n + 2:]
+    all_ref, cont_ref = refs[2 * n + 2:2 * n + 4]
+    kt_ref, vt_ref, s_ref, p_ref, ds_ref, dka_ref, dva_ref = refs[2 * n + 4:]
     per = half // QB
     wide = n * half
     count = wide // QB
@@ -485,17 +530,17 @@
 
     lax.fori_loop(0, 2 * per, block, 0)
 
-    def flush(out, to, frm, size):
-        out[to:to + size, :PAIR] = (dka_ref[frm:frm + size, :] * math.log(2.0)).astype(bf16)
-        out[to:to + size, PAIR:] = dva_ref[frm:frm + size, :].astype(bf16)
-
-    flush(g_refs[0], 0, 0, half)
-    flush(g_refs[0], half, wide, half)
-    for s in range(1, n):
-        flush(g_refs[s], 0, s * half, half)
-
-
-def attention(kind, cos_t, sin_t, q, do, ks, vs, first, pairs):
+    def flush(out, to, frm):
+        rows = pl.ds(to, half)
+        out[rows, :PAIR] = (dka_ref[frm:frm + half, :] * math.log(2.0)).astype(bf16)
+        out[rows, PAIR:] = dva_ref[frm:frm + half, :].astype(bf16)
+
+    flush(cont_ref, 0, wide)
+    for s in range(n):
+        flush(all_ref, pl.multiple_of(owner_ref[s] * half, half), s * half)
+
+
+def attention(kind, owners, cos_t, sin_t, q, do, ks, vs, first, pairs):
     rows = q.shape[0]
     half = rows // 2
     n = len(ks)
@@ -506,16 +551,16 @@
     ospec = pl.BlockSpec((rows, PAIR), lambda p: (0, p))
     table = pl.BlockSpec((ROT // 2, rows), lambda p: (0, 0))
     kspecs = [pl.BlockSpec((k.shape[0], PAIR), lambda p: (0, p + first)) for k in ks]
-    gspecs = [pl.BlockSpec((k.shape[0], 2 * PAIR), lambda p: (0, p)) for k in ks]
+    gspecs = [pl.BlockSpec((size, 2 * PAIR), lambda p: (0, p)) for size in (wide, half)]
     s = jax.ShapeDtypeStruct
     pieces = pairs * rows // QB
     return pl.pallas_call(
         partial(attention_kernel, half, n),
         grid=(pairs,),
-        in_specs=[pl.BlockSpec(memory_space=pltpu.SMEM), table, table, qspec, qspec] + kspecs + kspecs,
+        in_specs=[pl.BlockSpec(memory_space=pltpu.SMEM), pl.BlockSpec(memory_space=pltpu.SMEM), table, table, qspec, qspec] + kspecs + kspecs,
         out_specs=[ospec, ospec] + gspecs,
         out_shape=[s((rows, pairs * PAIR), bf16), s((rows, pairs * PAIR), bf16)]
-        + [s((k.shape[0], 2 * pairs * PAIR), bf16) for k in ks],
+        + [s((size, 2 * pairs * PAIR), bf16) for size in (wide, half)],
         scratch_shapes=[pltpu.VMEM((PAIR, keys), bf16), pltpu.VMEM((PAIR, keys), bf16),
                         pltpu.VMEM((2, total, QB), f32), pltpu.VMEM((2, total, QB), bf16),
                         pltpu.VMEM((2, total, QB), bf16),
@@ -524,7 +569,7 @@
         cost_estimate=pl.CostEstimate(flops=pieces * 24 * total * QB * HD * 4, bytes_accessed=16 << 20,
                                       transcendentals=pieces * 2 * total * QB),
         name="attention",
-    )(kind, cos_t, sin_t, q, do, *ks, *vs)
+    )(kind, owners, cos_t, sin_t, q, do, *ks, *vs)
 
 
 def pairs_of(bit, size):
@@ -539,19 +584,34 @@
     return (a.astype(f32) + b.astype(f32)).astype(bf16)
 
 
-def scatter_sum(terms):
-    me = lax.axis_index("fsdp")
-    y, x, core = me // 4, (me // 2) % 2, me % 2
-    rows, cols = terms.shape
-    t = terms.reshape(2, 2, 2, rows // 8, cols)
-    t = plus(pick(t, 2, core), lax.ppermute(pick(t, 2, 1 - core), "fsdp", pairs_of(1, 8)))
-    a, b = t[..., :cols // 2], t[..., cols // 2:]
-    a = plus(pick(a, 1, x), lax.ppermute(pick(a, 1, 1 - x), "fsdp", pairs_of(2, 8)))
-    b = plus(pick(b, 0, y), lax.ppermute(pick(b, 0, 1 - y), "fsdp", pairs_of(4, 8)))
-    a = plus(pick(a, 0, y), lax.ppermute(pick(a, 0, 1 - y), "fsdp", pairs_of(4, 8)))
-    b = plus(pick(b, 0, x), lax.ppermute(pick(b, 0, 1 - x), "fsdp", pairs_of(2, 8)))
-    part = jnp.concatenate([a, b], axis=-1)
+def core_step(send, keep):
+    rows, cols = send.shape
+    size = rows // 8
+    got = lax.ppermute(send, "fsdp", pairs_of(1, 8)).reshape(2, 2, 2, size, cols)
+    keep = keep.reshape(2, 2, 2, size, cols)
+
+    def part(*at):
+        return plus(keep[at], got[at])
+
+    every = slice(None)
+    return part(every, 1, 0), part(every, 0, 0), part(1, every, 1), part(0, every, 1)
+
+
+def side_step(send_a, keep_a, send_b, keep_b):
+    got_a = lax.ppermute(send_a, "fsdp", pairs_of(2, 8))
+    got_b = lax.ppermute(send_b, "fsdp", pairs_of(4, 8))
+    return plus(keep_a[1], got_a[1]), plus(keep_a[0], got_a[0]), plus(keep_b[1], got_b[1]), plus(keep_b[0], got_b[0])
+
+
+def last_step(send_a, keep_a, send_b, keep_b):
+    got_a = lax.ppermute(send_a, "fsdp", pairs_of(4, 8))
+    got_b = lax.ppermute(send_b, "fsdp", pairs_of(2, 8))
+    part = jnp.concatenate([plus(keep_a, got_a), plus(keep_b, got_b)], axis=0)
     return lax.psum_scatter(part, "ctx", scatter_dimension=0, tiled=True)
+
+
+def scatter_sum(send, keep):
+    return last_step(*side_step(*core_step(send, keep)))
 
 
 def after(value, *others):
@@ -580,9 +640,9 @@
         at += a.shape[0]
     gain_attn, shift_attn, bias_qkv, bias_out, gain_mlp, shift_mlp, bias_in = full
     weight_qkv = lax.all_gather(w_qkv, "fsdp", axis=0, tiled=True)
-    weight_attn = lax.all_gather(w_attn_out, "fsdp", axis=0, tiled=True)
-    weight_in = lax.all_gather(w_in, "fsdp", axis=0, tiled=True)
-    weight_out = lax.all_gather(w_out, "fsdp", axis=0, tiled=True)
+    weight_attn = lax.all_gather(after(w_attn_out, weight_qkv), "fsdp", axis=0, tiled=True)
+    weight_in = lax.all_gather(after(w_in, weight_attn), "fsdp", axis=0, tiled=True)
+    weight_out = lax.all_gather(after(w_out, weight_attn), "fsdp", axis=0, tiled=True)
 
     lane = jnp.arange(PAIR) % HD
     inverse = jnp.exp(-math.log(10000.0) * (2.0 / ROT) * (lane % (ROT // 2)).astype(f32))
@@ -608,34 +668,35 @@
     seen_far = jnp.repeat(earlier[None, :] | (local_row >= per), per, axis=1)
     kind = jnp.where(jnp.concatenate([seen_own, seen_far], axis=1), 0.0, MASKED).astype(f32)
 
+    me, place = lax.axis_index("fsdp"), lax.axis_index("ctx")
+    relative = [4 * dy + 2 * dx + 1 - keep for keep in (0, 1) for dy in (0, 1) for dx in (0, 1)]
+    order = jnp.bitwise_xor(me, jnp.array(relative, jnp.int32))
+    owners = lax.rem(place + n - jnp.arange(n), n)
     groups = 2
     count = HEADS // 2 // groups
     attended, grad_q, own_kv, come_kv = [], [], [], []
     for g in range(groups):
-        out = attention(kind, cos_t, sin_t, queries, grad_att, keys, values, g * count, count)
+        out = attention(kind, owners, cos_t, sin_t, queries, grad_att, keys, values, g * count, count)
         attended.append(out[0])
         grad_q.append(out[1])
-        own_kv.append(out[2])
-        run = out[2 + n - 1]
-        for s in range(n - 2, 0, -1):
-            run = plus(lax.ppermute(run, "ctx", back), out[2 + s])
-        come_kv.append(lax.ppermute(run, "ctx", back))
-    attended = jnp.concatenate(attended, axis=1)
+        come_kv.append(lax.psum_scatter(out[2], "ctx", scatter_dimension=0, tiled=True))
+        own_kv.append(out[3])
 
     x_late, attended = lax.optimization_barrier((x, attended))
-    mlp_out, grad_mlp, dw_in, dw_out, db_in, db_out, dgain_mlp, dshift_mlp = mlp(
-        x_late, grad_out, gain_mlp, shift_mlp, weight_in, bias_in, weight_out)
-    output, dw_attn = join(x, grad_out, attended, weight_attn, mlp_out, bias_out)
-    sum_out = scatter_sum(dw_out)
-    sum_in = scatter_sum(dw_in)
-    sum_attn = scatter_sum(dw_attn)
-    grad_inputs, dw_qkv, db_qkv, dgain_attn, dshift_attn = tail(
-        spots[0], x, normed, gain_attn, weight_qkv, tables, grad_mlp, grad_q, own_kv, come_kv)
-    sum_qkv = scatter_sum(dw_qkv)
+    mlp_out, grad_mlp, in_send, in_keep, out_send, out_keep, db_in, db_out, dgain_mlp, dshift_mlp = mlp(
+        order, x_late, grad_out, gain_mlp, shift_mlp, weight_in, bias_in, weight_out)
+    output, attn_send, attn_keep = join(order, x, grad_out, attended, weight_attn, mlp_out, bias_out)
+    sum_out = scatter_sum(out_send, out_keep)
+    sum_in = scatter_sum(in_send, in_keep)
+    sum_attn = scatter_sum(attn_send, attn_keep)
+    grad_inputs, qkv_send, qkv_keep, db_qkv, dgain_attn, dshift_attn = tail(
+        spots[0], order, after(x, output), normed, gain_attn, weight_qkv, tables, grad_mlp, grad_q, own_kv, come_kv)
+    sum_qkv = scatter_sum(qkv_send, qkv_keep)
     smalls = [a.reshape(width, -1) for a in (dgain_attn, dshift_attn, db_qkv, db_out, dgain_mlp, dshift_mlp, db_in)]
     used = sum(a.shape[1] for a in smalls)
     packed = jnp.concatenate(smalls + [jnp.zeros((width, PAIR - used), f32)], axis=1).astype(bf16)
-    packed = scatter_sum(packed).astype(f32)
+    packed = packed.reshape(8, width // 8, PAIR)[order].reshape(2, width // 2, PAIR)
+    packed = scatter_sum(packed[0], packed[1]).astype(f32)
     done, at = [], 0
     for a in smalls:
         done.append(packed[:, at:at + a.shape[1]].reshape(-1))

time: 686 us -> 681 us (level)
  starting transfers between devices: 45.8 us -> 31.8 us
  local copies, waits for them, and re-layouts: 37.3 us -> 24.8 us
  waiting for transfers between devices: 204 us -> 214 us
  other arithmetic: 56.5 us -> 65.5 us
    ppermute x31 -> x25, waiting for transfers between devices: 130 us -> 68.7 us  [the longest x5 31.7 us: last_step(): got_b = lax.ppermute(send_b, 'fsdp', pairs_of(2, 8))]
    all_gather x1, waiting for transfers between devices: 13.5 us -> 50.2 us  [fast(): weight_qkv = lax.all_gather(w_qkv, 'fsdp', axis=0, tiled=True)]
    all_gather x3, waiting for transfers between devices: 0.01 us -> 29.7 us  [the longest x1 29.7 us: fast(): lax.all_gather(after(w_attn_out, weight_qkv), 'fsdp', axis=0, tiled=True)]
    squeeze x25 -> x0, local copies, waits for them, and re-layouts: 18.5 us -> none  [pick(): return lax.dynamic_index_in_dim(a, i, axis, keepdims=False)]
    convert_element_type x29 -> x30, other arithmetic: 30 us -> 41.2 us  [plus(): return (a.astype(f32) + b.astype(f32)).astype(bf16)]
    ppermute x31 -> x25, starting transfers between devices: 36 us -> 25.2 us  [the longest x5 7.12 us: last_step(): got_b = lax.ppermute(send_b, 'fsdp', pairs_of(2, 8))]
    ppermute x3, waiting for transfers between devices: 27.9 us -> 35.7 us  [fast(): run = lax.ppermute(run, 'ctx', ring)]
    reduce_scatter x5 -> x7, waiting for transfers between devices: 31.4 us -> 28.5 us  [the longest x5 28.5 us: last_step(): return lax.psum_scatter(part, 'ctx', scatter_dimension=0, tiled=True)]
  transfers between devices with their start and end apart: 46 -> 42, of which waited for: 19 -> 21; matrix products, arithmetic and copies ran while one was open for 13% -> 12% of each run, Pallas kernels for 40% -> 41%
where the time goes in v3:
time: 681 us; the launch traced here: 676 us
  Pallas kernels  311 us (46%)
  waiting for transfers between devices  214 us (31%)
  other arithmetic  65.5 us (10%)
  starting transfers between devices  31.8 us (5%)
  local copies, waits for them, and re-layouts  24.8 us (4%)
  between operations  14.8 us (2%)
  blocking collectives  9.11 us (1%)
    pallas_call x2, Pallas kernels, attention(): pl.pallas_call(partial(attention_kernel, half, n), grid=(pairs,), in_spec...  154 us
    pallas_call x1, Pallas kernels, mlp(): pl.pallas_call(mlp_kernel, grid_spec=pltpu.PrefetchScalarGridSpec(num_sca...  75.4 us
    all_gather x1, waiting for transfers between devices, fast(): weight_qkv = lax.all_gather(w_qkv, 'fsdp', axis=0, tiled=True)  50.2 us
    convert_element_type x30, other arithmetic, plus(): return (a.astype(f32) + b.astype(f32)).astype(bf16)  41.2 us
    pallas_call x4, Pallas kernels, qkv(): pl.pallas_call(partial(qkv_kernel, with_q), grid_spec=pltpu.PrefetchScala...  37.5 us
    ppermute x3, waiting for transfers between devices, fast(): run = lax.ppermute(run, 'ctx', ring)  35.7 us
    pallas_call x1, Pallas kernels, tail(): pl.pallas_call(partial(tail_kernel, groups), grid_spec=pltpu.PrefetchScal...  31.8 us
    ppermute x5, waiting for transfers between devices, last_step(): got_b = lax.ppermute(send_b, 'fsdp', pairs_of(2, 8))  31.7 us
  transfers between devices with their start and end apart: 42, of which 21 were waited for; matrix products, arithmetic and copies ran while one was open for 12% of the time, Pallas kernels for 41%

profile of v3, /device:TPU:0, one launch (start us, length us, event | category | flops | bytes accessed | tf_op | source)
XLA Modules:
  0.0 676.1 jit_solution(12006273708942735992)
XLA Ops:
  8.0 50.2 %all-gather.7.cloned.1.call-done.w_ref = bf16[1024,3072]{1,0:T(8,128)(2,1)} async-done(((bf16[128,3072]{1,0:T(8,128)(2,1)}), bf16[1024,3072]{1,0:T(8,128)(2,1)}) %all-gather.7.cloned.1.call-update) | async-done | bytes 6291472 | tf_op jit(solution)/shard_map/all_gather | solution.py:642
  58.3 29.7 %all-gather.9.cloned.1.call-done.w_ref = bf16[1024,1024]{1,0:T(8,128)(2,1)} async-done(((bf16[128,1024]{1,0:T(8,128)(2,1)}), bf16[1024,1024]{1,0:T(8,128)(2,1)}) %all-gather.9.cloned.1.call-update) | async-done | bytes 2097168 | tf_op jit(solution)/shard_map/all_gather | solution.py:643
  97.4 9.1 %all-gather.1 = bf16[8,1,1536]{2,1,0:T(2,128)(2,1)S(1)} all-gather(bf16[1,1,1536]{2,1,0:T(2,128)(2,1)S(1)} %reshape.569), channel_id=2, replica_groups=mesh['fsdp'=8,'ctx'=4] {'fsdp'}, dimensions={0}, use_global_device_ids=true | all-gather | bytes 27648 | tf_op jit(solution)/shard_map/all_gather | solution.py:636
  106.6 10.6 %collective-permute-done.3.x_ref = bf16[512,1024]{1,0:T(8,128)(2,1)S(1)} collective-permute-done((bf16[512,1024]{1,0:T(8,128)(2,1)S(1)}, bf16[512,1024]{1,0:T(8,128)(2,1)S(1)}, u32[]{:S(2)}, u32[]{:S(2)}) %collective-permute-start.3) | collective-permute-done | bytes 1048608 | tf_op jit(solution)/shard_map/ppermute | solution.py:632
  119.1 6.5 fusion
  125.7 17.8 %collective-permute-done.4.x_ref = bf16[512,1024]{1,0:T(8,128)(2,1)S(1)} collective-permute-done((bf16[512,1024]{1,0:T(8,128)(2,1)S(1)}, bf16[512,1024]{1,0:T(8,128)(2,1)S(1)}, u32[]{:S(2)}, u32[]{:S(2)}) %collective-permute-start.4) | collective-permute-done | bytes 1048608 | tf_op jit(solution)/shard_map/ppermute | solution.py:632
  145.5 7.8 %kv_remote.4 = (bf16[512,1024]{1,0:T(8,128)(2,1)}, bf16[512,1024]{1,0:T(8,128)(2,1)}) custom-call(s32[2]{0:T(128)} %copy-done.22, bf16[512,1024]{1,0:T(8,128)(2,1)} %copy-done.11, f32[1,1024]{1,0:T(1,128)} %bitcast.266, f32[1,1024]{1,0:T(1,128)} %bitcast.271, bf16[1024,3072]{1,0:T(8,128)(2,1)} %all-gather.7.cloned.1.call-done.w_ref, f32[1,3072]{1,0:T(1,128)} %bitcast.256, ...), custom_call_target="tpu_custom_call" | custom-call | flops 2147483648 | bytes 16777216 | tf_op jit(solution)/shard_map/kv_remote/pallas_call | solution.py:257
  153.3 8.2 %kv_remote.3 = (bf16[512,1024]{1,0:T(8,128)(2,1)}, bf16[512,1024]{1,0:T(8,128)(2,1)}) custom-call(s32[2]{0:T(128)} %copy-done.21, bf16[512,1024]{1,0:T(8,128)(2,1)} %copy-done.10, f32[1,1024]{1,0:T(1,128)} %bitcast.267, f32[1,1024]{1,0:T(1,128)} %bitcast.272, bf16[1024,3072]{1,0:T(8,128)(2,1)} %all-gather.7.cloned.1.call-done.w_ref, f32[1,3072]{1,0:T(1,128)} %bitcast.257, ...), custom_call_target="tpu_custom_call" | custom-call | flops 2147483648 | bytes 16777216 | tf_op jit(solution)/shard_map/kv_remote/pallas_call | solution.py:257
  161.6 7.3 %collective-permute-done.5.x_ref = bf16[512,1024]{1,0:T(8,128)(2,1)S(1)} collective-permute-done((bf16[512,1024]{1,0:T(8,128)(2,1)S(1)}, bf16[512,1024]{1,0:T(8,128)(2,1)S(1)}, u32[]{:S(2)}, u32[]{:S(2)}) %collective-permute-start.5) | collective-permute-done | bytes 1048608 | tf_op jit(solution)/shard_map/ppermute | solution.py:632
  169.9 7.8 %kv_remote.5 = (bf16[512,1024]{1,0:T(8,128)(2,1)}, bf16[512,1024]{1,0:T(8,128)(2,1)}) custom-call(s32[2]{0:T(128)} %copy-done.20, bf16[512,1024]{1,0:T(8,128)(2,1)} %copy-done.12, f32[1,1024]{1,0:T(1,128)} %bitcast.268, f32[1,1024]{1,0:T(1,128)} %bitcast.273, bf16[1024,3072]{1,0:T(8,128)(2,1)} %all-gather.7.cloned.1.call-done.w_ref, f32[1,3072]{1,0:T(1,128)} %bitcast.258, ...), custom_call_target="tpu_custom_call" | custom-call | flops 2147483648 | bytes 16777216 | tf_op jit(solution)/shard_map/kv_remote/pallas_call | solution.py:257
  177.7 13.6 %qkv_own.1 = (bf16[1024,1024]{1,0:T(8,128)(2,1)}, bf16[1024,1024]{1,0:T(8,128)(2,1)}, bf16[1024,1024]{1,0:T(8,128)(2,1)}, bf16[1024,1024]{1,0:T(8,128)(2,1)}) custom-call(s32[4]{0:T(128)} %copy-done.30, bf16[1024,1024]{1,0:T(8,128)(2,1)} %bitcast.250, f32[1,1024]{1,0:T(1,128)} %bitcast.269, f32[1,1024]{1,0:T(1,128)} %bitcast.274, ...), custom_call_target="tpu_custom_call" | custom-call | flops 6442450944 | bytes 16777216 | tf_op jit(solution)/shard_map/qkv_own/pallas_call | solution.py:257
  191.4 5.3 convert_bitcast_fusion.do_ref
  196.7 77.0 %attention.3 = (bf16[1024,512]{1,0:T(8,128)(2,1)}, bf16[1024,512]{1,0:T(8,128)(2,1)}, bf16[2048,1024]{1,0:T(8,128)(2,1)}, bf16[512,1024]{1,0:T(8,128)(2,1)}) custom-call(f32[4,8]{1,0:T(4,128)} %add_select_fusion.kind_ref, s32[4]{0:T(128)} %compare_select_fusion.3.owner_ref, f32[8,1024]{1,0:T(8,128)} %get-tuple-element.137.cos_ref, ...), custom_call_target="tpu_custom_call" | custom-call | flops 57982058496 | bytes 16777216 | tf_op jit(solution)/shard_map/attention/pallas_call | solution.py:557
  273.7 76.9 %attention.2 = (bf16[1024,512]{1,0:T(8,128)(2,1)}, bf16[1024,512]{1,0:T(8,128)(2,1)}, bf16[2048,1024]{1,0:T(8,128)(2,1)}, bf16[512,1024]{1,0:T(8,128)(2,1)}) custom-call(f32[4,8]{1,0:T(4,128)} %add_select_fusion.kind_ref, s32[4]{0:T(128)} %compare_select_fusion.3.owner_ref, f32[8,1024]{1,0:T(8,128)} %get-tuple-element.137.cos_ref, ...), custom_call_target="tpu_custom_call" | custom-call | flops 57982058496 | bytes 16777216 | tf_op jit(solution)/shard_map/attention/pallas_call | solution.py:557
  351.9 75.4 %mlp.1 = (f32[1024,1024]{1,0:T(8,128)}, f32[1024,1024]{1,0:T(8,128)}, bf16[512,4096]{1,0:T(8,128)(2,1)}, bf16[512,4096]{1,0:T(8,128)(2,1)}, bf16[2048,1024]{1,0:...) custom-call(s32[8]{0:T(128)} %get-tuple-element.139.order_ref, ...), custom_call_target="tpu_custom_call" | custom-call | flops 51539607552 | bytes 50331648 | tf_op jit(solution)/shard_map/mlp/pallas_call | solution.py:202
  427.3 12.0 %join.1 = (bf16[1024,1024]{1,0:T(8,128)(2,1)}, bf16[512,1024]{1,0:T(8,128)(2,1)}, bf16[512,1024]{1,0:T(8,128)(2,1)}) custom-call(s32[8]{0:T(128)} %get-tuple-element.139.order_ref, bf16[1024,1024]{1,0:T(8,128)(2,1)} %bitcast.252, bf16[1024,1024]{1,0:T(8,128)(2,1)} %bitcast.286, bf16[1024,1024]{1,0:T(8,128)(2,1)} %all-gather.9.cloned.1.call-done.w_ref, ...), custom_call_target="tpu_custom_call" | custom-call | flops 4294967296 | bytes 16777216 | tf_op jit(solution)/shard_map/join/pallas_call | solution.py:401
  439.4 31.8 %tail.1 = (f32[1024,1024]{1,0:T(8,128)}, bf16[512,3072]{1,0:T(8,128)(2,1)}, bf16[512,3072]{1,0:T(8,128)(2,1)}, f32[1,3072]{1,0:T(1,128)}, f32[1,1024]{1,0:T(1,128)}, /*index=5*/f32[1,1024]{1,0:T(1,128)}) custom-call(s32[4]{0:T(128)} %copy-done.30, s32[8]{0:T(128)} %get-tuple-element.139.order_ref, bf16[1024,1024]{1,0:T(8,128)(2,1)} %bitcast.253, ...), custom_call_target="tpu_custom_call" | custom-call | flops 12884901888 | bytes 33554432 | tf_op jit(solution)/shard_map/tail/pallas_call | solution.py:353
  482.5 3.2 concatenate.49
  490.9 2.7 collective-permute-done.9
  502.4 2.5 collective-permute-done.8
  510.6 3.1 collective-permute-done.19
  525.1 2.6 add_convert_fusion.9
  532.4 9.4 %collective-permute-done.14 = bf16[2,64,3072]{2,1,0:T(8,128)(2,1)} collective-permute-done((bf16[2,64,3072]{2,1,0:T(8,128)(2,1)S(1)}, bf16[2,64,3072]{2,1,0:T(8,128)(2,1)}, u32[]{:S(2)}, u32[]{:S(2)}) %collective-permute-start.14) | collective-permute-done | bytes 786464 | tf_op jit(solution)/shard_map/ppermute | solution.py:602
  544.8 2.7 collective-permute-done.12
  549.8 4.4 add_convert_fusion.5
  555.2 3.7 add_convert_fusion.7
  559.7 3.5 add_convert_fusion.1
  564.6 3.6 add_convert_fusion.3
  572.3 11.0 %collective-permute-done.24 = bf16[2,64,4096]{2,1,0:T(8,128)(2,1)} collective-permute-done((bf16[2,64,4096]{2,1,0:T(8,128)(2,1)}, bf16[2,64,4096]{2,1,0:T(8,128)(2,1)}, u32[]{:S(2)}, u32[]{:S(2)}) %collective-permute-start.24) | collective-permute-done | bytes 1048608 | tf_op jit(solution)/shard_map/ppermute | solution.py:602
  588.5 22.5 %collective-permute-done.25 = bf16[64,4096]{1,0:T(8,128)(2,1)S(1)} collective-permute-done((bf16[64,4096]{1,0:T(8,128)(2,1)S(1)}, bf16[64,4096]{1,0:T(8,128)(2,1)S(1)}, u32[]{:S(2)}, u32[]{:S(2)}) %collective-permute-start.25) | collective-permute-done | bytes 524320 | tf_op jit(solution)/shard_map/ppermute | solution.py:608
  619.5 5.7 collective-permute-done.30
  641.1 26.4 %reduce-scatter.20.cloned.1.call-done = bf16[128,1024]{1,0:T(8,128)(2,1)} async-done(((bf16[512,1024]{1,0:T(8,128)(2,1)}), bf16[128,1024]{1,0:T(8,128)(2,1)}) %reduce-scatter.20.cloned.1.call-update) | async-done | bytes 262160 | tf_op jit(solution)/shard_map/reduce_scatter | solution.py:610
  (235 shorter events, 107.1 us)
Async XLA Ops:
  7.2 51.0 %all-gather.7.cloned.1.call-start = ((), (), s32[]{:S(2)}) async-start(), calls=%async_computation.7 | async-start | bytes 7077888 | tf_op jit(solution)/shard_map/all_gather | solution.py:642
  7.9 80.1 %all-gather.9.cloned.1.call-start = ((), (), s32[]{:S(2)}) async-start(), calls=%async_computation.8 | async-start | bytes 2359296 | tf_op jit(solution)/shard_map/all_gather | solution.py:643
  58.3 293.6 %all-gather.11.cloned.1.call-start = ((), (), s32[]{:S(2)}) async-start(), calls=%async_computation.9 | async-start | bytes 9437184 | tf_op jit(solution)/shard_map/all_gather | solution.py:644
  88.0 263.9 %all-gather.13.cloned.1.call-start = ((), (), s32[]{:S(2)}) async-start(), calls=%async_computation.10 | async-start | bytes 9437184 | tf_op jit(solution)/shard_map/all_gather | solution.py:645
  88.6 350.8 %reduce-scatter.10.cloned.1.call-start = ((), (), s32[]{:S(2)}) async-start(), calls=%async_computation.12 | async-start | bytes 5242880 | tf_op jit(solution)/shard_map/reduce_scatter | solution.py:682
  89.9 27.2 %collective-permute-start.3 = (bf16[512,1024]{1,0:T(8,128)(2,1)S(1)}, bf16[512,1024]{1,0:T(8,128)(2,1)S(1)}, u32[]{:S(2)}, u32[]{:S(2)}) collective-permute-start(bf16[512,1024]{1,0:T(8,128)(2,1)S(1)} %slice_bitcast_fusion), channel_id=1, source_target_pairs={{0,1},{1,2},{2,3},{3,0},{4,5},{5,6},{6,7},{7,4},{8,9},{9,10},{10,1... | collective-permute-start | bytes 3145736 | tf_op jit(solution)/shard_map/ppermute | solution.py:632
  91.6 52.8 %collective-permute-start.2 = (s32[2]{0:T(128)S(1)}, s32[2]{0:T(128)S(1)}, u32[]{:S(2)}, u32[]{:S(2)}) collective-permute-start(s32[2]{0:T(128)S(1)} %bitcast.287), channel_id=1, source_target_pairs={{0,3},{1,0},{2,1},{3,2},{4,7},{5,4},{6,5},{7,6},{8,11},{9,8},{10,9... | collective-permute-start | bytes 32 | tf_op jit(solution)/shard_map/ppermute | solution.py:634
  94.0 50.4 %collective-permute-start.1 = (s32[2]{0:T(128)S(1)}, s32[2]{0:T(128)S(1)}, u32[]{:S(2)}, u32[]{:S(2)}) collective-permute-start(s32[2]{0:T(128)S(1)} %bitcast.288), channel_id=1, source_target_pairs={{0,2},{1,3},{2,0},{3,1},{4,6},{5,7},{6,4},{7,5},{8,10},{9,11},{10,... | collective-permute-start | bytes 32 | tf_op jit(solution)/shard_map/ppermute | solution.py:634
  94.6 49.9 %collective-permute-start = (s32[2]{0:T(128)S(1)}, s32[2]{0:T(128)S(1)}, u32[]{:S(2)}, u32[]{:S(2)}) collective-permute-start(s32[2]{0:T(128)S(1)} %bitcast.289), channel_id=1, source_target_pairs={{0,1},{1,2},{2,3},{3,0},{4,5},{5,6},{6,7},{7,4},{8,9},{9,10},{10,1... | collective-permute-start | bytes 32 | tf_op jit(solution)/shard_map/ppermute | solution.py:634
  117.1 26.3 %collective-permute-start.4 = (bf16[512,1024]{1,0:T(8,128)(2,1)S(1)}, bf16[512,1024]{1,0:T(8,128)(2,1)S(1)}, u32[]{:S(2)}, u32[]{:S(2)}) collective-permute-start(bf16[512,1024]{1,0:T(8,128)(2,1)S(1)} %collective-permute-done.3.x_ref), channel_id=1, source_target_pairs={{0,1},{1,2},{2,3},{3,0},{4,5},{5,6},{6,7},{7,4},{8,9},{9,10},{10,1... | collective-permute-start | bytes 3145736 | tf_op jit(solution)/shard_map/ppermute | solution.py:632
  143.4 25.5 %collective-permute-start.5 = (bf16[512,1024]{1,0:T(8,128)(2,1)S(1)}, bf16[512,1024]{1,0:T(8,128)(2,1)S(1)}, u32[]{:S(2)}, u32[]{:S(2)}) collective-permute-start(bf16[512,1024]{1,0:T(8,128)(2,1)S(1)} %collective-permute-done.4.x_ref), channel_id=1, source_target_pairs={{0,1},{1,2},{2,3},{3,0},{4,5},{5,6},{6,7},{7,4},{8,9},{9,10},{10,1... | collective-permute-start | bytes 3145736 | tf_op jit(solution)/shard_map/ppermute | solution.py:632
  273.7 165.7 %reduce-scatter.8.cloned.1.call-start = ((), (), s32[]{:S(2)}) async-start(), calls=%async_computation.11 | async-start | bytes 5242880 | tf_op jit(solution)/shard_map/reduce_scatter | solution.py:682
  350.7 279.1 %reduce-scatter.12.cloned.1.call-start = ((), (), s32[]{:S(2)}) async-start(), calls=%async_computation.13 | async-start | bytes 40960 | tf_op jit(solution)/shard_map/reduce_scatter | solution.py:610
  481.7 41.7 %collective-permute-start.11 = (bf16[512,3072]{1,0:T(8,128)(2,1)}, bf16[512,3072]{1,0:T(8,128)(2,1)S(1)}, u32[]{:S(2)}, u32[]{:S(2)}) collective-permute-start(bf16[512,3072]{1,0:T(8,128)(2,1)} %get-tuple-element.94), channel_id=1, source_target_pairs={{0,4},{4,0},{8,12},{12,8},{16,20},{20,16},{24,28},{28,24},{1,5},{5... | collective-permute-start | bytes 9437192 | tf_op jit(solution)/shard_map/ppermute | solution.py:590
  488.6 16.4 %collective-permute-start.16 = (bf16[512,1024]{1,0:T(8,128)(2,1)}, bf16[512,1024]{1,0:T(8,128)(2,1)S(1)}, u32[]{:S(2)}, u32[]{:S(2)}) collective-permute-start(bf16[512,1024]{1,0:T(8,128)(2,1)} %get-tuple-element.96), channel_id=1, source_target_pairs={{0,4},{4,0},{8,12},{12,8},{16,20},{20,16},{24,28},{28,24},{1,5},{5... | collective-permute-start | bytes 3145736 | tf_op jit(solution)/shard_map/ppermute | solution.py:590
  488.7 61.1 %collective-permute-start.21 = (bf16[512,4096]{1,0:T(8,128)(2,1)}, bf16[512,4096]{1,0:T(8,128)(2,1)}, u32[]{:S(2)}, u32[]{:S(2)}) collective-permute-start(bf16[512,4096]{1,0:T(8,128)(2,1)} %get-tuple-element.98), channel_id=1, source_target_pairs={{0,4},{4,0},{8,12},{12,8},{16,20},{20,16},{24,28},{28,24},{1,5},{5... | collective-permute-start | bytes 12582920 | tf_op jit(solution)/shard_map/ppermute | solution.py:590
  489.1 70.6 %collective-permute-start.26 = (bf16[2048,1024]{1,0:T(8,128)(2,1)}, bf16[2048,1024]{1,0:T(8,128)(2,1)}, u32[]{:S(2)}, u32[]{:S(2)}) collective-permute-start(bf16[2048,1024]{1,0:T(8,128)(2,1)} %get-tuple-element.100), channel_id=1, source_target_pairs={{0,4},{4,0},{8,12},{12,8},{16,20},{20,16},{24,28},{28,24},{1,5},{5... | collective-permute-start | bytes 12582920 | tf_op jit(solution)/shard_map/ppermute | solution.py:590
  510.6 123.5 %reduce-scatter.16.cloned.1.call-start = ((), (), s32[]{:S(2)}) async-start(), calls=%async_computation.15 | async-start | bytes 327680 | tf_op jit(solution)/shard_map/reduce_scatter | solution.py:610
  527.7 14.1 %collective-permute-start.14 = (bf16[2,64,3072]{2,1,0:T(8,128)(2,1)S(1)}, bf16[2,64,3072]{2,1,0:T(8,128)(2,1)}, u32[]{:S(2)}, u32[]{:S(2)}) collective-permute-start(bf16[2,64,3072]{2,1,0:T(8,128)(2,1)S(1)} %get-tuple-element.117), channel_id=1, source_target_pairs={{0,16},{4,20},{8,24},{12,28},{16,0},{20,4},{24,8},{28,12},{1,17},{... | collective-permute-start | bytes 2359304 | tf_op jit(solution)/shard_map/ppermute | solution.py:602
  530.7 16.8 %collective-permute-start.12 = (bf16[2,64,3072]{2,1,0:T(8,128)(2,1)S(1)}, bf16[2,64,3072]{2,1,0:T(8,128)(2,1)}, u32[]{:S(2)}, u32[]{:S(2)}) collective-permute-start(bf16[2,64,3072]{2,1,0:T(8,128)(2,1)S(1)} %get-tuple-element.115), channel_id=1, source_target_pairs={{0,8},{4,12},{8,0},{12,4},{16,24},{20,28},{24,16},{28,20},{1,9},{5... | collective-permute-start | bytes 2359304 | tf_op jit(solution)/shard_map/ppermute | solution.py:601
  532.3 103.3 %reduce-scatter.14.cloned.1.call-start = ((), (), s32[]{:S(2)}) async-start(), calls=%async_computation.14 | async-start | bytes 983040 | tf_op jit(solution)/shard_map/reduce_scatter | solution.py:610
  542.9 25.3 %collective-permute-start.15 = (bf16[64,3072]{1,0:T(8,128)(2,1)S(1)}, bf16[64,3072]{1,0:T(8,128)(2,1)S(1)}, u32[]{:S(2)}, u32[]{:S(2)}) collective-permute-start(bf16[64,3072]{1,0:T(8,128)(2,1)S(1)} %fusion.38), channel_id=1, source_target_pairs={{0,8},{4,12},{8,0},{12,4},{16,24},{20,28},{24,16},{28,20},{1,9},{5... | collective-permute-start | bytes 1179656 | tf_op jit(solution)/shard_map/ppermute | solution.py:608
  548.6 21.5 %collective-permute-start.13 = (bf16[64,3072]{1,0:T(8,128)(2,1)S(1)}, bf16[64,3072]{1,0:T(8,128)(2,1)S(1)}, u32[]{:S(2)}, u32[]{:S(2)}) collective-permute-start(bf16[64,3072]{1,0:T(8,128)(2,1)S(1)} %fusion.36), channel_id=1, source_target_pairs={{0,16},{4,20},{8,24},{12,28},{16,0},{20,4},{24,8},{28,12},{1,17},{... | collective-permute-start | bytes 1179656 | tf_op jit(solution)/shard_map/ppermute | solution.py:607
  554.2 29.1 %collective-permute-start.24 = (bf16[2,64,4096]{2,1,0:T(8,128)(2,1)}, bf16[2,64,4096]{2,1,0:T(8,128)(2,1)}, u32[]{:S(2)}, u32[]{:S(2)}) collective-permute-start(bf16[2,64,4096]{2,1,0:T(8,128)(2,1)} %get-tuple-element.113), channel_id=1, source_target_pairs={{0,16},{4,20},{8,24},{12,28},{16,0},{20,4},{24,8},{28,12},{1,17},{... | collective-permute-start | bytes 3145736 | tf_op jit(solution)/shard_map/ppermute | solution.py:602
  558.8 26.9 %collective-permute-start.22 = (bf16[2,64,4096]{2,1,0:T(8,128)(2,1)}, bf16[2,64,4096]{2,1,0:T(8,128)(2,1)}, u32[]{:S(2)}, u32[]{:S(2)}) collective-permute-start(bf16[2,64,4096]{2,1,0:T(8,128)(2,1)} %get-tuple-element.111), channel_id=1, source_target_pairs={{0,8},{4,12},{8,0},{12,4},{16,24},{20,28},{24,16},{28,20},{1,9},{5... | collective-permute-start | bytes 3145736 | tf_op jit(solution)/shard_map/ppermute | solution.py:601
  563.3 51.4 %collective-permute-start.29 = (bf16[2,256,1024]{2,1,0:T(8,128)(2,1)}, bf16[2,256,1024]{2,1,0:T(8,128)(2,1)}, u32[]{:S(2)}, u32[]{:S(2)}) collective-permute-start(bf16[2,256,1024]{2,1,0:T(8,128)(2,1)} %get-tuple-element.109), channel_id=1, source_target_pairs={{0,16},{4,20},{8,24},{12,28},{16,0},{20,4},{24,8},{28,12},{1,17},{... | collective-permute-start | bytes 3145736 | tf_op jit(solution)/shard_map/ppermute | solution.py:602
  568.2 48.7 %collective-permute-start.27 = (bf16[2,256,1024]{2,1,0:T(8,128)(2,1)}, bf16[2,256,1024]{2,1,0:T(8,128)(2,1)}, u32[]{:S(2)}, u32[]{:S(2)}) collective-permute-start(bf16[2,256,1024]{2,1,0:T(8,128)(2,1)} %get-tuple-element.107), channel_id=1, source_target_pairs={{0,8},{4,12},{8,0},{12,4},{16,24},{20,28},{24,16},{28,20},{1,9},{5... | collective-permute-start | bytes 3145736 | tf_op jit(solution)/shard_map/ppermute | solution.py:601
  572.3 67.0 %reduce-scatter.18.cloned.1.call-start = ((), (), s32[]{:S(2)}) async-start(), calls=%async_computation.16 | async-start | bytes 1310720 | tf_op jit(solution)/shard_map/reduce_scatter | solution.py:610
  584.7 26.3 %collective-permute-start.25 = (bf16[64,4096]{1,0:T(8,128)(2,1)S(1)}, bf16[64,4096]{1,0:T(8,128)(2,1)S(1)}, u32[]{:S(2)}, u32[]{:S(2)}) collective-permute-start(bf16[64,4096]{1,0:T(8,128)(2,1)S(1)} %fusion.30), channel_id=1, source_target_pairs={{0,8},{4,12},{8,0},{12,4},{16,24},{20,28},{24,16},{28,20},{1,9},{5... | collective-permute-start | bytes 1572872 | tf_op jit(solution)/shard_map/ppermute | solution.py:608
  586.9 25.4 %collective-permute-start.23 = (bf16[64,4096]{1,0:T(8,128)(2,1)S(1)}, bf16[64,4096]{1,0:T(8,128)(2,1)S(1)}, u32[]{:S(2)}, u32[]{:S(2)}) collective-permute-start(bf16[64,4096]{1,0:T(8,128)(2,1)S(1)} %fusion.28), channel_id=1, source_target_pairs={{0,16},{4,20},{8,24},{12,28},{16,0},{20,4},{24,8},{28,12},{1,17},{... | collective-permute-start | bytes 1572872 | tf_op jit(solution)/shard_map/ppermute | solution.py:607
  614.6 52.9 %reduce-scatter.20.cloned.1.call-start = ((), (), s32[]{:S(2)}) async-start(), calls=%async_computation.17 | async-start | bytes 1310720 | tf_op jit(solution)/shard_map/reduce_scatter | solution.py:610
  615.9 9.2 %collective-permute-start.30 = (bf16[256,1024]{1,0:T(8,128)(2,1)S(1)}, bf16[256,1024]{1,0:T(8,128)(2,1)S(1)}, u32[]{:S(2)}, u32[]{:S(2)}) collective-permute-start(bf16[256,1024]{1,0:T(8,128)(2,1)S(1)} %fusion.34), channel_id=1, source_target_pairs={{0,8},{4,12},{8,0},{12,4},{16,24},{20,28},{24,16},{28,20},{1,9},{5... | collective-permute-start | bytes 1572872 | tf_op jit(solution)/shard_map/ppermute | solution.py:608
  (41 other events, 747.3 us)
Sparse Core Ops, SparseCore 0:
  9.9 48.2 all-gather.6
  60.0 27.8 all-gather.8
  89.9 54.5 all-gather.10
  146.2 54.3 all-gather.12
  273.8 74.0 reduce-scatter.9
  350.8 76.6 reduce-scatter.7
  510.7 16.1 reduce-scatter.11
  532.4 17.0 reduce-scatter.15
  572.4 20.4 reduce-scatter.13
  614.7 24.5 reduce-scatter.17
  641.7 25.7 reduce-scatter.19

commit v4 on v3

--- a/solution.py
+++ b/solution.py
@@ -271,61 +271,76 @@
     )(spots, x, gain.reshape(1, -1), shift.reshape(1, -1), weight, bias.reshape(1, -1), *tables)
 
 
-def tail_kernel(groups, spot_ref, order_ref, x_ref, h_ref, gain_ref, w_ref, cos_ref, low_ref, high_ref, gin_ref, *refs):
-    dq_refs, own_refs, come_refs = refs[:groups], refs[groups:2 * groups], refs[2 * groups:3 * groups]
-    grad_ref, send_ref, keep_ref, db_ref, dgain_ref, dshift_ref, p_ref, turned_ref, gh_ref = refs[3 * groups:]
+def tail_kernel(groups, spot_ref, order_ref, x_ref, c_ref, h_ref, gain_ref, w_ref, cos_ref, low_ref, high_ref, gin_ref, *refs):
+    att_refs, dq_refs, own_refs, come_refs = (refs[i * groups:(i + 1) * groups] for i in range(4))
+    grad_ref, send_ref, keep_ref, db_ref, dgain_ref, dshift_ref, p_ref, turned_ref, gh_ref = refs[4 * groups:]
     step = pl.program_id(0)
     rows = x_ref.shape[0]
     half = rows // 2
     blocks = [slice(r, r + RB) for r in range(0, rows, RB)]
-    part = dq_refs[0].shape[1]
+    columns = []
+    for g in range(groups):
+        columns += [(g, at) for at in range(0, dq_refs[g].shape[1], PAIR)]
 
     def put(shift):
         for r in blocks:
             spot = pl.ds(pl.multiple_of(spot_ref[r.start // RB] * RB, RB), RB)
-            for g in range(groups):
-                for at in range(0, part, PAIR):
-                    if shift is None:
-                        p_ref[r, g * part + at:g * part + at + PAIR] = dq_refs[g][r, at:at + PAIR]
-                        continue
-                    lanes = slice(2 * at + shift, 2 * at + shift + PAIR)
-                    if r.start < half:
-                        t = come_refs[g][r, lanes].astype(f32)
-                    else:
-                        t = own_refs[g][r.start - half:r.stop - half, lanes].astype(f32)
-                    if shift == 0:
-                        t = turn_lanes(t, cos_ref[spot, :], low_ref[spot, :], high_ref[spot, :], -1.0)
-                    p_ref[r, g * part + at:g * part + at + PAIR] = t.astype(bf16)
+            for to, (g, at) in enumerate(columns):
+                lanes = slice(2 * at + shift, 2 * at + shift + PAIR)
+                if r.start < half:
+                    t = come_refs[g][r, lanes].astype(f32)
+                else:
+                    t = own_refs[g][r.start - half:r.stop - half, lanes].astype(f32)
+                if shift == 0:
+                    t = turn_lanes(t, cos_ref[spot, :], low_ref[spot, :], high_ref[spot, :], -1.0)
+                p_ref[r, to * PAIR:(to + 1) * PAIR] = t.astype(bf16)
+
+    def lay(some):
+        for to, (g, at) in enumerate(columns):
+            p_ref[:, to * PAIR:(to + 1) * PAIR] = some[g][:, at:at + PAIR]
+
+    def give(dw):
+        send_ref[...] = dw[:send_ref.shape[0]]
+        keep_ref[...] = dw[send_ref.shape[0]:]
 
     @pl.when(step == 0)
     def _():
+        lay(att_refs)
+        reorder(order_ref, p_ref, turned_ref)
+        give(mm(turned_ref[...], c_ref[...], TN).astype(bf16))
+
+    @pl.when(step == 1)
+    def _():
         reorder(order_ref, h_ref, turned_ref)
-        put(None)
+        lay(dq_refs)
+
+    @pl.when(step == 2)
+    def _():
+        put(0)
+
+    @pl.when(step == 3)
+    def _():
+        put(PAIR)
+
+    @pl.when(step == 1)
+    def _():
         for r in blocks:
             gh_ref[r, :] = mm(p_ref[r, :], w_ref[...], NT)
 
-    @pl.when(step == 1)
-    def _():
-        put(0)
-
-    @pl.when(step == 2)
-    def _():
-        put(PAIR)
-
-    @pl.when(step > 0)
+    @pl.when(step > 1)
     def _():
         for r in blocks:
             gh_ref[r, :] += mm(p_ref[r, :], w_ref[...], NT)
 
-    dw = mm(turned_ref[...], p_ref[...], TN).astype(bf16)
-    send_ref[...] = dw[:send_ref.shape[0]]
-    keep_ref[...] = dw[send_ref.shape[0]:]
-    db = jnp.zeros(db_ref.shape, f32)
-    for r in blocks:
-        db += col_sum(p_ref[r, :].astype(f32))
-    db_ref[...] = db
-
-    @pl.when(step == 2)
+    @pl.when(step > 0)
+    def _():
+        give(mm(turned_ref[...], p_ref[...], TN).astype(bf16))
+        db = jnp.zeros(db_ref.shape, f32)
+        for r in blocks:
+            db += col_sum(p_ref[r, :].astype(f32))
+        db_ref[...] = db
+
+    @pl.when(step == 3)
     def _():
         dgain = jnp.zeros(dgain_ref.shape, f32)
         dshift = jnp.zeros(dshift_ref.shape, f32)
@@ -339,7 +354,7 @@
         dshift_ref[...] = dshift
 
 
-def tail(spots, order, x, h, gain, weight, tables, gin, dqs, owns, comes):
+def tail(spots, order, x, c, h, gain, weights, tables, gin, attended, dqs, owns, comes):
     rows, width = x.shape
     groups = len(dqs)
     s = jax.ShapeDtypeStruct
@@ -347,73 +362,75 @@
     def full(a):
         return pl.BlockSpec(a.shape, lambda j, spot, o: (0, 0))
 
+    def behind(j):
+        return jnp.maximum(j - 1, 0)
+
     line = pl.BlockSpec((1, width), lambda j, spot, o: (0, 0))
-    down = pl.BlockSpec((width // 2, width), lambda j, spot, o: (0, j))
-    arrays = [*tables, gin, *dqs, *owns, *comes]
+    down = pl.BlockSpec((width // 2, width), lambda j, spot, o: (0, lax.rem(j + 3, 4)))
+    arrays = [*tables, gin, *attended, *dqs, *owns, *comes]
     return pl.pallas_call(
         partial(tail_kernel, groups),
         grid_spec=pltpu.PrefetchScalarGridSpec(
             num_scalar_prefetch=2,
-            grid=(3,),
-            in_specs=[full(x), full(h), line, pl.BlockSpec((width, width), lambda j, spot, o: (0, j))] + [full(a) for a in arrays],
-            out_specs=[full(x), down, down,
-                       pl.BlockSpec((1, width), lambda j, spot, o: (0, j)), line, line],
+            grid=(4,),
+            in_specs=[full(x), full(c), full(h), line, pl.BlockSpec((width, width), lambda j, spot, o: (0, behind(j)))]
+            + [full(a) for a in arrays],
+            out_specs=[full(x), down, down, pl.BlockSpec((1, width), lambda j, spot, o: (0, behind(j))), line, line],
             scratch_shapes=[vmem(rows, width, dtype=bf16), vmem(rows, width, dtype=bf16), vmem(rows, width)],
         ),
-        out_shape=[s((rows, width), f32), s((width // 2, 3 * width), bf16), s((width // 2, 3 * width), bf16), s((1, 3 * width), f32), s((1, width), f32),
-                   s((1, width), f32)],
+        out_shape=[s((rows, width), f32), s((width // 2, 4 * width), bf16), s((width // 2, 4 * width), bf16),
+                   s((1, 3 * width), f32), s((1, width), f32), s((1, width), f32)],
         compiler_params=params(),
-        cost_estimate=pl.CostEstimate(flops=12 * rows * width * width, bytes_accessed=32 << 20, transcendentals=0),
+        cost_estimate=pl.CostEstimate(flops=14 * rows * width * width, bytes_accessed=32 << 20, transcendentals=0),
         name="tail",
-    )(spots, order, x, h, gain.reshape(1, -1), weight, *arrays)
-
-
-def join_kernel(groups, order_ref, x_ref, c_ref, w_ref, mlp_ref, b_ref, *refs):
-    att_refs, (out_ref, send_ref, keep_ref, att_ref, turned_ref, acc_ref) = refs[:groups], refs[groups:]
-    step = pl.program_id(0)
-    part = att_refs[0].shape[1]
-    for g in range(groups):
-        att_ref[:, g * part:(g + 1) * part] = att_refs[g][...]
+    )(spots, order, x, c, h, gain.reshape(1, -1), weights, *arrays)
+
+
+def join_kernel(groups, x_ref, w_ref, mlp_ref, b_ref, *refs):
+    att_refs, (out_ref, att_ref) = refs[:groups], refs[groups:]
+    at = 0
+    for ref in att_refs:
+        att_ref[:, at:at + ref.shape[1]] = ref[...]
+        at += ref.shape[1]
     out = x_ref[...].astype(f32) + mm(att_ref[...], w_ref[...], NN) + mlp_ref[...] + b_ref[...]
     out_ref[...] = out.astype(bf16)
-    reorder(order_ref, att_ref, turned_ref)
-
-    @pl.when(step == 0)
-    def _():
-        acc_ref[...] = mm(turned_ref[...], c_ref[...], TN)
-
-    @pl.when(step > 0)
-    def _():
-        acc_ref[...] += mm(turned_ref[...], c_ref[...], TN)
-
-    @pl.when(step == pl.num_programs(0) - 1)
-    def _():
-        half = send_ref.shape[0]
-        send_ref[...] = acc_ref[:half, :].astype(bf16)
-        keep_ref[...] = acc_ref[half:, :].astype(bf16)
-
-
-def join(order, x, c, attended, weight, mlp_out, bias):
+
+
+def join(x, attended, weights, mlp_out, bias):
     rows, width = x.shape
     s = jax.ShapeDtypeStruct
-    block = pl.BlockSpec((RB, width), lambda j, o: (j, 0))
-    half = pl.BlockSpec((width // 2, width), lambda j, o: (0, 0))
+    block = pl.BlockSpec((RB, width), lambda j: (j, 0))
     return pl.pallas_call(
         partial(join_kernel, len(attended)),
-        grid_spec=pltpu.PrefetchScalarGridSpec(
-            num_scalar_prefetch=1,
-            grid=(rows // RB,),
-            in_specs=[block, block, pl.BlockSpec((width, width), lambda j, o: (0, 0)), block,
-                      pl.BlockSpec((1, width), lambda j, o: (0, 0))]
-            + [pl.BlockSpec((RB, a.shape[1]), lambda j, o: (j, 0)) for a in attended],
-            out_specs=[block, half, half],
-            scratch_shapes=[vmem(RB, width, dtype=bf16), vmem(RB, width, dtype=bf16), vmem(width, width)],
-        ),
-        out_shape=[s((rows, width), bf16), s((width // 2, width), bf16), s((width // 2, width), bf16)],
+        grid=(rows // RB,),
+        in_specs=[block, pl.BlockSpec((width, width), lambda j: (0, 3)), block, pl.BlockSpec((1, width), lambda j: (0, 0))]
+        + [pl.BlockSpec((RB, a.shape[1]), lambda j: (j, 0)) for a in attended],
+        out_specs=block,
+        out_shape=s((rows, width), bf16),
+        scratch_shapes=[vmem(RB, width, dtype=bf16)],
         compiler_params=params(),
-        cost_estimate=pl.CostEstimate(flops=4 * rows * width * width, bytes_accessed=16 << 20, transcendentals=0),
+        cost_estimate=pl.CostEstimate(flops=2 * rows * width * width, bytes_accessed=12 << 20, transcendentals=0),
         name="join",
-    )(order, x, c, weight, mlp_out, bias.reshape(1, -1), *attended)
+    )(x, weights, mlp_out, bias.reshape(1, -1), *attended)
+
+
+def spread_kernel(c_ref, w_ref, out_ref):
+    out_ref[...] = mm(c_ref[...], w_ref[...], NT).astype(bf16)
+
+
+def spread(c, weights):
+    rows, width = c.shape
+    block = pl.BlockSpec((RB, width), lambda j: (j, 0))
+    return pl.pallas_call(
+        spread_kernel,
+        grid=(rows // RB,),
+        in_specs=[block, pl.BlockSpec((width, width), lambda j: (0, 3))],
+        out_specs=block,
+        out_shape=jax.ShapeDtypeStruct((rows, width), bf16),
+        compiler_params=params(),
+        cost_estimate=pl.CostEstimate(flops=2 * rows * width * width, bytes_accessed=8 << 20, transcendentals=0),
+        name="spread",
+    )(c, weights)
 
 
 def fold(x, op):
@@ -639,10 +656,7 @@
         full.append(small[:, at:at + a.shape[0]].reshape(-1).astype(f32))
         at += a.shape[0]
     gain_attn, shift_attn, bias_qkv, bias_out, gain_mlp, shift_mlp, bias_in = full
-    weight_qkv = lax.all_gather(w_qkv, "fsdp", axis=0, tiled=True)
-    weight_attn = lax.all_gather(after(w_attn_out, weight_qkv), "fsdp", axis=0, tiled=True)
-    weight_in = lax.all_gather(after(w_in, weight_attn), "fsdp", axis=0, tiled=True)
-    weight_out = lax.all_gather(after(w_out, weight_attn), "fsdp", axis=0, tiled=True)
+    weights = lax.all_gather(jnp.concatenate([w_qkv, w_attn_out], axis=1), "fsdp", axis=0, tiled=True)
 
     lane = jnp.arange(PAIR) % HD
     inverse = jnp.exp(-math.log(10000.0) * (2.0 / ROT) * (lane % (ROT // 2)).astype(f32))
@@ -653,13 +667,15 @@
     angles_t = pos.astype(f32)[None, :] * inverse[:ROT // 2, None]
     cos_t, sin_t = jnp.cos(angles_t), jnp.sin(angles_t)
 
-    normed, queries, key, value = qkv(spots[0], x, gain_attn, shift_attn, weight_qkv, bias_qkv, tables, True)
+    normed, queries, key, value = qkv(spots[0], x, gain_attn, shift_attn, weights, bias_qkv, tables, True)
     keys, values = [key], [value]
     for s in range(1, n):
-        key, value = qkv(spots[s], xs[s], gain_attn, shift_attn, weight_qkv, bias_qkv, tables, False)
+        key, value = qkv(spots[s], xs[s], gain_attn, shift_attn, weights, bias_qkv, tables, False)
         keys.append(key)
         values.append(value)
-    grad_att = mm(grad_out, weight_attn, NT).astype(bf16)
+    grad_att = spread(grad_out, weights)
+    weight_in = lax.all_gather(after(w_in, queries), "fsdp", axis=0, tiled=True)
+    weight_out = lax.all_gather(after(w_out, queries), "fsdp", axis=0, tiled=True)
 
     per = half // QB
     earlier = jnp.stack([spots[s][0] < spots[0][0] for s in range(1, n)])
@@ -672,26 +688,32 @@
     relative = [4 * dy + 2 * dx + 1 - keep for keep in (0, 1) for dy in (0, 1) for dx in (0, 1)]
     order = jnp.bitwise_xor(me, jnp.array(relative, jnp.int32))
     owners = lax.rem(place + n - jnp.arange(n), n)
-    groups = 2
-    count = HEADS // 2 // groups
     attended, grad_q, own_kv, come_kv = [], [], [], []
-    for g in range(groups):
-        out = attention(kind, owners, cos_t, sin_t, queries, grad_att, keys, values, g * count, count)
+
+    def attend(first, count, wait):
+        out = attention(kind, owners, cos_t, sin_t, after(queries, *wait), grad_att, keys, values, first, count)
         attended.append(out[0])
         grad_q.append(out[1])
         come_kv.append(lax.psum_scatter(out[2], "ctx", scatter_dimension=0, tiled=True))
         own_kv.append(out[3])
 
-    x_late, attended = lax.optimization_barrier((x, attended))
+    attend(0, 5, ())
     mlp_out, grad_mlp, in_send, in_keep, out_send, out_keep, db_in, db_out, dgain_mlp, dshift_mlp = mlp(
-        order, x_late, grad_out, gain_mlp, shift_mlp, weight_in, bias_in, weight_out)
-    output, attn_send, attn_keep = join(order, x, grad_out, attended, weight_attn, mlp_out, bias_out)
-    sum_out = scatter_sum(out_send, out_keep)
-    sum_in = scatter_sum(in_send, in_keep)
-    sum_attn = scatter_sum(attn_send, attn_keep)
+        order, after(x, *attended), grad_out, gain_mlp, shift_mlp, weight_in, bias_in, weight_out)
+    attend(5, 2, (mlp_out,))
+    steps_out = core_step(out_send, out_keep)
+    steps_in = core_step(in_send, in_keep)
+    attend(7, 1, (*attended, *steps_out, *steps_in))
+    output = join(x, attended, weights, mlp_out, bias_out)
+    steps_out = side_step(*steps_out)
+    steps_in = side_step(*steps_in)
     grad_inputs, qkv_send, qkv_keep, db_qkv, dgain_attn, dshift_attn = tail(
-        spots[0], order, after(x, output), normed, gain_attn, weight_qkv, tables, grad_mlp, grad_q, own_kv, come_kv)
-    sum_qkv = scatter_sum(qkv_send, qkv_keep)
+        spots[0], order, after(x, output, *steps_out, *steps_in), grad_out, normed, gain_attn, weights, tables, grad_mlp,
+        attended, grad_q, own_kv, come_kv)
+    sum_out = last_step(*steps_out)
+    sum_in = last_step(*steps_in)
+    both = scatter_sum(qkv_send, qkv_keep)
+    sum_qkv, sum_attn = both[:, :3 * width], both[:, 3 * width:]
     smalls = [a.reshape(width, -1) for a in (dgain_attn, dshift_attn, db_qkv, db_out, dgain_mlp, dshift_mlp, db_in)]
     used = sum(a.shape[1] for a in smalls)
     packed = jnp.concatenate(smalls + [jnp.zeros((width, PAIR - used), f32)], axis=1).astype(bf16)

time: 681 us -> 647 us (0.950)
  waiting for transfers between devices: 214 us -> 183 us
  Pallas kernels: 311 us -> 322 us
  local copies, waits for them, and re-layouts: 24.8 us -> 17.7 us
    all_gather x4 -> x3, waiting for transfers between devices: 79.9 us -> 37.7 us  [the longest x1 37.7 us: fast(): lax.all_gather(jnp.concatenate([w_qkv, w_attn_out], axis=1), 'fsdp', axis...]
    ppermute x3, waiting for transfers between devices: 0.01 us -> 20.5 us  [fast(): lax.ppermute(spots[0][:half // RB], 'ctx', [(i, (i + s) % n) for i in ran...]
    reduce_scatter x5 -> x4, waiting for transfers between devices: 28.5 us -> 43.6 us  [last_step(): return lax.psum_scatter(part, 'ctx', scatter_dimension=0, tiled=True)]
    ppermute x5 -> x4, waiting for transfers between devices: 26.2 us -> 17.6 us  [side_step(): got_b = lax.ppermute(send_b, 'fsdp', pairs_of(4, 8))]
    ppermute x3, waiting for transfers between devices: 35.7 us -> 27.5 us  [fast(): run = lax.ppermute(run, 'ctx', ring)]
    ppermute x5 -> x4, waiting for transfers between devices: 31.7 us -> 24.7 us  [last_step(): got_b = lax.ppermute(send_b, 'fsdp', pairs_of(2, 8))]
    pallas_call x2 -> x3, Pallas kernels: 154 us -> 156 us  [attention(): pl.pallas_call(partial(attention_kernel, half, n), grid=(pairs,), in_spec...]
    pallas_call x1 -> x2, Pallas kernels: 12 us -> 13.8 us  [the longest x1 7.61 us: join(): pl.pallas_call(partial(join_kernel, len(attended)), grid=(rows // RB,), i...]
  transfers between devices with their start and end apart: 42 -> 36, of which waited for: 21 -> 18; matrix products, arithmetic and copies ran while one was open for 12% -> 12% of each run, Pallas kernels for 41% -> 42%
where the time goes in v4:
time: 647 us; the launch traced here: 640 us
  Pallas kernels  322 us (50%)
  waiting for transfers between devices  183 us (28%)
  other arithmetic  65.8 us (10%)
  starting transfers between devices  26 us (4%)
  local copies, waits for them, and re-layouts  17.7 us (3%)
  between operations  15.1 us (2%)
  blocking collectives  10.6 us (2%)
    pallas_call x3, Pallas kernels, attention(): pl.pallas_call(partial(attention_kernel, half, n), grid=(pairs,), in_spec...  156 us
    pallas_call x1, Pallas kernels, mlp(): pl.pallas_call(mlp_kernel, grid_spec=pltpu.PrefetchScalarGridSpec(num_sca...  76.2 us
    reduce_scatter x4, waiting for transfers between devices, last_step(): return lax.psum_scatter(part, 'ctx', scatter_dimension=0, tiled=True)  43.6 us
    convert_element_type x26, other arithmetic, plus(): return (a.astype(f32) + b.astype(f32)).astype(bf16)  39.6 us
    pallas_call x4, Pallas kernels, qkv(): pl.pallas_call(partial(qkv_kernel, with_q), grid_spec=pltpu.PrefetchScala...  38.1 us
    all_gather x1, waiting for transfers between devices, fast(): lax.all_gather(jnp.concatenate([w_qkv, w_attn_out], axis=1), 'fsdp', axis...  37.7 us
    pallas_call x1, Pallas kernels, tail(): pl.pallas_call(partial(tail_kernel, groups), grid_spec=pltpu.PrefetchScal...  37.5 us
    ppermute x3, waiting for transfers between devices, fast(): run = lax.ppermute(run, 'ctx', ring)  27.5 us
  transfers between devices with their start and end apart: 36, of which 18 were waited for; matrix products, arithmetic and copies ran while one was open for 12% of the time, Pallas kernels for 42%

profile of v4, /device:TPU:0, one launch (start us, length us, event | category | flops | bytes accessed | tf_op | source)
XLA Modules:
  0.0 640.4 jit_solution(2905253330147018254)
XLA Ops:
  7.3 2.3 pad_maximum_fusion
  11.1 10.6 %all-gather.1 = bf16[8,1,1536]{2,1,0:T(2,128)(2,1)S(1)} all-gather(bf16[1,1,1536]{2,1,0:T(2,128)(2,1)S(1)} %reshape.495), channel_id=2, replica_groups=mesh['fsdp'=8,'ctx'=4] {'fsdp'}, dimensions={0}, use_global_device_ids=true | all-gather | bytes 27648 | tf_op jit(solution)/shard_map/all_gather | solution.py:653
  23.5 6.5 %fusion = (f32[2304,128]{1,0:T(8,128)}, f32[2304,128]{1,0:T(8,128)}, f32[2304,128]{1,0:T(8,128)}) fusion(f32[128]{0:T(128)S(1)} %fusion.49, f32[2304]{0:T(1024)S(1)} %iota_convert_fusion, pred[128]{0:T(512)(128)(4,1)S(1)} %get-tuple-element.140, pred[128]{0:T(512)(128)(4,1)S(1)} %broadcast_compare_fusion.1, pred[128]{0:T(512)(128)(4,1)S(1)} %get-tuple-element.141), kind=kLoop, calls=%fused_computation.15 | loop fusion | flops 1179648 | bytes 3549056 | tf_op jit(solution)/shard_map/jit(_where)/select_n | solution.py:666
  30.0 37.7 %all-gather.6.cloned.1.call-done.w_ref = bf16[1024,4096]{1,0:T(8,128)(2,1)} async-done(((bf16[128,4096]{1,0:T(8,128)(2,1)}), bf16[1024,4096]{1,0:T(8,128)(2,1)}) %all-gather.6.cloned.1.call-update) | async-done | bytes 8388624 | tf_op jit(solution)/shard_map/all_gather | solution.py:659
  67.7 13.5 %qkv_own.1 = (bf16[1024,1024]{1,0:T(8,128)(2,1)}, bf16[1024,1024]{1,0:T(8,128)(2,1)}, bf16[1024,1024]{1,0:T(8,128)(2,1)}, bf16[1024,1024]{1,0:T(8,128)(2,1)}) custom-call(s32[4]{0:T(128)} %and_select_fusion.2.spot_ref, bf16[1024,1024]{1,0:T(8,128)(2,1)} %bitcast.205, f32[1,1024]{1,0:T(1,128)} %bitcast.233, f32[1,1024]{1,0:T(1,128)} %bitcast.238, ...), custom_call_target="tpu_custom_call" | custom-call | flops 6442450944 | bytes 16777216 | tf_op jit(solution)/shard_map/qkv_own/pallas_call | solution.py:257
  84.4 25.6 %collective-permute-done.3.x_ref = bf16[512,1024]{1,0:T(8,128)(2,1)S(1)} collective-permute-done((bf16[512,1024]{1,0:T(8,128)(2,1)S(1)}, bf16[512,1024]{1,0:T(8,128)(2,1)S(1)}, u32[]{:S(2)}, u32[]{:S(2)}) %collective-permute-start.3) | collective-permute-done | bytes 1048608 | tf_op jit(solution)/shard_map/ppermute | solution.py:649
  110.0 3.8 collective-permute-start.2
  115.7 16.6 %collective-permute-done.2.spot_ref = s32[2]{0:T(128)S(1)} collective-permute-done((s32[2]{0:T(128)S(1)}, s32[2]{0:T(128)S(1)}, u32[]{:S(2)}, u32[]{:S(2)}) %collective-permute-start.2) | collective-permute-done | bytes 40 | tf_op jit(solution)/shard_map/ppermute | solution.py:651
  132.5 3.9 collective-permute-done.spot_ref
  138.2 7.8 %kv_remote.4 = (bf16[512,1024]{1,0:T(8,128)(2,1)}, bf16[512,1024]{1,0:T(8,128)(2,1)}) custom-call(s32[2]{0:T(128)} %copy-done.16, bf16[512,1024]{1,0:T(8,128)(2,1)} %copy-done.5, f32[1,1024]{1,0:T(1,128)} %bitcast.234, f32[1,1024]{1,0:T(1,128)} %bitcast.239, bf16[1024,4096]{1,0:T(8,128)(2,1)} %all-gather.6.cloned.1.call-done.w_ref, f32[1,3072]{1,0:T(1,128)} %bitcast.224, ...), custom_call_target="tpu_custom_call" | custom-call | flops 2147483648 | bytes 16777216 | tf_op jit(solution)/shard_map/kv_remote/pallas_call | solution.py:257
  146.0 7.9 %kv_remote.3 = (bf16[512,1024]{1,0:T(8,128)(2,1)}, bf16[512,1024]{1,0:T(8,128)(2,1)}) custom-call(s32[2]{0:T(128)} %copy-done.15, bf16[512,1024]{1,0:T(8,128)(2,1)} %copy-done.4, f32[1,1024]{1,0:T(1,128)} %bitcast.235, f32[1,1024]{1,0:T(1,128)} %bitcast.240, bf16[1024,4096]{1,0:T(8,128)(2,1)} %all-gather.6.cloned.1.call-done.w_ref, f32[1,3072]{1,0:T(1,128)} %bitcast.225, ...), custom_call_target="tpu_custom_call" | custom-call | flops 2147483648 | bytes 16777216 | tf_op jit(solution)/shard_map/kv_remote/pallas_call | solution.py:257
  153.9 6.1 spread.1.do_ref
  163.0 8.9 %kv_remote.5 = (bf16[512,1024]{1,0:T(8,128)(2,1)}, bf16[512,1024]{1,0:T(8,128)(2,1)}) custom-call(s32[2]{0:T(128)} %copy-done.14, bf16[512,1024]{1,0:T(8,128)(2,1)} %copy-done.6, f32[1,1024]{1,0:T(1,128)} %bitcast.236, f32[1,1024]{1,0:T(1,128)} %bitcast.241, bf16[1024,4096]{1,0:T(8,128)(2,1)} %all-gather.6.cloned.1.call-done.w_ref, f32[1,3072]{1,0:T(1,128)} %bitcast.226, ...), custom_call_target="tpu_custom_call" | custom-call | flops 2147483648 | bytes 16777216 | tf_op jit(solution)/shard_map/kv_remote/pallas_call | solution.py:257
  171.9 95.4 %attention.3 = (bf16[1024,640]{1,0:T(8,128)(2,1)}, bf16[1024,640]{1,0:T(8,128)(2,1)}, bf16[2048,1280]{1,0:T(8,128)(2,1)}, bf16[512,1280]{1,0:T(8,128)(2,1)}) custom-call(f32[4,8]{1,0:T(4,128)} %add_select_fusion.kind_ref, s32[4]{0:T(128)} %compare_select_fusion.3.owner_ref, f32[8,1024]{1,0:T(8,128)} %get-tuple-element.137.cos_ref, ...), custom_call_target="tpu_custom_call" | custom-call | flops 72477573120 | bytes 16777216 | tf_op jit(solution)/shard_map/attention/pallas_call | solution.py:574
  268.6 76.2 %mlp.1 = (f32[1024,1024]{1,0:T(8,128)}, f32[1024,1024]{1,0:T(8,128)}, bf16[512,4096]{1,0:T(8,128)(2,1)}, bf16[512,4096]{1,0:T(8,128)(2,1)}, bf16[2048,1024]{1,0:...) custom-call(s32[8]{0:T(128)} %get-tuple-element.139.order_ref, ...), custom_call_target="tpu_custom_call" | custom-call | flops 51539607552 | bytes 50331648 | tf_op jit(solution)/shard_map/mlp/pallas_call | solution.py:202
  345.4 39.7 %attention.4 = (bf16[1024,256]{1,0:T(8,128)(2,1)}, bf16[1024,256]{1,0:T(8,128)(2,1)}, bf16[2048,512]{1,0:T(8,128)(2,1)}, bf16[512,512]{1,0:T(8,128)(2,1)}) custom-call(f32[4,8]{1,0:T(4,128)} %add_select_fusion.kind_ref, s32[4]{0:T(128)} %compare_select_fusion.3.owner_ref, f32[8,1024]{1,0:T(8,128)} %get-tuple-element.137.cos_ref, ...), custom_call_target="tpu_custom_call" | custom-call | flops 28991029248 | bytes 16777216 | tf_op jit(solution)/shard_map/attention/pallas_call | solution.py:574
  385.2 4.3 add_convert_fusion.6
  389.5 2.9 fusion.3
  393.5 3.3 add_convert_fusion.4
  398.9 2.5 fusion.5
  403.7 21.1 %attention.5 = (bf16[1024,128]{1,0:T(8,128)(2,1)}, bf16[1024,128]{1,0:T(8,128)(2,1)}, bf16[2048,256]{1,0:T(8,128)(2,1)}, bf16[512,256]{1,0:T(8,128)(2,1)}) custom-call(f32[4,8]{1,0:T(4,128)} %add_select_fusion.kind_ref, s32[4]{0:T(128)} %compare_select_fusion.3.owner_ref, f32[8,1024]{1,0:T(8,128)} %get-tuple-element.137.cos_ref, ...), custom_call_target="tpu_custom_call" | custom-call | flops 14495514624 | bytes 16777216 | tf_op jit(solution)/shard_map/attention/pallas_call | solution.py:574
  424.9 7.6 %join.1 = bf16[1024,1024]{1,0:T(8,128)(2,1)} custom-call(bf16[1024,1024]{1,0:T(8,128)(2,1)} %bitcast.207, bf16[1024,4096]{1,0:T(8,128)(2,1)} %all-gather.6.cloned.1.call-done.w_ref, f32[1024,1024]{1,0:T(8,128)} %get-tuple-element.70.mlp_ref, f32[1,1024]{1,0:T(1,128)} %bitcast.242, bf16[1024,640]{1,0:T(8,128)(2,1)} %get-tuple-element.66.refs_0_, ...), custom_call_target="tpu_custom_call" | custom-call | flops 2147483648 | bytes 12582912 | tf_op jit(solution)/shard_map/join/pallas_call | solution.py:403
  444.5 18.2 %collective-permute-done.23 = bf16[64,4096]{1,0:T(8,128)(2,1)S(1)} collective-permute-done((bf16[64,4096]{1,0:T(8,128)(2,1)S(1)}, bf16[64,4096]{1,0:T(8,128)(2,1)S(1)}, u32[]{:S(2)}, u32[]{:S(2)}) %collective-permute-start.23) | collective-permute-done | bytes 524320 | tf_op jit(solution)/shard_map/ppermute | solution.py:625
  468.7 37.5 %tail.1 = (f32[1024,1024]{1,0:T(8,128)}, bf16[512,4096]{1,0:T(8,128)(2,1)}, bf16[512,4096]{1,0:T(8,128)(2,1)}, f32[1,3072]{1,0:T(1,128)}, f32[1,1024]{1,0:T(1,128)}, /*index=5*/f32[1,1024]{1,0:T(1,128)}) custom-call(s32[4]{0:T(128)} %and_select_fusion.2.spot_ref, s32[8]{0:T(128)} %get-tuple-element.139.order_ref, bf16[1024,1024]{1,0:T(8,128)(2,1)} %bitcast.208, ...), custom_call_target="tpu_custom_call" | custom-call | flops 15032385536 | bytes 33554432 | tf_op jit(solution)/shard_map/tail/pallas_call | solution.py:371
  513.3 4.2 concatenate.50
  531.2 4.1 add_convert_fusion.1
  536.4 3.4 add_convert_fusion.3
  541.9 16.6 %collective-permute-done.20 = bf16[2,64,4096]{2,1,0:T(8,128)(2,1)} collective-permute-done((bf16[2,64,4096]{2,1,0:T(8,128)(2,1)}, bf16[2,64,4096]{2,1,0:T(8,128)(2,1)}, u32[]{:S(2)}, u32[]{:S(2)}) %collective-permute-start.20) | collective-permute-done | bytes 1048608 | tf_op jit(solution)/shard_map/ppermute | solution.py:619
  560.8 5.2 collective-permute-done.18
  568.1 5.7 collective-permute-done.21
  584.8 17.3 %reduce-scatter.18.cloned.1.call-done = bf16[32,4096]{1,0:T(8,128)(2,1)} async-done(((bf16[128,4096]{1,0:T(8,128)(2,1)}), bf16[32,4096]{1,0:T(8,128)(2,1)}) %reduce-scatter.18.cloned.1.call-update) | async-done | bytes 262160 | tf_op jit(solution)/shard_map/reduce_scatter | solution.py:627
  603.9 26.3 %reduce-scatter.16.cloned.1.call-done = bf16[32,4096]{1,0:T(8,128)(2,1)} async-done(((bf16[128,4096]{1,0:T(8,128)(2,1)}), bf16[32,4096]{1,0:T(8,128)(2,1)}) %reduce-scatter.16.cloned.1.call-update) | async-done | bytes 262160 | tf_op jit(solution)/shard_map/reduce_scatter | solution.py:627
  (205 shorter events, 82.5 us)
Async XLA Ops:
  7.3 60.4 %all-gather.6.cloned.1.call-start = ((), (), s32[]{:S(2)}) async-start(), calls=%async_computation.7 | async-start | bytes 9437184 | tf_op jit(solution)/shard_map/all_gather | solution.py:659
  9.6 259.0 %all-gather.8.cloned.1.call-start = ((), (), s32[]{:S(2)}) async-start(), calls=%async_computation.8 | async-start | bytes 9437184 | tf_op jit(solution)/shard_map/all_gather | solution.py:677
  81.2 187.4 %all-gather.10.cloned.1.call-start = ((), (), s32[]{:S(2)}) async-start(), calls=%async_computation.9 | async-start | bytes 9437184 | tf_op jit(solution)/shard_map/all_gather | solution.py:678
  81.9 386.7 %reduce-scatter.8.cloned.1.call-start = ((), (), s32[]{:S(2)}) async-start(), calls=%async_computation.10 | async-start | bytes 6553600 | tf_op jit(solution)/shard_map/reduce_scatter | solution.py:697
  82.8 27.2 %collective-permute-start.3 = (bf16[512,1024]{1,0:T(8,128)(2,1)S(1)}, bf16[512,1024]{1,0:T(8,128)(2,1)S(1)}, u32[]{:S(2)}, u32[]{:S(2)}) collective-permute-start(bf16[512,1024]{1,0:T(8,128)(2,1)S(1)} %slice_bitcast_fusion.4), channel_id=1, source_target_pairs={{0,1},{1,2},{2,3},{3,0},{4,5},{5,6},{6,7},{7,4},{8,9},{9,10},{10,1... | collective-permute-start | bytes 3145736 | tf_op jit(solution)/shard_map/ppermute | solution.py:649
  110.0 26.5 %collective-permute-start.4 = (bf16[512,1024]{1,0:T(8,128)(2,1)S(1)}, bf16[512,1024]{1,0:T(8,128)(2,1)S(1)}, u32[]{:S(2)}, u32[]{:S(2)}) collective-permute-start(bf16[512,1024]{1,0:T(8,128)(2,1)S(1)} %collective-permute-done.3.x_ref), channel_id=1, source_target_pairs={{0,1},{1,2},{2,3},{3,0},{4,5},{5,6},{6,7},{7,4},{8,9},{9,10},{10,1... | collective-permute-start | bytes 3145736 | tf_op jit(solution)/shard_map/ppermute | solution.py:649
  110.0 22.4 %collective-permute-start.2 = (s32[2]{0:T(128)S(1)}, s32[2]{0:T(128)S(1)}, u32[]{:S(2)}, u32[]{:S(2)}) collective-permute-start(s32[2]{0:T(128)S(1)} %bitcast.252), channel_id=1, source_target_pairs={{0,3},{1,0},{2,1},{3,2},{4,7},{5,4},{6,5},{7,6},{8,11},{9,8},{10,9... | collective-permute-start | bytes 32 | tf_op jit(solution)/shard_map/ppermute | solution.py:651
  113.8 18.6 %collective-permute-start.1 = (s32[2]{0:T(128)S(1)}, s32[2]{0:T(128)S(1)}, u32[]{:S(2)}, u32[]{:S(2)}) collective-permute-start(s32[2]{0:T(128)S(1)} %bitcast.253), channel_id=1, source_target_pairs={{0,2},{1,3},{2,0},{3,1},{4,6},{5,7},{6,4},{7,5},{8,10},{9,11},{10,... | collective-permute-start | bytes 32 | tf_op jit(solution)/shard_map/ppermute | solution.py:651
  113.8 22.6 %collective-permute-start = (s32[2]{0:T(128)S(1)}, s32[2]{0:T(128)S(1)}, u32[]{:S(2)}, u32[]{:S(2)}) collective-permute-start(s32[2]{0:T(128)S(1)} %bitcast.254), channel_id=1, source_target_pairs={{0,1},{1,2},{2,3},{3,0},{4,5},{5,6},{6,7},{7,4},{8,9},{9,10},{10,1... | collective-permute-start | bytes 32 | tf_op jit(solution)/shard_map/ppermute | solution.py:651
  136.5 25.5 %collective-permute-start.5 = (bf16[512,1024]{1,0:T(8,128)(2,1)S(1)}, bf16[512,1024]{1,0:T(8,128)(2,1)S(1)}, u32[]{:S(2)}, u32[]{:S(2)}) collective-permute-start(bf16[512,1024]{1,0:T(8,128)(2,1)S(1)} %collective-permute-done.4.x_ref), channel_id=1, source_target_pairs={{0,1},{1,2},{2,3},{3,0},{4,5},{5,6},{6,7},{7,4},{8,9},{9,10},{10,1... | collective-permute-start | bytes 3145736 | tf_op jit(solution)/shard_map/ppermute | solution.py:649
  267.4 201.3 %reduce-scatter.10.cloned.1.call-start = ((), (), s32[]{:S(2)}) async-start(), calls=%async_computation.11 | async-start | bytes 2621440 | tf_op jit(solution)/shard_map/reduce_scatter | solution.py:697
  344.8 40.3 %collective-permute-start.6 = (bf16[2048,1024]{1,0:T(8,128)(2,1)}, bf16[2048,1024]{1,0:T(8,128)(2,1)}, u32[]{:S(2)}, u32[]{:S(2)}) collective-permute-start(bf16[2048,1024]{1,0:T(8,128)(2,1)} %get-tuple-element.74), channel_id=1, source_target_pairs={{0,4},{4,0},{8,12},{12,8},{16,20},{20,16},{24,28},{28,24},{1,5},{5... | collective-permute-start | bytes 12582920 | tf_op jit(solution)/shard_map/ppermute | solution.py:607
  344.9 48.6 %collective-permute-start.7 = (bf16[512,4096]{1,0:T(8,128)(2,1)}, bf16[512,4096]{1,0:T(8,128)(2,1)}, u32[]{:S(2)}, u32[]{:S(2)}) collective-permute-start(bf16[512,4096]{1,0:T(8,128)(2,1)} %get-tuple-element.76), channel_id=1, source_target_pairs={{0,4},{4,0},{8,12},{12,8},{16,20},{20,16},{24,28},{28,24},{1,5},{5... | collective-permute-start | bytes 12582920 | tf_op jit(solution)/shard_map/ppermute | solution.py:607
  385.1 83.6 %reduce-scatter.12.cloned.1.call-start = ((), (), s32[]{:S(2)}) async-start(), calls=%async_computation.12 | async-start | bytes 1310720 | tf_op jit(solution)/shard_map/reduce_scatter | solution.py:697
  389.5 45.1 %collective-permute-start.9 = (bf16[2,256,1024]{2,1,0:T(8,128)(2,1)}, bf16[2,256,1024]{2,1,0:T(8,128)(2,1)}, u32[]{:S(2)}, u32[]{:S(2)}) collective-permute-start(bf16[2,256,1024]{2,1,0:T(8,128)(2,1)} %get-tuple-element.121), channel_id=1, source_target_pairs={{0,16},{4,20},{8,24},{12,28},{16,0},{20,4},{24,8},{28,12},{1,17},{... | collective-permute-start | bytes 3145736 | tf_op jit(solution)/shard_map/ppermute | solution.py:619
  392.4 44.5 %collective-permute-start.8 = (bf16[2,256,1024]{2,1,0:T(8,128)(2,1)}, bf16[2,256,1024]{2,1,0:T(8,128)(2,1)}, u32[]{:S(2)}, u32[]{:S(2)}) collective-permute-start(bf16[2,256,1024]{2,1,0:T(8,128)(2,1)} %fusion.3), channel_id=1, source_target_pairs={{0,8},{4,12},{8,0},{12,4},{16,24},{20,28},{24,16},{28,20},{1,9},{5... | collective-permute-start | bytes 3145736 | tf_op jit(solution)/shard_map/ppermute | solution.py:618
  396.8 41.4 %collective-permute-start.11 = (bf16[2,64,4096]{2,1,0:T(8,128)(2,1)}, bf16[2,64,4096]{2,1,0:T(8,128)(2,1)}, u32[]{:S(2)}, u32[]{:S(2)}) collective-permute-start(bf16[2,64,4096]{2,1,0:T(8,128)(2,1)} %get-tuple-element.119), channel_id=1, source_target_pairs={{0,16},{4,20},{8,24},{12,28},{16,0},{20,4},{24,8},{28,12},{1,17},{... | collective-permute-start | bytes 3145736 | tf_op jit(solution)/shard_map/ppermute | solution.py:619
  401.3 39.9 %collective-permute-start.10 = (bf16[2,64,4096]{2,1,0:T(8,128)(2,1)}, bf16[2,64,4096]{2,1,0:T(8,128)(2,1)}, u32[]{:S(2)}, u32[]{:S(2)}) collective-permute-start(bf16[2,64,4096]{2,1,0:T(8,128)(2,1)} %fusion.5), channel_id=1, source_target_pairs={{0,8},{4,12},{8,0},{12,4},{16,24},{20,28},{24,16},{28,20},{1,9},{5... | collective-permute-start | bytes 3145736 | tf_op jit(solution)/shard_map/ppermute | solution.py:618
  424.8 153.9 %reduce-scatter.14.cloned.1.call-start = ((), (), s32[]{:S(2)}) async-start(), calls=%async_computation.13 | async-start | bytes 40960 | tf_op jit(solution)/shard_map/reduce_scatter | solution.py:627
  435.9 28.9 %collective-permute-start.25 = (bf16[256,1024]{1,0:T(8,128)(2,1)S(1)}, bf16[256,1024]{1,0:T(8,128)(2,1)S(1)}, u32[]{:S(2)}, u32[]{:S(2)}) collective-permute-start(bf16[256,1024]{1,0:T(8,128)(2,1)S(1)} %fusion.25), channel_id=1, source_target_pairs={{0,8},{4,12},{8,0},{12,4},{16,24},{20,28},{24,16},{28,20},{1,9},{5... | collective-permute-start | bytes 1572872 | tf_op jit(solution)/shard_map/ppermute | solution.py:625
  438.1 27.9 %collective-permute-start.24 = (bf16[256,1024]{1,0:T(8,128)(2,1)S(1)}, bf16[256,1024]{1,0:T(8,128)(2,1)S(1)}, u32[]{:S(2)}, u32[]{:S(2)}) collective-permute-start(bf16[256,1024]{1,0:T(8,128)(2,1)S(1)} %fusion.23), channel_id=1, source_target_pairs={{0,16},{4,20},{8,24},{12,28},{16,0},{20,4},{24,8},{28,12},{1,17},{... | collective-permute-start | bytes 1572872 | tf_op jit(solution)/shard_map/ppermute | solution.py:624
  439.4 23.3 %collective-permute-start.23 = (bf16[64,4096]{1,0:T(8,128)(2,1)S(1)}, bf16[64,4096]{1,0:T(8,128)(2,1)S(1)}, u32[]{:S(2)}, u32[]{:S(2)}) collective-permute-start(bf16[64,4096]{1,0:T(8,128)(2,1)S(1)} %fusion.29), channel_id=1, source_target_pairs={{0,8},{4,12},{8,0},{12,4},{16,24},{20,28},{24,16},{28,20},{1,9},{5... | collective-permute-start | bytes 1572872 | tf_op jit(solution)/shard_map/ppermute | solution.py:625
  442.4 25.0 %collective-permute-start.22 = (bf16[64,4096]{1,0:T(8,128)(2,1)S(1)}, bf16[64,4096]{1,0:T(8,128)(2,1)S(1)}, u32[]{:S(2)}, u32[]{:S(2)}) collective-permute-start(bf16[64,4096]{1,0:T(8,128)(2,1)S(1)} %fusion.27), channel_id=1, source_target_pairs={{0,16},{4,20},{8,24},{12,28},{16,0},{20,4},{24,8},{28,12},{1,17},{... | collective-permute-start | bytes 1572872 | tf_op jit(solution)/shard_map/ppermute | solution.py:624
  506.2 25.0 %collective-permute-start.17 = (bf16[512,4096]{1,0:T(8,128)(2,1)}, bf16[512,4096]{1,0:T(8,128)(2,1)}, u32[]{:S(2)}, u32[]{:S(2)}) collective-permute-start(bf16[512,4096]{1,0:T(8,128)(2,1)} %get-tuple-element.100), channel_id=1, source_target_pairs={{0,4},{4,0},{8,12},{12,8},{16,20},{20,16},{24,28},{28,24},{1,5},{5... | collective-permute-start | bytes 12582920 | tf_op jit(solution)/shard_map/ppermute | solution.py:607
  519.7 4.0 collective-permute-start.15
  530.0 53.0 %reduce-scatter.20.cloned.1.call-start = ((), (), s32[]{:S(2)}) async-start(), calls=%async_computation.16 | async-start | bytes 1310720 | tf_op jit(solution)/shard_map/reduce_scatter | solution.py:627
  531.1 71.0 %reduce-scatter.18.cloned.1.call-start = ((), (), s32[]{:S(2)}) async-start(), calls=%async_computation.15 | async-start | bytes 1310720 | tf_op jit(solution)/shard_map/reduce_scatter | solution.py:627
  535.3 23.1 %collective-permute-start.20 = (bf16[2,64,4096]{2,1,0:T(8,128)(2,1)}, bf16[2,64,4096]{2,1,0:T(8,128)(2,1)}, u32[]{:S(2)}, u32[]{:S(2)}) collective-permute-start(bf16[2,64,4096]{2,1,0:T(8,128)(2,1)} %get-tuple-element.117), channel_id=1, source_target_pairs={{0,16},{4,20},{8,24},{12,28},{16,0},{20,4},{24,8},{28,12},{1,17},{... | collective-permute-start | bytes 3145736 | tf_op jit(solution)/shard_map/ppermute | solution.py:619
  539.8 26.2 %collective-permute-start.18 = (bf16[2,64,4096]{2,1,0:T(8,128)(2,1)}, bf16[2,64,4096]{2,1,0:T(8,128)(2,1)}, u32[]{:S(2)}, u32[]{:S(2)}) collective-permute-start(bf16[2,64,4096]{2,1,0:T(8,128)(2,1)} %get-tuple-element.115), channel_id=1, source_target_pairs={{0,8},{4,12},{8,0},{12,4},{16,24},{20,28},{24,16},{28,20},{1,9},{5... | collective-permute-start | bytes 3145736 | tf_op jit(solution)/shard_map/ppermute | solution.py:618
  541.8 88.4 %reduce-scatter.16.cloned.1.call-start = ((), (), s32[]{:S(2)}) async-start(), calls=%async_computation.14 | async-start | bytes 1310720 | tf_op jit(solution)/shard_map/reduce_scatter | solution.py:627
  559.6 14.1 %collective-permute-start.21 = (bf16[64,4096]{1,0:T(8,128)(2,1)S(1)}, bf16[64,4096]{1,0:T(8,128)(2,1)S(1)}, u32[]{:S(2)}, u32[]{:S(2)}) collective-permute-start(bf16[64,4096]{1,0:T(8,128)(2,1)S(1)} %fusion.34), channel_id=1, source_target_pairs={{0,8},{4,12},{8,0},{12,4},{16,24},{20,28},{24,16},{28,20},{1,9},{5... | collective-permute-start | bytes 1572872 | tf_op jit(solution)/shard_map/ppermute | solution.py:625
  567.2 9.2 %collective-permute-start.19 = (bf16[64,4096]{1,0:T(8,128)(2,1)S(1)}, bf16[64,4096]{1,0:T(8,128)(2,1)S(1)}, u32[]{:S(2)}, u32[]{:S(2)}) collective-permute-start(bf16[64,4096]{1,0:T(8,128)(2,1)S(1)} %fusion.32), channel_id=1, source_target_pairs={{0,16},{4,20},{8,24},{12,28},{16,0},{20,4},{24,8},{28,12},{1,17},{... | collective-permute-start | bytes 1572872 | tf_op jit(solution)/shard_map/ppermute | solution.py:624
  (28 other events, 309.6 us)
Sparse Core Ops, SparseCore 0:
  10.6 57.0 all-gather.5
  81.3 54.3 all-gather.7
  137.6 54.3 all-gather.9
  267.5 91.0 reduce-scatter.7
  385.2 40.7 reduce-scatter.9
  428.2 26.4 reduce-scatter.11
  530.1 16.1 reduce-scatter.13
  548.7 25.2 reduce-scatter.19
  576.3 25.8 reduce-scatter.17
  604.4 25.7 reduce-scatter.15

commit v5 on v4

--- a/solution.py
+++ b/solution.py
@@ -231,13 +231,14 @@
     return jnp.concatenate(parts, axis=1)
 
 
-def qkv_kernel(with_q, spot_ref, x_ref, gain_ref, shift_ref, w_ref, b_ref, cos_ref, low_ref, high_ref, *outs):
+def qkv_kernel(with_q, spot_ref, order_ref, x_ref, gain_ref, shift_ref, w_ref, b_ref, cos_ref, low_ref, high_ref, *outs):
     width = x_ref.shape[1]
     h = norm_rows(x_ref[...].astype(f32), gain_ref[...], shift_ref[...])
     tables = (cos_ref[...], low_ref[...], high_ref[...])
     if with_q:
-        h_ref, q_ref, k_ref, v_ref = outs
-        h_ref[...] = h
+        h_ref, q_ref, k_ref, v_ref, plain_ref = outs
+        plain_ref[...] = h
+        reorder(order_ref, plain_ref, h_ref)
         q = mm(h, w_ref[:, :width], NN) + b_ref[:, :width]
         q_ref[...] = (turn_lanes(q, *tables, 1.0) * (HD ** (-0.5) / math.log(2.0))).astype(bf16)
     else:
@@ -247,105 +248,131 @@
     v_ref[...] = (mm(h, w_ref[:, 2 * width:], NN) + b_ref[:, 2 * width:]).astype(bf16)
 
 
-def qkv(spots, x, gain, shift, weight, bias, tables, with_q):
+def qkv(spots, order, x, gain, shift, weight, bias, tables, with_q):
     rows, width = x.shape
     s = jax.ShapeDtypeStruct((rows, width), bf16)
-    block = pl.BlockSpec((RB, width), lambda j, spot: (j, 0))
-    line = pl.BlockSpec((1, width), lambda j, spot: (0, 0))
-    table = pl.BlockSpec((RB, PAIR), lambda j, spot: (spot[j], 0))
+    block = pl.BlockSpec((RB, width), lambda j, spot, o: (j, 0))
+    line = pl.BlockSpec((1, width), lambda j, spot, o: (0, 0))
+    table = pl.BlockSpec((RB, PAIR), lambda j, spot, o: (spot[j], 0))
     count = 4 if with_q else 2
     return pl.pallas_call(
         partial(qkv_kernel, with_q),
         grid_spec=pltpu.PrefetchScalarGridSpec(
-            num_scalar_prefetch=1,
+            num_scalar_prefetch=2,
             grid=(rows // RB,),
-            in_specs=[block, line, line, pl.BlockSpec((width, 3 * width), lambda j, spot: (0, 0)),
-                      pl.BlockSpec((1, 3 * width), lambda j, spot: (0, 0)), table, table, table],
+            in_specs=[block, line, line, pl.BlockSpec((width, 3 * width), lambda j, spot, o: (0, 0)),
+                      pl.BlockSpec((1, 3 * width), lambda j, spot, o: (0, 0)), table, table, table],
             out_specs=[block] * count,
+            scratch_shapes=[vmem(RB, width, dtype=bf16)] if with_q else [],
         ),
         out_shape=[s] * count,
         compiler_params=params(),
-        cost_estimate=pl.CostEstimate(flops=2 * rows * width * width * (3 if with_q else 2), bytes_accessed=16 << 20,
-                                      transcendentals=0),
+        cost_estimate=pl.CostEstimate(flops=1 << 20, bytes_accessed=1 << 16, transcendentals=0),
         name="qkv_own" if with_q else "kv_remote",
-    )(spots, x, gain.reshape(1, -1), shift.reshape(1, -1), weight, bias.reshape(1, -1), *tables)
-
-
-def tail_kernel(groups, spot_ref, order_ref, x_ref, c_ref, h_ref, gain_ref, w_ref, cos_ref, low_ref, high_ref, gin_ref, *refs):
-    att_refs, dq_refs, own_refs, come_refs = (refs[i * groups:(i + 1) * groups] for i in range(4))
-    grad_ref, send_ref, keep_ref, db_ref, dgain_ref, dshift_ref, p_ref, turned_ref, gh_ref = refs[4 * groups:]
+    )(spots, order, x, gain.reshape(1, -1), shift.reshape(1, -1), weight, bias.reshape(1, -1), *tables)
+
+
+def first_kernel(groups, order_ref, c_ref, h_ref, w_ref, *refs):
+    att_refs, dq_refs = refs[:groups], refs[groups:2 * groups]
+    send_ref, keep_ref, gh_ref, db_ref, p_ref, turned_ref = refs[2 * groups:]
+    step = pl.program_id(0)
+    blocks = [slice(r, r + RB) for r in range(0, c_ref.shape[0], RB)]
+
+    def lay(some):
+        at = 0
+        for ref in some:
+            p_ref[:, at:at + ref.shape[1]] = ref[...]
+            at += ref.shape[1]
+
+    def give(dw):
+        send_ref[...] = dw[:send_ref.shape[0]]
+        keep_ref[...] = dw[send_ref.shape[0]:]
+
+    @pl.when(step == 0)
+    def _():
+        lay(att_refs)
+        reorder(order_ref, p_ref, turned_ref)
+        give(mm(turned_ref[...], c_ref[...], TN).astype(bf16))
+
+    @pl.when(step == 1)
+    def _():
+        lay(dq_refs)
+        db = jnp.zeros(db_ref.shape, f32)
+        for r in blocks:
+            gh_ref[r, :] = mm(p_ref[r, :], w_ref[...], NT)
+            db += col_sum(p_ref[r, :].astype(f32))
+        db_ref[...] = db
+        give(mm(h_ref[...], p_ref[...], TN).astype(bf16))
+
+
+def first_tail(order, c, h, weights, attended, dqs):
+    rows, width = c.shape
+    s = jax.ShapeDtypeStruct
+
+    def full(a):
+        return pl.BlockSpec(a.shape, lambda j, o: (0, 0))
+
+    down = pl.BlockSpec((width // 2, width), lambda j, o: (0, j))
+    arrays = [*attended, *dqs]
+    return pl.pallas_call(
+        partial(first_kernel, len(dqs)),
+        grid_spec=pltpu.PrefetchScalarGridSpec(
+            num_scalar_prefetch=1,
+            grid=(2,),
+            in_specs=[full(c), full(h), pl.BlockSpec((width, width), lambda j, o: (0, 0))] + [full(a) for a in arrays],
+            out_specs=[down, down, full(c), pl.BlockSpec((1, width), lambda j, o: (0, 0))],
+            scratch_shapes=[vmem(rows, width, dtype=bf16), vmem(rows, width, dtype=bf16)],
+        ),
+        out_shape=[s((width // 2, 2 * width), bf16), s((width // 2, 2 * width), bf16), s((rows, width), f32), s((1, width), f32)],
+        compiler_params=params(),
+        cost_estimate=pl.CostEstimate(flops=6 * rows * width * width, bytes_accessed=24 << 20, transcendentals=0),
+        name="first_tail",
+    )(order, c, h, weights, *arrays)
+
+
+def last_kernel(groups, spot_ref, x_ref, h_ref, gain_ref, w_ref, cos_ref, low_ref, high_ref, gin_ref, ghq_ref, *refs):
+    own_refs, come_refs = refs[:groups], refs[groups:2 * groups]
+    grad_ref, send_ref, keep_ref, db_ref, dgain_ref, dshift_ref, p_ref, gh_ref = refs[2 * groups:]
     step = pl.program_id(0)
     rows = x_ref.shape[0]
     half = rows // 2
     blocks = [slice(r, r + RB) for r in range(0, rows, RB)]
     columns = []
     for g in range(groups):
-        columns += [(g, at) for at in range(0, dq_refs[g].shape[1], PAIR)]
+        columns += [(g, at) for at in range(0, own_refs[g].shape[1], 2 * PAIR)]
 
     def put(shift):
+        db = jnp.zeros(db_ref.shape, f32)
         for r in blocks:
             spot = pl.ds(pl.multiple_of(spot_ref[r.start // RB] * RB, RB), RB)
             for to, (g, at) in enumerate(columns):
-                lanes = slice(2 * at + shift, 2 * at + shift + PAIR)
+                lanes = slice(at + shift, at + shift + PAIR)
                 if r.start < half:
-                    t = come_refs[g][r, lanes].astype(f32)
+                    t = come_refs[g][r, lanes]
                 else:
-                    t = own_refs[g][r.start - half:r.stop - half, lanes].astype(f32)
+                    t = own_refs[g][r.start - half:r.stop - half, lanes]
                 if shift == 0:
-                    t = turn_lanes(t, cos_ref[spot, :], low_ref[spot, :], high_ref[spot, :], -1.0)
-                p_ref[r, to * PAIR:(to + 1) * PAIR] = t.astype(bf16)
-
-    def lay(some):
-        for to, (g, at) in enumerate(columns):
-            p_ref[:, to * PAIR:(to + 1) * PAIR] = some[g][:, at:at + PAIR]
-
-    def give(dw):
+                    t = turn_lanes(t.astype(f32), cos_ref[spot, :], low_ref[spot, :], high_ref[spot, :], -1.0).astype(bf16)
+                p_ref[r, to * PAIR:(to + 1) * PAIR] = t
+            db += col_sum(p_ref[r, :].astype(f32))
+        db_ref[...] = db
+        dw = mm(h_ref[...], p_ref[...], TN).astype(bf16)
         send_ref[...] = dw[:send_ref.shape[0]]
         keep_ref[...] = dw[send_ref.shape[0]:]
 
     @pl.when(step == 0)
     def _():
-        lay(att_refs)
-        reorder(order_ref, p_ref, turned_ref)
-        give(mm(turned_ref[...], c_ref[...], TN).astype(bf16))
+        put(0)
+        for r in blocks:
+            gh_ref[r, :] = ghq_ref[r, :] + mm(p_ref[r, :], w_ref[...], NT)
 
     @pl.when(step == 1)
     def _():
-        reorder(order_ref, h_ref, turned_ref)
-        lay(dq_refs)
-
-    @pl.when(step == 2)
-    def _():
-        put(0)
-
-    @pl.when(step == 3)
-    def _():
         put(PAIR)
-
-    @pl.when(step == 1)
-    def _():
-        for r in blocks:
-            gh_ref[r, :] = mm(p_ref[r, :], w_ref[...], NT)
-
-    @pl.when(step > 1)
-    def _():
-        for r in blocks:
-            gh_ref[r, :] += mm(p_ref[r, :], w_ref[...], NT)
-
-    @pl.when(step > 0)
-    def _():
-        give(mm(turned_ref[...], p_ref[...], TN).astype(bf16))
-        db = jnp.zeros(db_ref.shape, f32)
-        for r in blocks:
-            db += col_sum(p_ref[r, :].astype(f32))
-        db_ref[...] = db
-
-    @pl.when(step == 3)
-    def _():
         dgain = jnp.zeros(dgain_ref.shape, f32)
         dshift = jnp.zeros(dshift_ref.shape, f32)
         for r in blocks:
-            grad = gh_ref[r, :]
+            grad = gh_ref[r, :] + mm(p_ref[r, :], w_ref[...], NT)
             back, scaled = norm_back(x_ref[r, :].astype(f32), grad, gain_ref[...])
             grad_ref[r, :] = back + gin_ref[r, :]
             dgain += col_sum(scaled)
@@ -354,36 +381,31 @@
         dshift_ref[...] = dshift
 
 
-def tail(spots, order, x, c, h, gain, weights, tables, gin, attended, dqs, owns, comes):
+def last_tail(spots, x, h, gain, weights, tables, gin, ghq, owns, comes):
     rows, width = x.shape
-    groups = len(dqs)
     s = jax.ShapeDtypeStruct
 
     def full(a):
-        return pl.BlockSpec(a.shape, lambda j, spot, o: (0, 0))
-
-    def behind(j):
-        return jnp.maximum(j - 1, 0)
-
-    line = pl.BlockSpec((1, width), lambda j, spot, o: (0, 0))
-    down = pl.BlockSpec((width // 2, width), lambda j, spot, o: (0, lax.rem(j + 3, 4)))
-    arrays = [*tables, gin, *attended, *dqs, *owns, *comes]
+        return pl.BlockSpec(a.shape, lambda j, spot: (0, 0))
+
+    line = pl.BlockSpec((1, width), lambda j, spot: (0, 0))
+    down = pl.BlockSpec((width // 2, width), lambda j, spot: (0, j))
+    arrays = [*tables, gin, ghq, *owns, *comes]
     return pl.pallas_call(
-        partial(tail_kernel, groups),
+        partial(last_kernel, len(owns)),
         grid_spec=pltpu.PrefetchScalarGridSpec(
-            num_scalar_prefetch=2,
-            grid=(4,),
-            in_specs=[full(x), full(c), full(h), line, pl.BlockSpec((width, width), lambda j, spot, o: (0, behind(j)))]
-            + [full(a) for a in arrays],
-            out_specs=[full(x), down, down, pl.BlockSpec((1, width), lambda j, spot, o: (0, behind(j))), line, line],
-            scratch_shapes=[vmem(rows, width, dtype=bf16), vmem(rows, width, dtype=bf16), vmem(rows, width)],
+            num_scalar_prefetch=1,
+            grid=(2,),
+            in_specs=[full(x), full(h), line, pl.BlockSpec((width, width), lambda j, spot: (0, j + 1))] + [full(a) for a in arrays],
+            out_specs=[full(x), down, down, pl.BlockSpec((1, width), lambda j, spot: (0, j)), line, line],
+            scratch_shapes=[vmem(rows, width, dtype=bf16), vmem(rows, width)],
         ),
-        out_shape=[s((rows, width), f32), s((width // 2, 4 * width), bf16), s((width // 2, 4 * width), bf16),
-                   s((1, 3 * width), f32), s((1, width), f32), s((1, width), f32)],
+        out_shape=[s((rows, width), f32), s((width // 2, 2 * width), bf16), s((width // 2, 2 * width), bf16),
+                   s((1, 2 * width), f32), s((1, width), f32), s((1, width), f32)],
         compiler_params=params(),
-        cost_estimate=pl.CostEstimate(flops=14 * rows * width * width, bytes_accessed=32 << 20, transcendentals=0),
-        name="tail",
-    )(spots, order, x, c, h, gain.reshape(1, -1), weights, *arrays)
+        cost_estimate=pl.CostEstimate(flops=8 * rows * width * width, bytes_accessed=32 << 20, transcendentals=0),
+        name="last_tail",
+    )(spots, x, h, gain.reshape(1, -1), weights, *arrays)
 
 
 def join_kernel(groups, x_ref, w_ref, mlp_ref, b_ref, *refs):
@@ -428,7 +450,7 @@
         out_specs=block,
         out_shape=jax.ShapeDtypeStruct((rows, width), bf16),
         compiler_params=params(),
-        cost_estimate=pl.CostEstimate(flops=2 * rows * width * width, bytes_accessed=8 << 20, transcendentals=0),
+        cost_estimate=pl.CostEstimate(flops=1 << 20, bytes_accessed=1 << 16, transcendentals=0),
         name="spread",
     )(c, weights)
 
@@ -623,12 +645,11 @@
 def last_step(send_a, keep_a, send_b, keep_b):
     got_a = lax.ppermute(send_a, "fsdp", pairs_of(4, 8))
     got_b = lax.ppermute(send_b, "fsdp", pairs_of(2, 8))
-    part = jnp.concatenate([plus(keep_a, got_a), plus(keep_b, got_b)], axis=0)
+    return jnp.concatenate([plus(keep_a, got_a), plus(keep_b, got_b)], axis=0)
+
+
+def along(part):
     return lax.psum_scatter(part, "ctx", scatter_dimension=0, tiled=True)
-
-
-def scatter_sum(send, keep):
-    return last_step(*side_step(*core_step(send, keep)))
 
 
 def after(value, *others):
@@ -643,6 +664,10 @@
     n = lax.axis_size("ctx")
     ring = [(i, (i + 1) % n) for i in range(n)]
     back = [(i, (i - 1) % n) for i in range(n)]
+    me, place = lax.axis_index("fsdp"), lax.axis_index("ctx")
+    relative = [4 * dy + 2 * dx + 1 - keep for keep in (0, 1) for dy in (0, 1) for dx in (0, 1)]
+    order = jnp.bitwise_xor(me, jnp.array(relative, jnp.int32))
+    owners = lax.rem(place + n - jnp.arange(n), n)
     xs, spots = [x], [pos[::RB] // RB]
     run = x[:half]
     for s in range(1, n):
@@ -667,10 +692,10 @@
     angles_t = pos.astype(f32)[None, :] * inverse[:ROT // 2, None]
     cos_t, sin_t = jnp.cos(angles_t), jnp.sin(angles_t)
 
-    normed, queries, key, value = qkv(spots[0], x, gain_attn, shift_attn, weights, bias_qkv, tables, True)
+    normed, queries, key, value = qkv(spots[0], order, after(x, xs[2], *spots[1:]), gain_attn, shift_attn, weights, bias_qkv, tables, True)
     keys, values = [key], [value]
     for s in range(1, n):
-        key, value = qkv(spots[s], xs[s], gain_attn, shift_attn, weights, bias_qkv, tables, False)
+        key, value = qkv(spots[s], order, xs[s], gain_attn, shift_attn, weights, bias_qkv, tables, False)
         keys.append(key)
         values.append(value)
     grad_att = spread(grad_out, weights)
@@ -684,10 +709,6 @@
     seen_far = jnp.repeat(earlier[None, :] | (local_row >= per), per, axis=1)
     kind = jnp.where(jnp.concatenate([seen_own, seen_far], axis=1), 0.0, MASKED).astype(f32)
 
-    me, place = lax.axis_index("fsdp"), lax.axis_index("ctx")
-    relative = [4 * dy + 2 * dx + 1 - keep for keep in (0, 1) for dy in (0, 1) for dx in (0, 1)]
-    order = jnp.bitwise_xor(me, jnp.array(relative, jnp.int32))
-    owners = lax.rem(place + n - jnp.arange(n), n)
     attended, grad_q, own_kv, come_kv = [], [], [], []
 
     def attend(first, count, wait):
@@ -707,18 +728,27 @@
     output = join(x, attended, weights, mlp_out, bias_out)
     steps_out = side_step(*steps_out)
     steps_in = side_step(*steps_in)
-    grad_inputs, qkv_send, qkv_keep, db_qkv, dgain_attn, dshift_attn = tail(
-        spots[0], order, after(x, output, *steps_out, *steps_in), grad_out, normed, gain_attn, weights, tables, grad_mlp,
-        attended, grad_q, own_kv, come_kv)
-    sum_out = last_step(*steps_out)
-    sum_in = last_step(*steps_in)
-    both = scatter_sum(qkv_send, qkv_keep)
-    sum_qkv, sum_attn = both[:, :3 * width], both[:, 3 * width:]
-    smalls = [a.reshape(width, -1) for a in (dgain_attn, dshift_attn, db_qkv, db_out, dgain_mlp, dshift_mlp, db_in)]
+    first_send, first_keep, grad_heads, db_q = first_tail(
+        order, after(grad_out, output), normed, weights, attended, grad_q)
+    steps_first = core_step(first_send, first_keep)
+    grad_inputs, last_send, last_keep, db_kv, dgain_attn, dshift_attn = last_tail(
+        spots[0], after(x, *steps_out, *steps_in, *steps_first), normed, gain_attn, weights, tables, grad_mlp, grad_heads,
+        own_kv, come_kv)
+    sum_out = along(last_step(*steps_out))
+    sum_in = along(last_step(*steps_in))
+    steps_first = side_step(*steps_first)
+    sum_first = along(last_step(*steps_first))
+    steps_last = core_step(after(last_send, *steps_first), last_keep)
+    smalls = [a.reshape(width, -1) for a in
+              (dgain_attn, dshift_attn, jnp.concatenate([db_q, db_kv], axis=1), db_out, dgain_mlp, dshift_mlp, db_in)]
     used = sum(a.shape[1] for a in smalls)
     packed = jnp.concatenate(smalls + [jnp.zeros((width, PAIR - used), f32)], axis=1).astype(bf16)
     packed = packed.reshape(8, width // 8, PAIR)[order].reshape(2, width // 2, PAIR)
-    packed = scatter_sum(packed[0], packed[1]).astype(f32)
+    part = last_step(*side_step(*core_step(packed[0], packed[1])))
+    joined = along(jnp.concatenate([last_step(*side_step(*steps_last)), part], axis=1))
+    packed = joined[:, 2 * width:].astype(f32)
+    sum_qkv = jnp.concatenate([sum_first[:, width:], joined[:, :2 * width]], axis=1)
+    sum_attn = sum_first[:, :width]
     done, at = [], 0
     for a in smalls:
         done.append(packed[:, at:at + a.shape[1]].reshape(-1))

time: 647 us -> 574 us (0.89)
  waiting for transfers between devices: 183 us -> 98.3 us
  starting transfers between devices: 26 us -> 32.6 us
    all_gather x1, waiting for transfers between devices: 37.7 us -> 3.42 us  [fast(): lax.all_gather(jnp.concatenate([w_qkv, w_attn_out], axis=1), 'fsdp', axis...]
    ppermute x3, waiting for transfers between devices: 20.5 us -> 0.01 us  [fast(): lax.ppermute(spots[0][:half // RB], 'ctx', [(i, (i + s) % n) for i in ran...]
    reduce_scatter x4, waiting for transfers between devices: 43.6 us -> 29.7 us  [along(): return lax.psum_scatter(part, 'ctx', scatter_dimension=0, tiled=True)]
    ppermute x4 -> x5, waiting for transfers between devices: 17.6 us -> 8.07 us  [side_step(): got_b = lax.ppermute(send_b, 'fsdp', pairs_of(4, 8))]
    ppermute x4 -> x5, waiting for transfers between devices: 24.7 us -> 17.6 us  [last_step(): got_b = lax.ppermute(send_b, 'fsdp', pairs_of(2, 8))]
    convert_element_type x26 -> x33, other arithmetic: 39.6 us -> 45.2 us  [plus(): return (a.astype(f32) + b.astype(f32)).astype(bf16)]
    pallas_call x1 -> x2, Pallas kernels: 37.5 us -> 39.3 us  [the longest x1 24.3 us: last_tail(): pl.pallas_call(partial(last_kernel, len(owns)), grid_spec=pltpu.PrefetchS...]
  transfers between devices with their start and end apart: 36 -> 41, of which waited for: 18 -> 21; matrix products, arithmetic and copies ran while one was open for 12% -> 14% of each run, Pallas kernels for 42% -> 54%
where the time goes in v5:
time: 574 us; the launch traced here: 568 us
  Pallas kernels  323 us (56%)
  waiting for transfers between devices  98.3 us (17%)
  other arithmetic  72.2 us (13%)
  starting transfers between devices  32.6 us (6%)
  local copies, waits for them, and re-layouts  17.3 us (3%)
  between operations  15.1 us (3%)
  blocking collectives  9.18 us (2%)
    pallas_call x3, Pallas kernels, attention(): pl.pallas_call(partial(attention_kernel, half, n), grid=(pairs,), in_spec...  157 us
    pallas_call x1, Pallas kernels, mlp(): pl.pallas_call(mlp_kernel, grid_spec=pltpu.PrefetchScalarGridSpec(num_sca...  75.3 us
    convert_element_type x33, other arithmetic, plus(): return (a.astype(f32) + b.astype(f32)).astype(bf16)  45.2 us
    pallas_call x4, Pallas kernels, qkv(): pl.pallas_call(partial(qkv_kernel, with_q), grid_spec=pltpu.PrefetchScala...  38.2 us
    reduce_scatter x4, waiting for transfers between devices, along(): return lax.psum_scatter(part, 'ctx', scatter_dimension=0, tiled=True)  29.7 us
    ppermute x3, waiting for transfers between devices, fast(): run = lax.ppermute(run, 'ctx', ring)  28.2 us
    pallas_call x1, Pallas kernels, last_tail(): pl.pallas_call(partial(last_kernel, len(owns)), grid_spec=pltpu.PrefetchS...  24.3 us
    ppermute x5, waiting for transfers between devices, last_step(): got_b = lax.ppermute(send_b, 'fsdp', pairs_of(2, 8))  17.6 us
  transfers between devices with their start and end apart: 41, of which 21 were waited for; matrix products, arithmetic and copies ran while one was open for 14% of the time, Pallas kernels for 54%

profile of v5, /device:TPU:0, one launch (start us, length us, event | category | flops | bytes accessed | tf_op | source)
XLA Modules:
  0.0 567.9 jit_solution(2163886063836839638)
XLA Ops:
  7.2 2.4 pad_maximum_fusion
  9.9 3.1 collective-permute-start.3
  13.1 2.5 collective-permute-start.2
  19.0 9.2 %all-gather.1 = bf16[8,1,1536]{2,1,0:T(2,128)(2,1)S(1)} all-gather(bf16[1,1,1536]{2,1,0:T(2,128)(2,1)S(1)} %reshape.551), channel_id=2, replica_groups=mesh['fsdp'=8,'ctx'=4] {'fsdp'}, dimensions={0}, use_global_device_ids=true | all-gather | bytes 27648 | tf_op jit(solution)/shard_map/all_gather | solution.py:678
  28.8 9.4 %collective-permute-done.3.x_ref = bf16[512,1024]{1,0:T(8,128)(2,1)S(1)} collective-permute-done((bf16[512,1024]{1,0:T(8,128)(2,1)S(1)}, bf16[512,1024]{1,0:T(8,128)(2,1)S(1)}, u32[]{:S(2)}, u32[]{:S(2)}) %collective-permute-start.3) | collective-permute-done | bytes 1048608 | tf_op jit(solution)/shard_map/ppermute | solution.py:674
  39.5 6.6 %fusion = (f32[2304,128]{1,0:T(8,128)}, f32[2304,128]{1,0:T(8,128)}, f32[2304,128]{1,0:T(8,128)}) fusion(f32[128]{0:T(128)S(1)} %fusion.59, f32[2304]{0:T(1024)S(1)} %iota_convert_fusion, pred[128]{0:T(512)(128)(4,1)S(1)} %get-tuple-element.162, pred[128]{0:T(512)(128)(4,1)S(1)} %broadcast_compare_fusion.1, pred[128]{0:T(512)(128)(4,1)S(1)} %get-tuple-element.163), kind=kLoop, calls=%fused_computation.11 | loop fusion | flops 1179648 | bytes 3549056 | tf_op jit(solution)/shard_map/jit(_where)/select_n | solution.py:691
  46.1 18.2 %collective-permute-done.4.x_ref = bf16[512,1024]{1,0:T(8,128)(2,1)S(1)} collective-permute-done((bf16[512,1024]{1,0:T(8,128)(2,1)S(1)}, bf16[512,1024]{1,0:T(8,128)(2,1)S(1)}, u32[]{:S(2)}, u32[]{:S(2)}) %collective-permute-start.4) | collective-permute-done | bytes 1048608 | tf_op jit(solution)/shard_map/ppermute | solution.py:674
  64.3 3.4 all-gather.6.cloned.1.call-done.w_ref
  67.7 13.9 %qkv_own.1 = (bf16[1024,1024]{1,0:T(8,128)(2,1)}, bf16[1024,1024]{1,0:T(8,128)(2,1)}, bf16[1024,1024]{1,0:T(8,128)(2,1)}, bf16[1024,1024]{1,0:T(8,128)(2,1)}) custom-call(s32[4]{0:T(128)} %copy-done.26, s32[8]{0:T(128)} %get-tuple-element.161.order_ref, bf16[1024,1024]{1,0:T(8,128)(2,1)} %bitcast.251, f32[1,1024]{1,0:T(1,128)} %bitcast.278, ...), custom_call_target="tpu_custom_call" | custom-call | flops 1048576 | bytes 65536 | tf_op jit(solution)/shard_map/qkv_own/pallas_call | solution.py:258
  86.6 8.6 %kv_remote.4 = (bf16[512,1024]{1,0:T(8,128)(2,1)}, bf16[512,1024]{1,0:T(8,128)(2,1)}) custom-call(s32[2]{0:T(128)} %copy-done.19, s32[8]{0:T(128)} %get-tuple-element.161.order_ref, bf16[512,1024]{1,0:T(8,128)(2,1)} %copy-done.5, f32[1,1024]{1,0:T(1,128)} %bitcast.279, f32[1,1024]{1,0:T(1,128)} %bitcast.284, ...), custom_call_target="tpu_custom_call" | custom-call | flops 1048576 | bytes 65536 | tf_op jit(solution)/shard_map/kv_remote/pallas_call | solution.py:258
  95.2 7.9 %kv_remote.3 = (bf16[512,1024]{1,0:T(8,128)(2,1)}, bf16[512,1024]{1,0:T(8,128)(2,1)}) custom-call(s32[2]{0:T(128)} %copy-done.18, s32[8]{0:T(128)} %get-tuple-element.161.order_ref, bf16[512,1024]{1,0:T(8,128)(2,1)} %copy-done.4, f32[1,1024]{1,0:T(1,128)} %bitcast.280, f32[1,1024]{1,0:T(1,128)} %bitcast.285, ...), custom_call_target="tpu_custom_call" | custom-call | flops 1048576 | bytes 65536 | tf_op jit(solution)/shard_map/kv_remote/pallas_call | solution.py:258
  103.1 6.1 %spread.1.do_ref = bf16[1024,1024]{1,0:T(8,128)(2,1)} custom-call(bf16[1024,1024]{1,0:T(8,128)(2,1)} %bitcast.267, bf16[1024,4096]{1,0:T(8,128)(2,1)} %all-gather.6.cloned.1.call-done.w_ref), custom_call_target="tpu_custom_call" | custom-call | flops 1048576 | bytes 65536 | tf_op jit(solution)/shard_map/spread/pallas_call | solution.py:446
  110.8 7.9 %kv_remote.5 = (bf16[512,1024]{1,0:T(8,128)(2,1)}, bf16[512,1024]{1,0:T(8,128)(2,1)}) custom-call(s32[2]{0:T(128)} %copy-done.17, s32[8]{0:T(128)} %get-tuple-element.161.order_ref, bf16[512,1024]{1,0:T(8,128)(2,1)} %copy-done.6, f32[1,1024]{1,0:T(1,128)} %bitcast.281, f32[1,1024]{1,0:T(1,128)} %bitcast.286, ...), custom_call_target="tpu_custom_call" | custom-call | flops 1048576 | bytes 65536 | tf_op jit(solution)/shard_map/kv_remote/pallas_call | solution.py:258
  118.7 95.4 %attention.3 = (bf16[1024,640]{1,0:T(8,128)(2,1)}, bf16[1024,640]{1,0:T(8,128)(2,1)}, bf16[2048,1280]{1,0:T(8,128)(2,1)}, bf16[512,1280]{1,0:T(8,128)(2,1)}) custom-call(f32[4,8]{1,0:T(4,128)} %add_select_fusion.kind_ref, s32[4]{0:T(128)} %compare_select_fusion.3.owner_ref, f32[8,1024]{1,0:T(8,128)} %get-tuple-element.159.cos_ref, ...), custom_call_target="tpu_custom_call" | custom-call | flops 72477573120 | bytes 16777216 | tf_op jit(solution)/shard_map/attention/pallas_call | solution.py:596
  214.8 75.3 %mlp.1 = (f32[1024,1024]{1,0:T(8,128)}, f32[1024,1024]{1,0:T(8,128)}, bf16[512,4096]{1,0:T(8,128)(2,1)}, bf16[512,4096]{1,0:T(8,128)(2,1)}, bf16[2048,1024]{1,0:...) custom-call(s32[8]{0:T(128)} %get-tuple-element.161.order_ref, ...), custom_call_target="tpu_custom_call" | custom-call | flops 51539607552 | bytes 50331648 | tf_op jit(solution)/shard_map/mlp/pallas_call | solution.py:202
  297.6 39.7 %attention.4 = (bf16[1024,256]{1,0:T(8,128)(2,1)}, bf16[1024,256]{1,0:T(8,128)(2,1)}, bf16[2048,512]{1,0:T(8,128)(2,1)}, bf16[512,512]{1,0:T(8,128)(2,1)}) custom-call(f32[4,8]{1,0:T(4,128)} %add_select_fusion.kind_ref, s32[4]{0:T(128)} %compare_select_fusion.3.owner_ref, f32[8,1024]{1,0:T(8,128)} %get-tuple-element.159.cos_ref, ...), custom_call_target="tpu_custom_call" | custom-call | flops 28991029248 | bytes 16777216 | tf_op jit(solution)/shard_map/attention/pallas_call | solution.py:596
  337.4 4.3 add_convert_fusion.2
  342.9 3.1 fusion.3
  347.2 3.3 add_convert_fusion
  351.8 2.5 fusion.5
  356.4 21.5 %attention.5 = (bf16[1024,128]{1,0:T(8,128)(2,1)}, bf16[1024,128]{1,0:T(8,128)(2,1)}, bf16[2048,256]{1,0:T(8,128)(2,1)}, bf16[512,256]{1,0:T(8,128)(2,1)}) custom-call(f32[4,8]{1,0:T(4,128)} %add_select_fusion.kind_ref, s32[4]{0:T(128)} %compare_select_fusion.3.owner_ref, f32[8,1024]{1,0:T(8,128)} %get-tuple-element.159.cos_ref, ...), custom_call_target="tpu_custom_call" | custom-call | flops 14495514624 | bytes 16777216 | tf_op jit(solution)/shard_map/attention/pallas_call | solution.py:596
  377.9 7.6 %join.1 = bf16[1024,1024]{1,0:T(8,128)(2,1)} custom-call(bf16[1024,1024]{1,0:T(8,128)(2,1)} %bitcast.253, bf16[1024,4096]{1,0:T(8,128)(2,1)} %all-gather.6.cloned.1.call-done.w_ref, f32[1024,1024]{1,0:T(8,128)} %get-tuple-element.78.mlp_ref, f32[1,1024]{1,0:T(1,128)} %bitcast.290, bf16[1024,640]{1,0:T(8,128)(2,1)} %get-tuple-element.74.refs_0_, ...), custom_call_target="tpu_custom_call" | custom-call | flops 2147483648 | bytes 12582912 | tf_op jit(solution)/shard_map/join/pallas_call | solution.py:425
  385.5 15.0 %first_tail.1 = (bf16[512,2048]{1,0:T(8,128)(2,1)}, bf16[512,2048]{1,0:T(8,128)(2,1)}, f32[1024,1024]{1,0:T(8,128)}, f32[1,1024]{1,0:T(1,128)}) custom-call(s32[8]{0:T(128)} %get-tuple-element.161.order_ref, bf16[1024,1024]{1,0:T(8,128)(2,1)} %bitcast.269, bf16[1024,1024]{1,0:T(8,128)(2,1)} %get-tuple-element.88.h_ref, ...), custom_call_target="tpu_custom_call" | custom-call | flops 6442450944 | bytes 25165824 | tf_op jit(solution)/shard_map/first_tail/pallas_call | solution.py:317
  414.0 5.4 collective-permute-done.30
  424.7 5.6 collective-permute-done.28
  438.6 24.3 %last_tail.1 = (f32[1024,1024]{1,0:T(8,128)}, bf16[512,2048]{1,0:T(8,128)(2,1)}, bf16[512,2048]{1,0:T(8,128)(2,1)}, f32[1,2048]{1,0:T(1,128)}, f32[1,1024]{1,0:T(1,128)}, /*index=5*/f32[1,1024]{1,0:T(1,128)}) custom-call(s32[4]{0:T(128)} %copy-done.26, bf16[1024,1024]{1,0:T(8,128)(2,1)} %bitcast.254, bf16[1024,1024]{1,0:T(8,128)(2,1)} %get-tuple-element.88.h_ref, ...), custom_call_target="tpu_custom_call" | custom-call | flops 8589934592 | bytes 33554432 | tf_op jit(solution)/shard_map/last_tail/pallas_call | solution.py:394
  469.8 3.3 collective-permute-done.26
  478.5 3.6 concatenate.65
  502.1 6.6 %collective-permute-done.18 = bf16[2,64,2048]{2,1,0:T(8,128)(2,1)} collective-permute-done((bf16[2,64,2048]{2,1,0:T(8,128)(2,1)}, bf16[2,64,2048]{2,1,0:T(8,128)(2,1)}, u32[]{:S(2)}, u32[]{:S(2)}) %collective-permute-start.18) | collective-permute-done | bytes 524320 | tf_op jit(solution)/shard_map/ppermute | solution.py:641
  510.7 3.3 collective-permute-done.16
  525.1 8.9 %reduce-scatter.16.cloned.1.call-done = bf16[32,2048]{1,0:T(8,128)(2,1)} async-done(((bf16[128,2048]{1,0:T(8,128)(2,1)}), bf16[32,2048]{1,0:T(8,128)(2,1)}) %reduce-scatter.16.cloned.1.call-update) | async-done | bytes 131088 | tf_op jit(solution)/shard_map/reduce_scatter | solution.py:652
  535.5 20.8 %reduce-scatter.14.cloned.1.call-done = bf16[32,2176]{1,0:T(8,128)(2,1)} async-done(((bf16[128,2176]{1,0:T(8,128)(2,1)}), bf16[32,2176]{1,0:T(8,128)(2,1)}) %reduce-scatter.14.cloned.1.call-update) | async-done | bytes 139280 | tf_op jit(solution)/shard_map/reduce_scatter | solution.py:652
  (234 shorter events, 104.3 us)
Async XLA Ops:
  7.2 60.5 %all-gather.6.cloned.1.call-start = ((), (), s32[]{:S(2)}) async-start(), calls=%async_computation.7 | async-start | bytes 9437184 | tf_op jit(solution)/shard_map/all_gather | solution.py:684
  9.7 205.1 %all-gather.8.cloned.1.call-start = ((), (), s32[]{:S(2)}) async-start(), calls=%async_computation.8 | async-start | bytes 9437184 | tf_op jit(solution)/shard_map/all_gather | solution.py:702
  9.9 28.3 %collective-permute-start.3 = (bf16[512,1024]{1,0:T(8,128)(2,1)S(1)}, bf16[512,1024]{1,0:T(8,128)(2,1)S(1)}, u32[]{:S(2)}, u32[]{:S(2)}) collective-permute-start(bf16[512,1024]{1,0:T(8,128)(2,1)S(1)} %slice_bitcast_fusion.4), channel_id=1, source_target_pairs={{0,1},{1,2},{2,3},{3,0},{4,5},{5,6},{6,7},{7,4},{8,9},{9,10},{10,1... | collective-permute-start | bytes 3145736 | tf_op jit(solution)/shard_map/ppermute | solution.py:674
  13.1 33.0 %collective-permute-start.2 = (s32[2]{0:T(128)S(1)}, s32[2]{0:T(128)S(1)}, u32[]{:S(2)}, u32[]{:S(2)}) collective-permute-start(s32[2]{0:T(128)S(1)} %bitcast.300), channel_id=1, source_target_pairs={{0,3},{1,0},{2,1},{3,2},{4,7},{5,4},{6,5},{7,6},{8,11},{9,8},{10,9... | collective-permute-start | bytes 32 | tf_op jit(solution)/shard_map/ppermute | solution.py:676
  15.5 30.5 %collective-permute-start.1 = (s32[2]{0:T(128)S(1)}, s32[2]{0:T(128)S(1)}, u32[]{:S(2)}, u32[]{:S(2)}) collective-permute-start(s32[2]{0:T(128)S(1)} %bitcast.301), channel_id=1, source_target_pairs={{0,2},{1,3},{2,0},{3,1},{4,6},{5,7},{6,4},{7,5},{8,10},{9,11},{10,... | collective-permute-start | bytes 32 | tf_op jit(solution)/shard_map/ppermute | solution.py:676
  16.1 29.9 %collective-permute-start = (s32[2]{0:T(128)S(1)}, s32[2]{0:T(128)S(1)}, u32[]{:S(2)}, u32[]{:S(2)}) collective-permute-start(s32[2]{0:T(128)S(1)} %bitcast.302), channel_id=1, source_target_pairs={{0,1},{1,2},{2,3},{3,0},{4,5},{5,6},{6,7},{7,4},{8,9},{9,10},{10,1... | collective-permute-start | bytes 32 | tf_op jit(solution)/shard_map/ppermute | solution.py:676
  38.2 26.1 %collective-permute-start.4 = (bf16[512,1024]{1,0:T(8,128)(2,1)S(1)}, bf16[512,1024]{1,0:T(8,128)(2,1)S(1)}, u32[]{:S(2)}, u32[]{:S(2)}) collective-permute-start(bf16[512,1024]{1,0:T(8,128)(2,1)S(1)} %collective-permute-done.3.x_ref), channel_id=1, source_target_pairs={{0,1},{1,2},{2,3},{3,0},{4,5},{5,6},{6,7},{7,4},{8,9},{9,10},{10,1... | collective-permute-start | bytes 3145736 | tf_op jit(solution)/shard_map/ppermute | solution.py:674
  81.7 133.2 %all-gather.10.cloned.1.call-start = ((), (), s32[]{:S(2)}) async-start(), calls=%async_computation.9 | async-start | bytes 9437184 | tf_op jit(solution)/shard_map/all_gather | solution.py:703
  82.4 356.2 %reduce-scatter.8.cloned.1.call-start = ((), (), s32[]{:S(2)}) async-start(), calls=%async_computation.10 | async-start | bytes 6553600 | tf_op jit(solution)/shard_map/reduce_scatter | solution.py:718
  82.5 27.4 %collective-permute-start.5 = (bf16[512,1024]{1,0:T(8,128)(2,1)S(1)}, bf16[512,1024]{1,0:T(8,128)(2,1)S(1)}, u32[]{:S(2)}, u32[]{:S(2)}) collective-permute-start(bf16[512,1024]{1,0:T(8,128)(2,1)S(1)} %collective-permute-done.4.x_ref), channel_id=1, source_target_pairs={{0,1},{1,2},{2,3},{3,0},{4,5},{5,6},{6,7},{7,4},{8,9},{9,10},{10,1... | collective-permute-start | bytes 3145736 | tf_op jit(solution)/shard_map/ppermute | solution.py:674
  214.1 224.5 %reduce-scatter.10.cloned.1.call-start = ((), (), s32[]{:S(2)}) async-start(), calls=%async_computation.11 | async-start | bytes 2621440 | tf_op jit(solution)/shard_map/reduce_scatter | solution.py:718
  290.1 47.3 %collective-permute-start.6 = (bf16[2048,1024]{1,0:T(8,128)(2,1)}, bf16[2048,1024]{1,0:T(8,128)(2,1)}, u32[]{:S(2)}, u32[]{:S(2)}) collective-permute-start(bf16[2048,1024]{1,0:T(8,128)(2,1)} %get-tuple-element.82), channel_id=1, source_target_pairs={{0,4},{4,0},{8,12},{12,8},{16,20},{20,16},{24,28},{28,24},{1,5},{5... | collective-permute-start | bytes 12582920 | tf_op jit(solution)/shard_map/ppermute | solution.py:629
  290.2 57.0 %collective-permute-start.7 = (bf16[512,4096]{1,0:T(8,128)(2,1)}, bf16[512,4096]{1,0:T(8,128)(2,1)}, u32[]{:S(2)}, u32[]{:S(2)}) collective-permute-start(bf16[512,4096]{1,0:T(8,128)(2,1)} %get-tuple-element.84), channel_id=1, source_target_pairs={{0,4},{4,0},{8,12},{12,8},{16,20},{20,16},{24,28},{28,24},{1,5},{5... | collective-permute-start | bytes 12582920 | tf_op jit(solution)/shard_map/ppermute | solution.py:629
  337.4 101.3 %reduce-scatter.12.cloned.1.call-start = ((), (), s32[]{:S(2)}) async-start(), calls=%async_computation.12 | async-start | bytes 1310720 | tf_op jit(solution)/shard_map/reduce_scatter | solution.py:718
  341.7 61.6 %collective-permute-start.9 = (bf16[2,256,1024]{2,1,0:T(8,128)(2,1)}, bf16[2,256,1024]{2,1,0:T(8,128)(2,1)}, u32[]{:S(2)}, u32[]{:S(2)}) collective-permute-start(bf16[2,256,1024]{2,1,0:T(8,128)(2,1)} %get-tuple-element.135), channel_id=1, source_target_pairs={{0,16},{4,20},{8,24},{12,28},{16,0},{20,4},{24,8},{28,12},{1,17},{... | collective-permute-start | bytes 3145736 | tf_op jit(solution)/shard_map/ppermute | solution.py:641
  345.9 60.2 %collective-permute-start.8 = (bf16[2,256,1024]{2,1,0:T(8,128)(2,1)}, bf16[2,256,1024]{2,1,0:T(8,128)(2,1)}, u32[]{:S(2)}, u32[]{:S(2)}) collective-permute-start(bf16[2,256,1024]{2,1,0:T(8,128)(2,1)} %fusion.3), channel_id=1, source_target_pairs={{0,8},{4,12},{8,0},{12,4},{16,24},{20,28},{24,16},{28,20},{1,9},{5... | collective-permute-start | bytes 3145736 | tf_op jit(solution)/shard_map/ppermute | solution.py:640
  350.5 57.6 %collective-permute-start.11 = (bf16[2,64,4096]{2,1,0:T(8,128)(2,1)}, bf16[2,64,4096]{2,1,0:T(8,128)(2,1)}, u32[]{:S(2)}, u32[]{:S(2)}) collective-permute-start(bf16[2,64,4096]{2,1,0:T(8,128)(2,1)} %get-tuple-element.133), channel_id=1, source_target_pairs={{0,16},{4,20},{8,24},{12,28},{16,0},{20,4},{24,8},{28,12},{1,17},{... | collective-permute-start | bytes 3145736 | tf_op jit(solution)/shard_map/ppermute | solution.py:641
  354.3 56.6 %collective-permute-start.10 = (bf16[2,64,4096]{2,1,0:T(8,128)(2,1)}, bf16[2,64,4096]{2,1,0:T(8,128)(2,1)}, u32[]{:S(2)}, u32[]{:S(2)}) collective-permute-start(bf16[2,64,4096]{2,1,0:T(8,128)(2,1)} %fusion.5), channel_id=1, source_target_pairs={{0,8},{4,12},{8,0},{12,4},{16,24},{20,28},{24,16},{28,20},{1,9},{5... | collective-permute-start | bytes 3145736 | tf_op jit(solution)/shard_map/ppermute | solution.py:640
  401.2 33.2 %collective-permute-start.12 = (bf16[512,2048]{1,0:T(8,128)(2,1)}, bf16[512,2048]{1,0:T(8,128)(2,1)}, u32[]{:S(2)}, u32[]{:S(2)}) collective-permute-start(bf16[512,2048]{1,0:T(8,128)(2,1)} %get-tuple-element.93), channel_id=1, source_target_pairs={{0,4},{4,0},{8,12},{12,8},{16,20},{20,16},{24,28},{28,24},{1,5},{5... | collective-permute-start | bytes 6291464 | tf_op jit(solution)/shard_map/ppermute | solution.py:629
  401.2 120.3 %reduce-scatter.20.cloned.1.call-start = ((), (), s32[]{:S(2)}) async-start(), calls=%async_computation.16 | async-start | bytes 1310720 | tf_op jit(solution)/shard_map/reduce_scatter | solution.py:652
  404.6 14.8 %collective-permute-start.30 = (bf16[256,1024]{1,0:T(8,128)(2,1)S(1)}, bf16[256,1024]{1,0:T(8,128)(2,1)S(1)}, u32[]{:S(2)}, u32[]{:S(2)}) collective-permute-start(bf16[256,1024]{1,0:T(8,128)(2,1)S(1)} %fusion.21), channel_id=1, source_target_pairs={{0,8},{4,12},{8,0},{12,4},{16,24},{20,28},{24,16},{28,20},{1,9},{5... | collective-permute-start | bytes 1572872 | tf_op jit(solution)/shard_map/ppermute | solution.py:647
  407.5 14.8 %collective-permute-start.29 = (bf16[256,1024]{1,0:T(8,128)(2,1)S(1)}, bf16[256,1024]{1,0:T(8,128)(2,1)S(1)}, u32[]{:S(2)}, u32[]{:S(2)}) collective-permute-start(bf16[256,1024]{1,0:T(8,128)(2,1)S(1)} %fusion.19), channel_id=1, source_target_pairs={{0,16},{4,20},{8,24},{12,28},{16,0},{20,4},{24,8},{28,12},{1,17},{... | collective-permute-start | bytes 1572872 | tf_op jit(solution)/shard_map/ppermute | solution.py:646
  410.1 20.2 %collective-permute-start.28 = (bf16[64,4096]{1,0:T(8,128)(2,1)}, bf16[64,4096]{1,0:T(8,128)(2,1)}, u32[]{:S(2)}, u32[]{:S(2)}) collective-permute-start(bf16[64,4096]{1,0:T(8,128)(2,1)} %fusion.25), channel_id=1, source_target_pairs={{0,8},{4,12},{8,0},{12,4},{16,24},{20,28},{24,16},{28,20},{1,9},{5... | collective-permute-start | bytes 1572872 | tf_op jit(solution)/shard_map/ppermute | solution.py:647
  412.9 20.0 %collective-permute-start.27 = (bf16[64,4096]{1,0:T(8,128)(2,1)}, bf16[64,4096]{1,0:T(8,128)(2,1)}, u32[]{:S(2)}, u32[]{:S(2)}) collective-permute-start(bf16[64,4096]{1,0:T(8,128)(2,1)} %fusion.23), channel_id=1, source_target_pairs={{0,16},{4,20},{8,24},{12,28},{16,0},{20,4},{24,8},{28,12},{1,17},{... | collective-permute-start | bytes 1572872 | tf_op jit(solution)/shard_map/ppermute | solution.py:646
  424.7 98.7 %reduce-scatter.18.cloned.1.call-start = ((), (), s32[]{:S(2)}) async-start(), calls=%async_computation.15 | async-start | bytes 1310720 | tf_op jit(solution)/shard_map/reduce_scatter | solution.py:652
  437.2 27.8 %collective-permute-start.14 = (bf16[2,64,2048]{2,1,0:T(8,128)(2,1)S(1)}, bf16[2,64,2048]{2,1,0:T(8,128)(2,1)}, u32[]{:S(2)}, u32[]{:S(2)}) collective-permute-start(bf16[2,64,2048]{2,1,0:T(8,128)(2,1)S(1)} %get-tuple-element.141), channel_id=1, source_target_pairs={{0,16},{4,20},{8,24},{12,28},{16,0},{20,4},{24,8},{28,12},{1,17},{... | collective-permute-start | bytes 1572872 | tf_op jit(solution)/shard_map/ppermute | solution.py:641
  437.9 29.5 %collective-permute-start.13 = (bf16[2,64,2048]{2,1,0:T(8,128)(2,1)S(1)}, bf16[2,64,2048]{2,1,0:T(8,128)(2,1)}, u32[]{:S(2)}, u32[]{:S(2)}) collective-permute-start(bf16[2,64,2048]{2,1,0:T(8,128)(2,1)S(1)} %fusion.15), channel_id=1, source_target_pairs={{0,8},{4,12},{8,0},{12,4},{16,24},{20,28},{24,16},{28,20},{1,9},{5... | collective-permute-start | bytes 1572872 | tf_op jit(solution)/shard_map/ppermute | solution.py:640
  476.9 17.4 %collective-permute-start.15 = (bf16[512,2048]{1,0:T(8,128)(2,1)}, bf16[512,2048]{1,0:T(8,128)(2,1)}, u32[]{:S(2)}, u32[]{:S(2)}) collective-permute-start(bf16[512,2048]{1,0:T(8,128)(2,1)} %get-tuple-element.106), channel_id=1, source_target_pairs={{0,4},{4,0},{8,12},{12,8},{16,20},{20,16},{24,28},{28,24},{1,5},{5... | collective-permute-start | bytes 6291464 | tf_op jit(solution)/shard_map/ppermute | solution.py:629
  484.9 49.0 %reduce-scatter.16.cloned.1.call-start = ((), (), s32[]{:S(2)}) async-start(), calls=%async_computation.14 | async-start | bytes 655360 | tf_op jit(solution)/shard_map/reduce_scatter | solution.py:652
  496.8 11.9 %collective-permute-start.18 = (bf16[2,64,2048]{2,1,0:T(8,128)(2,1)}, bf16[2,64,2048]{2,1,0:T(8,128)(2,1)}, u32[]{:S(2)}, u32[]{:S(2)}) collective-permute-start(bf16[2,64,2048]{2,1,0:T(8,128)(2,1)} %get-tuple-element.139), channel_id=1, source_target_pairs={{0,16},{4,20},{8,24},{12,28},{16,0},{20,4},{24,8},{28,12},{1,17},{... | collective-permute-start | bytes 1572872 | tf_op jit(solution)/shard_map/ppermute | solution.py:641
  500.1 13.9 %collective-permute-start.16 = (bf16[2,64,2048]{2,1,0:T(8,128)(2,1)}, bf16[2,64,2048]{2,1,0:T(8,128)(2,1)S(1)}, u32[]{:S(2)}, u32[]{:S(2)}) collective-permute-start(bf16[2,64,2048]{2,1,0:T(8,128)(2,1)} %get-tuple-element.137), channel_id=1, source_target_pairs={{0,8},{4,12},{8,0},{12,4},{16,24},{20,28},{24,16},{28,20},{1,9},{5... | collective-permute-start | bytes 1572872 | tf_op jit(solution)/shard_map/ppermute | solution.py:640
  502.1 54.2 %reduce-scatter.14.cloned.1.call-start = ((), (), s32[]{:S(2)}) async-start(), calls=%async_computation.13 | async-start | bytes 696320 | tf_op jit(solution)/shard_map/reduce_scatter | solution.py:652
  (37 other events, 473.0 us)
Sparse Core Ops, SparseCore 0:
  10.5 57.1 all-gather.5
  81.8 54.3 all-gather.7
  138.1 54.3 all-gather.9
  214.3 93.3 reduce-scatter.7
  337.5 43.4 reduce-scatter.9
  401.3 26.6 reduce-scatter.11
  430.3 25.8 reduce-scatter.19
  485.0 26.2 reduce-scatter.17
  513.6 20.2 reduce-scatter.15
  536.1 20.1 reduce-scatter.13

commit v6 on v5

--- a/solution.py
+++ b/solution.py
@@ -217,7 +217,7 @@
                    s((ff // 2, width), bf16), s((ff // 2, width), bf16), s((1, ff), f32), s((1, width), f32),
                    s((1, width), f32), s((1, width), f32)],
         compiler_params=params(),
-        cost_estimate=pl.CostEstimate(flops=12 * rows * width * ff, bytes_accessed=48 << 20, transcendentals=2 * rows * ff),
+        cost_estimate=pl.CostEstimate(flops=1 << 20, bytes_accessed=1 << 16, transcendentals=0),
         name="mlp",
     )(order, x, c, gain.reshape(1, -1), shift.reshape(1, -1), weight_in, bias_in.reshape(1, -1), weight_out)
 
@@ -231,7 +231,18 @@
     return jnp.concatenate(parts, axis=1)
 
 
-def qkv_kernel(with_q, spot_ref, order_ref, x_ref, gain_ref, shift_ref, w_ref, b_ref, cos_ref, low_ref, high_ref, *outs):
+def qkv_kernel(far, spot_ref, order_ref, gain_ref, shift_ref, w_ref, b_ref, cos_ref, low_ref, high_ref, *refs):
+    with_q = far == 0
+    if with_q:
+        x_ref, outs = refs[0], refs[1:]
+    else:
+        x_refs, outs, x_ref = refs[:far], refs[far:-1], refs[-1]
+        step = pl.program_id(0)
+        per = pl.num_programs(0) // far
+        for s in range(far):
+            @pl.when(step // per == s)
+            def _(s=s):
+                x_ref[...] = x_refs[s][...]
     width = x_ref.shape[1]
     h = norm_rows(x_ref[...].astype(f32), gain_ref[...], shift_ref[...])
     tables = (cos_ref[...], low_ref[...], high_ref[...])
@@ -248,28 +259,36 @@
     v_ref[...] = (mm(h, w_ref[:, 2 * width:], NN) + b_ref[:, 2 * width:]).astype(bf16)
 
 
-def qkv(spots, order, x, gain, shift, weight, bias, tables, with_q):
-    rows, width = x.shape
-    s = jax.ShapeDtypeStruct((rows, width), bf16)
+def qkv(spots, order, xs, gain, shift, weight, bias, tables):
+    far = len(xs) if len(xs) > 1 else 0
+    rows, width = xs[0].shape
+    per = rows // RB
+    total = len(xs) * rows
+    s = jax.ShapeDtypeStruct((total, width), bf16)
     block = pl.BlockSpec((RB, width), lambda j, spot, o: (j, 0))
     line = pl.BlockSpec((1, width), lambda j, spot, o: (0, 0))
     table = pl.BlockSpec((RB, PAIR), lambda j, spot, o: (spot[j], 0))
-    count = 4 if with_q else 2
+    count = 2 if far else 4
+
+    def window(i):
+        return pl.BlockSpec((RB, width), lambda j, spot, o: (jnp.clip(j - i * per, 0, per - 1), 0))
+
     return pl.pallas_call(
-        partial(qkv_kernel, with_q),
+        partial(qkv_kernel, far),
         grid_spec=pltpu.PrefetchScalarGridSpec(
             num_scalar_prefetch=2,
-            grid=(rows // RB,),
-            in_specs=[block, line, line, pl.BlockSpec((width, 3 * width), lambda j, spot, o: (0, 0)),
-                      pl.BlockSpec((1, 3 * width), lambda j, spot, o: (0, 0)), table, table, table],
+            grid=(total // RB,),
+            in_specs=[line, line, pl.BlockSpec((width, 3 * width), lambda j, spot, o: (0, 0)),
+                      pl.BlockSpec((1, 3 * width), lambda j, spot, o: (0, 0)), table, table, table]
+            + [window(i) for i in range(len(xs))],
             out_specs=[block] * count,
-            scratch_shapes=[vmem(RB, width, dtype=bf16)] if with_q else [],
+            scratch_shapes=[vmem(RB, width, dtype=bf16)],
         ),
         out_shape=[s] * count,
         compiler_params=params(),
         cost_estimate=pl.CostEstimate(flops=1 << 20, bytes_accessed=1 << 16, transcendentals=0),
-        name="qkv_own" if with_q else "kv_remote",
-    )(spots, order, x, gain.reshape(1, -1), shift.reshape(1, -1), weight, bias.reshape(1, -1), *tables)
+        name="kv_remote" if far else "qkv_own",
+    )(spots, order, gain.reshape(1, -1), shift.reshape(1, -1), weight, bias.reshape(1, -1), *tables, *xs)
 
 
 def first_kernel(groups, order_ref, c_ref, h_ref, w_ref, *refs):
@@ -325,54 +344,62 @@
         ),
         out_shape=[s((width // 2, 2 * width), bf16), s((width // 2, 2 * width), bf16), s((rows, width), f32), s((1, width), f32)],
         compiler_params=params(),
-        cost_estimate=pl.CostEstimate(flops=6 * rows * width * width, bytes_accessed=24 << 20, transcendentals=0),
+        cost_estimate=pl.CostEstimate(flops=12884901888, bytes_accessed=1048576, transcendentals=0),
         name="first_tail",
     )(order, c, h, weights, *arrays)
 
 
-def last_kernel(groups, spot_ref, x_ref, h_ref, gain_ref, w_ref, cos_ref, low_ref, high_ref, gin_ref, ghq_ref, *refs):
-    own_refs, come_refs = refs[:groups], refs[groups:2 * groups]
-    grad_ref, send_ref, keep_ref, db_ref, dgain_ref, dshift_ref, p_ref, gh_ref = refs[2 * groups:]
+def kv_kernel(groups, final, first, spot_ref, x_ref, h_ref, gain_ref, wk_ref, wv_ref, cos_ref, low_ref, high_ref, gin_ref,
+              gh_ref, *refs):
+    count = len(groups)
+    own_refs, come_refs = refs[:count], refs[count:2 * count]
+    send_ref, keep_ref, db_ref, grad_ref = refs[2 * count:2 * count + 4]
+    p_ref, w_ref, acc_ref = refs[-3:]
     step = pl.program_id(0)
     rows = x_ref.shape[0]
     half = rows // 2
     blocks = [slice(r, r + RB) for r in range(0, rows, RB)]
-    columns = []
-    for g in range(groups):
-        columns += [(g, at) for at in range(0, own_refs[g].shape[1], 2 * PAIR)]
-
-    def put(shift):
-        db = jnp.zeros(db_ref.shape, f32)
+
+    def put(own_ref, come_ref):
         for r in blocks:
             spot = pl.ds(pl.multiple_of(spot_ref[r.start // RB] * RB, RB), RB)
-            for to, (g, at) in enumerate(columns):
-                lanes = slice(at + shift, at + shift + PAIR)
-                if r.start < half:
-                    t = come_refs[g][r, lanes]
-                else:
-                    t = own_refs[g][r.start - half:r.stop - half, lanes]
-                if shift == 0:
-                    t = turn_lanes(t.astype(f32), cos_ref[spot, :], low_ref[spot, :], high_ref[spot, :], -1.0).astype(bf16)
-                p_ref[r, to * PAIR:(to + 1) * PAIR] = t
-            db += col_sum(p_ref[r, :].astype(f32))
-        db_ref[...] = db
-        dw = mm(h_ref[...], p_ref[...], TN).astype(bf16)
-        send_ref[...] = dw[:send_ref.shape[0]]
-        keep_ref[...] = dw[send_ref.shape[0]:]
+            t = come_ref[r, :] if r.start < half else own_ref[r.start - half:r.stop - half, :]
+            p_ref[r, :PAIR] = turn_lanes(t[:, :PAIR].astype(f32), cos_ref[spot, :], low_ref[spot, :], high_ref[spot, :],
+                                         -1.0).astype(bf16)
+            p_ref[r, PAIR:] = t[:, PAIR:]
+
+    at = 0
+    for g, size in enumerate(groups):
+        @pl.when((step >= at) & (step < at + size))
+        def _(g=g):
+            put(own_refs[g], come_refs[g])
+        at += size
+    w_ref[:, :PAIR] = wk_ref[...]
+    w_ref[:, PAIR:] = wv_ref[...]
 
     @pl.when(step == 0)
     def _():
-        put(0)
-        for r in blocks:
-            gh_ref[r, :] = ghq_ref[r, :] + mm(p_ref[r, :], w_ref[...], NT)
-
-    @pl.when(step == 1)
+        acc_ref[...] = gh_ref[...]
+
+    db = jnp.zeros(db_ref.shape, f32)
+    for r in blocks:
+        acc_ref[r, :] += mm(p_ref[r, :], w_ref[...], NT)
+        db += col_sum(p_ref[r, :].astype(f32))
+    db_ref[...] = db
+    dw = mm(h_ref[...], p_ref[...], TN).astype(bf16)
+    send_ref[...] = dw[:send_ref.shape[0]]
+    keep_ref[...] = dw[send_ref.shape[0]:]
+
+    @pl.when(step == pl.num_programs(0) - 1)
     def _():
-        put(PAIR)
+        if not final:
+            grad_ref[...] = acc_ref[...]
+            return
+        dgain_ref, dshift_ref = refs[2 * count + 4:2 * count + 6]
         dgain = jnp.zeros(dgain_ref.shape, f32)
         dshift = jnp.zeros(dshift_ref.shape, f32)
         for r in blocks:
-            grad = gh_ref[r, :] + mm(p_ref[r, :], w_ref[...], NT)
+            grad = acc_ref[r, :]
             back, scaled = norm_back(x_ref[r, :].astype(f32), grad, gain_ref[...])
             grad_ref[r, :] = back + gin_ref[r, :]
             dgain += col_sum(scaled)
@@ -381,31 +408,44 @@
         dshift_ref[...] = dshift
 
 
-def last_tail(spots, x, h, gain, weights, tables, gin, ghq, owns, comes):
+def kv_tail(final, first, spots, x, h, gain, weights, tables, gin, gh, owns, comes):
     rows, width = x.shape
+    groups = [a.shape[1] // (2 * PAIR) for a in owns]
+    pairs = sum(groups)
     s = jax.ShapeDtypeStruct
 
     def full(a):
-        return pl.BlockSpec(a.shape, lambda j, spot: (0, 0))
+        return pl.BlockSpec(a.shape, lambda j, spot: (0, 0), pipeline_mode=pl.Buffered(1))
+
+    def windows(arrays):
+        specs, at = [], 0
+        for a, size in zip(arrays, groups):
+            specs.append(pl.BlockSpec((a.shape[0], 2 * PAIR), lambda j, spot, at=at, size=size: (0, jnp.clip(j - at, 0, size - 1))))
+            at += size
+        return specs
 
     line = pl.BlockSpec((1, width), lambda j, spot: (0, 0))
-    down = pl.BlockSpec((width // 2, width), lambda j, spot: (0, j))
-    arrays = [*tables, gin, ghq, *owns, *comes]
+    down = pl.BlockSpec((width // 2, 2 * PAIR), lambda j, spot: (0, j))
+    column = width // PAIR
+    more = [line, line] if final else []
     return pl.pallas_call(
-        partial(last_kernel, len(owns)),
+        partial(kv_kernel, groups, final, first),
         grid_spec=pltpu.PrefetchScalarGridSpec(
             num_scalar_prefetch=1,
-            grid=(2,),
-            in_specs=[full(x), full(h), line, pl.BlockSpec((width, width), lambda j, spot: (0, j + 1))] + [full(a) for a in arrays],
-            out_specs=[full(x), down, down, pl.BlockSpec((1, width), lambda j, spot: (0, j)), line, line],
-            scratch_shapes=[vmem(rows, width, dtype=bf16), vmem(rows, width)],
+            grid=(pairs,),
+            in_specs=[full(x), full(h), line, pl.BlockSpec((width, PAIR), lambda j, spot: (0, column + first + j)),
+                      pl.BlockSpec((width, PAIR), lambda j, spot: (0, 2 * column + first + j))]
+            + [full(a) for a in (*tables, gin, gh)] + windows(owns) + windows(comes),
+            out_specs=[down, down, pl.BlockSpec((1, 2 * PAIR), lambda j, spot: (0, j)),
+                       pl.BlockSpec((rows, width), lambda j, spot: (0, 0))] + more,
+            scratch_shapes=[vmem(rows, 2 * PAIR, dtype=bf16), vmem(width, 2 * PAIR, dtype=bf16), vmem(rows, width)],
         ),
-        out_shape=[s((rows, width), f32), s((width // 2, 2 * width), bf16), s((width // 2, 2 * width), bf16),
-                   s((1, 2 * width), f32), s((1, width), f32), s((1, width), f32)],
+        out_shape=[s((width // 2, 2 * PAIR * pairs), bf16), s((width // 2, 2 * PAIR * pairs), bf16),
+                   s((1, 2 * PAIR * pairs), f32), s((rows, width), f32)] + [s((1, width), f32)] * len(more),
         compiler_params=params(),
-        cost_estimate=pl.CostEstimate(flops=8 * rows * width * width, bytes_accessed=32 << 20, transcendentals=0),
-        name="last_tail",
-    )(spots, x, h, gain.reshape(1, -1), weights, *arrays)
+        cost_estimate=pl.CostEstimate(flops=12884901888, bytes_accessed=1 << 20, transcendentals=0),
+        name="kv_last" if final else "kv_first",
+    )(spots, x, h, gain.reshape(1, -1), weights, weights, *tables, gin, gh, *owns, *comes)
 
 
 def join_kernel(groups, x_ref, w_ref, mlp_ref, b_ref, *refs):
@@ -431,7 +471,7 @@
         out_shape=s((rows, width), bf16),
         scratch_shapes=[vmem(RB, width, dtype=bf16)],
         compiler_params=params(),
-        cost_estimate=pl.CostEstimate(flops=2 * rows * width * width, bytes_accessed=12 << 20, transcendentals=0),
+        cost_estimate=pl.CostEstimate(flops=12884901888, bytes_accessed=1048576, transcendentals=0),
         name="join",
     )(x, weights, mlp_out, bias.reshape(1, -1), *attended)
 
@@ -464,14 +504,12 @@
 
 
 def attention_kernel(half, n, kind_ref, owner_ref, cos_ref, sin_ref, q_ref, do_ref, *refs):
-    k_refs, v_refs = refs[:n], refs[n:2 * n]
-    o_ref, dq_ref = refs[2 * n:2 * n + 2]
-    all_ref, cont_ref = refs[2 * n + 2:2 * n + 4]
-    kt_ref, vt_ref, s_ref, p_ref, ds_ref, dka_ref, dva_ref = refs[2 * n + 4:]
+    k_refs, v_refs = refs[:2], refs[2:4]
+    o_ref, dq_ref, all_ref, cont_ref, kt_ref, vt_ref, s_ref, p_ref, ds_ref, dka_ref, dva_ref = refs[4:]
     per = half // QB
     wide = n * half
     count = wide // QB
-    spots = [(0, c * QB) for c in range(per)] + [(s, c * QB) for s in range(1, n) for c in range(per)]
+    spots = [(0, c * QB) for c in range(per)] + [(1, c * QB) for c in range((n - 1) * per)]
 
     ident = eye(PAIR)
     for refs_in, out in ((k_refs, kt_ref), (v_refs, vt_ref)):
@@ -582,7 +620,7 @@
 def attention(kind, owners, cos_t, sin_t, q, do, ks, vs, first, pairs):
     rows = q.shape[0]
     half = rows // 2
-    n = len(ks)
+    n = 1 + ks[1].shape[0] // half
     wide = n * half
     keys = wide + half
     total = wide + QB
@@ -605,8 +643,7 @@
                         pltpu.VMEM((2, total, QB), bf16),
                         pltpu.VMEM((keys, PAIR), f32), pltpu.VMEM((keys, PAIR), f32)],
         compiler_params=pltpu.CompilerParams(vmem_limit_bytes=60 << 20),
-        cost_estimate=pl.CostEstimate(flops=pieces * 24 * total * QB * HD * 4, bytes_accessed=16 << 20,
-                                      transcendentals=pieces * 2 * total * QB),
+        cost_estimate=pl.CostEstimate(flops=1 << 20, bytes_accessed=1 << 16, transcendentals=0),
         name="attention",
     )(kind, owners, cos_t, sin_t, q, do, *ks, *vs)
 
@@ -615,37 +652,77 @@
     return [(a, a ^ bit) for a in range(size)]
 
 
-def pick(a, axis, i):
-    return lax.dynamic_index_in_dim(a, i, axis, keepdims=False)
-
-
-def plus(a, b):
-    return (a.astype(f32) + b.astype(f32)).astype(bf16)
-
-
-def core_step(send, keep):
-    rows, cols = send.shape
-    size = rows // 8
-    got = lax.ppermute(send, "fsdp", pairs_of(1, 8)).reshape(2, 2, 2, size, cols)
-    keep = keep.reshape(2, 2, 2, size, cols)
-
-    def part(*at):
-        return plus(keep[at], got[at])
-
-    every = slice(None)
-    return part(every, 1, 0), part(every, 0, 0), part(1, every, 1), part(0, every, 1)
-
-
-def side_step(send_a, keep_a, send_b, keep_b):
-    got_a = lax.ppermute(send_a, "fsdp", pairs_of(2, 8))
-    got_b = lax.ppermute(send_b, "fsdp", pairs_of(4, 8))
-    return plus(keep_a[1], got_a[1]), plus(keep_a[0], got_a[0]), plus(keep_b[1], got_b[1]), plus(keep_b[0], got_b[0])
-
-
-def last_step(send_a, keep_a, send_b, keep_b):
-    got_a = lax.ppermute(send_a, "fsdp", pairs_of(4, 8))
-    got_b = lax.ppermute(send_b, "fsdp", pairs_of(2, 8))
-    return jnp.concatenate([plus(keep_a, got_a), plus(keep_b, got_b)], axis=0)
+def add_kernel(plan, *refs):
+    for a, b, moves in plan:
+        for source, to, target in moves:
+            refs[to][target] = (refs[a][source].astype(f32) + refs[b][source].astype(f32)).astype(bf16)
+
+
+def add_parts(arrays, plan, shapes, steps):
+    def spec(shape):
+        block = (*shape[:-1], shape[-1] // steps)
+        return pl.BlockSpec(block, lambda j: (0,) * (len(shape) - 1) + (j,))
+
+    return pl.pallas_call(
+        partial(add_kernel, plan),
+        grid=(steps,),
+        in_specs=[spec(a.shape) for a in arrays],
+        out_specs=[spec(shape) for shape in shapes],
+        out_shape=[jax.ShapeDtypeStruct(shape, bf16) for shape in shapes],
+        compiler_params=params(),
+        cost_estimate=pl.CostEstimate(flops=1 << 20, bytes_accessed=1 << 16, transcendentals=0),
+        name="add_parts",
+    )(*arrays)
+
+
+EVERY = slice(None)
+
+
+def swap(a, bit):
+    return lax.ppermute(a, "fsdp", pairs_of(bit, 8))
+
+
+def steps_for(arrays):
+    smallest = min(a.shape[-1] for a in arrays)
+    return 4 if smallest % (4 * PAIR) == 0 else 1
+
+
+def core_step(sends, keeps):
+    count = len(sends)
+    arrays, plan, shapes = [], [], []
+    for send, keep in zip(sends, keeps):
+        rows, cols = send.shape
+        cut = (2, 2, 2, rows // 8, cols)
+        to = 2 * count + len(shapes)
+        moves = [((EVERY, 1, 0), to, (EVERY,)), ((EVERY, 0, 0), to + 1, (EVERY,)),
+                 ((1, EVERY, 1), to + 2, (EVERY,)), ((0, EVERY, 1), to + 3, (EVERY,))]
+        plan.append((len(arrays), len(arrays) + 1, moves))
+        arrays += [keep.reshape(cut), swap(send, 1).reshape(cut)]
+        shapes += [(2, rows // 8, cols)] * 4
+    return add_parts(arrays, plan, shapes, steps_for(arrays))
+
+
+def side_step(items):
+    arrays, plan, shapes = [], [], []
+    for i in range(0, len(items), 4):
+        for send, keep, bit in ((items[i], items[i + 1], 2), (items[i + 2], items[i + 3], 4)):
+            to = len(items) + len(shapes)
+            plan.append((len(arrays), len(arrays) + 1, [((1,), to, (EVERY,)), ((0,), to + 1, (EVERY,))]))
+            arrays += [keep, swap(send, bit)]
+            shapes += [keep.shape[1:]] * 2
+    return add_parts(arrays, plan, shapes, steps_for(arrays))
+
+
+def last_step(items):
+    arrays, plan, shapes = [], [], []
+    for i in range(0, len(items), 4):
+        to = len(items) + len(shapes)
+        for at, (send, keep, bit) in enumerate(((items[i], items[i + 1], 4), (items[i + 2], items[i + 3], 2))):
+            plan.append((len(arrays), len(arrays) + 1, [((EVERY,), to, (at,))]))
+            arrays += [keep, swap(send, bit)]
+        shapes.append((2, *keep.shape))
+    parts = add_parts(arrays, plan, shapes, steps_for(arrays))
+    return [part.reshape(-1, part.shape[-1]) for part in parts]
 
 
 def along(part):
@@ -654,6 +731,10 @@
 
 def after(value, *others):
     return lax.optimization_barrier((value, *others))[0]
+
+
+def kept_after(items, *others):
+    return [after(a, *others) if i % 2 else a for i, a in enumerate(items)]
 
 
 def fast(inputs, cotangent, positions, segments, ln1_gain, ln1_bias, w_qkv, b_qkv, w_attn_out, b_out,
@@ -668,11 +749,16 @@
     relative = [4 * dy + 2 * dx + 1 - keep for keep in (0, 1) for dy in (0, 1) for dx in (0, 1)]
     order = jnp.bitwise_xor(me, jnp.array(relative, jnp.int32))
     owners = lax.rem(place + n - jnp.arange(n), n)
-    xs, spots = [x], [pos[::RB] // RB]
-    run = x[:half]
+    far = [None] * n
+    toward, away = x[:half], x[:half]
+    for s in range(1, n // 2 + 1):
+        toward = lax.ppermute(toward, "ctx", ring)
+        far[s] = toward
+        if n - s > n // 2:
+            away = lax.ppermute(away, "ctx", back)
+            far[n - s] = away
+    spots = [pos[::RB] // RB]
     for s in range(1, n):
-        run = lax.ppermute(run, "ctx", ring)
-        xs.append(run)
         spots.append(lax.ppermute(spots[0][:half // RB], "ctx", [(i, (i + s) % n) for i in range(n)]))
     mine = (ln1_gain, ln1_bias, b_qkv, b_out, ln2_gain, ln2_bias, b_in)
     small = lax.all_gather(jnp.concatenate(mine).reshape(1, -1), "fsdp", axis=0, tiled=True)
@@ -692,12 +778,11 @@
     angles_t = pos.astype(f32)[None, :] * inverse[:ROT // 2, None]
     cos_t, sin_t = jnp.cos(angles_t), jnp.sin(angles_t)
 
-    normed, queries, key, value = qkv(spots[0], order, after(x, xs[2], *spots[1:]), gain_attn, shift_attn, weights, bias_qkv, tables, True)
-    keys, values = [key], [value]
-    for s in range(1, n):
-        key, value = qkv(spots[s], order, xs[s], gain_attn, shift_attn, weights, bias_qkv, tables, False)
-        keys.append(key)
-        values.append(value)
+    normed, queries, own_keys, own_values = qkv(
+        spots[0], order, [after(x, far[1], far[n - 1], *spots[1:])], gain_attn, shift_attn, weights, bias_qkv, tables)
+    far_keys, far_values = qkv(
+        jnp.concatenate(spots[1:]), order, far[1:], gain_attn, shift_attn, weights, bias_qkv, tables)
+    keys, values = (own_keys, far_keys), (own_values, far_values)
     grad_att = spread(grad_out, weights)
     weight_in = lax.all_gather(after(w_in, queries), "fsdp", axis=0, tiled=True)
     weight_out = lax.all_gather(after(w_out, queries), "fsdp", axis=0, tiled=True)
@@ -721,34 +806,40 @@
     attend(0, 5, ())
     mlp_out, grad_mlp, in_send, in_keep, out_send, out_keep, db_in, db_out, dgain_mlp, dshift_mlp = mlp(
         order, after(x, *attended), grad_out, gain_mlp, shift_mlp, weight_in, bias_in, weight_out)
-    attend(5, 2, (mlp_out,))
-    steps_out = core_step(out_send, out_keep)
-    steps_in = core_step(in_send, in_keep)
-    attend(7, 1, (*attended, *steps_out, *steps_in))
-    output = join(x, attended, weights, mlp_out, bias_out)
-    steps_out = side_step(*steps_out)
-    steps_in = side_step(*steps_in)
+    attend(5, 1, (mlp_out,))
+    steps_mlp = core_step([out_send, in_send], [out_keep, in_keep])
+    attend(6, 2, (*attended, *steps_mlp))
+    steps_mlp = side_step(kept_after(steps_mlp, *attended))
+    output = join(after(x, *steps_mlp), attended, weights, mlp_out, bias_out)
     first_send, first_keep, grad_heads, db_q = first_tail(
         order, after(grad_out, output), normed, weights, attended, grad_q)
-    steps_first = core_step(first_send, first_keep)
-    grad_inputs, last_send, last_keep, db_kv, dgain_attn, dshift_attn = last_tail(
-        spots[0], after(x, *steps_out, *steps_in, *steps_first), normed, gain_attn, weights, tables, grad_mlp, grad_heads,
-        own_kv, come_kv)
-    sum_out = along(last_step(*steps_out))
-    sum_in = along(last_step(*steps_in))
-    steps_first = side_step(*steps_first)
-    sum_first = along(last_step(*steps_first))
-    steps_last = core_step(after(last_send, *steps_first), last_keep)
+    next_send, next_keep, db_next, grad_heads = kv_tail(
+        False, 0, spots[0], x, normed, gain_attn, weights, tables, grad_mlp, grad_heads, own_kv[:1], come_kv[:1])
+    part_out, part_in = last_step(kept_after(steps_mlp, grad_heads))
+    steps_first = core_step([first_send, next_send], [first_keep, next_keep])
+    last_send, last_keep, db_last, grad_inputs, dgain_attn, dshift_attn = kv_tail(
+        True, 5, spots[0], after(x, part_out, part_in, *steps_first), normed, gain_attn, weights, tables, grad_mlp, grad_heads,
+        own_kv[1:], come_kv[1:])
+    sum_out, sum_in = along(part_out), along(part_in)
+    steps_first = side_step(kept_after(steps_first, last_send))
+
+    def halves(a, i):
+        return a.reshape(a.shape[0], -1, 2, PAIR)[:, :, i].reshape(a.shape[0], -1)
+
+    db_kv = [halves(jnp.concatenate([db_next, db_last], axis=1), i) for i in range(2)]
     smalls = [a.reshape(width, -1) for a in
-              (dgain_attn, dshift_attn, jnp.concatenate([db_q, db_kv], axis=1), db_out, dgain_mlp, dshift_mlp, db_in)]
+              (dgain_attn, dshift_attn, jnp.concatenate([db_q, *db_kv], axis=1), db_out, dgain_mlp, dshift_mlp, db_in)]
     used = sum(a.shape[1] for a in smalls)
     packed = jnp.concatenate(smalls + [jnp.zeros((width, PAIR - used), f32)], axis=1).astype(bf16)
     packed = packed.reshape(8, width // 8, PAIR)[order].reshape(2, width // 2, PAIR)
-    part = last_step(*side_step(*core_step(packed[0], packed[1])))
-    joined = along(jnp.concatenate([last_step(*side_step(*steps_last)), part], axis=1))
-    packed = joined[:, 2 * width:].astype(f32)
-    sum_qkv = jnp.concatenate([sum_first[:, width:], joined[:, :2 * width]], axis=1)
-    sum_attn = sum_first[:, :width]
+    steps_last = core_step([after(last_send, *steps_first), packed[0]], [last_keep, packed[1]])
+    part_first = jnp.concatenate(last_step(steps_first), axis=1)
+    sum_first = along(part_first)
+    sum_last = along(jnp.concatenate(last_step(side_step(kept_after(steps_last, part_first))), axis=1))
+    packed = sum_last[:, -PAIR:].astype(f32)
+    sum_attn, sum_q = sum_first[:, :width], sum_first[:, width:2 * width]
+    rest = jnp.concatenate([sum_first[:, 2 * width:], sum_last[:, :-PAIR]], axis=1)
+    sum_qkv = jnp.concatenate([sum_q, halves(rest, 0), halves(rest, 1)], axis=1)
     done, at = [], 0
     for a in smalls:
         done.append(packed[:, at:at + a.shape[1]].reshape(-1))

time: 574 us -> 578 us (level)
  other arithmetic: 72.2 us -> 23.3 us
  Pallas kernels: 323 us -> 363 us
  local copies, waits for them, and re-layouts: 17.3 us -> 27.1 us
    convert_element_type x34 -> x1, other arithmetic: 45.9 us -> 0.7 us  [fast(): packed = sum_last[:, -PAIR:].astype(f32)]
    pallas_call x5 -> x13, Pallas kernels: 62.5 us -> 103 us  [the longest x9 36.8 us: add_parts(): pl.pallas_call(partial(add_kernel, plan), grid=(steps,), in_specs=[spec(a...]
    ppermute x28 -> x33, waiting for transfers between devices: 64.4 us -> 55.9 us  [the longest x2 38 us: fast(): toward = lax.ppermute(toward, 'ctx', ring)]
    unnamed x66 -> x118, local copies, waits for them, and re-layouts: 3.68 us -> 11.3 us
    reduce_scatter x4, waiting for transfers between devices: 29.7 us -> 35.8 us  [along(): return lax.psum_scatter(part, 'ctx', scatter_dimension=0, tiled=True)]
    ppermute x28 -> x33, starting transfers between devices: 27.4 us -> 30.8 us  [the longest x30 26.1 us: swap(): return lax.ppermute(a, 'fsdp', pairs_of(bit, 8))]
  transfers between devices with their start and end apart: 41 -> 46, of which waited for: 21 -> 15; matrix products, arithmetic and copies ran while one was open for 14% -> 6% of each run, Pallas kernels for 54% -> 61%
where the time goes in v6:
time: 578 us; the launch traced here: 572 us
  Pallas kernels  363 us (63%)
  waiting for transfers between devices  96.5 us (17%)
  starting transfers between devices  37.5 us (6%)
  local copies, waits for them, and re-layouts  27.1 us (5%)
  other arithmetic  23.3 us (4%)
  between operations  15.5 us (3%)
  blocking collectives  9.17 us (2%)
    pallas_call x3, Pallas kernels, attention(): pl.pallas_call(partial(attention_kernel, half, n), grid=(pairs,), in_spec...  156 us
    pallas_call x1, Pallas kernels, mlp(): pl.pallas_call(mlp_kernel, grid_spec=pltpu.PrefetchScalarGridSpec(num_sca...  75.3 us
    ppermute x2, waiting for transfers between devices, fast(): toward = lax.ppermute(toward, 'ctx', ring)  38 us
    pallas_call x9, Pallas kernels, add_parts(): pl.pallas_call(partial(add_kernel, plan), grid=(steps,), in_specs=[spec(a...  36.8 us
    pallas_call x2, Pallas kernels, kv_tail(): pl.pallas_call(partial(kv_kernel, groups, final, first), grid_spec=pltpu....  36.7 us
    reduce_scatter x4, waiting for transfers between devices, along(): return lax.psum_scatter(part, 'ctx', scatter_dimension=0, tiled=True)  35.8 us
    pallas_call x2, Pallas kernels, qkv(): pl.pallas_call(partial(qkv_kernel, far), grid_spec=pltpu.PrefetchScalarGr...  29.2 us
    ppermute x30, starting transfers between devices, swap(): return lax.ppermute(a, 'fsdp', pairs_of(bit, 8))  26.1 us
  transfers between devices with their start and end apart: 46, of which 15 were waited for; matrix products, arithmetic and copies ran while one was open for 6% of the time, Pallas kernels for 61%

profile of v6, /device:TPU:0, one launch (start us, length us, event | category | flops | bytes accessed | tf_op | source)
XLA Modules:
  0.0 572.2 jit_solution(16565699958549625551)
XLA Ops:
  7.2 2.4 pad_maximum_fusion
  9.9 5.1 collective-permute-start.2
  16.1 2.9 collective-permute-start.4
  20.3 9.2 %all-gather.1 = bf16[8,1,1536]{2,1,0:T(2,128)(2,1)S(1)} all-gather(bf16[1,1,1536]{2,1,0:T(2,128)(2,1)S(1)} %reshape.337), channel_id=2, replica_groups=mesh['fsdp'=8,'ctx'=4] {'fsdp'}, dimensions={0}, use_global_device_ids=true | all-gather | bytes 27648 | tf_op jit(solution)/shard_map/all_gather | solution.py:764
  31.3 6.5 %fusion = (f32[2304,128]{1,0:T(8,128)}, f32[2304,128]{1,0:T(8,128)}, f32[2304,128]{1,0:T(8,128)}) fusion(f32[128]{0:T(128)S(1)} %fusion.6, f32[2304]{0:T(1024)S(1)} %iota_convert_fusion, pred[128]{0:T(512)(128)(4,1)S(1)} %get-tuple-element.282, pred[128]{0:T(512)(128)(4,1)S(1)} %broadcast_compare_fusion.1, pred[128]{0:T(512)(128)(4,1)S(1)} %get-tuple-element.283), kind=kLoop, calls=%fused_computation.3 | loop fusion | flops 1179648 | bytes 3549056 | tf_op jit(solution)/shard_map/jit(_where)/select_n | solution.py:777
  37.8 4.8 collective-permute-done.4.refs_2_
  42.6 21.8 %collective-permute-done.3.refs_0_ = bf16[512,1024]{1,0:T(8,128)(2,1)S(1)} collective-permute-done((bf16[512,1024]{1,0:T(8,128)(2,1)S(1)}, bf16[512,1024]{1,0:T(8,128)(2,1)S(1)}, u32[]{:S(2)}, u32[]{:S(2)}) %collective-permute-start.3) | collective-permute-done | bytes 1048608 | tf_op jit(solution)/shard_map/ppermute | solution.py:755
  64.4 3.4 all-gather.6.cloned.1.call-done.w_ref.wk_ref.wv_ref
  67.9 14.0 %qkv_own.1 = (bf16[1024,1024]{1,0:T(8,128)(2,1)}, bf16[1024,1024]{1,0:T(8,128)(2,1)}, bf16[1024,1024]{1,0:T(8,128)(2,1)}, bf16[1024,1024]{1,0:T(8,128)(2,1)}) custom-call(s32[4]{0:T(128)} %copy-done.51, s32[8]{0:T(128)} %get-tuple-element.281.order_ref, f32[1,1024]{1,0:T(1,128)} %bitcast.98, f32[1,1024]{1,0:T(1,128)} %bitcast.102, ...), custom_call_target="tpu_custom_call" | custom-call | flops 1048576 | bytes 65536 | tf_op jit(solution)/shard_map/qkv_own/pallas_call | solution.py:276
  87.5 6.4 %spread.1.do_ref = bf16[1024,1024]{1,0:T(8,128)(2,1)} custom-call(bf16[1024,1024]{1,0:T(8,128)(2,1)} %bitcast.69, bf16[1024,4096]{1,0:T(8,128)(2,1)} %all-gather.6.cloned.1.call-done.w_ref.wk_ref.wv_ref), custom_call_target="tpu_custom_call" | custom-call | flops 1048576 | bytes 65536 | tf_op jit(solution)/shard_map/spread/pallas_call | solution.py:486
  93.9 16.2 %collective-permute-done.5.refs_1_ = bf16[512,1024]{1,0:T(8,128)(2,1)S(1)} collective-permute-done((bf16[512,1024]{1,0:T(8,128)(2,1)S(1)}, bf16[512,1024]{1,0:T(8,128)(2,1)S(1)}, u32[]{:S(2)}, u32[]{:S(2)}) %collective-permute-start.5) | collective-permute-done | bytes 1048608 | tf_op jit(solution)/shard_map/ppermute | solution.py:755
  111.1 15.2 %kv_remote.1 = (bf16[1536,1024]{1,0:T(8,128)(2,1)}, bf16[1536,1024]{1,0:T(8,128)(2,1)}) custom-call(s32[6]{0:T(128)} %pad_add_fusion.1.spot_ref, s32[8]{0:T(128)} %get-tuple-element.281.order_ref, f32[1,1024]{1,0:T(1,128)} %bitcast.99, f32[1,1024]{1,0:T(1,128)} %bitcast.103, bf16[1024,4096]{1,0:T(8,128)(2,1)} %all-gather.6.cloned.1.call-done.w_ref.wk_ref.wv_ref, ...), custom_call_target="tpu_custom_call" | custom-call | flops 1048576 | bytes 65536 | tf_op jit(solution)/shard_map/kv_remote/pallas_call | solution.py:276
  126.3 95.3 %attention.3 = (bf16[1024,640]{1,0:T(8,128)(2,1)}, bf16[1024,640]{1,0:T(8,128)(2,1)}, bf16[2048,1280]{1,0:T(8,128)(2,1)}, bf16[512,1280]{1,0:T(8,128)(2,1)}) custom-call(f32[4,8]{1,0:T(4,128)} %add_select_fusion.kind_ref, s32[4]{0:T(128)} %compare_select_fusion.3.owner_ref, f32[8,1024]{1,0:T(8,128)} %get-tuple-element.277.cos_ref, ...), custom_call_target="tpu_custom_call" | custom-call | flops 1048576 | bytes 65536 | tf_op jit(solution)/shard_map/attention/pallas_call | solution.py:634
  222.3 75.3 %mlp.1 = (f32[1024,1024]{1,0:T(8,128)}, f32[1024,1024]{1,0:T(8,128)}, bf16[512,4096]{1,0:T(8,128)(2,1)}, bf16[512,4096]{1,0:T(8,128)(2,1)}, bf16[2048,1024]{1,0:...) custom-call(s32[8]{0:T(128)} %get-tuple-element.281.order_ref, ...), custom_call_target="tpu_custom_call" | custom-call | flops 1048576 | bytes 65536 | tf_op jit(solution)/shard_map/mlp/pallas_call | solution.py:202
  298.2 21.1 %attention.4 = (bf16[1024,128]{1,0:T(8,128)(2,1)}, bf16[1024,128]{1,0:T(8,128)(2,1)}, bf16[2048,256]{1,0:T(8,128)(2,1)}, bf16[512,256]{1,0:T(8,128)(2,1)}) custom-call(f32[4,8]{1,0:T(4,128)} %add_select_fusion.kind_ref, s32[4]{0:T(128)} %compare_select_fusion.3.owner_ref, f32[8,1024]{1,0:T(8,128)} %get-tuple-element.277.cos_ref, ...), custom_call_target="tpu_custom_call" | custom-call | flops 1048576 | bytes 65536 | tf_op jit(solution)/shard_map/attention/pallas_call | solution.py:634
  319.3 9.6 %add_parts.9 = (bf16[2,256,1024]{2,1,0:T(8,128)(2,1)}, bf16[2,256,1024]{2,1,0:T(8,128)(2,1)}, bf16[2,256,1024]{2,1,0:T(8,128)(2,1)}, bf16[2,256,1024]{2,1,0:T(8,...) custom-call(bf16[2,2,2,256,1024]{4,3,2,1,0:T(8,128)(2,1)} %bitcast.7, ...), custom_call_target="tpu_custom_call" | custom-call | flops 1048576 | bytes 65536 | tf_op jit(solution)/shard_map/add_parts/pallas_call | solution.py:666
  333.1 39.7 %attention.5 = (bf16[1024,256]{1,0:T(8,128)(2,1)}, bf16[1024,256]{1,0:T(8,128)(2,1)}, bf16[2048,512]{1,0:T(8,128)(2,1)}, bf16[512,512]{1,0:T(8,128)(2,1)}) custom-call(f32[4,8]{1,0:T(4,128)} %add_select_fusion.kind_ref, s32[4]{0:T(128)} %compare_select_fusion.3.owner_ref, f32[8,1024]{1,0:T(8,128)} %get-tuple-element.277.cos_ref, ...), custom_call_target="tpu_custom_call" | custom-call | flops 1048576 | bytes 65536 | tf_op jit(solution)/shard_map/attention/pallas_call | solution.py:634
  372.9 4.0 collective-permute-done.10.refs_5_
  378.3 6.2 %add_parts.10 = (bf16[256,1024]{1,0:T(8,128)(2,1)}, bf16[256,1024]{1,0:T(8,128)(2,1)}, bf16[256,1024]{1,0:T(8,128)(2,1)}, bf16[256,1024]{1,0:T(8,128)(2,1)}, bf1...) custom-call(bf16[2,256,1024]{2,1,0:T(8,128)(2,1)} %get-tuple-element.162., ...), custom_call_target="tpu_custom_call" | custom-call | flops 1048576 | bytes 65536 | tf_op jit(solution)/shard_map/add_parts/pallas_call | solution.py:666
  388.6 7.6 %join.1 = bf16[1024,1024]{1,0:T(8,128)(2,1)} custom-call(bf16[1024,1024]{1,0:T(8,128)(2,1)} %bitcast.66, bf16[1024,4096]{1,0:T(8,128)(2,1)} %all-gather.6.cloned.1.call-done.w_ref.wk_ref.wv_ref, f32[1024,1024]{1,0:T(8,128)} %get-tuple-element.150.mlp_ref, f32[1,1024]{1,0:T(1,128)} %bitcast.109, bf16[1024,640]{1,0:T(8,128)(2,1)} %get-tuple-element.141.refs_0_, ...), custom_call_target="tpu_custom_call" | custom-call | flops 12884901888 | bytes 1048576 | tf_op jit(solution)/shard_map/join/pallas_call | solution.py:465
  396.2 15.0 %first_tail.1 = (bf16[512,2048]{1,0:T(8,128)(2,1)}, bf16[512,2048]{1,0:T(8,128)(2,1)}, f32[1024,1024]{1,0:T(8,128)}, f32[1,1024]{1,0:T(1,128)}) custom-call(s32[8]{0:T(128)} %get-tuple-element.281.order_ref, bf16[1024,1024]{1,0:T(8,128)(2,1)} %bitcast.71, bf16[1024,1024]{1,0:T(8,128)(2,1)} %get-tuple-element.175.h_ref, ...), custom_call_target="tpu_custom_call" | custom-call | flops 12884901888 | bytes 1048576 | tf_op jit(solution)/shard_map/first_tail/pallas_call | solution.py:336
  411.2 18.7 %kv_first.1 = (bf16[512,1280]{1,0:T(8,128)(2,1)}, bf16[512,1280]{1,0:T(8,128)(2,1)}, f32[1,1280]{1,0:T(1,128)}, f32[1024,1024]{1,0:T(8,128)}) custom-call(s32[4]{0:T(128)} %copy-done.51, bf16[1024,1024]{1,0:T(8,128)(2,1)} %bitcast.67, bf16[1024,1024]{1,0:T(8,128)(2,1)} %get-tuple-element.175.h_ref, f32[1,1024]{1,0:T(1,128)} %bitcast.100, ...), custom_call_target="tpu_custom_call" | custom-call | flops 12884901888 | bytes 1048576 | tf_op jit(solution)/shard_map/kv_first/pallas_call | solution.py:431
  431.9 4.4 add_parts.11
  444.4 4.8 add_parts.12
  453.3 18.0 %kv_last.1 = (bf16[512,768]{1,0:T(8,128)(2,1)}, bf16[512,768]{1,0:T(8,128)(2,1)}, f32[1,768]{1,0:T(1,128)}, f32[1024,1024]{1,0:T(8,128)}, f32[1,1024]{1,0:T(1,128)}, /*index=5*/f32[1,1024]{1,0:T(1,128)}) custom-call(s32[4]{0:T(128)} %copy-done.51, bf16[1024,1024]{1,0:T(8,128)(2,1)} %bitcast.68, bf16[1024,1024]{1,0:T(8,128)(2,1)} %get-tuple-element.175.h_ref, ...), custom_call_target="tpu_custom_call" | custom-call | flops 12884901888 | bytes 1048576 | tf_op jit(solution)/shard_map/kv_last/pallas_call | solution.py:431
  473.2 3.2 add_parts.13
  482.1 3.6 concatenate.64
  488.4 2.4 add_parts.15
  491.8 2.4 add_parts.14
  500.2 2.3 collective-permute-done.28.refs_1_
  521.5 14.7 %reduce-scatter.14.cloned.1.call-done = bf16[32,896]{1,0:T(8,128)(2,1)} async-done(((bf16[128,896]{1,0:T(8,128)(2,1)}), bf16[32,896]{1,0:T(8,128)(2,1)}) %reduce-scatter.14.cloned.1.call-update) | async-done | bytes 57360 | tf_op jit(solution)/shard_map/reduce_scatter | solution.py:729
  539.8 21.0 %reduce-scatter.16.cloned.1.call-done = bf16[32,3328]{1,0:T(8,128)(2,1)} async-done(((bf16[128,3328]{1,0:T(8,128)(2,1)}), bf16[32,3328]{1,0:T(8,128)(2,1)}) %reduce-scatter.16.cloned.1.call-update) | async-done | bytes 213008 | tf_op jit(solution)/shard_map/reduce_scatter | solution.py:729
  (275 shorter events, 79.5 us)
Async XLA Ops:
  7.2 60.7 %all-gather.6.cloned.1.call-start = ((), (), s32[]{:S(2)}) async-start(), calls=%async_computation.7 | async-start | bytes 9437184 | tf_op jit(solution)/shard_map/all_gather | solution.py:770
  9.7 212.6 %all-gather.8.cloned.1.call-start = ((), (), s32[]{:S(2)}) async-start(), calls=%async_computation.8 | async-start | bytes 9437184 | tf_op jit(solution)/shard_map/all_gather | solution.py:787
  9.9 27.9 %collective-permute-start.2 = (s32[2]{0:T(128)S(1)}, s32[2]{0:T(128)S(1)}, u32[]{:S(2)}, u32[]{:S(2)}) collective-permute-start(s32[2]{0:T(128)S(1)} %bitcast.115), channel_id=1, source_target_pairs={{0,3},{1,0},{2,1},{3,2},{4,7},{5,4},{6,5},{7,6},{8,11},{9,8},{10,9... | collective-permute-start | bytes 32 | tf_op jit(solution)/shard_map/ppermute | solution.py:762
  15.0 22.8 %collective-permute-start.1 = (s32[2]{0:T(128)S(1)}, s32[2]{0:T(128)S(1)}, u32[]{:S(2)}, u32[]{:S(2)}) collective-permute-start(s32[2]{0:T(128)S(1)} %bitcast.116), channel_id=1, source_target_pairs={{0,2},{1,3},{2,0},{3,1},{4,6},{5,7},{6,4},{7,5},{8,10},{9,11},{10,... | collective-permute-start | bytes 32 | tf_op jit(solution)/shard_map/ppermute | solution.py:762
  15.0 22.8 %collective-permute-start = (s32[2]{0:T(128)S(1)}, s32[2]{0:T(128)S(1)}, u32[]{:S(2)}, u32[]{:S(2)}) collective-permute-start(s32[2]{0:T(128)S(1)} %bitcast.117), channel_id=1, source_target_pairs={{0,1},{1,2},{2,3},{3,0},{4,5},{5,6},{6,7},{7,4},{8,9},{9,10},{10,1... | collective-permute-start | bytes 32 | tf_op jit(solution)/shard_map/ppermute | solution.py:762
  16.1 26.5 %collective-permute-start.4 = (bf16[512,1024]{1,0:T(8,128)(2,1)S(1)}, bf16[512,1024]{1,0:T(8,128)(2,1)S(1)}, u32[]{:S(2)}, u32[]{:S(2)}) collective-permute-start(bf16[512,1024]{1,0:T(8,128)(2,1)S(1)} %slice_bitcast_fusion), channel_id=1, source_target_pairs={{0,3},{1,0},{2,1},{3,2},{4,7},{5,4},{6,5},{7,6},{8,11},{9,8},{10,9... | collective-permute-start | bytes 3145736 | tf_op jit(solution)/shard_map/ppermute | solution.py:758
  19.0 45.5 %collective-permute-start.3 = (bf16[512,1024]{1,0:T(8,128)(2,1)S(1)}, bf16[512,1024]{1,0:T(8,128)(2,1)S(1)}, u32[]{:S(2)}, u32[]{:S(2)}) collective-permute-start(bf16[512,1024]{1,0:T(8,128)(2,1)S(1)} %slice_bitcast_fusion), channel_id=1, source_target_pairs={{0,1},{1,2},{2,3},{3,0},{4,5},{5,6},{6,7},{7,4},{8,9},{9,10},{10,1... | collective-permute-start | bytes 3145736 | tf_op jit(solution)/shard_map/ppermute | solution.py:755
  81.9 140.4 %all-gather.10.cloned.1.call-start = ((), (), s32[]{:S(2)}) async-start(), calls=%async_computation.9 | async-start | bytes 9437184 | tf_op jit(solution)/shard_map/all_gather | solution.py:788
  82.6 328.6 %reduce-scatter.8.cloned.1.call-start = ((), (), s32[]{:S(2)}) async-start(), calls=%async_computation.10 | async-start | bytes 6553600 | tf_op jit(solution)/shard_map/reduce_scatter | solution.py:803
  82.7 27.4 %collective-permute-start.5 = (bf16[512,1024]{1,0:T(8,128)(2,1)S(1)}, bf16[512,1024]{1,0:T(8,128)(2,1)S(1)}, u32[]{:S(2)}, u32[]{:S(2)}) collective-permute-start(bf16[512,1024]{1,0:T(8,128)(2,1)S(1)} %collective-permute-done.3.refs_0_), channel_id=1, source_target_pairs={{0,1},{1,2},{2,3},{3,0},{4,5},{5,6},{6,7},{7,4},{8,9},{9,10},{10,1... | collective-permute-start | bytes 3145736 | tf_op jit(solution)/shard_map/ppermute | solution.py:755
  221.6 231.7 %reduce-scatter.10.cloned.1.call-start = ((), (), s32[]{:S(2)}) async-start(), calls=%async_computation.11 | async-start | bytes 1310720 | tf_op jit(solution)/shard_map/reduce_scatter | solution.py:803
  297.6 21.7 %collective-permute-start.6 = (bf16[2048,1024]{1,0:T(8,128)(2,1)}, bf16[2048,1024]{1,0:T(8,128)(2,1)}, u32[]{:S(2)}, u32[]{:S(2)}) collective-permute-start(bf16[2048,1024]{1,0:T(8,128)(2,1)} %get-tuple-element.146), channel_id=1, source_target_pairs={{0,4},{4,0},{8,12},{12,8},{16,20},{20,16},{24,28},{28,24},{1,5},{5... | collective-permute-start | bytes 12582920 | tf_op jit(solution)/shard_map/ppermute | solution.py:682
  297.7 21.7 %collective-permute-start.7 = (bf16[512,4096]{1,0:T(8,128)(2,1)}, bf16[512,4096]{1,0:T(8,128)(2,1)}, u32[]{:S(2)}, u32[]{:S(2)}) collective-permute-start(bf16[512,4096]{1,0:T(8,128)(2,1)} %get-tuple-element.148), channel_id=1, source_target_pairs={{0,4},{4,0},{8,12},{12,8},{16,20},{20,16},{24,28},{28,24},{1,5},{5... | collective-permute-start | bytes 12582920 | tf_op jit(solution)/shard_map/ppermute | solution.py:682
  319.3 134.0 %reduce-scatter.12.cloned.1.call-start = ((), (), s32[]{:S(2)}) async-start(), calls=%async_computation.12 | async-start | bytes 2621440 | tf_op jit(solution)/shard_map/reduce_scatter | solution.py:803
  329.0 43.9 %collective-permute-start.8 = (bf16[2,256,1024]{2,1,0:T(8,128)(2,1)}, bf16[2,256,1024]{2,1,0:T(8,128)(2,1)S(1)}, u32[]{:S(2)}, u32[]{:S(2)}) collective-permute-start(bf16[2,256,1024]{2,1,0:T(8,128)(2,1)} %get-tuple-element.153), channel_id=1, source_target_pairs={{0,8},{4,12},{8,0},{12,4},{16,24},{20,28},{24,16},{28,20},{1,9},{5... | collective-permute-start | bytes 3145736 | tf_op jit(solution)/shard_map/ppermute | solution.py:682
  330.6 42.3 %collective-permute-start.9 = (bf16[2,256,1024]{2,1,0:T(8,128)(2,1)}, bf16[2,256,1024]{2,1,0:T(8,128)(2,1)S(1)}, u32[]{:S(2)}, u32[]{:S(2)}) collective-permute-start(bf16[2,256,1024]{2,1,0:T(8,128)(2,1)} %get-tuple-element.154), channel_id=1, source_target_pairs={{0,16},{4,20},{8,24},{12,28},{16,0},{20,4},{24,8},{28,12},{1,17},{... | collective-permute-start | bytes 3145736 | tf_op jit(solution)/shard_map/ppermute | solution.py:682
  331.2 45.8 %collective-permute-start.10 = (bf16[2,64,4096]{2,1,0:T(8,128)(2,1)}, bf16[2,64,4096]{2,1,0:T(8,128)(2,1)S(1)}, u32[]{:S(2)}, u32[]{:S(2)}) collective-permute-start(bf16[2,64,4096]{2,1,0:T(8,128)(2,1)} %get-tuple-element.156), channel_id=1, source_target_pairs={{0,8},{4,12},{8,0},{12,4},{16,24},{20,28},{24,16},{28,20},{1,9},{5... | collective-permute-start | bytes 3145736 | tf_op jit(solution)/shard_map/ppermute | solution.py:682
  332.3 45.9 %collective-permute-start.11 = (bf16[2,64,4096]{2,1,0:T(8,128)(2,1)}, bf16[2,64,4096]{2,1,0:T(8,128)(2,1)}, u32[]{:S(2)}, u32[]{:S(2)}) collective-permute-start(bf16[2,64,4096]{2,1,0:T(8,128)(2,1)} %get-tuple-element.158), channel_id=1, source_target_pairs={{0,16},{4,20},{8,24},{12,28},{16,0},{20,4},{24,8},{28,12},{1,17},{... | collective-permute-start | bytes 3145736 | tf_op jit(solution)/shard_map/ppermute | solution.py:682
  372.8 145.1 %reduce-scatter.20.cloned.1.call-start = ((), (), s32[]{:S(2)}) async-start(), calls=%async_computation.16 | async-start | bytes 1310720 | tf_op jit(solution)/shard_map/reduce_scatter | solution.py:729
  384.5 45.5 %collective-permute-start.12 = (bf16[256,1024]{1,0:T(8,128)(2,1)}, bf16[256,1024]{1,0:T(8,128)(2,1)S(1)}, u32[]{:S(2)}, u32[]{:S(2)}) collective-permute-start(bf16[256,1024]{1,0:T(8,128)(2,1)} %get-tuple-element.166), channel_id=1, source_target_pairs={{0,16},{4,20},{8,24},{12,28},{16,0},{20,4},{24,8},{28,12},{1,17},{... | collective-permute-start | bytes 1572872 | tf_op jit(solution)/shard_map/ppermute | solution.py:682
  385.7 44.2 %collective-permute-start.13 = (bf16[256,1024]{1,0:T(8,128)(2,1)}, bf16[256,1024]{1,0:T(8,128)(2,1)S(1)}, u32[]{:S(2)}, u32[]{:S(2)}) collective-permute-start(bf16[256,1024]{1,0:T(8,128)(2,1)} %get-tuple-element.168), channel_id=1, source_target_pairs={{0,8},{4,12},{8,0},{12,4},{16,24},{20,28},{24,16},{28,20},{1,9},{5... | collective-permute-start | bytes 1572872 | tf_op jit(solution)/shard_map/ppermute | solution.py:682
  386.4 43.6 %collective-permute-start.14 = (bf16[64,4096]{1,0:T(8,128)(2,1)}, bf16[64,4096]{1,0:T(8,128)(2,1)S(1)}, u32[]{:S(2)}, u32[]{:S(2)}) collective-permute-start(bf16[64,4096]{1,0:T(8,128)(2,1)} %get-tuple-element.170), channel_id=1, source_target_pairs={{0,16},{4,20},{8,24},{12,28},{16,0},{20,4},{24,8},{28,12},{1,17},{... | collective-permute-start | bytes 1572872 | tf_op jit(solution)/shard_map/ppermute | solution.py:682
  388.0 42.1 %collective-permute-start.15 = (bf16[64,4096]{1,0:T(8,128)(2,1)}, bf16[64,4096]{1,0:T(8,128)(2,1)S(1)}, u32[]{:S(2)}, u32[]{:S(2)}) collective-permute-start(bf16[64,4096]{1,0:T(8,128)(2,1)} %get-tuple-element.172), channel_id=1, source_target_pairs={{0,8},{4,12},{8,0},{12,4},{16,24},{20,28},{24,16},{28,20},{1,9},{5... | collective-permute-start | bytes 1572872 | tf_op jit(solution)/shard_map/ppermute | solution.py:682
  436.3 83.4 %reduce-scatter.18.cloned.1.call-start = ((), (), s32[]{:S(2)}) async-start(), calls=%async_computation.15 | async-start | bytes 1310720 | tf_op jit(solution)/shard_map/reduce_scatter | solution.py:729
  441.9 94.3 %reduce-scatter.14.cloned.1.call-start = ((), (), s32[]{:S(2)}) async-start(), calls=%async_computation.13 | async-start | bytes 286720 | tf_op jit(solution)/shard_map/reduce_scatter | solution.py:729
  449.3 22.1 %collective-permute-start.20 = (bf16[2,64,1280]{2,1,0:T(8,128)(2,1)}, bf16[2,64,1280]{2,1,0:T(8,128)(2,1)S(1)}, u32[]{:S(2)}, u32[]{:S(2)}) collective-permute-start(bf16[2,64,1280]{2,1,0:T(8,128)(2,1)} %get-tuple-element.199), channel_id=1, source_target_pairs={{0,8},{4,12},{8,0},{12,4},{16,24},{20,28},{24,16},{28,20},{1,9},{5... | collective-permute-start | bytes 983048 | tf_op jit(solution)/shard_map/ppermute | solution.py:682
  450.7 20.7 %collective-permute-start.21 = (bf16[2,64,1280]{2,1,0:T(8,128)(2,1)}, bf16[2,64,1280]{2,1,0:T(8,128)(2,1)S(1)}, u32[]{:S(2)}, u32[]{:S(2)}) collective-permute-start(bf16[2,64,1280]{2,1,0:T(8,128)(2,1)} %get-tuple-element.201), channel_id=1, source_target_pairs={{0,16},{4,20},{8,24},{12,28},{16,0},{20,4},{24,8},{28,12},{1,17},{... | collective-permute-start | bytes 983048 | tf_op jit(solution)/shard_map/ppermute | solution.py:682
  451.1 20.3 %collective-permute-start.18 = (bf16[2,64,2048]{2,1,0:T(8,128)(2,1)}, bf16[2,64,2048]{2,1,0:T(8,128)(2,1)S(1)}, u32[]{:S(2)}, u32[]{:S(2)}) collective-permute-start(bf16[2,64,2048]{2,1,0:T(8,128)(2,1)} %get-tuple-element.195), channel_id=1, source_target_pairs={{0,8},{4,12},{8,0},{12,4},{16,24},{20,28},{24,16},{28,20},{1,9},{5... | collective-permute-start | bytes 1572872 | tf_op jit(solution)/shard_map/ppermute | solution.py:682
  452.5 19.1 %collective-permute-start.19 = (bf16[2,64,2048]{2,1,0:T(8,128)(2,1)}, bf16[2,64,2048]{2,1,0:T(8,128)(2,1)S(1)}, u32[]{:S(2)}, u32[]{:S(2)}) collective-permute-start(bf16[2,64,2048]{2,1,0:T(8,128)(2,1)} %get-tuple-element.197), channel_id=1, source_target_pairs={{0,16},{4,20},{8,24},{12,28},{16,0},{20,4},{24,8},{28,12},{1,17},{... | collective-permute-start | bytes 1572872 | tf_op jit(solution)/shard_map/ppermute | solution.py:682
  476.4 10.5 %collective-permute-start.26 = (bf16[64,1280]{1,0:T(8,128)(2,1)}, bf16[64,1280]{1,0:T(8,128)(2,1)}, u32[]{:S(2)}, u32[]{:S(2)}) collective-permute-start(bf16[64,1280]{1,0:T(8,128)(2,1)} %get-tuple-element.219), channel_id=1, source_target_pairs={{0,16},{4,20},{8,24},{12,28},{16,0},{20,4},{24,8},{28,12},{1,17},{... | collective-permute-start | bytes 491528 | tf_op jit(solution)/shard_map/ppermute | solution.py:682
  480.5 10.4 %collective-permute-start.22 = (bf16[512,768]{1,0:T(8,128)(2,1)}, bf16[512,768]{1,0:T(8,128)(2,1)S(1)}, u32[]{:S(2)}, u32[]{:S(2)}) collective-permute-start(bf16[512,768]{1,0:T(8,128)(2,1)} %get-tuple-element.223), channel_id=1, source_target_pairs={{0,4},{4,0},{8,12},{12,8},{16,20},{20,16},{24,28},{28,24},{1,5},{5... | collective-permute-start | bytes 2359304 | tf_op jit(solution)/shard_map/ppermute | solution.py:682
  517.3 43.6 %reduce-scatter.16.cloned.1.call-start = ((), (), s32[]{:S(2)}) async-start(), calls=%async_computation.14 | async-start | bytes 1064960 | tf_op jit(solution)/shard_map/reduce_scatter | solution.py:729
  (67 other events, 445.1 us)
Sparse Core Ops, SparseCore 0:
  10.5 57.3 all-gather.5
  82.0 54.3 all-gather.7
  138.4 54.3 all-gather.9
  221.7 93.2 reduce-scatter.7
  319.4 26.6 reduce-scatter.9
  372.9 43.4 reduce-scatter.11
  436.4 26.2 reduce-scatter.19
  465.2 25.8 reduce-scatter.17
  517.4 18.7 reduce-scatter.13
  538.4 22.3 reduce-scatter.15

commit v7 on v6

--- a/solution.py
+++ b/solution.py
@@ -291,161 +291,174 @@
     )(spots, order, gain.reshape(1, -1), shift.reshape(1, -1), weight, bias.reshape(1, -1), *tables, *xs)
 
 
-def first_kernel(groups, order_ref, c_ref, h_ref, w_ref, *refs):
+def gather_rows(step, spot, tables, own_refs, come_refs, p_ref, k_at, v_at):
+    half = pl.num_programs(0) // 2
+    columns = [(g, at) for g in range(len(own_refs)) for at in range(0, own_refs[g].shape[1], 2 * PAIR)]
+
+    def put(refs):
+        for to, (g, at) in enumerate(columns):
+            turned = turn_lanes(refs[g][:, at:at + PAIR].astype(f32), *tables, -1.0).astype(bf16)
+            p_ref[spot, k_at + to * PAIR:k_at + (to + 1) * PAIR] = turned
+            p_ref[spot, v_at + to * PAIR:v_at + (to + 1) * PAIR] = refs[g][:, at + PAIR:at + 2 * PAIR]
+
+    @pl.when(step < half)
+    def _():
+        put(come_refs)
+
+    @pl.when(step >= half)
+    def _():
+        put(own_refs)
+
+
+def half_windows(arrays, count):
+    half = count // 2
+    come = [pl.BlockSpec((RB, a.shape[1]), lambda j, *o: (jnp.clip(j, 0, half - 1), 0)) for a in arrays]
+    own = [pl.BlockSpec((RB, a.shape[1]), lambda j, *o: (jnp.clip(j - half, 0, half - 1), 0)) for a in arrays]
+    return own, come
+
+
+def first_kernel(groups, spot_ref, order_ref, c_ref, h_ref, wq_ref, wk_ref, wv_ref, cos_ref, low_ref, high_ref, own_ref,
+                 come_ref, *refs):
     att_refs, dq_refs = refs[:groups], refs[groups:2 * groups]
-    send_ref, keep_ref, gh_ref, db_ref, p_ref, turned_ref = refs[2 * groups:]
+    send_ref, keep_ref, gh_ref, db_ref, p_ref, att_ref, turned_ref = refs[2 * groups:]
     step = pl.program_id(0)
-    blocks = [slice(r, r + RB) for r in range(0, c_ref.shape[0], RB)]
-
-    def lay(some):
-        at = 0
-        for ref in some:
-            p_ref[:, at:at + ref.shape[1]] = ref[...]
-            at += ref.shape[1]
-
-    def give(dw):
-        send_ref[...] = dw[:send_ref.shape[0]]
-        keep_ref[...] = dw[send_ref.shape[0]:]
+    width = c_ref.shape[1]
+    spot = pl.ds(pl.multiple_of(step * RB, RB), RB)
+    at = 0
+    for g in range(groups):
+        size = att_refs[g].shape[1]
+        att_ref[:, at:at + size] = att_refs[g][...]
+        p_ref[spot, at:at + size] = dq_refs[g][...]
+        at += size
+    for i in range(order_ref.shape[0]):
+        size = width // order_ref.shape[0]
+        lanes = pl.ds(pl.multiple_of(order_ref[i] * size, size), size)
+        turned_ref[spot, i * size:(i + 1) * size] = att_ref[:, lanes]
+    count = wk_ref.shape[1]
+    gather_rows(step, spot, (cos_ref[...], low_ref[...], high_ref[...]), [own_ref], [come_ref], p_ref, width, width + count)
+    gh_ref[...] = (mm(p_ref[spot, :width], wq_ref[...], NT) + mm(p_ref[spot, width:width + count], wk_ref[...], NT)
+                   + mm(p_ref[spot, width + count:], wv_ref[...], NT))
+    db = col_sum(p_ref[spot, :].astype(f32))
 
     @pl.when(step == 0)
     def _():
-        lay(att_refs)
-        reorder(order_ref, p_ref, turned_ref)
-        give(mm(turned_ref[...], c_ref[...], TN).astype(bf16))
-
-    @pl.when(step == 1)
+        db_ref[...] = db
+
+    @pl.when(step > 0)
     def _():
-        lay(dq_refs)
-        db = jnp.zeros(db_ref.shape, f32)
-        for r in blocks:
-            gh_ref[r, :] = mm(p_ref[r, :], w_ref[...], NT)
-            db += col_sum(p_ref[r, :].astype(f32))
-        db_ref[...] = db
-        give(mm(h_ref[...], p_ref[...], TN).astype(bf16))
-
-
-def first_tail(order, c, h, weights, attended, dqs):
+        db_ref[...] += db
+
+    @pl.when(step == pl.num_programs(0) - 1)
+    def _():
+        half = send_ref.shape[0]
+        for to in range(0, send_ref.shape[1], 512):
+            if to < width:
+                dw = mm(turned_ref[...], c_ref[:, to:to + 512], TN)
+            else:
+                dw = mm(h_ref[...], p_ref[:, to - width:to - width + 512], TN)
+            dw = dw.astype(bf16)
+            send_ref[:, to:to + 512] = dw[:half]
+            keep_ref[:, to:to + 512] = dw[half:]
+
+
+def first_tail(spots, order, c, h, weights, tables, attended, dqs, own, come):
     rows, width = c.shape
+    cols = own.shape[1] // 2
+    steps = rows // RB
+    total = 2 * width + 2 * cols
     s = jax.ShapeDtypeStruct
 
-    def full(a):
-        return pl.BlockSpec(a.shape, lambda j, o: (0, 0))
-
-    down = pl.BlockSpec((width // 2, width), lambda j, o: (0, j))
-    arrays = [*attended, *dqs]
+    def full(shape):
+        return pl.BlockSpec(shape, lambda j, spot, o: (0, 0), pipeline_mode=pl.Buffered(1))
+
+    def weight(size, at):
+        return pl.BlockSpec((width, size), lambda j, spot, o: (0, at // size), pipeline_mode=pl.Buffered(1))
+
+    def window(a):
+        return pl.BlockSpec((RB, a.shape[1]), lambda j, spot, o: (j, 0))
+
+    table = pl.BlockSpec((RB, PAIR), lambda j, spot, o: (spot[j], 0))
+    owns, comes = half_windows([own], steps)
     return pl.pallas_call(
         partial(first_kernel, len(dqs)),
         grid_spec=pltpu.PrefetchScalarGridSpec(
-            num_scalar_prefetch=1,
-            grid=(2,),
-            in_specs=[full(c), full(h), pl.BlockSpec((width, width), lambda j, o: (0, 0))] + [full(a) for a in arrays],
-            out_specs=[down, down, full(c), pl.BlockSpec((1, width), lambda j, o: (0, 0))],
-            scratch_shapes=[vmem(rows, width, dtype=bf16), vmem(rows, width, dtype=bf16)],
+            num_scalar_prefetch=2,
+            grid=(steps,),
+            in_specs=[full(c.shape), full(h.shape), weight(width, 0), weight(cols, width), weight(cols, 2 * width)] + [table] * 3
+            + owns + comes + [window(a) for a in (*attended, *dqs)],
+            out_specs=[full((width // 2, total)), full((width // 2, total)), window(c), full((1, total - width))],
+            scratch_shapes=[vmem(rows, total - width, dtype=bf16), vmem(RB, width, dtype=bf16), vmem(rows, width, dtype=bf16)],
         ),
-        out_shape=[s((width // 2, 2 * width), bf16), s((width // 2, 2 * width), bf16), s((rows, width), f32), s((1, width), f32)],
+        out_shape=[s((width // 2, total), bf16), s((width // 2, total), bf16), s((rows, width), f32), s((1, total - width), f32)],
         compiler_params=params(),
-        cost_estimate=pl.CostEstimate(flops=12884901888, bytes_accessed=1048576, transcendentals=0),
+        cost_estimate=pl.CostEstimate(flops=24 << 30, bytes_accessed=1 << 20, transcendentals=0),
         name="first_tail",
-    )(order, c, h, weights, *arrays)
-
-
-def kv_kernel(groups, final, first, spot_ref, x_ref, h_ref, gain_ref, wk_ref, wv_ref, cos_ref, low_ref, high_ref, gin_ref,
-              gh_ref, *refs):
-    count = len(groups)
-    own_refs, come_refs = refs[:count], refs[count:2 * count]
-    send_ref, keep_ref, db_ref, grad_ref = refs[2 * count:2 * count + 4]
-    p_ref, w_ref, acc_ref = refs[-3:]
+    )(spots, order, c, h, weights, weights, weights, *tables, own, come, *attended, *dqs)
+
+
+def last_kernel(groups, spot_ref, h_ref, gain_ref, wk_ref, wv_ref, x_ref, cos_ref, low_ref, high_ref, gin_ref, ghin_ref, *refs):
+    own_refs, come_refs = refs[:groups], refs[groups:2 * groups]
+    grad_ref, send_ref, keep_ref, db_ref, dgain_ref, dshift_ref, p_ref = refs[2 * groups:]
     step = pl.program_id(0)
-    rows = x_ref.shape[0]
-    half = rows // 2
-    blocks = [slice(r, r + RB) for r in range(0, rows, RB)]
-
-    def put(own_ref, come_ref):
-        for r in blocks:
-            spot = pl.ds(pl.multiple_of(spot_ref[r.start // RB] * RB, RB), RB)
-            t = come_ref[r, :] if r.start < half else own_ref[r.start - half:r.stop - half, :]
-            p_ref[r, :PAIR] = turn_lanes(t[:, :PAIR].astype(f32), cos_ref[spot, :], low_ref[spot, :], high_ref[spot, :],
-                                         -1.0).astype(bf16)
-            p_ref[r, PAIR:] = t[:, PAIR:]
-
-    at = 0
-    for g, size in enumerate(groups):
-        @pl.when((step >= at) & (step < at + size))
-        def _(g=g):
-            put(own_refs[g], come_refs[g])
-        at += size
-    w_ref[:, :PAIR] = wk_ref[...]
-    w_ref[:, PAIR:] = wv_ref[...]
+    spot = pl.ds(pl.multiple_of(step * RB, RB), RB)
+    count = wk_ref.shape[1]
+    gather_rows(step, spot, (cos_ref[...], low_ref[...], high_ref[...]), own_refs, come_refs, p_ref, 0, count)
+    grad = (ghin_ref[...] + mm(p_ref[spot, :count], wk_ref[...], NT) + mm(p_ref[spot, count:], wv_ref[...], NT))
+    back, scaled = norm_back(x_ref[...].astype(f32), grad, gain_ref[...])
+    grad_ref[...] = back + gin_ref[...]
+    sums = col_sum(p_ref[spot, :].astype(f32)), col_sum(scaled), col_sum(grad)
 
     @pl.when(step == 0)
     def _():
-        acc_ref[...] = gh_ref[...]
-
-    db = jnp.zeros(db_ref.shape, f32)
-    for r in blocks:
-        acc_ref[r, :] += mm(p_ref[r, :], w_ref[...], NT)
-        db += col_sum(p_ref[r, :].astype(f32))
-    db_ref[...] = db
-    dw = mm(h_ref[...], p_ref[...], TN).astype(bf16)
-    send_ref[...] = dw[:send_ref.shape[0]]
-    keep_ref[...] = dw[send_ref.shape[0]:]
+        for ref, value in zip((db_ref, dgain_ref, dshift_ref), sums):
+            ref[...] = value
+
+    @pl.when(step > 0)
+    def _():
+        for ref, value in zip((db_ref, dgain_ref, dshift_ref), sums):
+            ref[...] += value
 
     @pl.when(step == pl.num_programs(0) - 1)
     def _():
-        if not final:
-            grad_ref[...] = acc_ref[...]
-            return
-        dgain_ref, dshift_ref = refs[2 * count + 4:2 * count + 6]
-        dgain = jnp.zeros(dgain_ref.shape, f32)
-        dshift = jnp.zeros(dshift_ref.shape, f32)
-        for r in blocks:
-            grad = acc_ref[r, :]
-            back, scaled = norm_back(x_ref[r, :].astype(f32), grad, gain_ref[...])
-            grad_ref[r, :] = back + gin_ref[r, :]
-            dgain += col_sum(scaled)
-            dshift += col_sum(grad)
-        dgain_ref[...] = dgain
-        dshift_ref[...] = dshift
-
-
-def kv_tail(final, first, spots, x, h, gain, weights, tables, gin, gh, owns, comes):
+        half = send_ref.shape[0]
+        for to in range(0, send_ref.shape[1], 512):
+            dw = mm(h_ref[...], p_ref[:, to:to + 512], TN).astype(bf16)
+            send_ref[:, to:to + 512] = dw[:half]
+            keep_ref[:, to:to + 512] = dw[half:]
+
+
+def last_tail(spots, x, h, gain, weights, tables, gin, gh, owns, comes):
     rows, width = x.shape
-    groups = [a.shape[1] // (2 * PAIR) for a in owns]
-    pairs = sum(groups)
+    cols = sum(a.shape[1] for a in owns) // 2
+    steps = rows // RB
     s = jax.ShapeDtypeStruct
 
-    def full(a):
-        return pl.BlockSpec(a.shape, lambda j, spot: (0, 0), pipeline_mode=pl.Buffered(1))
-
-    def windows(arrays):
-        specs, at = [], 0
-        for a, size in zip(arrays, groups):
-            specs.append(pl.BlockSpec((a.shape[0], 2 * PAIR), lambda j, spot, at=at, size=size: (0, jnp.clip(j - at, 0, size - 1))))
-            at += size
-        return specs
-
-    line = pl.BlockSpec((1, width), lambda j, spot: (0, 0))
-    down = pl.BlockSpec((width // 2, 2 * PAIR), lambda j, spot: (0, j))
-    column = width // PAIR
-    more = [line, line] if final else []
+    def full(shape):
+        return pl.BlockSpec(shape, lambda j, spot: (0, 0), pipeline_mode=pl.Buffered(1))
+
+    def weight(at):
+        return pl.BlockSpec((width, cols), lambda j, spot: (0, at // cols), pipeline_mode=pl.Buffered(1))
+
+    block = pl.BlockSpec((RB, width), lambda j, spot: (j, 0))
+    table = pl.BlockSpec((RB, PAIR), lambda j, spot: (spot[j], 0))
+    own_windows, come_windows = half_windows(owns, steps)
     return pl.pallas_call(
-        partial(kv_kernel, groups, final, first),
+        partial(last_kernel, len(owns)),
         grid_spec=pltpu.PrefetchScalarGridSpec(
             num_scalar_prefetch=1,
-            grid=(pairs,),
-            in_specs=[full(x), full(h), line, pl.BlockSpec((width, PAIR), lambda j, spot: (0, column + first + j)),
-                      pl.BlockSpec((width, PAIR), lambda j, spot: (0, 2 * column + first + j))]
-            + [full(a) for a in (*tables, gin, gh)] + windows(owns) + windows(comes),
-            out_specs=[down, down, pl.BlockSpec((1, 2 * PAIR), lambda j, spot: (0, j)),
-                       pl.BlockSpec((rows, width), lambda j, spot: (0, 0))] + more,
-            scratch_shapes=[vmem(rows, 2 * PAIR, dtype=bf16), vmem(width, 2 * PAIR, dtype=bf16), vmem(rows, width)],
+            grid=(steps,),
+            in_specs=[full(h.shape), full((1, width)), weight(2 * width - cols), weight(3 * width - cols), block] + [table] * 3
+            + [block, block] + own_windows + come_windows,
+            out_specs=[block, full((width // 2, 2 * cols)), full((width // 2, 2 * cols)), full((1, 2 * cols)), full((1, width)),
+                       full((1, width))],
+            scratch_shapes=[vmem(rows, 2 * cols, dtype=bf16)],
         ),
-        out_shape=[s((width // 2, 2 * PAIR * pairs), bf16), s((width // 2, 2 * PAIR * pairs), bf16),
-                   s((1, 2 * PAIR * pairs), f32), s((rows, width), f32)] + [s((1, width), f32)] * len(more),
+        out_shape=[s((rows, width), f32), s((width // 2, 2 * cols), bf16), s((width // 2, 2 * cols), bf16), s((1, 2 * cols), f32),
+                   s((1, width), f32), s((1, width), f32)],
         compiler_params=params(),
-        cost_estimate=pl.CostEstimate(flops=12884901888, bytes_accessed=1 << 20, transcendentals=0),
-        name="kv_last" if final else "kv_first",
-    )(spots, x, h, gain.reshape(1, -1), weights, weights, *tables, gin, gh, *owns, *comes)
+        cost_estimate=pl.CostEstimate(flops=12 << 30, bytes_accessed=1 << 20, transcendentals=0),
+        name="last_tail",
+    )(spots, h, gain.reshape(1, -1), weights, weights, x, *tables, gin, gh, *owns, *comes)
 
 
 def join_kernel(groups, x_ref, w_ref, mlp_ref, b_ref, *refs):
@@ -471,7 +484,7 @@
         out_shape=s((rows, width), bf16),
         scratch_shapes=[vmem(RB, width, dtype=bf16)],
         compiler_params=params(),
-        cost_estimate=pl.CostEstimate(flops=12884901888, bytes_accessed=1048576, transcendentals=0),
+        cost_estimate=pl.CostEstimate(flops=12 << 30, bytes_accessed=1 << 20, transcendentals=0),
         name="join",
     )(x, weights, mlp_out, bias.reshape(1, -1), *attended)
 
@@ -658,7 +671,7 @@
             refs[to][target] = (refs[a][source].astype(f32) + refs[b][source].astype(f32)).astype(bf16)
 
 
-def add_parts(arrays, plan, shapes, steps):
+def add_parts(arrays, plan, shapes, steps, load=0):
     def spec(shape):
         block = (*shape[:-1], shape[-1] // steps)
         return pl.BlockSpec(block, lambda j: (0,) * (len(shape) - 1) + (j,))
@@ -670,7 +683,7 @@
         out_specs=[spec(shape) for shape in shapes],
         out_shape=[jax.ShapeDtypeStruct(shape, bf16) for shape in shapes],
         compiler_params=params(),
-        cost_estimate=pl.CostEstimate(flops=1 << 20, bytes_accessed=1 << 16, transcendentals=0),
+        cost_estimate=pl.CostEstimate(flops=(load << 30) + 1, bytes_accessed=1 << 16, transcendentals=0),
         name="add_parts",
     )(*arrays)
 
@@ -713,7 +726,7 @@
     return add_parts(arrays, plan, shapes, steps_for(arrays))
 
 
-def last_step(items):
+def last_step(items, load=0):
     arrays, plan, shapes = [], [], []
     for i in range(0, len(items), 4):
         to = len(items) + len(shapes)
@@ -721,7 +734,7 @@
             plan.append((len(arrays), len(arrays) + 1, [((EVERY,), to, (at,))]))
             arrays += [keep, swap(send, bit)]
         shapes.append((2, *keep.shape))
-    parts = add_parts(arrays, plan, shapes, steps_for(arrays))
+    parts = add_parts(arrays, plan, shapes, steps_for(arrays), load)
     return [part.reshape(-1, part.shape[-1]) for part in parts]
 
 
@@ -783,7 +796,7 @@
     far_keys, far_values = qkv(
         jnp.concatenate(spots[1:]), order, far[1:], gain_attn, shift_attn, weights, bias_qkv, tables)
     keys, values = (own_keys, far_keys), (own_values, far_values)
-    grad_att = spread(grad_out, weights)
+    grad_att = spread(after(grad_out, far[n // 2]), weights)
     weight_in = lax.all_gather(after(w_in, queries), "fsdp", axis=0, tiled=True)
     weight_out = lax.all_gather(after(w_out, queries), "fsdp", axis=0, tiled=True)
 
@@ -803,43 +816,41 @@
         come_kv.append(lax.psum_scatter(out[2], "ctx", scatter_dimension=0, tiled=True))
         own_kv.append(out[3])
 
-    attend(0, 5, ())
+    attend(0, 4, ())
     mlp_out, grad_mlp, in_send, in_keep, out_send, out_keep, db_in, db_out, dgain_mlp, dshift_mlp = mlp(
         order, after(x, *attended), grad_out, gain_mlp, shift_mlp, weight_in, bias_in, weight_out)
-    attend(5, 1, (mlp_out,))
+    attend(4, 2, (mlp_out,))
     steps_mlp = core_step([out_send, in_send], [out_keep, in_keep])
     attend(6, 2, (*attended, *steps_mlp))
     steps_mlp = side_step(kept_after(steps_mlp, *attended))
     output = join(after(x, *steps_mlp), attended, weights, mlp_out, bias_out)
-    first_send, first_keep, grad_heads, db_q = first_tail(
-        order, after(grad_out, output), normed, weights, attended, grad_q)
-    next_send, next_keep, db_next, grad_heads = kv_tail(
-        False, 0, spots[0], x, normed, gain_attn, weights, tables, grad_mlp, grad_heads, own_kv[:1], come_kv[:1])
-    part_out, part_in = last_step(kept_after(steps_mlp, grad_heads))
-    steps_first = core_step([first_send, next_send], [first_keep, next_keep])
-    last_send, last_keep, db_last, grad_inputs, dgain_attn, dshift_attn = kv_tail(
-        True, 5, spots[0], after(x, part_out, part_in, *steps_first), normed, gain_attn, weights, tables, grad_mlp, grad_heads,
+    first_send, first_keep, grad_heads, db_first = first_tail(
+        spots[0], order, after(grad_out, output), normed, weights, tables, attended, grad_q, own_kv[0], come_kv[0])
+    part_out, part_in = last_step(kept_after(steps_mlp, grad_heads), 48)
+    steps_first = core_step([first_send], [first_keep])
+    grad_inputs, last_send, last_keep, db_last, dgain_attn, dshift_attn = last_tail(
+        spots[0], after(x, part_out, part_in, *steps_first), normed, gain_attn, weights, tables, grad_mlp, grad_heads,
         own_kv[1:], come_kv[1:])
     sum_out, sum_in = along(part_out), along(part_in)
     steps_first = side_step(kept_after(steps_first, last_send))
-
-    def halves(a, i):
-        return a.reshape(a.shape[0], -1, 2, PAIR)[:, :, i].reshape(a.shape[0], -1)
-
-    db_kv = [halves(jnp.concatenate([db_next, db_last], axis=1), i) for i in range(2)]
+    cols = db_last.shape[1] // 2
+    split = [width, width + (db_first.shape[1] - width) // 2]
+    db_q, db_k, db_v = jnp.split(db_first, split, axis=1)
+    db_qkv = jnp.concatenate([db_q, db_k, db_last[:, :cols], db_v, db_last[:, cols:]], axis=1)
     smalls = [a.reshape(width, -1) for a in
-              (dgain_attn, dshift_attn, jnp.concatenate([db_q, *db_kv], axis=1), db_out, dgain_mlp, dshift_mlp, db_in)]
+              (dgain_attn, dshift_attn, db_qkv, db_out, dgain_mlp, dshift_mlp, db_in)]
     used = sum(a.shape[1] for a in smalls)
     packed = jnp.concatenate(smalls + [jnp.zeros((width, PAIR - used), f32)], axis=1).astype(bf16)
     packed = packed.reshape(8, width // 8, PAIR)[order].reshape(2, width // 2, PAIR)
     steps_last = core_step([after(last_send, *steps_first), packed[0]], [last_keep, packed[1]])
-    part_first = jnp.concatenate(last_step(steps_first), axis=1)
-    sum_first = along(part_first)
-    sum_last = along(jnp.concatenate(last_step(side_step(kept_after(steps_last, part_first))), axis=1))
-    packed = sum_last[:, -PAIR:].astype(f32)
-    sum_attn, sum_q = sum_first[:, :width], sum_first[:, width:2 * width]
-    rest = jnp.concatenate([sum_first[:, 2 * width:], sum_last[:, :-PAIR]], axis=1)
-    sum_qkv = jnp.concatenate([sum_q, halves(rest, 0), halves(rest, 1)], axis=1)
+    part_first = last_step(steps_first)
+    part_last = last_step(side_step(kept_after(steps_last, *part_first)))
+    total = along(jnp.concatenate([*part_first, *part_last], axis=1))
+    ends = [width, 2 * width, split[1] + width, db_first.shape[1] + width]
+    ends += [ends[-1] + cols, ends[-1] + 2 * cols]
+    sum_attn, sum_q, sum_k, sum_v, end_k, end_v, packed = jnp.split(total, ends, axis=1)
+    sum_qkv = jnp.concatenate([sum_q, sum_k, end_k, sum_v, end_v], axis=1)
+    packed = packed.astype(f32)
     done, at = [], 0
     for a in smalls:
         done.append(packed[:, at:at + a.shape[1]].reshape(-1))

time: 578 us -> 552 us (0.955)
  Pallas kernels: 363 us -> 354 us
    pallas_call x2 -> x1, Pallas kernels: 36.7 us -> 16 us  [last_tail(): pl.pallas_call(partial(last_kernel, len(owns)), grid_spec=pltpu.PrefetchS...]
    reduce_scatter x4 -> x3, waiting for transfers between devices: 35.8 us -> 22.4 us  [along(): return lax.psum_scatter(part, 'ctx', scatter_dimension=0, tiled=True)]
    pallas_call x1, Pallas kernels: 15 us -> 23.3 us  [first_tail(): pl.pallas_call(partial(first_kernel, len(dqs)), grid_spec=pltpu.PrefetchS...]
    ppermute x2, waiting for transfers between devices: 38 us -> 44.4 us  [fast(): toward = lax.ppermute(toward, 'ctx', ring)]
    ppermute x30 -> x25, starting transfers between devices: 26.1 us -> 20.8 us  [swap(): return lax.ppermute(a, 'fsdp', pairs_of(bit, 8))]
    ppermute x30 -> x25, waiting for transfers between devices: 13.1 us -> 15.9 us  [swap(): return lax.ppermute(a, 'fsdp', pairs_of(bit, 8))]
  transfers between devices with their start and end apart: 46 -> 40, of which waited for: 15 -> 16; matrix products, arithmetic and copies ran while one was open for 6% -> 5% of each run, Pallas kernels for 61% -> 62%
where the time goes in v7:
time: 552 us; the launch traced here: 546 us
  Pallas kernels  354 us (64%)
  waiting for transfers between devices  92.4 us (17%)
  starting transfers between devices  31.9 us (6%)
  other arithmetic  21.7 us (4%)
  local copies, waits for them, and re-layouts  21.4 us (4%)
  between operations  15.1 us (3%)
  blocking collectives  9.17 us (2%)
    pallas_call x3, Pallas kernels, attention(): pl.pallas_call(partial(attention_kernel, half, n), grid=(pairs,), in_spec...  156 us
    pallas_call x1, Pallas kernels, mlp(): pl.pallas_call(mlp_kernel, grid_spec=pltpu.PrefetchScalarGridSpec(num_sca...  75.9 us
    ppermute x2, waiting for transfers between devices, fast(): toward = lax.ppermute(toward, 'ctx', ring)  44.4 us
    pallas_call x9, Pallas kernels, add_parts(): pl.pallas_call(partial(add_kernel, plan), grid=(steps,), in_specs=[spec(a...  39.5 us
    pallas_call x2, Pallas kernels, qkv(): pl.pallas_call(partial(qkv_kernel, far), grid_spec=pltpu.PrefetchScalarGr...  29.3 us
    pallas_call x1, Pallas kernels, first_tail(): pl.pallas_call(partial(first_kernel, len(dqs)), grid_spec=pltpu.PrefetchS...  23.3 us
    reduce_scatter x3, waiting for transfers between devices, along(): return lax.psum_scatter(part, 'ctx', scatter_dimension=0, tiled=True)  22.4 us
    ppermute x25, starting transfers between devices, swap(): return lax.ppermute(a, 'fsdp', pairs_of(bit, 8))  20.8 us
  transfers between devices with their start and end apart: 40, of which 16 were waited for; matrix products, arithmetic and copies ran while one was open for 5% of the time, Pallas kernels for 62%

profile of v7, /device:TPU:0, one launch (start us, length us, event | category | flops | bytes accessed | tf_op | source)
XLA Modules:
  0.0 545.8 jit_solution(8391054511300843250)
XLA Ops:
  7.2 2.4 pad_maximum_fusion.1
  9.9 5.1 collective-permute-start.2
  16.1 2.9 collective-permute-start.4
  20.3 9.2 %all-gather.1 = bf16[8,1,1536]{2,1,0:T(2,128)(2,1)S(1)} all-gather(bf16[1,1,1536]{2,1,0:T(2,128)(2,1)S(1)} %reshape.313), channel_id=2, replica_groups=mesh['fsdp'=8,'ctx'=4] {'fsdp'}, dimensions={0}, use_global_device_ids=true | all-gather | bytes 27648 | tf_op jit(solution)/shard_map/all_gather | solution.py:777
  31.3 6.5 %fusion = (f32[2304,128]{1,0:T(8,128)}, f32[2304,128]{1,0:T(8,128)}, f32[2304,128]{1,0:T(8,128)}) fusion(f32[128]{0:T(128)S(1)} %fusion.5, f32[2304]{0:T(1024)S(1)} %iota_convert_fusion, pred[128]{0:T(512)(128)(4,1)S(1)} %get-tuple-element.251, pred[128]{0:T(512)(128)(4,1)S(1)} %broadcast_compare_fusion.1, pred[128]{0:T(512)(128)(4,1)S(1)} %get-tuple-element.252), kind=kLoop, calls=%fused_computation.3 | loop fusion | flops 1179648 | bytes 3549056 | tf_op jit(solution)/shard_map/jit(_where)/select_n | solution.py:790
  37.8 4.8 collective-permute-done.4.refs_2_
  42.6 21.8 %collective-permute-done.3.refs_0_ = bf16[512,1024]{1,0:T(8,128)(2,1)S(1)} collective-permute-done((bf16[512,1024]{1,0:T(8,128)(2,1)S(1)}, bf16[512,1024]{1,0:T(8,128)(2,1)S(1)}, u32[]{:S(2)}, u32[]{:S(2)}) %collective-permute-start.3) | collective-permute-done | bytes 1048608 | tf_op jit(solution)/shard_map/ppermute | solution.py:768
  64.4 3.5 all-gather.6.cloned.1.call-done.w_ref.wq_ref.wk_ref.wv_ref
  67.9 14.0 %qkv_own.1 = (bf16[1024,1024]{1,0:T(8,128)(2,1)}, bf16[1024,1024]{1,0:T(8,128)(2,1)}, bf16[1024,1024]{1,0:T(8,128)(2,1)}, bf16[1024,1024]{1,0:T(8,128)(2,1)}) custom-call(s32[4]{0:T(128)} %copy-done.40, s32[8]{0:T(128)} %get-tuple-element.250.order_ref, f32[1,1024]{1,0:T(1,128)} %bitcast.74, f32[1,1024]{1,0:T(1,128)} %bitcast.77, ...), custom_call_target="tpu_custom_call" | custom-call | flops 1048576 | bytes 65536 | tf_op jit(solution)/shard_map/qkv_own/pallas_call | solution.py:276
  87.5 22.6 %collective-permute-done.5.refs_1_ = bf16[512,1024]{1,0:T(8,128)(2,1)S(1)} collective-permute-done((bf16[512,1024]{1,0:T(8,128)(2,1)S(1)}, bf16[512,1024]{1,0:T(8,128)(2,1)S(1)}, u32[]{:S(2)}, u32[]{:S(2)}) %collective-permute-start.5) | collective-permute-done | bytes 1048608 | tf_op jit(solution)/shard_map/ppermute | solution.py:768
  110.1 6.6 %spread.1.do_ref = bf16[1024,1024]{1,0:T(8,128)(2,1)} custom-call(bf16[1024,1024]{1,0:T(8,128)(2,1)} %bitcast.52, bf16[1024,4096]{1,0:T(8,128)(2,1)} %all-gather.6.cloned.1.call-done.w_ref.wq_ref.wk_ref.wv_ref), custom_call_target="tpu_custom_call" | custom-call | flops 1048576 | bytes 65536 | tf_op jit(solution)/shard_map/spread/pallas_call | solution.py:499
  116.7 15.3 %kv_remote.1 = (bf16[1536,1024]{1,0:T(8,128)(2,1)}, bf16[1536,1024]{1,0:T(8,128)(2,1)}) custom-call(s32[6]{0:T(128)} %pad_add_fusion.1.spot_ref, s32[8]{0:T(128)} %get-tuple-element.250.order_ref, f32[1,1024]{1,0:T(1,128)} %bitcast.75, f32[1,1024]{1,0:T(1,128)} %bitcast.78, bf16[1024,4096]{1,0:T(8,128)(2,1)} %all-gather.6.cloned.1.call-done.w_ref.wq_ref.wk_ref.wv_ref, ...), custom_call_target="tpu_custom_call" | custom-call | flops 1048576 | bytes 65536 | tf_op jit(solution)/shard_map/kv_remote/pallas_call | solution.py:276
  132.1 76.7 %attention.3 = (bf16[1024,512]{1,0:T(8,128)(2,1)}, bf16[1024,512]{1,0:T(8,128)(2,1)}, bf16[2048,1024]{1,0:T(8,128)(2,1)}, bf16[512,1024]{1,0:T(8,128)(2,1)}) custom-call(f32[4,8]{1,0:T(4,128)} %add_select_fusion.kind_ref, s32[4]{0:T(128)} %compare_select_fusion.3.owner_ref, f32[8,1024]{1,0:T(8,128)} %get-tuple-element.246.cos_ref, ...), custom_call_target="tpu_custom_call" | custom-call | flops 1048576 | bytes 65536 | tf_op jit(solution)/shard_map/attention/pallas_call | solution.py:647
  209.5 75.9 %mlp.1 = (f32[1024,1024]{1,0:T(8,128)}, f32[1024,1024]{1,0:T(8,128)}, bf16[512,4096]{1,0:T(8,128)(2,1)}, bf16[512,4096]{1,0:T(8,128)(2,1)}, bf16[2048,1024]{1,0:...) custom-call(s32[8]{0:T(128)} %get-tuple-element.250.order_ref, ...), custom_call_target="tpu_custom_call" | custom-call | flops 1048576 | bytes 65536 | tf_op jit(solution)/shard_map/mlp/pallas_call | solution.py:202
  286.0 39.6 %attention.4 = (bf16[1024,256]{1,0:T(8,128)(2,1)}, bf16[1024,256]{1,0:T(8,128)(2,1)}, bf16[2048,512]{1,0:T(8,128)(2,1)}, bf16[512,512]{1,0:T(8,128)(2,1)}) custom-call(f32[4,8]{1,0:T(4,128)} %add_select_fusion.kind_ref, s32[4]{0:T(128)} %compare_select_fusion.3.owner_ref, f32[8,1024]{1,0:T(8,128)} %get-tuple-element.246.cos_ref, ...), custom_call_target="tpu_custom_call" | custom-call | flops 1048576 | bytes 65536 | tf_op jit(solution)/shard_map/attention/pallas_call | solution.py:647
  325.7 9.6 %add_parts.9 = (bf16[2,256,1024]{2,1,0:T(8,128)(2,1)}, bf16[2,256,1024]{2,1,0:T(8,128)(2,1)}, bf16[2,256,1024]{2,1,0:T(8,128)(2,1)}, bf16[2,256,1024]{2,1,0:T(8,...) custom-call(bf16[2,2,2,256,1024]{4,3,2,1,0:T(8,128)(2,1)} %bitcast.5, ...), custom_call_target="tpu_custom_call" | custom-call | flops 1 | bytes 65536 | tf_op jit(solution)/shard_map/add_parts/pallas_call | solution.py:679
  339.4 39.7 %attention.5 = (bf16[1024,256]{1,0:T(8,128)(2,1)}, bf16[1024,256]{1,0:T(8,128)(2,1)}, bf16[2048,512]{1,0:T(8,128)(2,1)}, bf16[512,512]{1,0:T(8,128)(2,1)}) custom-call(f32[4,8]{1,0:T(4,128)} %add_select_fusion.kind_ref, s32[4]{0:T(128)} %compare_select_fusion.3.owner_ref, f32[8,1024]{1,0:T(8,128)} %get-tuple-element.246.cos_ref, ...), custom_call_target="tpu_custom_call" | custom-call | flops 1048576 | bytes 65536 | tf_op jit(solution)/shard_map/attention/pallas_call | solution.py:647
  379.2 4.1 collective-permute-done.10.refs_5_
  384.8 6.2 %add_parts.10 = (bf16[256,1024]{1,0:T(8,128)(2,1)}, bf16[256,1024]{1,0:T(8,128)(2,1)}, bf16[256,1024]{1,0:T(8,128)(2,1)}, bf16[256,1024]{1,0:T(8,128)(2,1)}, bf1...) custom-call(bf16[2,256,1024]{2,1,0:T(8,128)(2,1)} %get-tuple-element.148., ...), custom_call_target="tpu_custom_call" | custom-call | flops 1 | bytes 65536 | tf_op jit(solution)/shard_map/add_parts/pallas_call | solution.py:679
  395.1 7.6 %join.1 = bf16[1024,1024]{1,0:T(8,128)(2,1)} custom-call(bf16[1024,1024]{1,0:T(8,128)(2,1)} %bitcast.50, bf16[1024,4096]{1,0:T(8,128)(2,1)} %all-gather.6.cloned.1.call-done.w_ref.wq_ref.wk_ref.wv_ref, f32[1024,1024]{1,0:T(8,128)} %get-tuple-element.136.mlp_ref, f32[1,1024]{1,0:T(1,128)} %bitcast.83, bf16[1024,512]{1,0:T(8,128)(2,1)} %get-tuple-element.127.refs_0_, ...), custom_call_target="tpu_custom_call" | custom-call | flops 12884901888 | bytes 1048576 | tf_op jit(solution)/shard_map/join/pallas_call | solution.py:478
  402.7 23.3 %first_tail.1 = (bf16[512,3072]{1,0:T(8,128)(2,1)}, bf16[512,3072]{1,0:T(8,128)(2,1)}, f32[1024,1024]{1,0:T(8,128)}, f32[1,2048]{1,0:T(1,128)}) custom-call(s32[4]{0:T(128)} %copy-done.40, s32[8]{0:T(128)} %get-tuple-element.250.order_ref, bf16[1024,1024]{1,0:T(8,128)(2,1)} %bitcast.54, bf16[1024,1024]{1,0:T(8,128)(2,1)} %get-tuple-element.161.h_ref, ...), custom_call_target="tpu_custom_call" | custom-call | flops 25769803776 | bytes 1048576 | tf_op jit(solution)/shard_map/first_tail/pallas_call | solution.py:382
  426.1 4.4 add_parts.11
  433.6 5.3 add_parts.12
  440.7 16.0 %last_tail.1 = (f32[1024,1024]{1,0:T(8,128)}, bf16[512,1024]{1,0:T(8,128)(2,1)}, bf16[512,1024]{1,0:T(8,128)(2,1)}, f32[1,1024]{1,0:T(1,128)}, f32[1,1024]{1,0:T(1,128)}, /*index=5*/f32[1,1024]{1,0:T(1,128)}) custom-call(s32[4]{0:T(128)} %copy-done.40, bf16[1024,1024]{1,0:T(8,128)(2,1)} %get-tuple-element.161.h_ref, f32[1,1024]{1,0:T(1,128)} %bitcast.76, ...), custom_call_target="tpu_custom_call" | custom-call | flops 12884901888 | bytes 1048576 | tf_op jit(solution)/shard_map/last_tail/pallas_call | solution.py:445
  460.6 3.9 add_parts.13
  468.1 3.6 concatenate.55
  477.2 2.7 add_parts.15
  486.2 3.6 add_parts.14
  492.5 2.0 add_parts.16
  498.6 2.2 collective-permute-done.29.refs_5_
  503.9 2.1 pad_maximum_fusion
  509.6 22.3 %reduce-scatter.13.cloned.1.call-done = bf16[32,4224]{1,0:T(8,128)(2,1)} async-done(((bf16[128,4224]{1,0:T(8,128)(2,1)}), bf16[32,4224]{1,0:T(8,128)(2,1)}) %reduce-scatter.13.cloned.1.call-update) | async-done | bytes 270352 | tf_op jit(solution)/shard_map/reduce_scatter | solution.py:742
  (235 shorter events, 65.4 us)
Async XLA Ops:
  7.2 60.7 %all-gather.6.cloned.1.call-start = ((), (), s32[]{:S(2)}) async-start(), calls=%async_computation.6 | async-start | bytes 9437184 | tf_op jit(solution)/shard_map/all_gather | solution.py:783
  9.7 199.8 %all-gather.8.cloned.1.call-start = ((), (), s32[]{:S(2)}) async-start(), calls=%async_computation.7 | async-start | bytes 9437184 | tf_op jit(solution)/shard_map/all_gather | solution.py:800
  9.9 27.9 %collective-permute-start.2 = (s32[2]{0:T(128)S(1)}, s32[2]{0:T(128)S(1)}, u32[]{:S(2)}, u32[]{:S(2)}) collective-permute-start(s32[2]{0:T(128)S(1)} %bitcast.89), channel_id=1, source_target_pairs={{0,3},{1,0},{2,1},{3,2},{4,7},{5,4},{6,5},{7,6},{8,11},{9,8},{10,9... | collective-permute-start | bytes 32 | tf_op jit(solution)/shard_map/ppermute | solution.py:775
  15.0 22.8 %collective-permute-start.1 = (s32[2]{0:T(128)S(1)}, s32[2]{0:T(128)S(1)}, u32[]{:S(2)}, u32[]{:S(2)}) collective-permute-start(s32[2]{0:T(128)S(1)} %bitcast.90), channel_id=1, source_target_pairs={{0,2},{1,3},{2,0},{3,1},{4,6},{5,7},{6,4},{7,5},{8,10},{9,11},{10,... | collective-permute-start | bytes 32 | tf_op jit(solution)/shard_map/ppermute | solution.py:775
  15.0 22.8 %collective-permute-start = (s32[2]{0:T(128)S(1)}, s32[2]{0:T(128)S(1)}, u32[]{:S(2)}, u32[]{:S(2)}) collective-permute-start(s32[2]{0:T(128)S(1)} %bitcast.91), channel_id=1, source_target_pairs={{0,1},{1,2},{2,3},{3,0},{4,5},{5,6},{6,7},{7,4},{8,9},{9,10},{10,1... | collective-permute-start | bytes 32 | tf_op jit(solution)/shard_map/ppermute | solution.py:775
  16.1 26.5 %collective-permute-start.4 = (bf16[512,1024]{1,0:T(8,128)(2,1)S(1)}, bf16[512,1024]{1,0:T(8,128)(2,1)S(1)}, u32[]{:S(2)}, u32[]{:S(2)}) collective-permute-start(bf16[512,1024]{1,0:T(8,128)(2,1)S(1)} %slice_bitcast_fusion), channel_id=1, source_target_pairs={{0,3},{1,0},{2,1},{3,2},{4,7},{5,4},{6,5},{7,6},{8,11},{9,8},{10,9... | collective-permute-start | bytes 3145736 | tf_op jit(solution)/shard_map/ppermute | solution.py:771
  19.0 45.5 %collective-permute-start.3 = (bf16[512,1024]{1,0:T(8,128)(2,1)S(1)}, bf16[512,1024]{1,0:T(8,128)(2,1)S(1)}, u32[]{:S(2)}, u32[]{:S(2)}) collective-permute-start(bf16[512,1024]{1,0:T(8,128)(2,1)S(1)} %slice_bitcast_fusion), channel_id=1, source_target_pairs={{0,1},{1,2},{2,3},{3,0},{4,5},{5,6},{6,7},{7,4},{8,9},{9,10},{10,1... | collective-permute-start | bytes 3145736 | tf_op jit(solution)/shard_map/ppermute | solution.py:768
  81.9 127.6 %all-gather.10.cloned.1.call-start = ((), (), s32[]{:S(2)}) async-start(), calls=%async_computation.8 | async-start | bytes 9437184 | tf_op jit(solution)/shard_map/all_gather | solution.py:801
  82.7 320.0 %reduce-scatter.7.cloned.1.call-start = ((), (), s32[]{:S(2)}) async-start(), calls=%async_computation.9 | async-start | bytes 5242880 | tf_op jit(solution)/shard_map/reduce_scatter | solution.py:816
  82.7 27.4 %collective-permute-start.5 = (bf16[512,1024]{1,0:T(8,128)(2,1)S(1)}, bf16[512,1024]{1,0:T(8,128)(2,1)S(1)}, u32[]{:S(2)}, u32[]{:S(2)}) collective-permute-start(bf16[512,1024]{1,0:T(8,128)(2,1)S(1)} %collective-permute-done.3.refs_0_), channel_id=1, source_target_pairs={{0,1},{1,2},{2,3},{3,0},{4,5},{5,6},{6,7},{7,4},{8,9},{9,10},{10,1... | collective-permute-start | bytes 3145736 | tf_op jit(solution)/shard_map/ppermute | solution.py:768
  208.8 231.8 %reduce-scatter.9.cloned.1.call-start = ((), (), s32[]{:S(2)}) async-start(), calls=%async_computation.10 | async-start | bytes 2621440 | tf_op jit(solution)/shard_map/reduce_scatter | solution.py:816
  285.4 40.3 %collective-permute-start.6 = (bf16[2048,1024]{1,0:T(8,128)(2,1)}, bf16[2048,1024]{1,0:T(8,128)(2,1)}, u32[]{:S(2)}, u32[]{:S(2)}) collective-permute-start(bf16[2048,1024]{1,0:T(8,128)(2,1)} %get-tuple-element.132), channel_id=1, source_target_pairs={{0,4},{4,0},{8,12},{12,8},{16,20},{20,16},{24,28},{28,24},{1,5},{5... | collective-permute-start | bytes 12582920 | tf_op jit(solution)/shard_map/ppermute | solution.py:695
  285.5 40.2 %collective-permute-start.7 = (bf16[512,4096]{1,0:T(8,128)(2,1)}, bf16[512,4096]{1,0:T(8,128)(2,1)}, u32[]{:S(2)}, u32[]{:S(2)}) collective-permute-start(bf16[512,4096]{1,0:T(8,128)(2,1)} %get-tuple-element.134), channel_id=1, source_target_pairs={{0,4},{4,0},{8,12},{12,8},{16,20},{20,16},{24,28},{28,24},{1,5},{5... | collective-permute-start | bytes 12582920 | tf_op jit(solution)/shard_map/ppermute | solution.py:695
  325.6 115.0 %reduce-scatter.11.cloned.1.call-start = ((), (), s32[]{:S(2)}) async-start(), calls=%async_computation.11 | async-start | bytes 2621440 | tf_op jit(solution)/shard_map/reduce_scatter | solution.py:816
  335.3 43.9 %collective-permute-start.8 = (bf16[2,256,1024]{2,1,0:T(8,128)(2,1)}, bf16[2,256,1024]{2,1,0:T(8,128)(2,1)S(1)}, u32[]{:S(2)}, u32[]{:S(2)}) collective-permute-start(bf16[2,256,1024]{2,1,0:T(8,128)(2,1)} %get-tuple-element.139), channel_id=1, source_target_pairs={{0,8},{4,12},{8,0},{12,4},{16,24},{20,28},{24,16},{28,20},{1,9},{5... | collective-permute-start | bytes 3145736 | tf_op jit(solution)/shard_map/ppermute | solution.py:695
  337.1 42.0 %collective-permute-start.9 = (bf16[2,256,1024]{2,1,0:T(8,128)(2,1)}, bf16[2,256,1024]{2,1,0:T(8,128)(2,1)S(1)}, u32[]{:S(2)}, u32[]{:S(2)}) collective-permute-start(bf16[2,256,1024]{2,1,0:T(8,128)(2,1)} %get-tuple-element.140), channel_id=1, source_target_pairs={{0,16},{4,20},{8,24},{12,28},{16,0},{20,4},{24,8},{28,12},{1,17},{... | collective-permute-start | bytes 3145736 | tf_op jit(solution)/shard_map/ppermute | solution.py:695
  337.3 45.9 %collective-permute-start.10 = (bf16[2,64,4096]{2,1,0:T(8,128)(2,1)}, bf16[2,64,4096]{2,1,0:T(8,128)(2,1)S(1)}, u32[]{:S(2)}, u32[]{:S(2)}) collective-permute-start(bf16[2,64,4096]{2,1,0:T(8,128)(2,1)} %get-tuple-element.142), channel_id=1, source_target_pairs={{0,8},{4,12},{8,0},{12,4},{16,24},{20,28},{24,16},{28,20},{1,9},{5... | collective-permute-start | bytes 3145736 | tf_op jit(solution)/shard_map/ppermute | solution.py:695
  338.9 45.9 %collective-permute-start.11 = (bf16[2,64,4096]{2,1,0:T(8,128)(2,1)}, bf16[2,64,4096]{2,1,0:T(8,128)(2,1)}, u32[]{:S(2)}, u32[]{:S(2)}) collective-permute-start(bf16[2,64,4096]{2,1,0:T(8,128)(2,1)} %get-tuple-element.144), channel_id=1, source_target_pairs={{0,16},{4,20},{8,24},{12,28},{16,0},{20,4},{24,8},{28,12},{1,17},{... | collective-permute-start | bytes 3145736 | tf_op jit(solution)/shard_map/ppermute | solution.py:695
  379.1 127.0 %reduce-scatter.17.cloned.1.call-start = ((), (), s32[]{:S(2)}) async-start(), calls=%async_computation.14 | async-start | bytes 1310720 | tf_op jit(solution)/shard_map/reduce_scatter | solution.py:742
  391.0 35.1 %collective-permute-start.12 = (bf16[256,1024]{1,0:T(8,128)(2,1)}, bf16[256,1024]{1,0:T(8,128)(2,1)}, u32[]{:S(2)}, u32[]{:S(2)}) collective-permute-start(bf16[256,1024]{1,0:T(8,128)(2,1)} %get-tuple-element.152), channel_id=1, source_target_pairs={{0,16},{4,20},{8,24},{12,28},{16,0},{20,4},{24,8},{28,12},{1,17},{... | collective-permute-start | bytes 1572872 | tf_op jit(solution)/shard_map/ppermute | solution.py:695
  391.9 34.2 %collective-permute-start.13 = (bf16[256,1024]{1,0:T(8,128)(2,1)}, bf16[256,1024]{1,0:T(8,128)(2,1)}, u32[]{:S(2)}, u32[]{:S(2)}) collective-permute-start(bf16[256,1024]{1,0:T(8,128)(2,1)} %get-tuple-element.154), channel_id=1, source_target_pairs={{0,8},{4,12},{8,0},{12,4},{16,24},{20,28},{24,16},{28,20},{1,9},{5... | collective-permute-start | bytes 1572872 | tf_op jit(solution)/shard_map/ppermute | solution.py:695
  392.8 33.3 %collective-permute-start.14 = (bf16[64,4096]{1,0:T(8,128)(2,1)}, bf16[64,4096]{1,0:T(8,128)(2,1)}, u32[]{:S(2)}, u32[]{:S(2)}) collective-permute-start(bf16[64,4096]{1,0:T(8,128)(2,1)} %get-tuple-element.156), channel_id=1, source_target_pairs={{0,16},{4,20},{8,24},{12,28},{16,0},{20,4},{24,8},{28,12},{1,17},{... | collective-permute-start | bytes 1572872 | tf_op jit(solution)/shard_map/ppermute | solution.py:695
  394.2 31.9 %collective-permute-start.15 = (bf16[64,4096]{1,0:T(8,128)(2,1)}, bf16[64,4096]{1,0:T(8,128)(2,1)}, u32[]{:S(2)}, u32[]{:S(2)}) collective-permute-start(bf16[64,4096]{1,0:T(8,128)(2,1)} %get-tuple-element.158), channel_id=1, source_target_pairs={{0,8},{4,12},{8,0},{12,4},{16,24},{20,28},{24,16},{28,20},{1,9},{5... | collective-permute-start | bytes 1572872 | tf_op jit(solution)/shard_map/ppermute | solution.py:695
  430.5 77.4 %reduce-scatter.15.cloned.1.call-start = ((), (), s32[]{:S(2)}) async-start(), calls=%async_computation.13 | async-start | bytes 1310720 | tf_op jit(solution)/shard_map/reduce_scatter | solution.py:742
  431.3 100.7 %reduce-scatter.13.cloned.1.call-start = ((), (), s32[]{:S(2)}) async-start(), calls=%async_computation.12 | async-start | bytes 1351680 | tf_op jit(solution)/shard_map/reduce_scatter | solution.py:742
  438.9 19.8 %collective-permute-start.17 = (bf16[2,64,3072]{2,1,0:T(8,128)(2,1)}, bf16[2,64,3072]{2,1,0:T(8,128)(2,1)S(1)}, u32[]{:S(2)}, u32[]{:S(2)}) collective-permute-start(bf16[2,64,3072]{2,1,0:T(8,128)(2,1)} %get-tuple-element.177), channel_id=1, source_target_pairs={{0,8},{4,12},{8,0},{12,4},{16,24},{20,28},{24,16},{28,20},{1,9},{5... | collective-permute-start | bytes 2359304 | tf_op jit(solution)/shard_map/ppermute | solution.py:695
  440.1 19.5 %collective-permute-start.18 = (bf16[2,64,3072]{2,1,0:T(8,128)(2,1)}, bf16[2,64,3072]{2,1,0:T(8,128)(2,1)S(1)}, u32[]{:S(2)}, u32[]{:S(2)}) collective-permute-start(bf16[2,64,3072]{2,1,0:T(8,128)(2,1)} %get-tuple-element.179), channel_id=1, source_target_pairs={{0,16},{4,20},{8,24},{12,28},{16,0},{20,4},{24,8},{28,12},{1,17},{... | collective-permute-start | bytes 2359304 | tf_op jit(solution)/shard_map/ppermute | solution.py:695
  464.5 11.6 %collective-permute-start.21 = (bf16[512,1024]{1,0:T(8,128)(2,1)}, bf16[512,1024]{1,0:T(8,128)(2,1)S(1)}, u32[]{:S(2)}, u32[]{:S(2)}) collective-permute-start(bf16[512,1024]{1,0:T(8,128)(2,1)} %get-tuple-element.196), channel_id=1, source_target_pairs={{0,4},{4,0},{8,12},{12,8},{16,20},{20,16},{24,28},{28,24},{1,5},{5... | collective-permute-start | bytes 3145736 | tf_op jit(solution)/shard_map/ppermute | solution.py:695
  472.3 12.1 %collective-permute-start.19 = (bf16[64,3072]{1,0:T(8,128)(2,1)}, bf16[64,3072]{1,0:T(8,128)(2,1)S(1)}, u32[]{:S(2)}, u32[]{:S(2)}) collective-permute-start(bf16[64,3072]{1,0:T(8,128)(2,1)} %get-tuple-element.192), channel_id=1, source_target_pairs={{0,16},{4,20},{8,24},{12,28},{16,0},{20,4},{24,8},{28,12},{1,17},{... | collective-permute-start | bytes 1179656 | tf_op jit(solution)/shard_map/ppermute | solution.py:695
  473.3 12.2 %collective-permute-start.20 = (bf16[64,3072]{1,0:T(8,128)(2,1)}, bf16[64,3072]{1,0:T(8,128)(2,1)S(1)}, u32[]{:S(2)}, u32[]{:S(2)}) collective-permute-start(bf16[64,3072]{1,0:T(8,128)(2,1)} %get-tuple-element.194), channel_id=1, source_target_pairs={{0,8},{4,12},{8,0},{12,4},{16,24},{20,28},{24,16},{28,20},{1,9},{5... | collective-permute-start | bytes 1179656 | tf_op jit(solution)/shard_map/ppermute | solution.py:695
  479.8 11.2 %collective-permute-start.23 = (bf16[2,64,1024]{2,1,0:T(8,128)(2,1)}, bf16[2,64,1024]{2,1,0:T(8,128)(2,1)S(1)}, u32[]{:S(2)}, u32[]{:S(2)}) collective-permute-start(bf16[2,64,1024]{2,1,0:T(8,128)(2,1)} %get-tuple-element.207), channel_id=1, source_target_pairs={{0,8},{4,12},{8,0},{12,4},{16,24},{20,28},{24,16},{28,20},{1,9},{5... | collective-permute-start | bytes 786440 | tf_op jit(solution)/shard_map/ppermute | solution.py:695
  481.1 10.0 %collective-permute-start.24 = (bf16[2,64,1024]{2,1,0:T(8,128)(2,1)}, bf16[2,64,1024]{2,1,0:T(8,128)(2,1)S(1)}, u32[]{:S(2)}, u32[]{:S(2)}) collective-permute-start(bf16[2,64,1024]{2,1,0:T(8,128)(2,1)} %get-tuple-element.210), channel_id=1, source_target_pairs={{0,16},{4,20},{8,24},{12,28},{16,0},{20,4},{24,8},{28,12},{1,17},{... | collective-permute-start | bytes 786440 | tf_op jit(solution)/shard_map/ppermute | solution.py:695
  (50 other events, 351.6 us)
Sparse Core Ops, SparseCore 0:
  10.5 57.3 all-gather.5
  82.0 54.3 all-gather.7
  138.4 54.3 all-gather.9
  208.9 74.7 reduce-scatter.6
  325.8 41.4 reduce-scatter.8
  379.2 41.7 reduce-scatter.10
  430.6 24.7 reduce-scatter.16
  457.7 25.7 reduce-scatter.14
  506.2 25.7 reduce-scatter.12

commit v8 on v7

--- a/solution.py
+++ b/solution.py
@@ -763,13 +763,9 @@
     order = jnp.bitwise_xor(me, jnp.array(relative, jnp.int32))
     owners = lax.rem(place + n - jnp.arange(n), n)
     far = [None] * n
-    toward, away = x[:half], x[:half]
-    for s in range(1, n // 2 + 1):
-        toward = lax.ppermute(toward, "ctx", ring)
-        far[s] = toward
-        if n - s > n // 2:
-            away = lax.ppermute(away, "ctx", back)
-            far[n - s] = away
+    far[0] = x[:half]
+    for s in range(1, n):
+        far[s] = lax.ppermute(far[s - 1], "ctx", ring)
     spots = [pos[::RB] // RB]
     for s in range(1, n):
         spots.append(lax.ppermute(spots[0][:half // RB], "ctx", [(i, (i + s) % n) for i in range(n)]))
@@ -792,13 +788,13 @@
     cos_t, sin_t = jnp.cos(angles_t), jnp.sin(angles_t)
 
     normed, queries, own_keys, own_values = qkv(
-        spots[0], order, [after(x, far[1], far[n - 1], *spots[1:])], gain_attn, shift_attn, weights, bias_qkv, tables)
+        spots[0], order, [after(x, far[n - 2], *spots[1:])], gain_attn, shift_attn, weights, bias_qkv, tables)
     far_keys, far_values = qkv(
         jnp.concatenate(spots[1:]), order, far[1:], gain_attn, shift_attn, weights, bias_qkv, tables)
     keys, values = (own_keys, far_keys), (own_values, far_values)
-    grad_att = spread(after(grad_out, far[n // 2]), weights)
-    weight_in = lax.all_gather(after(w_in, queries), "fsdp", axis=0, tiled=True)
-    weight_out = lax.all_gather(after(w_out, queries), "fsdp", axis=0, tiled=True)
+    grad_att = spread(grad_out, weights)
+    weight_in = lax.all_gather(after(w_in, far[1]), "fsdp", axis=0, tiled=True)
+    weight_out = lax.all_gather(after(w_out, far[1]), "fsdp", axis=0, tiled=True)
 
     per = half // QB
     earlier = jnp.stack([spots[s][0] < spots[0][0] for s in range(1, n)])
@@ -837,10 +833,11 @@
     split = [width, width + (db_first.shape[1] - width) // 2]
     db_q, db_k, db_v = jnp.split(db_first, split, axis=1)
     db_qkv = jnp.concatenate([db_q, db_k, db_last[:, :cols], db_v, db_last[:, cols:]], axis=1)
-    smalls = [a.reshape(width, -1) for a in
-              (dgain_attn, dshift_attn, db_qkv, db_out, dgain_mlp, dshift_mlp, db_in)]
-    used = sum(a.shape[1] for a in smalls)
-    packed = jnp.concatenate(smalls + [jnp.zeros((width, PAIR - used), f32)], axis=1).astype(bf16)
+    parts = 8 * n
+    smalls = [a.reshape(parts, -1) for a in (dgain_attn, dshift_attn, db_qkv, db_out, dgain_mlp, dshift_mlp, db_in)]
+    flat = jnp.concatenate(smalls, axis=1).astype(bf16).reshape(parts, -1, PAIR)
+    lines = flat.shape[1]
+    packed = jnp.pad(flat, ((0, 0), (0, width // parts - lines), (0, 0))).reshape(width, PAIR)
     packed = packed.reshape(8, width // 8, PAIR)[order].reshape(2, width // 2, PAIR)
     steps_last = core_step([after(last_send, *steps_first), packed[0]], [last_keep, packed[1]])
     part_first = last_step(steps_first)
@@ -850,10 +847,10 @@
     ends += [ends[-1] + cols, ends[-1] + 2 * cols]
     sum_attn, sum_q, sum_k, sum_v, end_k, end_v, packed = jnp.split(total, ends, axis=1)
     sum_qkv = jnp.concatenate([sum_q, sum_k, end_k, sum_v, end_v], axis=1)
-    packed = packed.astype(f32)
+    packed = packed[:lines].astype(f32).reshape(-1)
     done, at = [], 0
     for a in smalls:
-        done.append(packed[:, at:at + a.shape[1]].reshape(-1))
+        done.append(packed[at:at + a.shape[1]])
         at += a.shape[1]
     return (output[None], grad_inputs[None], done[0], done[1], sum_qkv.astype(f32), done[2], sum_attn.astype(f32),
             done[3], done[4], done[5], sum_in.astype(f32), done[6], sum_out.astype(f32))

time: 552 us -> 525 us (0.951)
  waiting for transfers between devices: 92.4 us -> 70.5 us
  local copies, waits for them, and re-layouts: 21.4 us -> 15.7 us
    ppermute x3, waiting for transfers between devices: 49.2 us -> 32 us  [fast(): far[s] = lax.ppermute(far[s - 1], 'ctx', ring)]
    concatenate x8 -> x1, local copies, waits for them, and re-layouts: 6.77 us -> 0.1 us  [fast(): flat = jnp.concatenate(smalls, axis=1).astype(bf16).reshape(parts, -1, PAIR)]
  transfers between devices with their start and end apart: 40 -> 40, of which waited for: 16 -> 13; matrix products, arithmetic and copies ran while one was open for 5% -> 4% of each run, Pallas kernels for 62% -> 68%
where the time goes in v8:
time: 525 us; the launch traced here: 520 us
  Pallas kernels  356 us (68%)
  waiting for transfers between devices  70.5 us (13%)
  starting transfers between devices  32.8 us (6%)
  other arithmetic  21.7 us (4%)
  local copies, waits for them, and re-layouts  15.7 us (3%)
  between operations  14.8 us (3%)
  blocking collectives  9.2 us (2%)
    pallas_call x3, Pallas kernels, attention(): pl.pallas_call(partial(attention_kernel, half, n), grid=(pairs,), in_spec...  156 us
    pallas_call x1, Pallas kernels, mlp(): pl.pallas_call(mlp_kernel, grid_spec=pltpu.PrefetchScalarGridSpec(num_sca...  75.1 us
    pallas_call x9, Pallas kernels, add_parts(): pl.pallas_call(partial(add_kernel, plan), grid=(steps,), in_specs=[spec(a...  40.6 us
    ppermute x3, waiting for transfers between devices, fast(): far[s] = lax.ppermute(far[s - 1], 'ctx', ring)  32 us
    pallas_call x2, Pallas kernels, qkv(): pl.pallas_call(partial(qkv_kernel, far), grid_spec=pltpu.PrefetchScalarGr...  31.2 us
    pallas_call x1, Pallas kernels, first_tail(): pl.pallas_call(partial(first_kernel, len(dqs)), grid_spec=pltpu.PrefetchS...  23.3 us
    ppermute x25, starting transfers between devices, swap(): return lax.ppermute(a, 'fsdp', pairs_of(bit, 8))  22.9 us
    reduce_scatter x3, waiting for transfers between devices, along(): return lax.psum_scatter(part, 'ctx', scatter_dimension=0, tiled=True)  22.9 us
  transfers between devices with their start and end apart: 40, of which 13 were waited for; matrix products, arithmetic and copies ran while one was open for 4% of the time, Pallas kernels for 68%

profile of v8, /device:TPU:0, one launch (start us, length us, event | category | flops | bytes accessed | tf_op | source)
XLA Modules:
  0.0 520.5 jit_solution(14190575652768086076)
XLA Ops:
  7.2 2.4 pad_maximum_fusion.1
  9.9 3.1 collective-permute-start.3
  13.0 25.2 %collective-permute-done.3.refs_0_ = bf16[512,1024]{1,0:T(8,128)(2,1)S(1)} collective-permute-done((bf16[512,1024]{1,0:T(8,128)(2,1)S(1)}, bf16[512,1024]{1,0:T(8,128)(2,1)S(1)}, u32[]{:S(2)}, u32[]{:S(2)}) %collective-permute-start.3) | collective-permute-done | bytes 1048608 | tf_op jit(solution)/shard_map/ppermute | solution.py:768
  39.1 1.8 collective-permute-start.2
  43.8 2.5 collective-permute-start.4
  46.3 9.2 %all-gather.1 = bf16[8,1,1536]{2,1,0:T(2,128)(2,1)S(1)} all-gather(bf16[1,1,1536]{2,1,0:T(2,128)(2,1)S(1)} %reshape.298), channel_id=2, replica_groups=mesh['fsdp'=8,'ctx'=4] {'fsdp'}, dimensions={0}, use_global_device_ids=true | all-gather | bytes 27648 | tf_op jit(solution)/shard_map/all_gather | solution.py:773
  55.5 6.5 %fusion = (f32[2304,128]{1,0:T(8,128)}, f32[2304,128]{1,0:T(8,128)}, f32[2304,128]{1,0:T(8,128)}) fusion(f32[128]{0:T(128)S(1)} %fusion.5, f32[2304]{0:T(1024)S(1)} %iota_convert_fusion, pred[128]{0:T(512)(128)(4,1)S(1)} %get-tuple-element.251, pred[128]{0:T(512)(128)(4,1)S(1)} %broadcast_compare_fusion.1, pred[128]{0:T(512)(128)(4,1)S(1)} %get-tuple-element.252), kind=kLoop, calls=%fused_computation.3 | loop fusion | flops 1179648 | bytes 3549056 | tf_op jit(solution)/shard_map/jit(_where)/select_n | solution.py:786
  62.0 6.9 %collective-permute-done.4.refs_1_ = bf16[512,1024]{1,0:T(8,128)(2,1)S(1)} collective-permute-done((bf16[512,1024]{1,0:T(8,128)(2,1)S(1)}, bf16[512,1024]{1,0:T(8,128)(2,1)S(1)}, u32[]{:S(2)}, u32[]{:S(2)}) %collective-permute-start.4) | collective-permute-done | bytes 1048608 | tf_op jit(solution)/shard_map/ppermute | solution.py:768
  74.3 14.7 %qkv_own.1 = (bf16[1024,1024]{1,0:T(8,128)(2,1)}, bf16[1024,1024]{1,0:T(8,128)(2,1)}, bf16[1024,1024]{1,0:T(8,128)(2,1)}, bf16[1024,1024]{1,0:T(8,128)(2,1)}) custom-call(s32[4]{0:T(128)} %copy-done.40, s32[8]{0:T(128)} %get-tuple-element.250.order_ref, f32[1,1024]{1,0:T(1,128)} %bitcast.81, f32[1,1024]{1,0:T(1,128)} %bitcast.84, ...), custom_call_target="tpu_custom_call" | custom-call | flops 1048576 | bytes 65536 | tf_op jit(solution)/shard_map/qkv_own/pallas_call | solution.py:276
  89.1 6.1 %spread.1.do_ref = bf16[1024,1024]{1,0:T(8,128)(2,1)} custom-call(bf16[1024,1024]{1,0:T(8,128)(2,1)} %bitcast.58, bf16[1024,4096]{1,0:T(8,128)(2,1)} %all-gather.6.cloned.1.call-done.w_ref.wq_ref.wk_ref.wv_ref), custom_call_target="tpu_custom_call" | custom-call | flops 1048576 | bytes 65536 | tf_op jit(solution)/shard_map/spread/pallas_call | solution.py:499
  96.2 16.5 %kv_remote.1 = (bf16[1536,1024]{1,0:T(8,128)(2,1)}, bf16[1536,1024]{1,0:T(8,128)(2,1)}) custom-call(s32[6]{0:T(128)} %pad_add_fusion.1.spot_ref, s32[8]{0:T(128)} %get-tuple-element.250.order_ref, f32[1,1024]{1,0:T(1,128)} %bitcast.82, f32[1,1024]{1,0:T(1,128)} %bitcast.85, bf16[1024,4096]{1,0:T(8,128)(2,1)} %all-gather.6.cloned.1.call-done.w_ref.wq_ref.wk_ref.wv_ref, ...), custom_call_target="tpu_custom_call" | custom-call | flops 1048576 | bytes 65536 | tf_op jit(solution)/shard_map/kv_remote/pallas_call | solution.py:276
  112.6 76.7 %attention.3 = (bf16[1024,512]{1,0:T(8,128)(2,1)}, bf16[1024,512]{1,0:T(8,128)(2,1)}, bf16[2048,1024]{1,0:T(8,128)(2,1)}, bf16[512,1024]{1,0:T(8,128)(2,1)}) custom-call(f32[4,8]{1,0:T(4,128)} %add_select_fusion.kind_ref, s32[4]{0:T(128)} %compare_select_fusion.3.owner_ref, f32[8,1024]{1,0:T(8,128)} %get-tuple-element.241.cos_ref, ...), custom_call_target="tpu_custom_call" | custom-call | flops 1048576 | bytes 65536 | tf_op jit(solution)/shard_map/attention/pallas_call | solution.py:647
  190.0 75.1 %mlp.1 = (f32[1024,1024]{1,0:T(8,128)}, f32[1024,1024]{1,0:T(8,128)}, bf16[512,4096]{1,0:T(8,128)(2,1)}, bf16[512,4096]{1,0:T(8,128)(2,1)}, bf16[2048,1024]{1,0:...) custom-call(s32[8]{0:T(128)} %get-tuple-element.250.order_ref, ...), custom_call_target="tpu_custom_call" | custom-call | flops 1048576 | bytes 65536 | tf_op jit(solution)/shard_map/mlp/pallas_call | solution.py:202
  265.7 39.7 %attention.4 = (bf16[1024,256]{1,0:T(8,128)(2,1)}, bf16[1024,256]{1,0:T(8,128)(2,1)}, bf16[2048,512]{1,0:T(8,128)(2,1)}, bf16[512,512]{1,0:T(8,128)(2,1)}) custom-call(f32[4,8]{1,0:T(4,128)} %add_select_fusion.kind_ref, s32[4]{0:T(128)} %compare_select_fusion.3.owner_ref, f32[8,1024]{1,0:T(8,128)} %get-tuple-element.241.cos_ref, ...), custom_call_target="tpu_custom_call" | custom-call | flops 1048576 | bytes 65536 | tf_op jit(solution)/shard_map/attention/pallas_call | solution.py:647
  305.5 10.1 %add_parts.9 = (bf16[2,256,1024]{2,1,0:T(8,128)(2,1)}, bf16[2,256,1024]{2,1,0:T(8,128)(2,1)}, bf16[2,256,1024]{2,1,0:T(8,128)(2,1)}, bf16[2,256,1024]{2,1,0:T(8,...) custom-call(bf16[2,2,2,256,1024]{4,3,2,1,0:T(8,128)(2,1)} %bitcast.6, ...), custom_call_target="tpu_custom_call" | custom-call | flops 1 | bytes 65536 | tf_op jit(solution)/shard_map/add_parts/pallas_call | solution.py:679
  319.8 39.7 %attention.5 = (bf16[1024,256]{1,0:T(8,128)(2,1)}, bf16[1024,256]{1,0:T(8,128)(2,1)}, bf16[2048,512]{1,0:T(8,128)(2,1)}, bf16[512,512]{1,0:T(8,128)(2,1)}) custom-call(f32[4,8]{1,0:T(4,128)} %add_select_fusion.kind_ref, s32[4]{0:T(128)} %compare_select_fusion.3.owner_ref, f32[8,1024]{1,0:T(8,128)} %get-tuple-element.241.cos_ref, ...), custom_call_target="tpu_custom_call" | custom-call | flops 1048576 | bytes 65536 | tf_op jit(solution)/shard_map/attention/pallas_call | solution.py:647
  359.5 3.9 collective-permute-done.10.refs_5_
  364.7 6.6 %add_parts.10 = (bf16[256,1024]{1,0:T(8,128)(2,1)}, bf16[256,1024]{1,0:T(8,128)(2,1)}, bf16[256,1024]{1,0:T(8,128)(2,1)}, bf16[256,1024]{1,0:T(8,128)(2,1)}, bf1...) custom-call(bf16[2,256,1024]{2,1,0:T(8,128)(2,1)} %get-tuple-element.146., ...), custom_call_target="tpu_custom_call" | custom-call | flops 1 | bytes 65536 | tf_op jit(solution)/shard_map/add_parts/pallas_call | solution.py:679
  375.4 7.6 %join.1 = bf16[1024,1024]{1,0:T(8,128)(2,1)} custom-call(bf16[1024,1024]{1,0:T(8,128)(2,1)} %bitcast.56, bf16[1024,4096]{1,0:T(8,128)(2,1)} %all-gather.6.cloned.1.call-done.w_ref.wq_ref.wk_ref.wv_ref, f32[1024,1024]{1,0:T(8,128)} %get-tuple-element.134.mlp_ref, f32[1,1024]{1,0:T(1,128)} %bitcast.91, bf16[1024,512]{1,0:T(8,128)(2,1)} %get-tuple-element.125.refs_0_, ...), custom_call_target="tpu_custom_call" | custom-call | flops 12884901888 | bytes 1048576 | tf_op jit(solution)/shard_map/join/pallas_call | solution.py:478
  383.0 23.3 %first_tail.1 = (bf16[512,3072]{1,0:T(8,128)(2,1)}, bf16[512,3072]{1,0:T(8,128)(2,1)}, f32[1024,1024]{1,0:T(8,128)}, f32[1,2048]{1,0:T(1,128)}) custom-call(s32[4]{0:T(128)} %copy-done.40, s32[8]{0:T(128)} %get-tuple-element.250.order_ref, bf16[1024,1024]{1,0:T(8,128)(2,1)} %bitcast.60, bf16[1024,1024]{1,0:T(8,128)(2,1)} %get-tuple-element.159.h_ref, ...), custom_call_target="tpu_custom_call" | custom-call | flops 25769803776 | bytes 1048576 | tf_op jit(solution)/shard_map/first_tail/pallas_call | solution.py:382
  406.4 4.4 add_parts.11
  413.9 5.3 %add_parts.12 = (bf16[2,64,3072]{2,1,0:T(8,128)(2,1)}, bf16[2,64,3072]{2,1,0:T(8,128)(2,1)}, bf16[2,64,3072]{2,1,0:T(8,128)(2,1)}, bf16[2,64,3072]{2,1,0:T(8,128)(2,1)}) custom-call(bf16[2,2,2,64,3072]{4,3,2,1,0:T(8,128)(2,1)} %bitcast.63, bf16[2,2,2,64,3072]{4,3,2,1,0:T(8,128)(2,1)} %bitcast.64), custom_call_target="tpu_custom_call" | custom-call | flops 1 | bytes 65536 | tf_op jit(solution)/shard_map/add_parts/pallas_call | solution.py:679
  421.8 16.0 %last_tail.1 = (f32[1024,1024]{1,0:T(8,128)}, bf16[512,1024]{1,0:T(8,128)(2,1)}, bf16[512,1024]{1,0:T(8,128)(2,1)}, f32[1,1024]{1,0:T(1,128)}, f32[1,1024]{1,0:T(1,128)}, /*index=5*/f32[1,1024]{1,0:T(1,128)}) custom-call(s32[4]{0:T(128)} %copy-done.40, bf16[1024,1024]{1,0:T(8,128)(2,1)} %get-tuple-element.159.h_ref, f32[1,1024]{1,0:T(1,128)} %bitcast.83, ...), custom_call_target="tpu_custom_call" | custom-call | flops 12884901888 | bytes 1048576 | tf_op jit(solution)/shard_map/last_tail/pallas_call | solution.py:445
  440.8 3.9 add_parts.13
  452.1 2.7 add_parts.15
  458.2 2.0 collective-permute-start.26
  460.9 3.6 add_parts.14
  467.2 2.0 add_parts.16
  477.0 1.9 add_parts.17
  478.9 2.0 pad_maximum_fusion
  481.0 1.8 convert_element_type.199
  484.5 22.9 %reduce-scatter.13.cloned.1.call-done = bf16[32,4224]{1,0:T(8,128)(2,1)} async-done(((bf16[128,4224]{1,0:T(8,128)(2,1)}), bf16[32,4224]{1,0:T(8,128)(2,1)}) %reduce-scatter.13.cloned.1.call-update) | async-done | bytes 270352 | tf_op jit(solution)/shard_map/reduce_scatter | solution.py:742
  (233 shorter events, 59.7 us)
Async XLA Ops:
  7.2 67.1 %all-gather.6.cloned.1.call-start = ((), (), s32[]{:S(2)}) async-start(), calls=%async_computation.6 | async-start | bytes 9437184 | tf_op jit(solution)/shard_map/all_gather | solution.py:779
  9.8 180.3 %all-gather.8.cloned.1.call-start = ((), (), s32[]{:S(2)}) async-start(), calls=%async_computation.7 | async-start | bytes 9437184 | tf_op jit(solution)/shard_map/all_gather | solution.py:796
  9.9 28.3 %collective-permute-start.3 = (bf16[512,1024]{1,0:T(8,128)(2,1)S(1)}, bf16[512,1024]{1,0:T(8,128)(2,1)S(1)}, u32[]{:S(2)}, u32[]{:S(2)}) collective-permute-start(bf16[512,1024]{1,0:T(8,128)(2,1)S(1)} %slice_bitcast_fusion), channel_id=1, source_target_pairs={{0,1},{1,2},{2,3},{3,0},{4,5},{5,6},{6,7},{7,4},{8,9},{9,10},{10,1... | collective-permute-start | bytes 3145736 | tf_op jit(solution)/shard_map/ppermute | solution.py:768
  38.2 151.8 %all-gather.10.cloned.1.call-start = ((), (), s32[]{:S(2)}) async-start(), calls=%async_computation.8 | async-start | bytes 9437184 | tf_op jit(solution)/shard_map/all_gather | solution.py:797
  38.9 344.1 %reduce-scatter.7.cloned.1.call-start = ((), (), s32[]{:S(2)}) async-start(), calls=%async_computation.9 | async-start | bytes 5242880 | tf_op jit(solution)/shard_map/reduce_scatter | solution.py:812
  39.1 33.5 %collective-permute-start.2 = (s32[2]{0:T(128)S(1)}, s32[2]{0:T(128)S(1)}, u32[]{:S(2)}, u32[]{:S(2)}) collective-permute-start(s32[2]{0:T(128)S(1)} %bitcast.97), channel_id=1, source_target_pairs={{0,3},{1,0},{2,1},{3,2},{4,7},{5,4},{6,5},{7,6},{8,11},{9,8},{10,9... | collective-permute-start | bytes 32 | tf_op jit(solution)/shard_map/ppermute | solution.py:771
  40.9 31.8 %collective-permute-start.1 = (s32[2]{0:T(128)S(1)}, s32[2]{0:T(128)S(1)}, u32[]{:S(2)}, u32[]{:S(2)}) collective-permute-start(s32[2]{0:T(128)S(1)} %bitcast.98), channel_id=1, source_target_pairs={{0,2},{1,3},{2,0},{3,1},{4,6},{5,7},{6,4},{7,5},{8,10},{9,11},{10,... | collective-permute-start | bytes 32 | tf_op jit(solution)/shard_map/ppermute | solution.py:771
  40.9 31.8 %collective-permute-start = (s32[2]{0:T(128)S(1)}, s32[2]{0:T(128)S(1)}, u32[]{:S(2)}, u32[]{:S(2)}) collective-permute-start(s32[2]{0:T(128)S(1)} %bitcast.99), channel_id=1, source_target_pairs={{0,1},{1,2},{2,3},{3,0},{4,5},{5,6},{6,7},{7,4},{8,9},{9,10},{10,1... | collective-permute-start | bytes 32 | tf_op jit(solution)/shard_map/ppermute | solution.py:771
  43.8 25.1 %collective-permute-start.4 = (bf16[512,1024]{1,0:T(8,128)(2,1)S(1)}, bf16[512,1024]{1,0:T(8,128)(2,1)S(1)}, u32[]{:S(2)}, u32[]{:S(2)}) collective-permute-start(bf16[512,1024]{1,0:T(8,128)(2,1)S(1)} %collective-permute-done.3.refs_0_), channel_id=1, source_target_pairs={{0,1},{1,2},{2,3},{3,0},{4,5},{5,6},{6,7},{7,4},{8,9},{9,10},{10,1... | collective-permute-start | bytes 3145736 | tf_op jit(solution)/shard_map/ppermute | solution.py:768
  68.9 26.3 %collective-permute-start.5 = (bf16[512,1024]{1,0:T(8,128)(2,1)S(1)}, bf16[512,1024]{1,0:T(8,128)(2,1)S(1)}, u32[]{:S(2)}, u32[]{:S(2)}) collective-permute-start(bf16[512,1024]{1,0:T(8,128)(2,1)S(1)} %collective-permute-done.4.refs_1_), channel_id=1, source_target_pairs={{0,1},{1,2},{2,3},{3,0},{4,5},{5,6},{6,7},{7,4},{8,9},{9,10},{10,1... | collective-permute-start | bytes 3145736 | tf_op jit(solution)/shard_map/ppermute | solution.py:768
  189.3 232.4 %reduce-scatter.9.cloned.1.call-start = ((), (), s32[]{:S(2)}) async-start(), calls=%async_computation.10 | async-start | bytes 2621440 | tf_op jit(solution)/shard_map/reduce_scatter | solution.py:812
  265.1 40.4 %collective-permute-start.6 = (bf16[2048,1024]{1,0:T(8,128)(2,1)}, bf16[2048,1024]{1,0:T(8,128)(2,1)}, u32[]{:S(2)}, u32[]{:S(2)}) collective-permute-start(bf16[2048,1024]{1,0:T(8,128)(2,1)} %get-tuple-element.130), channel_id=1, source_target_pairs={{0,4},{4,0},{8,12},{12,8},{16,20},{20,16},{24,28},{28,24},{1,5},{5... | collective-permute-start | bytes 12582920 | tf_op jit(solution)/shard_map/ppermute | solution.py:695
  265.2 40.3 %collective-permute-start.7 = (bf16[512,4096]{1,0:T(8,128)(2,1)}, bf16[512,4096]{1,0:T(8,128)(2,1)}, u32[]{:S(2)}, u32[]{:S(2)}) collective-permute-start(bf16[512,4096]{1,0:T(8,128)(2,1)} %get-tuple-element.132), channel_id=1, source_target_pairs={{0,4},{4,0},{8,12},{12,8},{16,20},{20,16},{24,28},{28,24},{1,5},{5... | collective-permute-start | bytes 12582920 | tf_op jit(solution)/shard_map/ppermute | solution.py:695
  305.4 116.3 %reduce-scatter.11.cloned.1.call-start = ((), (), s32[]{:S(2)}) async-start(), calls=%async_computation.11 | async-start | bytes 2621440 | tf_op jit(solution)/shard_map/reduce_scatter | solution.py:812
  315.6 43.8 %collective-permute-start.8 = (bf16[2,256,1024]{2,1,0:T(8,128)(2,1)}, bf16[2,256,1024]{2,1,0:T(8,128)(2,1)S(1)}, u32[]{:S(2)}, u32[]{:S(2)}) collective-permute-start(bf16[2,256,1024]{2,1,0:T(8,128)(2,1)} %get-tuple-element.137), channel_id=1, source_target_pairs={{0,8},{4,12},{8,0},{12,4},{16,24},{20,28},{24,16},{28,20},{1,9},{5... | collective-permute-start | bytes 3145736 | tf_op jit(solution)/shard_map/ppermute | solution.py:695
  317.1 42.4 %collective-permute-start.9 = (bf16[2,256,1024]{2,1,0:T(8,128)(2,1)}, bf16[2,256,1024]{2,1,0:T(8,128)(2,1)S(1)}, u32[]{:S(2)}, u32[]{:S(2)}) collective-permute-start(bf16[2,256,1024]{2,1,0:T(8,128)(2,1)} %get-tuple-element.138), channel_id=1, source_target_pairs={{0,16},{4,20},{8,24},{12,28},{16,0},{20,4},{24,8},{28,12},{1,17},{... | collective-permute-start | bytes 3145736 | tf_op jit(solution)/shard_map/ppermute | solution.py:695
  318.6 44.9 %collective-permute-start.10 = (bf16[2,64,4096]{2,1,0:T(8,128)(2,1)}, bf16[2,64,4096]{2,1,0:T(8,128)(2,1)S(1)}, u32[]{:S(2)}, u32[]{:S(2)}) collective-permute-start(bf16[2,64,4096]{2,1,0:T(8,128)(2,1)} %get-tuple-element.140), channel_id=1, source_target_pairs={{0,8},{4,12},{8,0},{12,4},{16,24},{20,28},{24,16},{28,20},{1,9},{5... | collective-permute-start | bytes 3145736 | tf_op jit(solution)/shard_map/ppermute | solution.py:695
  319.2 45.5 %collective-permute-start.11 = (bf16[2,64,4096]{2,1,0:T(8,128)(2,1)}, bf16[2,64,4096]{2,1,0:T(8,128)(2,1)}, u32[]{:S(2)}, u32[]{:S(2)}) collective-permute-start(bf16[2,64,4096]{2,1,0:T(8,128)(2,1)} %get-tuple-element.142), channel_id=1, source_target_pairs={{0,16},{4,20},{8,24},{12,28},{16,0},{20,4},{24,8},{28,12},{1,17},{... | collective-permute-start | bytes 3145736 | tf_op jit(solution)/shard_map/ppermute | solution.py:695
  359.4 121.5 %reduce-scatter.17.cloned.1.call-start = ((), (), s32[]{:S(2)}) async-start(), calls=%async_computation.14 | async-start | bytes 1310720 | tf_op jit(solution)/shard_map/reduce_scatter | solution.py:742
  371.3 35.0 %collective-permute-start.12 = (bf16[256,1024]{1,0:T(8,128)(2,1)}, bf16[256,1024]{1,0:T(8,128)(2,1)}, u32[]{:S(2)}, u32[]{:S(2)}) collective-permute-start(bf16[256,1024]{1,0:T(8,128)(2,1)} %get-tuple-element.150), channel_id=1, source_target_pairs={{0,16},{4,20},{8,24},{12,28},{16,0},{20,4},{24,8},{28,12},{1,17},{... | collective-permute-start | bytes 1572872 | tf_op jit(solution)/shard_map/ppermute | solution.py:695
  372.9 33.4 %collective-permute-start.13 = (bf16[256,1024]{1,0:T(8,128)(2,1)}, bf16[256,1024]{1,0:T(8,128)(2,1)}, u32[]{:S(2)}, u32[]{:S(2)}) collective-permute-start(bf16[256,1024]{1,0:T(8,128)(2,1)} %get-tuple-element.152), channel_id=1, source_target_pairs={{0,8},{4,12},{8,0},{12,4},{16,24},{20,28},{24,16},{28,20},{1,9},{5... | collective-permute-start | bytes 1572872 | tf_op jit(solution)/shard_map/ppermute | solution.py:695
  373.8 32.5 %collective-permute-start.14 = (bf16[64,4096]{1,0:T(8,128)(2,1)}, bf16[64,4096]{1,0:T(8,128)(2,1)}, u32[]{:S(2)}, u32[]{:S(2)}) collective-permute-start(bf16[64,4096]{1,0:T(8,128)(2,1)} %get-tuple-element.154), channel_id=1, source_target_pairs={{0,16},{4,20},{8,24},{12,28},{16,0},{20,4},{24,8},{28,12},{1,17},{... | collective-permute-start | bytes 1572872 | tf_op jit(solution)/shard_map/ppermute | solution.py:695
  374.4 32.0 %collective-permute-start.15 = (bf16[64,4096]{1,0:T(8,128)(2,1)}, bf16[64,4096]{1,0:T(8,128)(2,1)}, u32[]{:S(2)}, u32[]{:S(2)}) collective-permute-start(bf16[64,4096]{1,0:T(8,128)(2,1)} %get-tuple-element.156), channel_id=1, source_target_pairs={{0,8},{4,12},{8,0},{12,4},{16,24},{20,28},{24,16},{28,20},{1,9},{5... | collective-permute-start | bytes 1572872 | tf_op jit(solution)/shard_map/ppermute | solution.py:695
  410.8 72.0 %reduce-scatter.15.cloned.1.call-start = ((), (), s32[]{:S(2)}) async-start(), calls=%async_computation.13 | async-start | bytes 1310720 | tf_op jit(solution)/shard_map/reduce_scatter | solution.py:742
  411.6 95.9 %reduce-scatter.13.cloned.1.call-start = ((), (), s32[]{:S(2)}) async-start(), calls=%async_computation.12 | async-start | bytes 1351680 | tf_op jit(solution)/shard_map/reduce_scatter | solution.py:742
  419.2 19.8 %collective-permute-start.17 = (bf16[2,64,3072]{2,1,0:T(8,128)(2,1)}, bf16[2,64,3072]{2,1,0:T(8,128)(2,1)S(1)}, u32[]{:S(2)}, u32[]{:S(2)}) collective-permute-start(bf16[2,64,3072]{2,1,0:T(8,128)(2,1)} %get-tuple-element.175), channel_id=1, source_target_pairs={{0,8},{4,12},{8,0},{12,4},{16,24},{20,28},{24,16},{28,20},{1,9},{5... | collective-permute-start | bytes 2359304 | tf_op jit(solution)/shard_map/ppermute | solution.py:695
  420.3 19.5 %collective-permute-start.18 = (bf16[2,64,3072]{2,1,0:T(8,128)(2,1)}, bf16[2,64,3072]{2,1,0:T(8,128)(2,1)S(1)}, u32[]{:S(2)}, u32[]{:S(2)}) collective-permute-start(bf16[2,64,3072]{2,1,0:T(8,128)(2,1)} %get-tuple-element.177), channel_id=1, source_target_pairs={{0,16},{4,20},{8,24},{12,28},{16,0},{20,4},{24,8},{28,12},{1,17},{... | collective-permute-start | bytes 2359304 | tf_op jit(solution)/shard_map/ppermute | solution.py:695
  446.4 11.8 %collective-permute-start.19 = (bf16[64,3072]{1,0:T(8,128)(2,1)}, bf16[64,3072]{1,0:T(8,128)(2,1)S(1)}, u32[]{:S(2)}, u32[]{:S(2)}) collective-permute-start(bf16[64,3072]{1,0:T(8,128)(2,1)} %get-tuple-element.190), channel_id=1, source_target_pairs={{0,16},{4,20},{8,24},{12,28},{16,0},{20,4},{24,8},{28,12},{1,17},{... | collective-permute-start | bytes 1179656 | tf_op jit(solution)/shard_map/ppermute | solution.py:695
  448.0 12.2 %collective-permute-start.20 = (bf16[64,3072]{1,0:T(8,128)(2,1)}, bf16[64,3072]{1,0:T(8,128)(2,1)S(1)}, u32[]{:S(2)}, u32[]{:S(2)}) collective-permute-start(bf16[64,3072]{1,0:T(8,128)(2,1)} %get-tuple-element.192), channel_id=1, source_target_pairs={{0,8},{4,12},{8,0},{12,4},{16,24},{20,28},{24,16},{28,20},{1,9},{5... | collective-permute-start | bytes 1179656 | tf_op jit(solution)/shard_map/ppermute | solution.py:695
  454.8 11.0 %collective-permute-start.23 = (bf16[2,64,1024]{2,1,0:T(8,128)(2,1)}, bf16[2,64,1024]{2,1,0:T(8,128)(2,1)S(1)}, u32[]{:S(2)}, u32[]{:S(2)}) collective-permute-start(bf16[2,64,1024]{2,1,0:T(8,128)(2,1)} %get-tuple-element.205), channel_id=1, source_target_pairs={{0,8},{4,12},{8,0},{12,4},{16,24},{20,28},{24,16},{28,20},{1,9},{5... | collective-permute-start | bytes 786440 | tf_op jit(solution)/shard_map/ppermute | solution.py:695
  455.8 10.0 %collective-permute-start.24 = (bf16[2,64,1024]{2,1,0:T(8,128)(2,1)}, bf16[2,64,1024]{2,1,0:T(8,128)(2,1)S(1)}, u32[]{:S(2)}, u32[]{:S(2)}) collective-permute-start(bf16[2,64,1024]{2,1,0:T(8,128)(2,1)} %get-tuple-element.208), channel_id=1, source_target_pairs={{0,16},{4,20},{8,24},{12,28},{16,0},{20,4},{24,8},{28,12},{1,17},{... | collective-permute-start | bytes 786440 | tf_op jit(solution)/shard_map/ppermute | solution.py:695
  456.2 9.6 %collective-permute-start.25 = (bf16[2,64,128]{2,1,0:T(8,128)(2,1)}, bf16[2,64,128]{2,1,0:T(8,128)(2,1)S(1)}, u32[]{:S(2)}, u32[]{:S(2)}) collective-permute-start(bf16[2,64,128]{2,1,0:T(8,128)(2,1)} %get-tuple-element.211), channel_id=1, source_target_pairs={{0,8},{4,12},{8,0},{12,4},{16,24},{20,28},{24,16},{28,20},{1,9},{5... | collective-permute-start | bytes 98312 | tf_op jit(solution)/shard_map/ppermute | solution.py:695
  (50 other events, 521.2 us)
Sparse Core Ops, SparseCore 0:
  10.5 57.2 all-gather.5
  69.7 54.4 all-gather.7
  126.1 54.3 all-gather.9
  189.5 77.3 reduce-scatter.6
  305.6 44.5 reduce-scatter.8
  359.6 44.0 reduce-scatter.10
  410.9 26.9 reduce-scatter.16
  440.2 25.8 reduce-scatter.14
  481.1 26.3 reduce-scatter.12

commit v9 on v8

--- a/solution.py
+++ b/solution.py
@@ -530,8 +530,9 @@
             out[:, c * QB:(c + 1) * QB] = refs_in[s][at:at + QB, :].T
         for c in range(per):
             out[:, wide + c * QB:wide + (c + 1) * QB] = refs_in[0][half + c * QB:half + (c + 1) * QB, :].T
-    dka_ref[...] = jnp.zeros_like(dka_ref)
-    dva_ref[...] = jnp.zeros_like(dva_ref)
+    cont = slice(wide, wide + half)
+    dka_ref[cont, :] = jnp.zeros((half, PAIR), f32)
+    dva_ref[cont, :] = jnp.zeros((half, PAIR), f32)
 
 
     def block(qb, carry):
@@ -604,15 +605,21 @@
             lines = slice(h * HD, (h + 1) * HD)
             for c in range(count + 1):
                 dp = mm(keys_of(v_refs, c), d_cols[h], NN)
-                ds_ref[h, cut(c)] = (p_ref[h, cut(c)].astype(f32) * (dp - deltas[h])).astype(bf16)
+                ds_ref[h, cut(c)] = p_ref[h, cut(c)] * (dp - deltas[h]).astype(bf16)
             dq = mm(kt_ref[lines, 0:wide], ds_ref[h, 0:wide], NN) + mm(kt_ref[lines, slot], ds_ref[h, wide:], NN)
             a, b = dq[:ROT // 2], dq[ROT // 2:ROT]
             cosine, sine = cos_ref[:, own], sin_ref[:, own]
             grads.append(jnp.concatenate([a * cosine + b * sine, b * cosine - a * sine, dq[ROT:]], axis=0))
         for c in range(count + 1):
             at = slot if c == count else cut(c)
-            dva_ref[at, :] += mm(p_ref[0, cut(c)], do_heads[0], NN) + mm(p_ref[1, cut(c)], do_heads[1], NN)
-            dka_ref[at, :] += mm(ds_ref[0, cut(c)], q_heads[0], NN) + mm(ds_ref[1, cut(c)], q_heads[1], NN)
+            dv = mm(p_ref[0, cut(c)], do_heads[0], NN) + mm(p_ref[1, cut(c)], do_heads[1], NN)
+            dk = mm(ds_ref[0, cut(c)], q_heads[0], NN) + mm(ds_ref[1, cut(c)], q_heads[1], NN)
+            if c == count:
+                dva_ref[at, :] += dv
+                dka_ref[at, :] += dk
+            else:
+                dva_ref[at, :] = jnp.where(qb == 0, dv, dva_ref[at, :] + dv)
+                dka_ref[at, :] = jnp.where(qb == 0, dk, dka_ref[at, :] + dk)
         o_ref[own, :] = mm(ident, jnp.concatenate(outs, axis=0).astype(bf16), NT).astype(bf16)
         dq_ref[own, :] = mm(ident, (jnp.concatenate(grads, axis=0) * (HD ** (-0.5))).astype(bf16), NT).astype(bf16)
 
@@ -793,8 +800,8 @@
         jnp.concatenate(spots[1:]), order, far[1:], gain_attn, shift_attn, weights, bias_qkv, tables)
     keys, values = (own_keys, far_keys), (own_values, far_values)
     grad_att = spread(grad_out, weights)
-    weight_in = lax.all_gather(after(w_in, far[1]), "fsdp", axis=0, tiled=True)
-    weight_out = lax.all_gather(after(w_out, far[1]), "fsdp", axis=0, tiled=True)
+    weight_in = lax.all_gather(after(w_in, far[1], *full, *tables, cos_t, sin_t), "fsdp", axis=0, tiled=True)
+    weight_out = lax.all_gather(after(w_out, far[1], *full, *tables, cos_t, sin_t), "fsdp", axis=0, tiled=True)
 
     per = half // QB
     earlier = jnp.stack([spots[s][0] < spots[0][0] for s in range(1, n)])
@@ -839,7 +846,7 @@
     lines = flat.shape[1]
     packed = jnp.pad(flat, ((0, 0), (0, width // parts - lines), (0, 0))).reshape(width, PAIR)
     packed = packed.reshape(8, width // 8, PAIR)[order].reshape(2, width // 2, PAIR)
-    steps_last = core_step([after(last_send, *steps_first), packed[0]], [last_keep, packed[1]])
+    steps_last = core_step([last_send, packed[0]], [after(last_keep, *steps_first), packed[1]])
     part_first = last_step(steps_first)
     part_last = last_step(side_step(kept_after(steps_last, *part_first)))
     total = along(jnp.concatenate([*part_first, *part_last], axis=1))

time: 525 us -> 516 us (0.983)
  Pallas kernels: 356 us -> 350 us
    unnamed x94 -> x86, local copies, waits for them, and re-layouts: 10.1 us -> 11 us
  transfers between devices with their start and end apart: 40 -> 40, of which waited for: 13 -> 13; matrix products, arithmetic and copies ran while one was open for 4% -> 5% of each run, Pallas kernels for 68% -> 68%
where the time goes in v9:
time: 516 us; the launch traced here: 512 us
  Pallas kernels  350 us (68%)
  waiting for transfers between devices  68.9 us (13%)
  starting transfers between devices  29.3 us (6%)
  other arithmetic  23.7 us (5%)
  local copies, waits for them, and re-layouts  16.7 us (3%)
  between operations  14.7 us (3%)
  blocking collectives  9.16 us (2%)
    pallas_call x3, Pallas kernels, attention(): pl.pallas_call(partial(attention_kernel, half, n), grid=(pairs,), in_spec...  152 us
    pallas_call x1, Pallas kernels, mlp(): pl.pallas_call(mlp_kernel, grid_spec=pltpu.PrefetchScalarGridSpec(num_sca...  75.1 us
    pallas_call x9, Pallas kernels, add_parts(): pl.pallas_call(partial(add_kernel, plan), grid=(steps,), in_specs=[spec(a...  40 us
    ppermute x3, waiting for transfers between devices, fast(): far[s] = lax.ppermute(far[s - 1], 'ctx', ring)  29.9 us
    pallas_call x2, Pallas kernels, qkv(): pl.pallas_call(partial(qkv_kernel, far), grid_spec=pltpu.PrefetchScalarGr...  29.2 us
    reduce_scatter x3, waiting for transfers between devices, along(): return lax.psum_scatter(part, 'ctx', scatter_dimension=0, tiled=True)  23.5 us
    pallas_call x1, Pallas kernels, first_tail(): pl.pallas_call(partial(first_kernel, len(dqs)), grid_spec=pltpu.PrefetchS...  23.3 us
    ppermute x25, starting transfers between devices, swap(): return lax.ppermute(a, 'fsdp', pairs_of(bit, 8))  20.8 us
  transfers between devices with their start and end apart: 40, of which 13 were waited for; matrix products, arithmetic and copies ran while one was open for 5% of the time, Pallas kernels for 68%

profile of v9, /device:TPU:0, one launch (start us, length us, event | category | flops | bytes accessed | tf_op | source)
XLA Modules:
  0.0 511.9 jit_solution(16253822240757023522)
XLA Ops:
  7.2 2.4 pad_maximum_fusion.1
  9.9 3.1 collective-permute-start.3
  14.2 9.2 %all-gather.1 = bf16[8,1,1536]{2,1,0:T(2,128)(2,1)S(1)} all-gather(bf16[1,1,1536]{2,1,0:T(2,128)(2,1)S(1)} %reshape.319), channel_id=2, replica_groups=mesh['fsdp'=8,'ctx'=4] {'fsdp'}, dimensions={0}, use_global_device_ids=true | all-gather | bytes 27648 | tf_op jit(solution)/shard_map/all_gather | solution.py:780
  24.9 6.5 %fusion = (f32[2304,128]{1,0:T(8,128)}, f32[2304,128]{1,0:T(8,128)}, f32[2304,128]{1,0:T(8,128)}) fusion(f32[128]{0:T(128)S(1)} %fusion.11, f32[2304]{0:T(1024)S(1)} %iota_convert_fusion, pred[128]{0:T(512)(128)(4,1)S(1)} %get-tuple-element.260, pred[128]{0:T(512)(128)(4,1)S(1)} %broadcast_compare_fusion.1, pred[128]{0:T(512)(128)(4,1)S(1)} %get-tuple-element.261), kind=kLoop, calls=%fused_computation.3 | loop fusion | flops 1179648 | bytes 3549056 | tf_op jit(solution)/shard_map/jit(_where)/select_n | solution.py:793
  31.4 6.7 %collective-permute-done.3.refs_0_ = bf16[512,1024]{1,0:T(8,128)(2,1)S(1)} collective-permute-done((bf16[512,1024]{1,0:T(8,128)(2,1)S(1)}, bf16[512,1024]{1,0:T(8,128)(2,1)S(1)}, u32[]{:S(2)}, u32[]{:S(2)}) %collective-permute-start.3) | collective-permute-done | bytes 1048608 | tf_op jit(solution)/shard_map/ppermute | solution.py:775
  39.1 3.9 collective-permute-start.2
  43.6 21.5 %collective-permute-done.4.refs_1_ = bf16[512,1024]{1,0:T(8,128)(2,1)S(1)} collective-permute-done((bf16[512,1024]{1,0:T(8,128)(2,1)S(1)}, bf16[512,1024]{1,0:T(8,128)(2,1)S(1)}, u32[]{:S(2)}, u32[]{:S(2)}) %collective-permute-start.4) | collective-permute-done | bytes 1048608 | tf_op jit(solution)/shard_map/ppermute | solution.py:775
  69.0 14.0 %qkv_own.1 = (bf16[1024,1024]{1,0:T(8,128)(2,1)}, bf16[1024,1024]{1,0:T(8,128)(2,1)}, bf16[1024,1024]{1,0:T(8,128)(2,1)}, bf16[1024,1024]{1,0:T(8,128)(2,1)}) custom-call(s32[4]{0:T(128)} %copy-done.37, s32[8]{0:T(128)} %get-tuple-element.259.order_ref, f32[1,1024]{1,0:T(1,128)} %bitcast.94, f32[1,1024]{1,0:T(1,128)} %bitcast.97, ...), custom_call_target="tpu_custom_call" | custom-call | flops 1048576 | bytes 65536 | tf_op jit(solution)/shard_map/qkv_own/pallas_call | solution.py:276
  83.0 6.1 %spread.1.do_ref = bf16[1024,1024]{1,0:T(8,128)(2,1)} custom-call(bf16[1024,1024]{1,0:T(8,128)(2,1)} %bitcast.71, bf16[1024,4096]{1,0:T(8,128)(2,1)} %all-gather.6.cloned.1.call-done.w_ref.wq_ref.wk_ref.wv_ref), custom_call_target="tpu_custom_call" | custom-call | flops 1048576 | bytes 65536 | tf_op jit(solution)/shard_map/spread/pallas_call | solution.py:499
  91.8 15.2 %kv_remote.1 = (bf16[1536,1024]{1,0:T(8,128)(2,1)}, bf16[1536,1024]{1,0:T(8,128)(2,1)}) custom-call(s32[6]{0:T(128)} %pad_add_fusion.1.spot_ref, s32[8]{0:T(128)} %get-tuple-element.259.order_ref, f32[1,1024]{1,0:T(1,128)} %bitcast.95, f32[1,1024]{1,0:T(1,128)} %bitcast.98, bf16[1024,4096]{1,0:T(8,128)(2,1)} %all-gather.6.cloned.1.call-done.w_ref.wq_ref.wk_ref.wv_ref, ...), custom_call_target="tpu_custom_call" | custom-call | flops 1048576 | bytes 65536 | tf_op jit(solution)/shard_map/kv_remote/pallas_call | solution.py:276
  107.0 74.8 %attention.3 = (bf16[1024,512]{1,0:T(8,128)(2,1)}, bf16[1024,512]{1,0:T(8,128)(2,1)}, bf16[2048,1024]{1,0:T(8,128)(2,1)}, bf16[512,1024]{1,0:T(8,128)(2,1)}) custom-call(f32[4,8]{1,0:T(4,128)} %add_select_fusion.kind_ref, s32[4]{0:T(128)} %compare_select_fusion.3.owner_ref, f32[8,1024]{1,0:T(8,128)} %get-tuple-element.250.cos_ref, ...), custom_call_target="tpu_custom_call" | custom-call | flops 1048576 | bytes 65536 | tf_op jit(solution)/shard_map/attention/pallas_call | solution.py:654
  182.5 75.1 %mlp.1 = (f32[1024,1024]{1,0:T(8,128)}, f32[1024,1024]{1,0:T(8,128)}, bf16[512,4096]{1,0:T(8,128)(2,1)}, bf16[512,4096]{1,0:T(8,128)(2,1)}, bf16[2048,1024]{1,0:...) custom-call(s32[8]{0:T(128)} %get-tuple-element.259.order_ref, ...), custom_call_target="tpu_custom_call" | custom-call | flops 1048576 | bytes 65536 | tf_op jit(solution)/shard_map/mlp/pallas_call | solution.py:202
  258.2 38.8 %attention.4 = (bf16[1024,256]{1,0:T(8,128)(2,1)}, bf16[1024,256]{1,0:T(8,128)(2,1)}, bf16[2048,512]{1,0:T(8,128)(2,1)}, bf16[512,512]{1,0:T(8,128)(2,1)}) custom-call(f32[4,8]{1,0:T(4,128)} %add_select_fusion.kind_ref, s32[4]{0:T(128)} %compare_select_fusion.3.owner_ref, f32[8,1024]{1,0:T(8,128)} %get-tuple-element.250.cos_ref, ...), custom_call_target="tpu_custom_call" | custom-call | flops 1048576 | bytes 65536 | tf_op jit(solution)/shard_map/attention/pallas_call | solution.py:654
  297.1 9.7 %add_parts.9 = (bf16[2,256,1024]{2,1,0:T(8,128)(2,1)}, bf16[2,256,1024]{2,1,0:T(8,128)(2,1)}, bf16[2,256,1024]{2,1,0:T(8,128)(2,1)}, bf16[2,256,1024]{2,1,0:T(8,...) custom-call(bf16[2,2,2,256,1024]{4,3,2,1,0:T(8,128)(2,1)} %bitcast.7, ...), custom_call_target="tpu_custom_call" | custom-call | flops 1 | bytes 65536 | tf_op jit(solution)/shard_map/add_parts/pallas_call | solution.py:686
  310.9 38.7 %attention.5 = (bf16[1024,256]{1,0:T(8,128)(2,1)}, bf16[1024,256]{1,0:T(8,128)(2,1)}, bf16[2048,512]{1,0:T(8,128)(2,1)}, bf16[512,512]{1,0:T(8,128)(2,1)}) custom-call(f32[4,8]{1,0:T(4,128)} %add_select_fusion.kind_ref, s32[4]{0:T(128)} %compare_select_fusion.3.owner_ref, f32[8,1024]{1,0:T(8,128)} %get-tuple-element.250.cos_ref, ...), custom_call_target="tpu_custom_call" | custom-call | flops 1048576 | bytes 65536 | tf_op jit(solution)/shard_map/attention/pallas_call | solution.py:654
  349.8 5.0 collective-permute-done.10.refs_5_
  355.9 6.4 %add_parts.10 = (bf16[256,1024]{1,0:T(8,128)(2,1)}, bf16[256,1024]{1,0:T(8,128)(2,1)}, bf16[256,1024]{1,0:T(8,128)(2,1)}, bf16[256,1024]{1,0:T(8,128)(2,1)}, bf1...) custom-call(bf16[2,256,1024]{2,1,0:T(8,128)(2,1)} %get-tuple-element.146., ...), custom_call_target="tpu_custom_call" | custom-call | flops 1 | bytes 65536 | tf_op jit(solution)/shard_map/add_parts/pallas_call | solution.py:686
  366.4 7.6 %join.1 = bf16[1024,1024]{1,0:T(8,128)(2,1)} custom-call(bf16[1024,1024]{1,0:T(8,128)(2,1)} %bitcast.69, bf16[1024,4096]{1,0:T(8,128)(2,1)} %all-gather.6.cloned.1.call-done.w_ref.wq_ref.wk_ref.wv_ref, f32[1024,1024]{1,0:T(8,128)} %get-tuple-element.134.mlp_ref, f32[1,1024]{1,0:T(1,128)} %bitcast.104, bf16[1024,512]{1,0:T(8,128)(2,1)} %get-tuple-element.125.refs_0_, ...), custom_call_target="tpu_custom_call" | custom-call | flops 12884901888 | bytes 1048576 | tf_op jit(solution)/shard_map/join/pallas_call | solution.py:478
  374.0 23.3 %first_tail.1 = (bf16[512,3072]{1,0:T(8,128)(2,1)}, bf16[512,3072]{1,0:T(8,128)(2,1)}, f32[1024,1024]{1,0:T(8,128)}, f32[1,2048]{1,0:T(1,128)}) custom-call(s32[4]{0:T(128)} %copy-done.37, s32[8]{0:T(128)} %get-tuple-element.259.order_ref, bf16[1024,1024]{1,0:T(8,128)(2,1)} %bitcast.73, bf16[1024,1024]{1,0:T(8,128)(2,1)} %get-tuple-element.159.h_ref, ...), custom_call_target="tpu_custom_call" | custom-call | flops 25769803776 | bytes 1048576 | tf_op jit(solution)/shard_map/first_tail/pallas_call | solution.py:382
  397.4 4.4 add_parts.11
  404.9 5.3 %add_parts.12 = (bf16[2,64,3072]{2,1,0:T(8,128)(2,1)}, bf16[2,64,3072]{2,1,0:T(8,128)(2,1)}, bf16[2,64,3072]{2,1,0:T(8,128)(2,1)}, bf16[2,64,3072]{2,1,0:T(8,128)(2,1)}) custom-call(bf16[2,2,2,64,3072]{4,3,2,1,0:T(8,128)(2,1)} %bitcast.76, bf16[2,2,2,64,3072]{4,3,2,1,0:T(8,128)(2,1)} %bitcast.77), custom_call_target="tpu_custom_call" | custom-call | flops 1 | bytes 65536 | tf_op jit(solution)/shard_map/add_parts/pallas_call | solution.py:686
  412.9 16.0 %last_tail.1 = (f32[1024,1024]{1,0:T(8,128)}, bf16[512,1024]{1,0:T(8,128)(2,1)}, bf16[512,1024]{1,0:T(8,128)(2,1)}, f32[1,1024]{1,0:T(1,128)}, f32[1,1024]{1,0:T(1,128)}, /*index=5*/f32[1,1024]{1,0:T(1,128)}) custom-call(s32[4]{0:T(128)} %copy-done.37, bf16[1024,1024]{1,0:T(8,128)(2,1)} %get-tuple-element.159.h_ref, f32[1,1024]{1,0:T(1,128)} %bitcast.96, ...), custom_call_target="tpu_custom_call" | custom-call | flops 12884901888 | bytes 1048576 | tf_op jit(solution)/shard_map/last_tail/pallas_call | solution.py:445
  434.4 4.0 add_parts.13
  442.8 2.7 add_parts.15
  452.0 3.6 add_parts.14
  458.1 2.0 add_parts.16
  464.2 2.3 collective-permute-done.29.refs_5_
  467.9 1.9 add_parts.17
  469.7 2.0 pad_maximum_fusion
  471.8 1.8 convert_element_type.272
  473.6 1.8 convert_element_type.271
  475.4 23.5 %reduce-scatter.13.cloned.1.call-done = bf16[32,4224]{1,0:T(8,128)(2,1)} async-done(((bf16[128,4224]{1,0:T(8,128)(2,1)}), bf16[32,4224]{1,0:T(8,128)(2,1)}) %reduce-scatter.13.cloned.1.call-update) | async-done | bytes 270352 | tf_op jit(solution)/shard_map/reduce_scatter | solution.py:749
  (225 shorter events, 58.1 us)
Async XLA Ops:
  7.2 61.8 %all-gather.6.cloned.1.call-start = ((), (), s32[]{:S(2)}) async-start(), calls=%async_computation.6 | async-start | bytes 9437184 | tf_op jit(solution)/shard_map/all_gather | solution.py:786
  9.7 172.8 %all-gather.10.cloned.1.call-start = ((), (), s32[]{:S(2)}) async-start(), calls=%async_computation.8 | async-start | bytes 9437184 | tf_op jit(solution)/shard_map/all_gather | solution.py:804
  9.9 28.3 %collective-permute-start.3 = (bf16[512,1024]{1,0:T(8,128)(2,1)S(1)}, bf16[512,1024]{1,0:T(8,128)(2,1)S(1)}, u32[]{:S(2)}, u32[]{:S(2)}) collective-permute-start(bf16[512,1024]{1,0:T(8,128)(2,1)S(1)} %slice_bitcast_fusion), channel_id=1, source_target_pairs={{0,1},{1,2},{2,3},{3,0},{4,5},{5,6},{6,7},{7,4},{8,9},{9,10},{10,1... | collective-permute-start | bytes 3145736 | tf_op jit(solution)/shard_map/ppermute | solution.py:775
  38.1 144.4 %all-gather.8.cloned.1.call-start = ((), (), s32[]{:S(2)}) async-start(), calls=%async_computation.7 | async-start | bytes 9437184 | tf_op jit(solution)/shard_map/all_gather | solution.py:803
  38.9 335.1 %reduce-scatter.7.cloned.1.call-start = ((), (), s32[]{:S(2)}) async-start(), calls=%async_computation.9 | async-start | bytes 5242880 | tf_op jit(solution)/shard_map/reduce_scatter | solution.py:819
  38.9 26.2 %collective-permute-start.4 = (bf16[512,1024]{1,0:T(8,128)(2,1)S(1)}, bf16[512,1024]{1,0:T(8,128)(2,1)S(1)}, u32[]{:S(2)}, u32[]{:S(2)}) collective-permute-start(bf16[512,1024]{1,0:T(8,128)(2,1)S(1)} %collective-permute-done.3.refs_0_), channel_id=1, source_target_pairs={{0,1},{1,2},{2,3},{3,0},{4,5},{5,6},{6,7},{7,4},{8,9},{9,10},{10,1... | collective-permute-start | bytes 3145736 | tf_op jit(solution)/shard_map/ppermute | solution.py:775
  39.1 28.2 %collective-permute-start.2 = (s32[2]{0:T(128)S(1)}, s32[2]{0:T(128)S(1)}, u32[]{:S(2)}, u32[]{:S(2)}) collective-permute-start(s32[2]{0:T(128)S(1)} %bitcast.110), channel_id=1, source_target_pairs={{0,3},{1,0},{2,1},{3,2},{4,7},{5,4},{6,5},{7,6},{8,11},{9,8},{10,9... | collective-permute-start | bytes 32 | tf_op jit(solution)/shard_map/ppermute | solution.py:778
  43.0 24.4 %collective-permute-start.1 = (s32[2]{0:T(128)S(1)}, s32[2]{0:T(128)S(1)}, u32[]{:S(2)}, u32[]{:S(2)}) collective-permute-start(s32[2]{0:T(128)S(1)} %bitcast.111), channel_id=1, source_target_pairs={{0,2},{1,3},{2,0},{3,1},{4,6},{5,7},{6,4},{7,5},{8,10},{9,11},{10,... | collective-permute-start | bytes 32 | tf_op jit(solution)/shard_map/ppermute | solution.py:778
  43.0 24.5 %collective-permute-start = (s32[2]{0:T(128)S(1)}, s32[2]{0:T(128)S(1)}, u32[]{:S(2)}, u32[]{:S(2)}) collective-permute-start(s32[2]{0:T(128)S(1)} %bitcast.112), channel_id=1, source_target_pairs={{0,1},{1,2},{2,3},{3,0},{4,5},{5,6},{6,7},{7,4},{8,9},{9,10},{10,1... | collective-permute-start | bytes 32 | tf_op jit(solution)/shard_map/ppermute | solution.py:778
  65.2 25.7 %collective-permute-start.5 = (bf16[512,1024]{1,0:T(8,128)(2,1)S(1)}, bf16[512,1024]{1,0:T(8,128)(2,1)S(1)}, u32[]{:S(2)}, u32[]{:S(2)}) collective-permute-start(bf16[512,1024]{1,0:T(8,128)(2,1)S(1)} %collective-permute-done.4.refs_1_), channel_id=1, source_target_pairs={{0,1},{1,2},{2,3},{3,0},{4,5},{5,6},{6,7},{7,4},{8,9},{9,10},{10,1... | collective-permute-start | bytes 3145736 | tf_op jit(solution)/shard_map/ppermute | solution.py:775
  181.8 231.0 %reduce-scatter.9.cloned.1.call-start = ((), (), s32[]{:S(2)}) async-start(), calls=%async_computation.10 | async-start | bytes 2621440 | tf_op jit(solution)/shard_map/reduce_scatter | solution.py:819
  257.6 39.4 %collective-permute-start.6 = (bf16[2048,1024]{1,0:T(8,128)(2,1)}, bf16[2048,1024]{1,0:T(8,128)(2,1)}, u32[]{:S(2)}, u32[]{:S(2)}) collective-permute-start(bf16[2048,1024]{1,0:T(8,128)(2,1)} %get-tuple-element.130), channel_id=1, source_target_pairs={{0,4},{4,0},{8,12},{12,8},{16,20},{20,16},{24,28},{28,24},{1,5},{5... | collective-permute-start | bytes 12582920 | tf_op jit(solution)/shard_map/ppermute | solution.py:702
  257.7 39.4 %collective-permute-start.7 = (bf16[512,4096]{1,0:T(8,128)(2,1)}, bf16[512,4096]{1,0:T(8,128)(2,1)}, u32[]{:S(2)}, u32[]{:S(2)}) collective-permute-start(bf16[512,4096]{1,0:T(8,128)(2,1)} %get-tuple-element.132), channel_id=1, source_target_pairs={{0,4},{4,0},{8,12},{12,8},{16,20},{20,16},{24,28},{28,24},{1,5},{5... | collective-permute-start | bytes 12582920 | tf_op jit(solution)/shard_map/ppermute | solution.py:702
  297.0 115.9 %reduce-scatter.11.cloned.1.call-start = ((), (), s32[]{:S(2)}) async-start(), calls=%async_computation.11 | async-start | bytes 2621440 | tf_op jit(solution)/shard_map/reduce_scatter | solution.py:819
  306.8 42.9 %collective-permute-start.8 = (bf16[2,256,1024]{2,1,0:T(8,128)(2,1)}, bf16[2,256,1024]{2,1,0:T(8,128)(2,1)S(1)}, u32[]{:S(2)}, u32[]{:S(2)}) collective-permute-start(bf16[2,256,1024]{2,1,0:T(8,128)(2,1)} %get-tuple-element.137), channel_id=1, source_target_pairs={{0,8},{4,12},{8,0},{12,4},{16,24},{20,28},{24,16},{28,20},{1,9},{5... | collective-permute-start | bytes 3145736 | tf_op jit(solution)/shard_map/ppermute | solution.py:702
  308.2 41.6 %collective-permute-start.9 = (bf16[2,256,1024]{2,1,0:T(8,128)(2,1)}, bf16[2,256,1024]{2,1,0:T(8,128)(2,1)S(1)}, u32[]{:S(2)}, u32[]{:S(2)}) collective-permute-start(bf16[2,256,1024]{2,1,0:T(8,128)(2,1)} %get-tuple-element.138), channel_id=1, source_target_pairs={{0,16},{4,20},{8,24},{12,28},{16,0},{20,4},{24,8},{28,12},{1,17},{... | collective-permute-start | bytes 3145736 | tf_op jit(solution)/shard_map/ppermute | solution.py:702
  309.7 45.0 %collective-permute-start.10 = (bf16[2,64,4096]{2,1,0:T(8,128)(2,1)}, bf16[2,64,4096]{2,1,0:T(8,128)(2,1)S(1)}, u32[]{:S(2)}, u32[]{:S(2)}) collective-permute-start(bf16[2,64,4096]{2,1,0:T(8,128)(2,1)} %get-tuple-element.140), channel_id=1, source_target_pairs={{0,8},{4,12},{8,0},{12,4},{16,24},{20,28},{24,16},{28,20},{1,9},{5... | collective-permute-start | bytes 3145736 | tf_op jit(solution)/shard_map/ppermute | solution.py:702
  310.3 45.6 %collective-permute-start.11 = (bf16[2,64,4096]{2,1,0:T(8,128)(2,1)}, bf16[2,64,4096]{2,1,0:T(8,128)(2,1)}, u32[]{:S(2)}, u32[]{:S(2)}) collective-permute-start(bf16[2,64,4096]{2,1,0:T(8,128)(2,1)} %get-tuple-element.142), channel_id=1, source_target_pairs={{0,16},{4,20},{8,24},{12,28},{16,0},{20,4},{24,8},{28,12},{1,17},{... | collective-permute-start | bytes 3145736 | tf_op jit(solution)/shard_map/ppermute | solution.py:702
  349.7 122.1 %reduce-scatter.17.cloned.1.call-start = ((), (), s32[]{:S(2)}) async-start(), calls=%async_computation.14 | async-start | bytes 1310720 | tf_op jit(solution)/shard_map/reduce_scatter | solution.py:749
  362.3 35.1 %collective-permute-start.12 = (bf16[256,1024]{1,0:T(8,128)(2,1)}, bf16[256,1024]{1,0:T(8,128)(2,1)}, u32[]{:S(2)}, u32[]{:S(2)}) collective-permute-start(bf16[256,1024]{1,0:T(8,128)(2,1)} %get-tuple-element.150), channel_id=1, source_target_pairs={{0,16},{4,20},{8,24},{12,28},{16,0},{20,4},{24,8},{28,12},{1,17},{... | collective-permute-start | bytes 1572872 | tf_op jit(solution)/shard_map/ppermute | solution.py:702
  363.9 33.5 %collective-permute-start.13 = (bf16[256,1024]{1,0:T(8,128)(2,1)}, bf16[256,1024]{1,0:T(8,128)(2,1)}, u32[]{:S(2)}, u32[]{:S(2)}) collective-permute-start(bf16[256,1024]{1,0:T(8,128)(2,1)} %get-tuple-element.152), channel_id=1, source_target_pairs={{0,8},{4,12},{8,0},{12,4},{16,24},{20,28},{24,16},{28,20},{1,9},{5... | collective-permute-start | bytes 1572872 | tf_op jit(solution)/shard_map/ppermute | solution.py:702
  365.0 32.4 %collective-permute-start.14 = (bf16[64,4096]{1,0:T(8,128)(2,1)}, bf16[64,4096]{1,0:T(8,128)(2,1)}, u32[]{:S(2)}, u32[]{:S(2)}) collective-permute-start(bf16[64,4096]{1,0:T(8,128)(2,1)} %get-tuple-element.154), channel_id=1, source_target_pairs={{0,16},{4,20},{8,24},{12,28},{16,0},{20,4},{24,8},{28,12},{1,17},{... | collective-permute-start | bytes 1572872 | tf_op jit(solution)/shard_map/ppermute | solution.py:702
  365.5 31.9 %collective-permute-start.15 = (bf16[64,4096]{1,0:T(8,128)(2,1)}, bf16[64,4096]{1,0:T(8,128)(2,1)}, u32[]{:S(2)}, u32[]{:S(2)}) collective-permute-start(bf16[64,4096]{1,0:T(8,128)(2,1)} %get-tuple-element.156), channel_id=1, source_target_pairs={{0,8},{4,12},{8,0},{12,4},{16,24},{20,28},{24,16},{28,20},{1,9},{5... | collective-permute-start | bytes 1572872 | tf_op jit(solution)/shard_map/ppermute | solution.py:702
  401.8 71.8 %reduce-scatter.15.cloned.1.call-start = ((), (), s32[]{:S(2)}) async-start(), calls=%async_computation.13 | async-start | bytes 1310720 | tf_op jit(solution)/shard_map/reduce_scatter | solution.py:749
  402.6 96.3 %reduce-scatter.13.cloned.1.call-start = ((), (), s32[]{:S(2)}) async-start(), calls=%async_computation.12 | async-start | bytes 1351680 | tf_op jit(solution)/shard_map/reduce_scatter | solution.py:749
  410.2 22.4 %collective-permute-start.17 = (bf16[2,64,3072]{2,1,0:T(8,128)(2,1)}, bf16[2,64,3072]{2,1,0:T(8,128)(2,1)S(1)}, u32[]{:S(2)}, u32[]{:S(2)}) collective-permute-start(bf16[2,64,3072]{2,1,0:T(8,128)(2,1)} %get-tuple-element.175), channel_id=1, source_target_pairs={{0,8},{4,12},{8,0},{12,4},{16,24},{20,28},{24,16},{28,20},{1,9},{5... | collective-permute-start | bytes 2359304 | tf_op jit(solution)/shard_map/ppermute | solution.py:702
  411.4 21.3 %collective-permute-start.18 = (bf16[2,64,3072]{2,1,0:T(8,128)(2,1)}, bf16[2,64,3072]{2,1,0:T(8,128)(2,1)S(1)}, u32[]{:S(2)}, u32[]{:S(2)}) collective-permute-start(bf16[2,64,3072]{2,1,0:T(8,128)(2,1)} %get-tuple-element.177), channel_id=1, source_target_pairs={{0,16},{4,20},{8,24},{12,28},{16,0},{20,4},{24,8},{28,12},{1,17},{... | collective-permute-start | bytes 2359304 | tf_op jit(solution)/shard_map/ppermute | solution.py:702
  428.9 12.9 %collective-permute-start.21 = (bf16[512,1024]{1,0:T(8,128)(2,1)}, bf16[512,1024]{1,0:T(8,128)(2,1)S(1)}, u32[]{:S(2)}, u32[]{:S(2)}) collective-permute-start(bf16[512,1024]{1,0:T(8,128)(2,1)} %get-tuple-element.186), channel_id=1, source_target_pairs={{0,4},{4,0},{8,12},{12,8},{16,20},{20,16},{24,28},{28,24},{1,5},{5... | collective-permute-start | bytes 3145736 | tf_op jit(solution)/shard_map/ppermute | solution.py:702
  438.4 12.1 %collective-permute-start.19 = (bf16[64,3072]{1,0:T(8,128)(2,1)}, bf16[64,3072]{1,0:T(8,128)(2,1)S(1)}, u32[]{:S(2)}, u32[]{:S(2)}) collective-permute-start(bf16[64,3072]{1,0:T(8,128)(2,1)} %get-tuple-element.190), channel_id=1, source_target_pairs={{0,16},{4,20},{8,24},{12,28},{16,0},{20,4},{24,8},{28,12},{1,17},{... | collective-permute-start | bytes 1179656 | tf_op jit(solution)/shard_map/ppermute | solution.py:702
  438.9 12.2 %collective-permute-start.20 = (bf16[64,3072]{1,0:T(8,128)(2,1)}, bf16[64,3072]{1,0:T(8,128)(2,1)S(1)}, u32[]{:S(2)}, u32[]{:S(2)}) collective-permute-start(bf16[64,3072]{1,0:T(8,128)(2,1)} %get-tuple-element.192), channel_id=1, source_target_pairs={{0,8},{4,12},{8,0},{12,4},{16,24},{20,28},{24,16},{28,20},{1,9},{5... | collective-permute-start | bytes 1179656 | tf_op jit(solution)/shard_map/ppermute | solution.py:702
  445.5 11.2 %collective-permute-start.23 = (bf16[2,64,1024]{2,1,0:T(8,128)(2,1)}, bf16[2,64,1024]{2,1,0:T(8,128)(2,1)S(1)}, u32[]{:S(2)}, u32[]{:S(2)}) collective-permute-start(bf16[2,64,1024]{2,1,0:T(8,128)(2,1)} %get-tuple-element.205), channel_id=1, source_target_pairs={{0,8},{4,12},{8,0},{12,4},{16,24},{20,28},{24,16},{28,20},{1,9},{5... | collective-permute-start | bytes 786440 | tf_op jit(solution)/shard_map/ppermute | solution.py:702
  446.7 10.0 %collective-permute-start.24 = (bf16[2,64,1024]{2,1,0:T(8,128)(2,1)}, bf16[2,64,1024]{2,1,0:T(8,128)(2,1)S(1)}, u32[]{:S(2)}, u32[]{:S(2)}) collective-permute-start(bf16[2,64,1024]{2,1,0:T(8,128)(2,1)} %get-tuple-element.208), channel_id=1, source_target_pairs={{0,16},{4,20},{8,24},{12,28},{16,0},{20,4},{24,8},{28,12},{1,17},{... | collective-permute-start | bytes 786440 | tf_op jit(solution)/shard_map/ppermute | solution.py:702
  (46 other events, 331.7 us)
Sparse Core Ops, SparseCore 0:
  10.5 57.0 all-gather.5
  69.5 54.5 all-gather.9
  125.9 54.2 all-gather.7
  182.4 76.7 reduce-scatter.6
  297.1 43.3 reduce-scatter.8
  349.8 43.3 reduce-scatter.10
  402.0 26.7 reduce-scatter.16
  431.0 25.7 reduce-scatter.14
  471.9 26.9 reduce-scatter.12

commit v10 on v9

--- a/solution.py
+++ b/solution.py
@@ -822,9 +822,9 @@
     attend(0, 4, ())
     mlp_out, grad_mlp, in_send, in_keep, out_send, out_keep, db_in, db_out, dgain_mlp, dshift_mlp = mlp(
         order, after(x, *attended), grad_out, gain_mlp, shift_mlp, weight_in, bias_in, weight_out)
-    attend(4, 2, (mlp_out,))
+    attend(4, 1, (mlp_out,))
     steps_mlp = core_step([out_send, in_send], [out_keep, in_keep])
-    attend(6, 2, (*attended, *steps_mlp))
+    attend(5, 3, (*attended, *steps_mlp))
     steps_mlp = side_step(kept_after(steps_mlp, *attended))
     output = join(after(x, *steps_mlp), attended, weights, mlp_out, bias_out)
     first_send, first_keep, grad_heads, db_first = first_tail(

time: 516 us -> 514 us (level)
  waiting for transfers between devices: 68.9 us -> 62.2 us
    ppermute x25, waiting for transfers between devices: 14 us -> 7.18 us  [swap(): return lax.ppermute(a, 'fsdp', pairs_of(bit, 8))]
  transfers between devices with their start and end apart: 40 -> 40, of which waited for: 13 -> 11; matrix products, arithmetic and copies ran while one was open for 5% -> 5% of each run, Pallas kernels for 68% -> 69%
where the time goes in v10:
time: 514 us; the launch traced here: 509 us
  Pallas kernels  350 us (68%)
  waiting for transfers between devices  62.2 us (12%)
  starting transfers between devices  31.6 us (6%)
  other arithmetic  23.7 us (5%)
  local copies, waits for them, and re-layouts  18.2 us (4%)
  between operations  14.7 us (3%)
  blocking collectives  9.16 us (2%)
    pallas_call x3, Pallas kernels, attention(): pl.pallas_call(partial(attention_kernel, half, n), grid=(pairs,), in_spec...  152 us
    pallas_call x1, Pallas kernels, mlp(): pl.pallas_call(mlp_kernel, grid_spec=pltpu.PrefetchScalarGridSpec(num_sca...  75.1 us
    pallas_call x9, Pallas kernels, add_parts(): pl.pallas_call(partial(add_kernel, plan), grid=(steps,), in_specs=[spec(a...  39.9 us
    ppermute x3, waiting for transfers between devices, fast(): far[s] = lax.ppermute(far[s - 1], 'ctx', ring)  29.9 us
    pallas_call x2, Pallas kernels, qkv(): pl.pallas_call(partial(qkv_kernel, far), grid_spec=pltpu.PrefetchScalarGr...  29.2 us
    pallas_call x1, Pallas kernels, first_tail(): pl.pallas_call(partial(first_kernel, len(dqs)), grid_spec=pltpu.PrefetchS...  23.3 us
    ppermute x25, starting transfers between devices, swap(): return lax.ppermute(a, 'fsdp', pairs_of(bit, 8))  23.1 us
    reduce_scatter x3, waiting for transfers between devices, along(): return lax.psum_scatter(part, 'ctx', scatter_dimension=0, tiled=True)  22.7 us
  transfers between devices with their start and end apart: 40, of which 11 were waited for; matrix products, arithmetic and copies ran while one was open for 5% of the time, Pallas kernels for 69%

profile of v10, /device:TPU:0, one launch (start us, length us, event | category | flops | bytes accessed | tf_op | source)
XLA Modules:
  0.0 509.3 jit_solution(9098689265231925175)
XLA Ops:
  7.2 2.4 pad_maximum_fusion.1
  9.9 3.1 collective-permute-start.3
  14.2 9.2 %all-gather.1 = bf16[8,1,1536]{2,1,0:T(2,128)(2,1)S(1)} all-gather(bf16[1,1,1536]{2,1,0:T(2,128)(2,1)S(1)} %reshape.319), channel_id=2, replica_groups=mesh['fsdp'=8,'ctx'=4] {'fsdp'}, dimensions={0}, use_global_device_ids=true | all-gather | bytes 27648 | tf_op jit(solution)/shard_map/all_gather | solution.py:780
  24.9 6.5 %fusion = (f32[2304,128]{1,0:T(8,128)}, f32[2304,128]{1,0:T(8,128)}, f32[2304,128]{1,0:T(8,128)}) fusion(f32[128]{0:T(128)S(1)} %fusion.11, f32[2304]{0:T(1024)S(1)} %iota_convert_fusion, pred[128]{0:T(512)(128)(4,1)S(1)} %get-tuple-element.260, pred[128]{0:T(512)(128)(4,1)S(1)} %broadcast_compare_fusion.1, pred[128]{0:T(512)(128)(4,1)S(1)} %get-tuple-element.261), kind=kLoop, calls=%fused_computation.3 | loop fusion | flops 1179648 | bytes 3549056 | tf_op jit(solution)/shard_map/jit(_where)/select_n | solution.py:793
  31.4 6.7 %collective-permute-done.3.refs_0_ = bf16[512,1024]{1,0:T(8,128)(2,1)S(1)} collective-permute-done((bf16[512,1024]{1,0:T(8,128)(2,1)S(1)}, bf16[512,1024]{1,0:T(8,128)(2,1)S(1)}, u32[]{:S(2)}, u32[]{:S(2)}) %collective-permute-start.3) | collective-permute-done | bytes 1048608 | tf_op jit(solution)/shard_map/ppermute | solution.py:775
  39.1 3.9 collective-permute-start.2
  43.6 21.5 %collective-permute-done.4.refs_1_ = bf16[512,1024]{1,0:T(8,128)(2,1)S(1)} collective-permute-done((bf16[512,1024]{1,0:T(8,128)(2,1)S(1)}, bf16[512,1024]{1,0:T(8,128)(2,1)S(1)}, u32[]{:S(2)}, u32[]{:S(2)}) %collective-permute-start.4) | collective-permute-done | bytes 1048608 | tf_op jit(solution)/shard_map/ppermute | solution.py:775
  69.0 14.0 %qkv_own.1 = (bf16[1024,1024]{1,0:T(8,128)(2,1)}, bf16[1024,1024]{1,0:T(8,128)(2,1)}, bf16[1024,1024]{1,0:T(8,128)(2,1)}, bf16[1024,1024]{1,0:T(8,128)(2,1)}) custom-call(s32[4]{0:T(128)} %copy-done.37, s32[8]{0:T(128)} %get-tuple-element.259.order_ref, f32[1,1024]{1,0:T(1,128)} %bitcast.94, f32[1,1024]{1,0:T(1,128)} %bitcast.97, ...), custom_call_target="tpu_custom_call" | custom-call | flops 1048576 | bytes 65536 | tf_op jit(solution)/shard_map/qkv_own/pallas_call | solution.py:276
  83.1 6.1 %spread.1.do_ref = bf16[1024,1024]{1,0:T(8,128)(2,1)} custom-call(bf16[1024,1024]{1,0:T(8,128)(2,1)} %bitcast.71, bf16[1024,4096]{1,0:T(8,128)(2,1)} %all-gather.6.cloned.1.call-done.w_ref.wq_ref.wk_ref.wv_ref), custom_call_target="tpu_custom_call" | custom-call | flops 1048576 | bytes 65536 | tf_op jit(solution)/shard_map/spread/pallas_call | solution.py:499
  91.8 15.2 %kv_remote.1 = (bf16[1536,1024]{1,0:T(8,128)(2,1)}, bf16[1536,1024]{1,0:T(8,128)(2,1)}) custom-call(s32[6]{0:T(128)} %pad_add_fusion.1.spot_ref, s32[8]{0:T(128)} %get-tuple-element.259.order_ref, f32[1,1024]{1,0:T(1,128)} %bitcast.95, f32[1,1024]{1,0:T(1,128)} %bitcast.98, bf16[1024,4096]{1,0:T(8,128)(2,1)} %all-gather.6.cloned.1.call-done.w_ref.wq_ref.wk_ref.wv_ref, ...), custom_call_target="tpu_custom_call" | custom-call | flops 1048576 | bytes 65536 | tf_op jit(solution)/shard_map/kv_remote/pallas_call | solution.py:276
  107.0 74.8 %attention.3 = (bf16[1024,512]{1,0:T(8,128)(2,1)}, bf16[1024,512]{1,0:T(8,128)(2,1)}, bf16[2048,1024]{1,0:T(8,128)(2,1)}, bf16[512,1024]{1,0:T(8,128)(2,1)}) custom-call(f32[4,8]{1,0:T(4,128)} %add_select_fusion.kind_ref, s32[4]{0:T(128)} %compare_select_fusion.3.owner_ref, f32[8,1024]{1,0:T(8,128)} %get-tuple-element.250.cos_ref, ...), custom_call_target="tpu_custom_call" | custom-call | flops 1048576 | bytes 65536 | tf_op jit(solution)/shard_map/attention/pallas_call | solution.py:654
  182.5 75.1 %mlp.1 = (f32[1024,1024]{1,0:T(8,128)}, f32[1024,1024]{1,0:T(8,128)}, bf16[512,4096]{1,0:T(8,128)(2,1)}, bf16[512,4096]{1,0:T(8,128)(2,1)}, bf16[2048,1024]{1,0:...) custom-call(s32[8]{0:T(128)} %get-tuple-element.259.order_ref, ...), custom_call_target="tpu_custom_call" | custom-call | flops 1048576 | bytes 65536 | tf_op jit(solution)/shard_map/mlp/pallas_call | solution.py:202
  258.2 20.7 %attention.4 = (bf16[1024,128]{1,0:T(8,128)(2,1)}, bf16[1024,128]{1,0:T(8,128)(2,1)}, bf16[2048,256]{1,0:T(8,128)(2,1)}, bf16[512,256]{1,0:T(8,128)(2,1)}) custom-call(f32[4,8]{1,0:T(4,128)} %add_select_fusion.kind_ref, s32[4]{0:T(128)} %compare_select_fusion.3.owner_ref, f32[8,1024]{1,0:T(8,128)} %get-tuple-element.250.cos_ref, ...), custom_call_target="tpu_custom_call" | custom-call | flops 1048576 | bytes 65536 | tf_op jit(solution)/shard_map/attention/pallas_call | solution.py:654
  279.0 9.5 %add_parts.9 = (bf16[2,256,1024]{2,1,0:T(8,128)(2,1)}, bf16[2,256,1024]{2,1,0:T(8,128)(2,1)}, bf16[2,256,1024]{2,1,0:T(8,128)(2,1)}, bf16[2,256,1024]{2,1,0:T(8,...) custom-call(bf16[2,2,2,256,1024]{4,3,2,1,0:T(8,128)(2,1)} %bitcast.7, ...), custom_call_target="tpu_custom_call" | custom-call | flops 1 | bytes 65536 | tf_op jit(solution)/shard_map/add_parts/pallas_call | solution.py:686
  292.7 56.8 %attention.5 = (bf16[1024,384]{1,0:T(8,128)(2,1)}, bf16[1024,384]{1,0:T(8,128)(2,1)}, bf16[2048,768]{1,0:T(8,128)(2,1)}, bf16[512,768]{1,0:T(8,128)(2,1)}) custom-call(f32[4,8]{1,0:T(4,128)} %add_select_fusion.kind_ref, s32[4]{0:T(128)} %compare_select_fusion.3.owner_ref, f32[8,1024]{1,0:T(8,128)} %get-tuple-element.250.cos_ref, ...), custom_call_target="tpu_custom_call" | custom-call | flops 1048576 | bytes 65536 | tf_op jit(solution)/shard_map/attention/pallas_call | solution.py:654
  351.3 6.7 %add_parts.10 = (bf16[256,1024]{1,0:T(8,128)(2,1)}, bf16[256,1024]{1,0:T(8,128)(2,1)}, bf16[256,1024]{1,0:T(8,128)(2,1)}, bf16[256,1024]{1,0:T(8,128)(2,1)}, bf1...) custom-call(bf16[2,256,1024]{2,1,0:T(8,128)(2,1)} %get-tuple-element.146., ...), custom_call_target="tpu_custom_call" | custom-call | flops 1 | bytes 65536 | tf_op jit(solution)/shard_map/add_parts/pallas_call | solution.py:686
  362.1 7.7 %join.1 = bf16[1024,1024]{1,0:T(8,128)(2,1)} custom-call(bf16[1024,1024]{1,0:T(8,128)(2,1)} %bitcast.69, bf16[1024,4096]{1,0:T(8,128)(2,1)} %all-gather.6.cloned.1.call-done.w_ref.wq_ref.wk_ref.wv_ref, f32[1024,1024]{1,0:T(8,128)} %get-tuple-element.134.mlp_ref, f32[1,1024]{1,0:T(1,128)} %bitcast.104, bf16[1024,512]{1,0:T(8,128)(2,1)} %get-tuple-element.125.refs_0_, ...), custom_call_target="tpu_custom_call" | custom-call | flops 12884901888 | bytes 1048576 | tf_op jit(solution)/shard_map/join/pallas_call | solution.py:478
  369.7 23.3 %first_tail.1 = (bf16[512,3072]{1,0:T(8,128)(2,1)}, bf16[512,3072]{1,0:T(8,128)(2,1)}, f32[1024,1024]{1,0:T(8,128)}, f32[1,2048]{1,0:T(1,128)}) custom-call(s32[4]{0:T(128)} %copy-done.37, s32[8]{0:T(128)} %get-tuple-element.259.order_ref, bf16[1024,1024]{1,0:T(8,128)(2,1)} %bitcast.73, bf16[1024,1024]{1,0:T(8,128)(2,1)} %get-tuple-element.159.h_ref, ...), custom_call_target="tpu_custom_call" | custom-call | flops 25769803776 | bytes 1048576 | tf_op jit(solution)/shard_map/first_tail/pallas_call | solution.py:382
  393.2 4.4 add_parts.11
  400.7 5.2 %add_parts.12 = (bf16[2,64,3072]{2,1,0:T(8,128)(2,1)}, bf16[2,64,3072]{2,1,0:T(8,128)(2,1)}, bf16[2,64,3072]{2,1,0:T(8,128)(2,1)}, bf16[2,64,3072]{2,1,0:T(8,128)(2,1)}) custom-call(bf16[2,2,2,64,3072]{4,3,2,1,0:T(8,128)(2,1)} %bitcast.76, bf16[2,2,2,64,3072]{4,3,2,1,0:T(8,128)(2,1)} %bitcast.77), custom_call_target="tpu_custom_call" | custom-call | flops 1 | bytes 65536 | tf_op jit(solution)/shard_map/add_parts/pallas_call | solution.py:686
  409.5 16.1 %last_tail.1 = (f32[1024,1024]{1,0:T(8,128)}, bf16[512,1024]{1,0:T(8,128)(2,1)}, bf16[512,1024]{1,0:T(8,128)(2,1)}, f32[1,1024]{1,0:T(1,128)}, f32[1,1024]{1,0:T(1,128)}, /*index=5*/f32[1,1024]{1,0:T(1,128)}) custom-call(s32[4]{0:T(128)} %copy-done.37, bf16[1024,1024]{1,0:T(8,128)(2,1)} %get-tuple-element.159.h_ref, f32[1,1024]{1,0:T(1,128)} %bitcast.96, ...), custom_call_target="tpu_custom_call" | custom-call | flops 12884901888 | bytes 1048576 | tf_op jit(solution)/shard_map/last_tail/pallas_call | solution.py:445
  431.1 4.0 add_parts.13
  441.1 2.7 add_parts.15
  446.8 1.9 collective-permute-start.26
  449.5 3.6 add_parts.14
  455.8 2.0 add_parts.16
  461.9 1.9 collective-permute-done.29.refs_5_
  466.0 1.9 add_parts.17
  467.9 2.0 pad_maximum_fusion
  470.0 1.8 convert_element_type.272
  471.8 1.8 convert_element_type.271
  473.6 22.7 %reduce-scatter.13.cloned.1.call-done = bf16[32,4224]{1,0:T(8,128)(2,1)} async-done(((bf16[128,4224]{1,0:T(8,128)(2,1)}), bf16[32,4224]{1,0:T(8,128)(2,1)}) %reduce-scatter.13.cloned.1.call-update) | async-done | bytes 270352 | tf_op jit(solution)/shard_map/reduce_scatter | solution.py:749
  (225 shorter events, 59.6 us)
Async XLA Ops:
  7.2 61.9 %all-gather.6.cloned.1.call-start = ((), (), s32[]{:S(2)}) async-start(), calls=%async_computation.6 | async-start | bytes 9437184 | tf_op jit(solution)/shard_map/all_gather | solution.py:786
  9.7 172.8 %all-gather.10.cloned.1.call-start = ((), (), s32[]{:S(2)}) async-start(), calls=%async_computation.8 | async-start | bytes 9437184 | tf_op jit(solution)/shard_map/all_gather | solution.py:804
  9.9 28.3 %collective-permute-start.3 = (bf16[512,1024]{1,0:T(8,128)(2,1)S(1)}, bf16[512,1024]{1,0:T(8,128)(2,1)S(1)}, u32[]{:S(2)}, u32[]{:S(2)}) collective-permute-start(bf16[512,1024]{1,0:T(8,128)(2,1)S(1)} %slice_bitcast_fusion), channel_id=1, source_target_pairs={{0,1},{1,2},{2,3},{3,0},{4,5},{5,6},{6,7},{7,4},{8,9},{9,10},{10,1... | collective-permute-start | bytes 3145736 | tf_op jit(solution)/shard_map/ppermute | solution.py:775
  38.1 144.4 %all-gather.8.cloned.1.call-start = ((), (), s32[]{:S(2)}) async-start(), calls=%async_computation.7 | async-start | bytes 9437184 | tf_op jit(solution)/shard_map/all_gather | solution.py:803
  38.9 330.9 %reduce-scatter.7.cloned.1.call-start = ((), (), s32[]{:S(2)}) async-start(), calls=%async_computation.9 | async-start | bytes 5242880 | tf_op jit(solution)/shard_map/reduce_scatter | solution.py:819
  38.9 26.2 %collective-permute-start.4 = (bf16[512,1024]{1,0:T(8,128)(2,1)S(1)}, bf16[512,1024]{1,0:T(8,128)(2,1)S(1)}, u32[]{:S(2)}, u32[]{:S(2)}) collective-permute-start(bf16[512,1024]{1,0:T(8,128)(2,1)S(1)} %collective-permute-done.3.refs_0_), channel_id=1, source_target_pairs={{0,1},{1,2},{2,3},{3,0},{4,5},{5,6},{6,7},{7,4},{8,9},{9,10},{10,1... | collective-permute-start | bytes 3145736 | tf_op jit(solution)/shard_map/ppermute | solution.py:775
  39.1 28.2 %collective-permute-start.2 = (s32[2]{0:T(128)S(1)}, s32[2]{0:T(128)S(1)}, u32[]{:S(2)}, u32[]{:S(2)}) collective-permute-start(s32[2]{0:T(128)S(1)} %bitcast.110), channel_id=1, source_target_pairs={{0,3},{1,0},{2,1},{3,2},{4,7},{5,4},{6,5},{7,6},{8,11},{9,8},{10,9... | collective-permute-start | bytes 32 | tf_op jit(solution)/shard_map/ppermute | solution.py:778
  43.0 24.4 %collective-permute-start.1 = (s32[2]{0:T(128)S(1)}, s32[2]{0:T(128)S(1)}, u32[]{:S(2)}, u32[]{:S(2)}) collective-permute-start(s32[2]{0:T(128)S(1)} %bitcast.111), channel_id=1, source_target_pairs={{0,2},{1,3},{2,0},{3,1},{4,6},{5,7},{6,4},{7,5},{8,10},{9,11},{10,... | collective-permute-start | bytes 32 | tf_op jit(solution)/shard_map/ppermute | solution.py:778
  43.0 24.5 %collective-permute-start = (s32[2]{0:T(128)S(1)}, s32[2]{0:T(128)S(1)}, u32[]{:S(2)}, u32[]{:S(2)}) collective-permute-start(s32[2]{0:T(128)S(1)} %bitcast.112), channel_id=1, source_target_pairs={{0,1},{1,2},{2,3},{3,0},{4,5},{5,6},{6,7},{7,4},{8,9},{9,10},{10,1... | collective-permute-start | bytes 32 | tf_op jit(solution)/shard_map/ppermute | solution.py:778
  65.2 25.7 %collective-permute-start.5 = (bf16[512,1024]{1,0:T(8,128)(2,1)S(1)}, bf16[512,1024]{1,0:T(8,128)(2,1)S(1)}, u32[]{:S(2)}, u32[]{:S(2)}) collective-permute-start(bf16[512,1024]{1,0:T(8,128)(2,1)S(1)} %collective-permute-done.4.refs_1_), channel_id=1, source_target_pairs={{0,1},{1,2},{2,3},{3,0},{4,5},{5,6},{6,7},{7,4},{8,9},{9,10},{10,1... | collective-permute-start | bytes 3145736 | tf_op jit(solution)/shard_map/ppermute | solution.py:775
  181.9 226.7 %reduce-scatter.9.cloned.1.call-start = ((), (), s32[]{:S(2)}) async-start(), calls=%async_computation.10 | async-start | bytes 1310720 | tf_op jit(solution)/shard_map/reduce_scatter | solution.py:819
  257.6 21.4 %collective-permute-start.6 = (bf16[2048,1024]{1,0:T(8,128)(2,1)}, bf16[2048,1024]{1,0:T(8,128)(2,1)}, u32[]{:S(2)}, u32[]{:S(2)}) collective-permute-start(bf16[2048,1024]{1,0:T(8,128)(2,1)} %get-tuple-element.130), channel_id=1, source_target_pairs={{0,4},{4,0},{8,12},{12,8},{16,20},{20,16},{24,28},{28,24},{1,5},{5... | collective-permute-start | bytes 12582920 | tf_op jit(solution)/shard_map/ppermute | solution.py:702
  257.7 21.3 %collective-permute-start.7 = (bf16[512,4096]{1,0:T(8,128)(2,1)}, bf16[512,4096]{1,0:T(8,128)(2,1)}, u32[]{:S(2)}, u32[]{:S(2)}) collective-permute-start(bf16[512,4096]{1,0:T(8,128)(2,1)} %get-tuple-element.132), channel_id=1, source_target_pairs={{0,4},{4,0},{8,12},{12,8},{16,20},{20,16},{24,28},{28,24},{1,5},{5... | collective-permute-start | bytes 12582920 | tf_op jit(solution)/shard_map/ppermute | solution.py:702
  279.0 130.5 %reduce-scatter.11.cloned.1.call-start = ((), (), s32[]{:S(2)}) async-start(), calls=%async_computation.11 | async-start | bytes 3932160 | tf_op jit(solution)/shard_map/reduce_scatter | solution.py:819
  288.6 61.0 %collective-permute-start.8 = (bf16[2,256,1024]{2,1,0:T(8,128)(2,1)}, bf16[2,256,1024]{2,1,0:T(8,128)(2,1)S(1)}, u32[]{:S(2)}, u32[]{:S(2)}) collective-permute-start(bf16[2,256,1024]{2,1,0:T(8,128)(2,1)} %get-tuple-element.137), channel_id=1, source_target_pairs={{0,8},{4,12},{8,0},{12,4},{16,24},{20,28},{24,16},{28,20},{1,9},{5... | collective-permute-start | bytes 3145736 | tf_op jit(solution)/shard_map/ppermute | solution.py:702
  289.6 60.0 %collective-permute-start.9 = (bf16[2,256,1024]{2,1,0:T(8,128)(2,1)}, bf16[2,256,1024]{2,1,0:T(8,128)(2,1)S(1)}, u32[]{:S(2)}, u32[]{:S(2)}) collective-permute-start(bf16[2,256,1024]{2,1,0:T(8,128)(2,1)} %get-tuple-element.138), channel_id=1, source_target_pairs={{0,16},{4,20},{8,24},{12,28},{16,0},{20,4},{24,8},{28,12},{1,17},{... | collective-permute-start | bytes 3145736 | tf_op jit(solution)/shard_map/ppermute | solution.py:702
  291.2 58.4 %collective-permute-start.10 = (bf16[2,64,4096]{2,1,0:T(8,128)(2,1)}, bf16[2,64,4096]{2,1,0:T(8,128)(2,1)S(1)}, u32[]{:S(2)}, u32[]{:S(2)}) collective-permute-start(bf16[2,64,4096]{2,1,0:T(8,128)(2,1)} %get-tuple-element.140), channel_id=1, source_target_pairs={{0,8},{4,12},{8,0},{12,4},{16,24},{20,28},{24,16},{28,20},{1,9},{5... | collective-permute-start | bytes 3145736 | tf_op jit(solution)/shard_map/ppermute | solution.py:702
  291.8 57.9 %collective-permute-start.11 = (bf16[2,64,4096]{2,1,0:T(8,128)(2,1)}, bf16[2,64,4096]{2,1,0:T(8,128)(2,1)}, u32[]{:S(2)}, u32[]{:S(2)}) collective-permute-start(bf16[2,64,4096]{2,1,0:T(8,128)(2,1)} %get-tuple-element.142), channel_id=1, source_target_pairs={{0,16},{4,20},{8,24},{12,28},{16,0},{20,4},{24,8},{28,12},{1,17},{... | collective-permute-start | bytes 3145736 | tf_op jit(solution)/shard_map/ppermute | solution.py:702
  349.5 120.4 %reduce-scatter.17.cloned.1.call-start = ((), (), s32[]{:S(2)}) async-start(), calls=%async_computation.14 | async-start | bytes 1310720 | tf_op jit(solution)/shard_map/reduce_scatter | solution.py:749
  358.0 35.2 %collective-permute-start.12 = (bf16[256,1024]{1,0:T(8,128)(2,1)}, bf16[256,1024]{1,0:T(8,128)(2,1)}, u32[]{:S(2)}, u32[]{:S(2)}) collective-permute-start(bf16[256,1024]{1,0:T(8,128)(2,1)} %get-tuple-element.150), channel_id=1, source_target_pairs={{0,16},{4,20},{8,24},{12,28},{16,0},{20,4},{24,8},{28,12},{1,17},{... | collective-permute-start | bytes 1572872 | tf_op jit(solution)/shard_map/ppermute | solution.py:702
  359.2 33.9 %collective-permute-start.13 = (bf16[256,1024]{1,0:T(8,128)(2,1)}, bf16[256,1024]{1,0:T(8,128)(2,1)}, u32[]{:S(2)}, u32[]{:S(2)}) collective-permute-start(bf16[256,1024]{1,0:T(8,128)(2,1)} %get-tuple-element.152), channel_id=1, source_target_pairs={{0,8},{4,12},{8,0},{12,4},{16,24},{20,28},{24,16},{28,20},{1,9},{5... | collective-permute-start | bytes 1572872 | tf_op jit(solution)/shard_map/ppermute | solution.py:702
  360.7 32.5 %collective-permute-start.14 = (bf16[64,4096]{1,0:T(8,128)(2,1)}, bf16[64,4096]{1,0:T(8,128)(2,1)}, u32[]{:S(2)}, u32[]{:S(2)}) collective-permute-start(bf16[64,4096]{1,0:T(8,128)(2,1)} %get-tuple-element.154), channel_id=1, source_target_pairs={{0,16},{4,20},{8,24},{12,28},{16,0},{20,4},{24,8},{28,12},{1,17},{... | collective-permute-start | bytes 1572872 | tf_op jit(solution)/shard_map/ppermute | solution.py:702
  361.0 32.1 %collective-permute-start.15 = (bf16[64,4096]{1,0:T(8,128)(2,1)}, bf16[64,4096]{1,0:T(8,128)(2,1)}, u32[]{:S(2)}, u32[]{:S(2)}) collective-permute-start(bf16[64,4096]{1,0:T(8,128)(2,1)} %get-tuple-element.156), channel_id=1, source_target_pairs={{0,8},{4,12},{8,0},{12,4},{16,24},{20,28},{24,16},{28,20},{1,9},{5... | collective-permute-start | bytes 1572872 | tf_op jit(solution)/shard_map/ppermute | solution.py:702
  397.6 74.2 %reduce-scatter.15.cloned.1.call-start = ((), (), s32[]{:S(2)}) async-start(), calls=%async_computation.13 | async-start | bytes 1310720 | tf_op jit(solution)/shard_map/reduce_scatter | solution.py:749
  398.3 97.9 %reduce-scatter.13.cloned.1.call-start = ((), (), s32[]{:S(2)}) async-start(), calls=%async_computation.12 | async-start | bytes 1351680 | tf_op jit(solution)/shard_map/reduce_scatter | solution.py:749
  405.9 23.4 %collective-permute-start.17 = (bf16[2,64,3072]{2,1,0:T(8,128)(2,1)}, bf16[2,64,3072]{2,1,0:T(8,128)(2,1)S(1)}, u32[]{:S(2)}, u32[]{:S(2)}) collective-permute-start(bf16[2,64,3072]{2,1,0:T(8,128)(2,1)} %get-tuple-element.175), channel_id=1, source_target_pairs={{0,8},{4,12},{8,0},{12,4},{16,24},{20,28},{24,16},{28,20},{1,9},{5... | collective-permute-start | bytes 2359304 | tf_op jit(solution)/shard_map/ppermute | solution.py:702
  406.9 22.4 %collective-permute-start.18 = (bf16[2,64,3072]{2,1,0:T(8,128)(2,1)}, bf16[2,64,3072]{2,1,0:T(8,128)(2,1)S(1)}, u32[]{:S(2)}, u32[]{:S(2)}) collective-permute-start(bf16[2,64,3072]{2,1,0:T(8,128)(2,1)} %get-tuple-element.177), channel_id=1, source_target_pairs={{0,16},{4,20},{8,24},{12,28},{16,0},{20,4},{24,8},{28,12},{1,17},{... | collective-permute-start | bytes 2359304 | tf_op jit(solution)/shard_map/ppermute | solution.py:702
  425.6 14.5 %collective-permute-start.21 = (bf16[512,1024]{1,0:T(8,128)(2,1)}, bf16[512,1024]{1,0:T(8,128)(2,1)S(1)}, u32[]{:S(2)}, u32[]{:S(2)}) collective-permute-start(bf16[512,1024]{1,0:T(8,128)(2,1)} %get-tuple-element.186), channel_id=1, source_target_pairs={{0,4},{4,0},{8,12},{12,8},{16,20},{20,16},{24,28},{28,24},{1,5},{5... | collective-permute-start | bytes 3145736 | tf_op jit(solution)/shard_map/ppermute | solution.py:702
  435.1 11.7 %collective-permute-start.19 = (bf16[64,3072]{1,0:T(8,128)(2,1)}, bf16[64,3072]{1,0:T(8,128)(2,1)S(1)}, u32[]{:S(2)}, u32[]{:S(2)}) collective-permute-start(bf16[64,3072]{1,0:T(8,128)(2,1)} %get-tuple-element.190), channel_id=1, source_target_pairs={{0,16},{4,20},{8,24},{12,28},{16,0},{20,4},{24,8},{28,12},{1,17},{... | collective-permute-start | bytes 1179656 | tf_op jit(solution)/shard_map/ppermute | solution.py:702
  436.6 12.2 %collective-permute-start.20 = (bf16[64,3072]{1,0:T(8,128)(2,1)}, bf16[64,3072]{1,0:T(8,128)(2,1)S(1)}, u32[]{:S(2)}, u32[]{:S(2)}) collective-permute-start(bf16[64,3072]{1,0:T(8,128)(2,1)} %get-tuple-element.192), channel_id=1, source_target_pairs={{0,8},{4,12},{8,0},{12,4},{16,24},{20,28},{24,16},{28,20},{1,9},{5... | collective-permute-start | bytes 1179656 | tf_op jit(solution)/shard_map/ppermute | solution.py:702
  443.8 10.6 %collective-permute-start.23 = (bf16[2,64,1024]{2,1,0:T(8,128)(2,1)}, bf16[2,64,1024]{2,1,0:T(8,128)(2,1)S(1)}, u32[]{:S(2)}, u32[]{:S(2)}) collective-permute-start(bf16[2,64,1024]{2,1,0:T(8,128)(2,1)} %get-tuple-element.205), channel_id=1, source_target_pairs={{0,8},{4,12},{8,0},{12,4},{16,24},{20,28},{24,16},{28,20},{1,9},{5... | collective-permute-start | bytes 786440 | tf_op jit(solution)/shard_map/ppermute | solution.py:702
  444.3 10.0 %collective-permute-start.24 = (bf16[2,64,1024]{2,1,0:T(8,128)(2,1)}, bf16[2,64,1024]{2,1,0:T(8,128)(2,1)S(1)}, u32[]{:S(2)}, u32[]{:S(2)}) collective-permute-start(bf16[2,64,1024]{2,1,0:T(8,128)(2,1)} %get-tuple-element.208), channel_id=1, source_target_pairs={{0,16},{4,20},{8,24},{12,28},{16,0},{20,4},{24,8},{28,12},{1,17},{... | collective-permute-start | bytes 786440 | tf_op jit(solution)/shard_map/ppermute | solution.py:702
  (46 other events, 329.5 us)
Sparse Core Ops, SparseCore 0:
  10.5 57.0 all-gather.5
  69.5 54.4 all-gather.9
  125.8 54.3 all-gather.7
  182.4 76.7 reduce-scatter.6
  279.1 26.5 reduce-scatter.8
  349.7 59.7 reduce-scatter.10
  411.8 27.1 reduce-scatter.16
  441.4 25.7 reduce-scatter.14
  470.1 26.1 reduce-scatter.12

commit v11 on v10

--- a/solution.py
+++ b/solution.py
@@ -846,7 +846,8 @@
     lines = flat.shape[1]
     packed = jnp.pad(flat, ((0, 0), (0, width // parts - lines), (0, 0))).reshape(width, PAIR)
     packed = packed.reshape(8, width // 8, PAIR)[order].reshape(2, width // 2, PAIR)
-    steps_last = core_step([last_send, packed[0]], [after(last_keep, *steps_first), packed[1]])
+    steps_last = core_step([jnp.concatenate([last_send, packed[0]], axis=1)],
+                           [jnp.concatenate([after(last_keep, *steps_first), packed[1]], axis=1)])
     part_first = last_step(steps_first)
     part_last = last_step(side_step(kept_after(steps_last, *part_first)))
     total = along(jnp.concatenate([*part_first, *part_last], axis=1))

time: 514 us -> 532 us (1.035)
  waiting for transfers between devices: 62.2 us -> 87 us
  starting transfers between devices: 31.6 us -> 25.7 us
    ppermute x25 -> x20, waiting for transfers between devices: 7.18 us -> 30 us  [swap(): return lax.ppermute(a, 'fsdp', pairs_of(bit, 8))]
    ppermute x25 -> x20, starting transfers between devices: 23.1 us -> 17.2 us  [swap(): return lax.ppermute(a, 'fsdp', pairs_of(bit, 8))]
    unnamed x86 -> x74, local copies, waits for them, and re-layouts: 12.5 us -> 10 us
  transfers between devices with their start and end apart: 40 -> 35, of which waited for: 11 -> 13; matrix products, arithmetic and copies ran while one was open for 5% -> 5% of each run, Pallas kernels for 69% -> 66%
where the time goes in v11:
time: 532 us; the launch traced here: 527 us
  Pallas kernels  350 us (66%)
  waiting for transfers between devices  87 us (16%)
  other arithmetic  25.8 us (5%)
  starting transfers between devices  25.7 us (5%)
  local copies, waits for them, and re-layouts  15 us (3%)
  between operations  14.7 us (3%)
  blocking collectives  9.16 us (2%)
    pallas_call x3, Pallas kernels, attention(): pl.pallas_call(partial(attention_kernel, half, n), grid=(pairs,), in_spec...  152 us
    pallas_call x1, Pallas kernels, mlp(): pl.pallas_call(mlp_kernel, grid_spec=pltpu.PrefetchScalarGridSpec(num_sca...  75.1 us
    pallas_call x9, Pallas kernels, add_parts(): pl.pallas_call(partial(add_kernel, plan), grid=(steps,), in_specs=[spec(a...  40.1 us
    ppermute x20, waiting for transfers between devices, swap(): return lax.ppermute(a, 'fsdp', pairs_of(bit, 8))  30 us
    ppermute x3, waiting for transfers between devices, fast(): far[s] = lax.ppermute(far[s - 1], 'ctx', ring)  29.9 us
    pallas_call x2, Pallas kernels, qkv(): pl.pallas_call(partial(qkv_kernel, far), grid_spec=pltpu.PrefetchScalarGr...  29.2 us
    reduce_scatter x3, waiting for transfers between devices, along(): return lax.psum_scatter(part, 'ctx', scatter_dimension=0, tiled=True)  23.5 us
    pallas_call x1, Pallas kernels, first_tail(): pl.pallas_call(partial(first_kernel, len(dqs)), grid_spec=pltpu.PrefetchS...  23.3 us
  transfers between devices with their start and end apart: 35, of which 13 were waited for; matrix products, arithmetic and copies ran while one was open for 5% of the time, Pallas kernels for 66%

profile of v11, /device:TPU:0, one launch (start us, length us, event | category | flops | bytes accessed | tf_op | source)
XLA Modules:
  0.0 527.3 jit_solution(6868121817190093220)
XLA Ops:
  7.2 2.4 pad_maximum_fusion.3
  9.9 3.1 collective-permute-start.3
  14.2 9.2 %all-gather.1 = bf16[8,1,1536]{2,1,0:T(2,128)(2,1)S(1)} all-gather(bf16[1,1,1536]{2,1,0:T(2,128)(2,1)S(1)} %reshape.311), channel_id=2, replica_groups=mesh['fsdp'=8,'ctx'=4] {'fsdp'}, dimensions={0}, use_global_device_ids=true | all-gather | bytes 27648 | tf_op jit(solution)/shard_map/all_gather | solution.py:780
  24.9 6.5 %fusion = (f32[2304,128]{1,0:T(8,128)}, f32[2304,128]{1,0:T(8,128)}, f32[2304,128]{1,0:T(8,128)}) fusion(f32[128]{0:T(128)S(1)} %fusion.11, f32[2304]{0:T(1024)S(1)} %iota_convert_fusion, pred[128]{0:T(512)(128)(4,1)S(1)} %get-tuple-element.236, pred[128]{0:T(512)(128)(4,1)S(1)} %broadcast_compare_fusion.1, pred[128]{0:T(512)(128)(4,1)S(1)} %get-tuple-element.237), kind=kLoop, calls=%fused_computation.3 | loop fusion | flops 1179648 | bytes 3549056 | tf_op jit(solution)/shard_map/jit(_where)/select_n | solution.py:793
  31.5 6.6 %collective-permute-done.3.refs_0_ = bf16[512,1024]{1,0:T(8,128)(2,1)S(1)} collective-permute-done((bf16[512,1024]{1,0:T(8,128)(2,1)S(1)}, bf16[512,1024]{1,0:T(8,128)(2,1)S(1)}, u32[]{:S(2)}, u32[]{:S(2)}) %collective-permute-start.3) | collective-permute-done | bytes 1048608 | tf_op jit(solution)/shard_map/ppermute | solution.py:775
  39.1 3.9 collective-permute-start.2
  43.6 21.5 %collective-permute-done.4.refs_1_ = bf16[512,1024]{1,0:T(8,128)(2,1)S(1)} collective-permute-done((bf16[512,1024]{1,0:T(8,128)(2,1)S(1)}, bf16[512,1024]{1,0:T(8,128)(2,1)S(1)}, u32[]{:S(2)}, u32[]{:S(2)}) %collective-permute-start.4) | collective-permute-done | bytes 1048608 | tf_op jit(solution)/shard_map/ppermute | solution.py:775
  69.0 14.0 %qkv_own.1 = (bf16[1024,1024]{1,0:T(8,128)(2,1)}, bf16[1024,1024]{1,0:T(8,128)(2,1)}, bf16[1024,1024]{1,0:T(8,128)(2,1)}, bf16[1024,1024]{1,0:T(8,128)(2,1)}) custom-call(s32[4]{0:T(128)} %copy-done.31, s32[8]{0:T(128)} %get-tuple-element.235.order_ref, f32[1,1024]{1,0:T(1,128)} %bitcast.91, f32[1,1024]{1,0:T(1,128)} %bitcast.94, ...), custom_call_target="tpu_custom_call" | custom-call | flops 1048576 | bytes 65536 | tf_op jit(solution)/shard_map/qkv_own/pallas_call | solution.py:276
  83.1 6.1 %spread.1.do_ref = bf16[1024,1024]{1,0:T(8,128)(2,1)} custom-call(bf16[1024,1024]{1,0:T(8,128)(2,1)} %bitcast.69, bf16[1024,4096]{1,0:T(8,128)(2,1)} %all-gather.6.cloned.1.call-done.w_ref.wq_ref.wk_ref.wv_ref), custom_call_target="tpu_custom_call" | custom-call | flops 1048576 | bytes 65536 | tf_op jit(solution)/shard_map/spread/pallas_call | solution.py:499
  91.8 15.2 %kv_remote.1 = (bf16[1536,1024]{1,0:T(8,128)(2,1)}, bf16[1536,1024]{1,0:T(8,128)(2,1)}) custom-call(s32[6]{0:T(128)} %pad_add_fusion.1.spot_ref, s32[8]{0:T(128)} %get-tuple-element.235.order_ref, f32[1,1024]{1,0:T(1,128)} %bitcast.92, f32[1,1024]{1,0:T(1,128)} %bitcast.95, bf16[1024,4096]{1,0:T(8,128)(2,1)} %all-gather.6.cloned.1.call-done.w_ref.wq_ref.wk_ref.wv_ref, ...), custom_call_target="tpu_custom_call" | custom-call | flops 1048576 | bytes 65536 | tf_op jit(solution)/shard_map/kv_remote/pallas_call | solution.py:276
  107.0 74.9 %attention.3 = (bf16[1024,512]{1,0:T(8,128)(2,1)}, bf16[1024,512]{1,0:T(8,128)(2,1)}, bf16[2048,1024]{1,0:T(8,128)(2,1)}, bf16[512,1024]{1,0:T(8,128)(2,1)}) custom-call(f32[4,8]{1,0:T(4,128)} %add_select_fusion.kind_ref, s32[4]{0:T(128)} %compare_select_fusion.3.owner_ref, f32[8,1024]{1,0:T(8,128)} %get-tuple-element.226.cos_ref, ...), custom_call_target="tpu_custom_call" | custom-call | flops 1048576 | bytes 65536 | tf_op jit(solution)/shard_map/attention/pallas_call | solution.py:654
  182.6 75.1 %mlp.1 = (f32[1024,1024]{1,0:T(8,128)}, f32[1024,1024]{1,0:T(8,128)}, bf16[512,4096]{1,0:T(8,128)(2,1)}, bf16[512,4096]{1,0:T(8,128)(2,1)}, bf16[2048,1024]{1,0:...) custom-call(s32[8]{0:T(128)} %get-tuple-element.235.order_ref, ...), custom_call_target="tpu_custom_call" | custom-call | flops 1048576 | bytes 65536 | tf_op jit(solution)/shard_map/mlp/pallas_call | solution.py:202
  258.3 20.7 %attention.4 = (bf16[1024,128]{1,0:T(8,128)(2,1)}, bf16[1024,128]{1,0:T(8,128)(2,1)}, bf16[2048,256]{1,0:T(8,128)(2,1)}, bf16[512,256]{1,0:T(8,128)(2,1)}) custom-call(f32[4,8]{1,0:T(4,128)} %add_select_fusion.kind_ref, s32[4]{0:T(128)} %compare_select_fusion.3.owner_ref, f32[8,1024]{1,0:T(8,128)} %get-tuple-element.226.cos_ref, ...), custom_call_target="tpu_custom_call" | custom-call | flops 1048576 | bytes 65536 | tf_op jit(solution)/shard_map/attention/pallas_call | solution.py:654
  279.1 9.5 %add_parts.9 = (bf16[2,256,1024]{2,1,0:T(8,128)(2,1)}, bf16[2,256,1024]{2,1,0:T(8,128)(2,1)}, bf16[2,256,1024]{2,1,0:T(8,128)(2,1)}, bf16[2,256,1024]{2,1,0:T(8,...) custom-call(bf16[2,2,2,256,1024]{4,3,2,1,0:T(8,128)(2,1)} %bitcast.7, ...), custom_call_target="tpu_custom_call" | custom-call | flops 1 | bytes 65536 | tf_op jit(solution)/shard_map/add_parts/pallas_call | solution.py:686
  293.2 56.8 %attention.5 = (bf16[1024,384]{1,0:T(8,128)(2,1)}, bf16[1024,384]{1,0:T(8,128)(2,1)}, bf16[2048,768]{1,0:T(8,128)(2,1)}, bf16[512,768]{1,0:T(8,128)(2,1)}) custom-call(f32[4,8]{1,0:T(4,128)} %add_select_fusion.kind_ref, s32[4]{0:T(128)} %compare_select_fusion.3.owner_ref, f32[8,1024]{1,0:T(8,128)} %get-tuple-element.226.cos_ref, ...), custom_call_target="tpu_custom_call" | custom-call | flops 1048576 | bytes 65536 | tf_op jit(solution)/shard_map/attention/pallas_call | solution.py:654
  351.8 6.7 %add_parts.10 = (bf16[256,1024]{1,0:T(8,128)(2,1)}, bf16[256,1024]{1,0:T(8,128)(2,1)}, bf16[256,1024]{1,0:T(8,128)(2,1)}, bf16[256,1024]{1,0:T(8,128)(2,1)}, bf1...) custom-call(bf16[2,256,1024]{2,1,0:T(8,128)(2,1)} %get-tuple-element.134., ...), custom_call_target="tpu_custom_call" | custom-call | flops 1 | bytes 65536 | tf_op jit(solution)/shard_map/add_parts/pallas_call | solution.py:686
  362.6 7.7 %join.1 = bf16[1024,1024]{1,0:T(8,128)(2,1)} custom-call(bf16[1024,1024]{1,0:T(8,128)(2,1)} %bitcast.67, bf16[1024,4096]{1,0:T(8,128)(2,1)} %all-gather.6.cloned.1.call-done.w_ref.wq_ref.wk_ref.wv_ref, f32[1024,1024]{1,0:T(8,128)} %get-tuple-element.122.mlp_ref, f32[1,1024]{1,0:T(1,128)} %bitcast.100, bf16[1024,512]{1,0:T(8,128)(2,1)} %get-tuple-element.113.refs_0_, ...), custom_call_target="tpu_custom_call" | custom-call | flops 12884901888 | bytes 1048576 | tf_op jit(solution)/shard_map/join/pallas_call | solution.py:478
  370.2 23.3 %first_tail.1 = (bf16[512,3072]{1,0:T(8,128)(2,1)}, bf16[512,3072]{1,0:T(8,128)(2,1)}, f32[1024,1024]{1,0:T(8,128)}, f32[1,2048]{1,0:T(1,128)}) custom-call(s32[4]{0:T(128)} %copy-done.31, s32[8]{0:T(128)} %get-tuple-element.235.order_ref, bf16[1024,1024]{1,0:T(8,128)(2,1)} %bitcast.71, bf16[1024,1024]{1,0:T(8,128)(2,1)} %get-tuple-element.147.h_ref, ...), custom_call_target="tpu_custom_call" | custom-call | flops 25769803776 | bytes 1048576 | tf_op jit(solution)/shard_map/first_tail/pallas_call | solution.py:382
  394.4 4.4 add_parts.11
  401.9 5.3 %add_parts.12 = (bf16[2,64,3072]{2,1,0:T(8,128)(2,1)}, bf16[2,64,3072]{2,1,0:T(8,128)(2,1)}, bf16[2,64,3072]{2,1,0:T(8,128)(2,1)}, bf16[2,64,3072]{2,1,0:T(8,128)(2,1)}) custom-call(bf16[2,2,2,64,3072]{4,3,2,1,0:T(8,128)(2,1)} %bitcast.74, bf16[2,2,2,64,3072]{4,3,2,1,0:T(8,128)(2,1)} %bitcast.75), custom_call_target="tpu_custom_call" | custom-call | flops 1 | bytes 65536 | tf_op jit(solution)/shard_map/add_parts/pallas_call | solution.py:686
  407.2 2.8 reduce-scatter.11.cloned.1.call-done.refs_3_
  410.0 16.1 %last_tail.1 = (f32[1024,1024]{1,0:T(8,128)}, bf16[512,1024]{1,0:T(8,128)(2,1)}, bf16[512,1024]{1,0:T(8,128)(2,1)}, f32[1,1024]{1,0:T(1,128)}, f32[1,1024]{1,0:T(1,128)}, /*index=5*/f32[1,1024]{1,0:T(1,128)}) custom-call(s32[4]{0:T(128)} %copy-done.31, bf16[1024,1024]{1,0:T(8,128)(2,1)} %get-tuple-element.147.h_ref, f32[1,1024]{1,0:T(1,128)} %bitcast.93, ...), custom_call_target="tpu_custom_call" | custom-call | flops 12884901888 | bytes 1048576 | tf_op jit(solution)/shard_map/last_tail/pallas_call | solution.py:445
  432.7 17.2 %collective-permute-done.17.refs_1_ = bf16[2,64,3072]{2,1,0:T(8,128)(2,1)} collective-permute-done((bf16[2,64,3072]{2,1,0:T(8,128)(2,1)}, bf16[2,64,3072]{2,1,0:T(8,128)(2,1)}, u32[]{:S(2)}, u32[]{:S(2)}) %collective-permute-start.17) | collective-permute-done | bytes 786464 | tf_op jit(solution)/shard_map/ppermute | solution.py:702
  451.1 4.0 add_parts.13
  459.3 2.7 add_parts.15
  464.1 2.4 collective-permute-done.19.refs_1_
  466.5 2.5 collective-permute-done.20.refs_3_
  468.9 3.6 add_parts.14
  474.6 2.1 add_parts.16
  477.8 4.2 collective-permute-done.24.refs_1_
  485.1 2.0 pad_maximum_fusion.2
  490.8 23.4 %reduce-scatter.13.cloned.1.call-done = bf16[32,4224]{1,0:T(8,128)(2,1)} async-done(((bf16[128,4224]{1,0:T(8,128)(2,1)}), bf16[32,4224]{1,0:T(8,128)(2,1)}) %reduce-scatter.13.cloned.1.call-update) | async-done | bytes 270352 | tf_op jit(solution)/shard_map/reduce_scatter | solution.py:749
  (207 shorter events, 56.7 us)
Async XLA Ops:
  7.2 61.8 %all-gather.6.cloned.1.call-start = ((), (), s32[]{:S(2)}) async-start(), calls=%async_computation.6 | async-start | bytes 9437184 | tf_op jit(solution)/shard_map/all_gather | solution.py:786
  9.7 172.9 %all-gather.10.cloned.1.call-start = ((), (), s32[]{:S(2)}) async-start(), calls=%async_computation.8 | async-start | bytes 9437184 | tf_op jit(solution)/shard_map/all_gather | solution.py:804
  9.9 28.3 %collective-permute-start.3 = (bf16[512,1024]{1,0:T(8,128)(2,1)S(1)}, bf16[512,1024]{1,0:T(8,128)(2,1)S(1)}, u32[]{:S(2)}, u32[]{:S(2)}) collective-permute-start(bf16[512,1024]{1,0:T(8,128)(2,1)S(1)} %slice_bitcast_fusion), channel_id=1, source_target_pairs={{0,1},{1,2},{2,3},{3,0},{4,5},{5,6},{6,7},{7,4},{8,9},{9,10},{10,1... | collective-permute-start | bytes 3145736 | tf_op jit(solution)/shard_map/ppermute | solution.py:775
  38.1 144.4 %all-gather.8.cloned.1.call-start = ((), (), s32[]{:S(2)}) async-start(), calls=%async_computation.7 | async-start | bytes 9437184 | tf_op jit(solution)/shard_map/all_gather | solution.py:803
  38.9 331.4 %reduce-scatter.7.cloned.1.call-start = ((), (), s32[]{:S(2)}) async-start(), calls=%async_computation.9 | async-start | bytes 5242880 | tf_op jit(solution)/shard_map/reduce_scatter | solution.py:819
  38.9 26.2 %collective-permute-start.4 = (bf16[512,1024]{1,0:T(8,128)(2,1)S(1)}, bf16[512,1024]{1,0:T(8,128)(2,1)S(1)}, u32[]{:S(2)}, u32[]{:S(2)}) collective-permute-start(bf16[512,1024]{1,0:T(8,128)(2,1)S(1)} %collective-permute-done.3.refs_0_), channel_id=1, source_target_pairs={{0,1},{1,2},{2,3},{3,0},{4,5},{5,6},{6,7},{7,4},{8,9},{9,10},{10,1... | collective-permute-start | bytes 3145736 | tf_op jit(solution)/shard_map/ppermute | solution.py:775
  39.1 28.2 %collective-permute-start.2 = (s32[2]{0:T(128)S(1)}, s32[2]{0:T(128)S(1)}, u32[]{:S(2)}, u32[]{:S(2)}) collective-permute-start(s32[2]{0:T(128)S(1)} %bitcast.106), channel_id=1, source_target_pairs={{0,3},{1,0},{2,1},{3,2},{4,7},{5,4},{6,5},{7,6},{8,11},{9,8},{10,9... | collective-permute-start | bytes 32 | tf_op jit(solution)/shard_map/ppermute | solution.py:778
  43.0 24.4 %collective-permute-start.1 = (s32[2]{0:T(128)S(1)}, s32[2]{0:T(128)S(1)}, u32[]{:S(2)}, u32[]{:S(2)}) collective-permute-start(s32[2]{0:T(128)S(1)} %bitcast.107), channel_id=1, source_target_pairs={{0,2},{1,3},{2,0},{3,1},{4,6},{5,7},{6,4},{7,5},{8,10},{9,11},{10,... | collective-permute-start | bytes 32 | tf_op jit(solution)/shard_map/ppermute | solution.py:778
  43.0 24.5 %collective-permute-start = (s32[2]{0:T(128)S(1)}, s32[2]{0:T(128)S(1)}, u32[]{:S(2)}, u32[]{:S(2)}) collective-permute-start(s32[2]{0:T(128)S(1)} %bitcast.108), channel_id=1, source_target_pairs={{0,1},{1,2},{2,3},{3,0},{4,5},{5,6},{6,7},{7,4},{8,9},{9,10},{10,1... | collective-permute-start | bytes 32 | tf_op jit(solution)/shard_map/ppermute | solution.py:778
  65.2 25.7 %collective-permute-start.5 = (bf16[512,1024]{1,0:T(8,128)(2,1)S(1)}, bf16[512,1024]{1,0:T(8,128)(2,1)S(1)}, u32[]{:S(2)}, u32[]{:S(2)}) collective-permute-start(bf16[512,1024]{1,0:T(8,128)(2,1)S(1)} %collective-permute-done.4.refs_1_), channel_id=1, source_target_pairs={{0,1},{1,2},{2,3},{3,0},{4,5},{5,6},{6,7},{7,4},{8,9},{9,10},{10,1... | collective-permute-start | bytes 3145736 | tf_op jit(solution)/shard_map/ppermute | solution.py:775
  181.9 225.3 %reduce-scatter.9.cloned.1.call-start = ((), (), s32[]{:S(2)}) async-start(), calls=%async_computation.10 | async-start | bytes 1310720 | tf_op jit(solution)/shard_map/reduce_scatter | solution.py:819
  257.7 21.4 %collective-permute-start.6 = (bf16[2048,1024]{1,0:T(8,128)(2,1)}, bf16[2048,1024]{1,0:T(8,128)(2,1)}, u32[]{:S(2)}, u32[]{:S(2)}) collective-permute-start(bf16[2048,1024]{1,0:T(8,128)(2,1)} %get-tuple-element.118), channel_id=1, source_target_pairs={{0,4},{4,0},{8,12},{12,8},{16,20},{20,16},{24,28},{28,24},{1,5},{5... | collective-permute-start | bytes 12582920 | tf_op jit(solution)/shard_map/ppermute | solution.py:702
  257.8 21.3 %collective-permute-start.7 = (bf16[512,4096]{1,0:T(8,128)(2,1)}, bf16[512,4096]{1,0:T(8,128)(2,1)}, u32[]{:S(2)}, u32[]{:S(2)}) collective-permute-start(bf16[512,4096]{1,0:T(8,128)(2,1)} %get-tuple-element.120), channel_id=1, source_target_pairs={{0,4},{4,0},{8,12},{12,8},{16,20},{20,16},{24,28},{28,24},{1,5},{5... | collective-permute-start | bytes 12582920 | tf_op jit(solution)/shard_map/ppermute | solution.py:702
  279.0 131.0 %reduce-scatter.11.cloned.1.call-start = ((), (), s32[]{:S(2)}) async-start(), calls=%async_computation.11 | async-start | bytes 3932160 | tf_op jit(solution)/shard_map/reduce_scatter | solution.py:819
  288.7 61.4 %collective-permute-start.8 = (bf16[2,256,1024]{2,1,0:T(8,128)(2,1)}, bf16[2,256,1024]{2,1,0:T(8,128)(2,1)S(1)}, u32[]{:S(2)}, u32[]{:S(2)}) collective-permute-start(bf16[2,256,1024]{2,1,0:T(8,128)(2,1)} %get-tuple-element.125), channel_id=1, source_target_pairs={{0,8},{4,12},{8,0},{12,4},{16,24},{20,28},{24,16},{28,20},{1,9},{5... | collective-permute-start | bytes 3145736 | tf_op jit(solution)/shard_map/ppermute | solution.py:702
  289.8 60.3 %collective-permute-start.9 = (bf16[2,256,1024]{2,1,0:T(8,128)(2,1)}, bf16[2,256,1024]{2,1,0:T(8,128)(2,1)S(1)}, u32[]{:S(2)}, u32[]{:S(2)}) collective-permute-start(bf16[2,256,1024]{2,1,0:T(8,128)(2,1)} %get-tuple-element.126), channel_id=1, source_target_pairs={{0,16},{4,20},{8,24},{12,28},{16,0},{20,4},{24,8},{28,12},{1,17},{... | collective-permute-start | bytes 3145736 | tf_op jit(solution)/shard_map/ppermute | solution.py:702
  291.3 58.8 %collective-permute-start.10 = (bf16[2,64,4096]{2,1,0:T(8,128)(2,1)}, bf16[2,64,4096]{2,1,0:T(8,128)(2,1)S(1)}, u32[]{:S(2)}, u32[]{:S(2)}) collective-permute-start(bf16[2,64,4096]{2,1,0:T(8,128)(2,1)} %get-tuple-element.128), channel_id=1, source_target_pairs={{0,8},{4,12},{8,0},{12,4},{16,24},{20,28},{24,16},{28,20},{1,9},{5... | collective-permute-start | bytes 3145736 | tf_op jit(solution)/shard_map/ppermute | solution.py:702
  291.9 58.2 %collective-permute-start.11 = (bf16[2,64,4096]{2,1,0:T(8,128)(2,1)}, bf16[2,64,4096]{2,1,0:T(8,128)(2,1)}, u32[]{:S(2)}, u32[]{:S(2)}) collective-permute-start(bf16[2,64,4096]{2,1,0:T(8,128)(2,1)} %get-tuple-element.130), channel_id=1, source_target_pairs={{0,16},{4,20},{8,24},{12,28},{16,0},{20,4},{24,8},{28,12},{1,17},{... | collective-permute-start | bytes 3145736 | tf_op jit(solution)/shard_map/ppermute | solution.py:702
  350.0 137.2 %reduce-scatter.17.cloned.1.call-start = ((), (), s32[]{:S(2)}) async-start(), calls=%async_computation.14 | async-start | bytes 1310720 | tf_op jit(solution)/shard_map/reduce_scatter | solution.py:749
  358.5 35.9 %collective-permute-start.12 = (bf16[256,1024]{1,0:T(8,128)(2,1)}, bf16[256,1024]{1,0:T(8,128)(2,1)}, u32[]{:S(2)}, u32[]{:S(2)}) collective-permute-start(bf16[256,1024]{1,0:T(8,128)(2,1)} %get-tuple-element.138), channel_id=1, source_target_pairs={{0,16},{4,20},{8,24},{12,28},{16,0},{20,4},{24,8},{28,12},{1,17},{... | collective-permute-start | bytes 1572872 | tf_op jit(solution)/shard_map/ppermute | solution.py:702
  359.8 34.6 %collective-permute-start.13 = (bf16[256,1024]{1,0:T(8,128)(2,1)}, bf16[256,1024]{1,0:T(8,128)(2,1)}, u32[]{:S(2)}, u32[]{:S(2)}) collective-permute-start(bf16[256,1024]{1,0:T(8,128)(2,1)} %get-tuple-element.140), channel_id=1, source_target_pairs={{0,8},{4,12},{8,0},{12,4},{16,24},{20,28},{24,16},{28,20},{1,9},{5... | collective-permute-start | bytes 1572872 | tf_op jit(solution)/shard_map/ppermute | solution.py:702
  361.2 33.2 %collective-permute-start.14 = (bf16[64,4096]{1,0:T(8,128)(2,1)}, bf16[64,4096]{1,0:T(8,128)(2,1)}, u32[]{:S(2)}, u32[]{:S(2)}) collective-permute-start(bf16[64,4096]{1,0:T(8,128)(2,1)} %get-tuple-element.142), channel_id=1, source_target_pairs={{0,16},{4,20},{8,24},{12,28},{16,0},{20,4},{24,8},{28,12},{1,17},{... | collective-permute-start | bytes 1572872 | tf_op jit(solution)/shard_map/ppermute | solution.py:702
  361.6 32.8 %collective-permute-start.15 = (bf16[64,4096]{1,0:T(8,128)(2,1)}, bf16[64,4096]{1,0:T(8,128)(2,1)}, u32[]{:S(2)}, u32[]{:S(2)}) collective-permute-start(bf16[64,4096]{1,0:T(8,128)(2,1)} %get-tuple-element.144), channel_id=1, source_target_pairs={{0,8},{4,12},{8,0},{12,4},{16,24},{20,28},{24,16},{28,20},{1,9},{5... | collective-permute-start | bytes 1572872 | tf_op jit(solution)/shard_map/ppermute | solution.py:702
  398.8 90.2 %reduce-scatter.15.cloned.1.call-start = ((), (), s32[]{:S(2)}) async-start(), calls=%async_computation.13 | async-start | bytes 1310720 | tf_op jit(solution)/shard_map/reduce_scatter | solution.py:749
  429.6 28.7 %collective-permute-start.21 = (bf16[512,1152]{1,0:T(8,128)(2,1)S(1)}, bf16[512,1152]{1,0:T(8,128)(2,1)S(1)}, u32[]{:S(2)}, u32[]{:S(2)}) collective-permute-start(bf16[512,1152]{1,0:T(8,128)(2,1)S(1)} %pad_maximum_fusion.1), channel_id=1, source_target_pairs={{0,4},{4,0},{8,12},{12,8},{16,20},{20,16},{24,28},{28,24},{1,5},{5... | collective-permute-start | bytes 3538952 | tf_op jit(solution)/shard_map/ppermute | solution.py:702
  429.7 20.3 %collective-permute-start.17 = (bf16[2,64,3072]{2,1,0:T(8,128)(2,1)}, bf16[2,64,3072]{2,1,0:T(8,128)(2,1)}, u32[]{:S(2)}, u32[]{:S(2)}) collective-permute-start(bf16[2,64,3072]{2,1,0:T(8,128)(2,1)} %get-tuple-element.163), channel_id=1, source_target_pairs={{0,8},{4,12},{8,0},{12,4},{16,24},{20,28},{24,16},{28,20},{1,9},{5... | collective-permute-start | bytes 2359304 | tf_op jit(solution)/shard_map/ppermute | solution.py:702
  431.2 19.9 %collective-permute-start.18 = (bf16[2,64,3072]{2,1,0:T(8,128)(2,1)}, bf16[2,64,3072]{2,1,0:T(8,128)(2,1)}, u32[]{:S(2)}, u32[]{:S(2)}) collective-permute-start(bf16[2,64,3072]{2,1,0:T(8,128)(2,1)} %get-tuple-element.165), channel_id=1, source_target_pairs={{0,16},{4,20},{8,24},{12,28},{16,0},{20,4},{24,8},{28,12},{1,17},{... | collective-permute-start | bytes 2359304 | tf_op jit(solution)/shard_map/ppermute | solution.py:702
  432.7 81.5 %reduce-scatter.13.cloned.1.call-start = ((), (), s32[]{:S(2)}) async-start(), calls=%async_computation.12 | async-start | bytes 1351680 | tf_op jit(solution)/shard_map/reduce_scatter | solution.py:749
  455.1 11.4 %collective-permute-start.19 = (bf16[64,3072]{1,0:T(8,128)(2,1)}, bf16[64,3072]{1,0:T(8,128)(2,1)S(1)}, u32[]{:S(2)}, u32[]{:S(2)}) collective-permute-start(bf16[64,3072]{1,0:T(8,128)(2,1)} %get-tuple-element.178), channel_id=1, source_target_pairs={{0,16},{4,20},{8,24},{12,28},{16,0},{20,4},{24,8},{28,12},{1,17},{... | collective-permute-start | bytes 1179656 | tf_op jit(solution)/shard_map/ppermute | solution.py:702
  456.6 12.4 %collective-permute-start.20 = (bf16[64,3072]{1,0:T(8,128)(2,1)}, bf16[64,3072]{1,0:T(8,128)(2,1)}, u32[]{:S(2)}, u32[]{:S(2)}) collective-permute-start(bf16[64,3072]{1,0:T(8,128)(2,1)} %get-tuple-element.180), channel_id=1, source_target_pairs={{0,8},{4,12},{8,0},{12,4},{16,24},{20,28},{24,16},{28,20},{1,9},{5... | collective-permute-start | bytes 1179656 | tf_op jit(solution)/shard_map/ppermute | solution.py:702
  462.0 11.1 %collective-permute-start.22 = (bf16[2,64,1152]{2,1,0:T(8,128)(2,1)}, bf16[2,64,1152]{2,1,0:T(8,128)(2,1)S(1)}, u32[]{:S(2)}, u32[]{:S(2)}) collective-permute-start(bf16[2,64,1152]{2,1,0:T(8,128)(2,1)} %get-tuple-element.193), channel_id=1, source_target_pairs={{0,8},{4,12},{8,0},{12,4},{16,24},{20,28},{24,16},{28,20},{1,9},{5... | collective-permute-start | bytes 884744 | tf_op jit(solution)/shard_map/ppermute | solution.py:702
  463.5 9.7 %collective-permute-start.23 = (bf16[2,64,1152]{2,1,0:T(8,128)(2,1)}, bf16[2,64,1152]{2,1,0:T(8,128)(2,1)S(1)}, u32[]{:S(2)}, u32[]{:S(2)}) collective-permute-start(bf16[2,64,1152]{2,1,0:T(8,128)(2,1)} %get-tuple-element.196), channel_id=1, source_target_pairs={{0,16},{4,20},{8,24},{12,28},{16,0},{20,4},{24,8},{28,12},{1,17},{... | collective-permute-start | bytes 884744 | tf_op jit(solution)/shard_map/ppermute | solution.py:702
  (37 other events, 346.0 us)
Sparse Core Ops, SparseCore 0:
  10.5 57.0 all-gather.5
  69.5 54.4 all-gather.9
  125.9 54.3 all-gather.7
  182.4 76.7 reduce-scatter.6
  279.1 26.5 reduce-scatter.8
  350.1 59.8 reduce-scatter.10
  412.3 27.1 reduce-scatter.16
  441.9 25.7 reduce-scatter.14
  487.3 26.8 reduce-scatter.12

commit v12 on v10

--- a/solution.py
+++ b/solution.py
@@ -722,7 +722,7 @@
     return add_parts(arrays, plan, shapes, steps_for(arrays))
 
 
-def side_step(items):
+def side_step(items, load=0):
     arrays, plan, shapes = [], [], []
     for i in range(0, len(items), 4):
         for send, keep, bit in ((items[i], items[i + 1], 2), (items[i + 2], items[i + 3], 4)):
@@ -730,7 +730,7 @@
             plan.append((len(arrays), len(arrays) + 1, [((1,), to, (EVERY,)), ((0,), to + 1, (EVERY,))]))
             arrays += [keep, swap(send, bit)]
             shapes += [keep.shape[1:]] * 2
-    return add_parts(arrays, plan, shapes, steps_for(arrays))
+    return add_parts(arrays, plan, shapes, steps_for(arrays), load)
 
 
 def last_step(items, load=0):
@@ -835,7 +835,7 @@
         spots[0], after(x, part_out, part_in, *steps_first), normed, gain_attn, weights, tables, grad_mlp, grad_heads,
         own_kv[1:], come_kv[1:])
     sum_out, sum_in = along(part_out), along(part_in)
-    steps_first = side_step(kept_after(steps_first, last_send))
+    steps_first = side_step(kept_after(steps_first, last_send), 48)
     cols = db_last.shape[1] // 2
     split = [width, width + (db_first.shape[1] - width) // 2]
     db_q, db_k, db_v = jnp.split(db_first, split, axis=1)
@@ -848,7 +848,7 @@
     packed = packed.reshape(8, width // 8, PAIR)[order].reshape(2, width // 2, PAIR)
     steps_last = core_step([last_send, packed[0]], [after(last_keep, *steps_first), packed[1]])
     part_first = last_step(steps_first)
-    part_last = last_step(side_step(kept_after(steps_last, *part_first)))
+    part_last = last_step(side_step(steps_last))
     total = along(jnp.concatenate([*part_first, *part_last], axis=1))
     ends = [width, 2 * width, split[1] + width, db_first.shape[1] + width]
     ends += [ends[-1] + cols, ends[-1] + 2 * cols]

time: 514 us -> 523 us (1.018)
  waiting for transfers between devices: 62.2 us -> 72.4 us
    ppermute x25, waiting for transfers between devices: 7.18 us -> 17.5 us  [swap(): return lax.ppermute(a, 'fsdp', pairs_of(bit, 8))]
    unnamed x86 -> x88, local copies, waits for them, and re-layouts: 12.5 us -> 12 us
  transfers between devices with their start and end apart: 40 -> 40, of which waited for: 11 -> 8; matrix products, arithmetic and copies ran while one was open for 5% -> 5% of each run, Pallas kernels for 69% -> 67%
where the time goes in v12:
time: 523 us; the launch traced here: 519 us
  Pallas kernels  350 us (67%)
  waiting for transfers between devices  72.4 us (14%)
  starting transfers between devices  30.7 us (6%)
  other arithmetic  24.1 us (5%)
  local copies, waits for them, and re-layouts  17.7 us (3%)
  between operations  14.8 us (3%)
  blocking collectives  9.16 us (2%)
    pallas_call x3, Pallas kernels, attention(): pl.pallas_call(partial(attention_kernel, half, n), grid=(pairs,), in_spec...  152 us
    pallas_call x1, Pallas kernels, mlp(): pl.pallas_call(mlp_kernel, grid_spec=pltpu.PrefetchScalarGridSpec(num_sca...  75.1 us
    pallas_call x9, Pallas kernels, add_parts(): pl.pallas_call(partial(add_kernel, plan), grid=(steps,), in_specs=[spec(a...  40.2 us
    ppermute x3, waiting for transfers between devices, fast(): far[s] = lax.ppermute(far[s - 1], 'ctx', ring)  29.8 us
    pallas_call x2, Pallas kernels, qkv(): pl.pallas_call(partial(qkv_kernel, far), grid_spec=pltpu.PrefetchScalarGr...  29.2 us
    pallas_call x1, Pallas kernels, first_tail(): pl.pallas_call(partial(first_kernel, len(dqs)), grid_spec=pltpu.PrefetchS...  23.4 us
    reduce_scatter x3, waiting for transfers between devices, along(): return lax.psum_scatter(part, 'ctx', scatter_dimension=0, tiled=True)  23.2 us
    ppermute x25, starting transfers between devices, swap(): return lax.ppermute(a, 'fsdp', pairs_of(bit, 8))  22.2 us
  transfers between devices with their start and end apart: 40, of which 8 were waited for; matrix products, arithmetic and copies ran while one was open for 5% of the time, Pallas kernels for 67%

profile of v12, /device:TPU:0, one launch (start us, length us, event | category | flops | bytes accessed | tf_op | source)
XLA Modules:
  0.0 518.8 jit_solution(9007526382845396708)
XLA Ops:
  7.2 2.4 pad_maximum_fusion.1
  9.9 3.1 collective-permute-start.3
  14.2 9.2 %all-gather.1 = bf16[8,1,1536]{2,1,0:T(2,128)(2,1)S(1)} all-gather(bf16[1,1,1536]{2,1,0:T(2,128)(2,1)S(1)} %reshape.319), channel_id=2, replica_groups=mesh['fsdp'=8,'ctx'=4] {'fsdp'}, dimensions={0}, use_global_device_ids=true | all-gather | bytes 27648 | tf_op jit(solution)/shard_map/all_gather | solution.py:780
  24.9 6.6 %fusion = (f32[2304,128]{1,0:T(8,128)}, f32[2304,128]{1,0:T(8,128)}, f32[2304,128]{1,0:T(8,128)}) fusion(f32[128]{0:T(128)S(1)} %fusion.11, f32[2304]{0:T(1024)S(1)} %iota_convert_fusion, pred[128]{0:T(512)(128)(4,1)S(1)} %get-tuple-element.252, pred[128]{0:T(512)(128)(4,1)S(1)} %broadcast_compare_fusion.1, pred[128]{0:T(512)(128)(4,1)S(1)} %get-tuple-element.253), kind=kLoop, calls=%fused_computation.3 | loop fusion | flops 1179648 | bytes 3549056 | tf_op jit(solution)/shard_map/jit(_where)/select_n | solution.py:793
  31.6 6.6 %collective-permute-done.3.refs_0_ = bf16[512,1024]{1,0:T(8,128)(2,1)S(1)} collective-permute-done((bf16[512,1024]{1,0:T(8,128)(2,1)S(1)}, bf16[512,1024]{1,0:T(8,128)(2,1)S(1)}, u32[]{:S(2)}, u32[]{:S(2)}) %collective-permute-start.3) | collective-permute-done | bytes 1048608 | tf_op jit(solution)/shard_map/ppermute | solution.py:775
  39.1 3.9 collective-permute-start.2
  43.6 21.5 %collective-permute-done.4.refs_1_ = bf16[512,1024]{1,0:T(8,128)(2,1)S(1)} collective-permute-done((bf16[512,1024]{1,0:T(8,128)(2,1)S(1)}, bf16[512,1024]{1,0:T(8,128)(2,1)S(1)}, u32[]{:S(2)}, u32[]{:S(2)}) %collective-permute-start.4) | collective-permute-done | bytes 1048608 | tf_op jit(solution)/shard_map/ppermute | solution.py:775
  69.0 14.0 %qkv_own.1 = (bf16[1024,1024]{1,0:T(8,128)(2,1)}, bf16[1024,1024]{1,0:T(8,128)(2,1)}, bf16[1024,1024]{1,0:T(8,128)(2,1)}, bf16[1024,1024]{1,0:T(8,128)(2,1)}) custom-call(s32[4]{0:T(128)} %copy-done.35, s32[8]{0:T(128)} %get-tuple-element.251.order_ref, f32[1,1024]{1,0:T(1,128)} %bitcast.94, f32[1,1024]{1,0:T(1,128)} %bitcast.97, ...), custom_call_target="tpu_custom_call" | custom-call | flops 1048576 | bytes 65536 | tf_op jit(solution)/shard_map/qkv_own/pallas_call | solution.py:276
  83.1 6.1 %spread.1.do_ref = bf16[1024,1024]{1,0:T(8,128)(2,1)} custom-call(bf16[1024,1024]{1,0:T(8,128)(2,1)} %bitcast.71, bf16[1024,4096]{1,0:T(8,128)(2,1)} %all-gather.6.cloned.1.call-done.w_ref.wq_ref.wk_ref.wv_ref), custom_call_target="tpu_custom_call" | custom-call | flops 1048576 | bytes 65536 | tf_op jit(solution)/shard_map/spread/pallas_call | solution.py:499
  91.8 15.2 %kv_remote.1 = (bf16[1536,1024]{1,0:T(8,128)(2,1)}, bf16[1536,1024]{1,0:T(8,128)(2,1)}) custom-call(s32[6]{0:T(128)} %pad_add_fusion.1.spot_ref, s32[8]{0:T(128)} %get-tuple-element.251.order_ref, f32[1,1024]{1,0:T(1,128)} %bitcast.95, f32[1,1024]{1,0:T(1,128)} %bitcast.98, bf16[1024,4096]{1,0:T(8,128)(2,1)} %all-gather.6.cloned.1.call-done.w_ref.wq_ref.wk_ref.wv_ref, ...), custom_call_target="tpu_custom_call" | custom-call | flops 1048576 | bytes 65536 | tf_op jit(solution)/shard_map/kv_remote/pallas_call | solution.py:276
  107.0 74.8 %attention.3 = (bf16[1024,512]{1,0:T(8,128)(2,1)}, bf16[1024,512]{1,0:T(8,128)(2,1)}, bf16[2048,1024]{1,0:T(8,128)(2,1)}, bf16[512,1024]{1,0:T(8,128)(2,1)}) custom-call(f32[4,8]{1,0:T(4,128)} %add_select_fusion.kind_ref, s32[4]{0:T(128)} %compare_select_fusion.3.owner_ref, f32[8,1024]{1,0:T(8,128)} %get-tuple-element.242.cos_ref, ...), custom_call_target="tpu_custom_call" | custom-call | flops 1048576 | bytes 65536 | tf_op jit(solution)/shard_map/attention/pallas_call | solution.py:654
  182.5 75.1 %mlp.1 = (f32[1024,1024]{1,0:T(8,128)}, f32[1024,1024]{1,0:T(8,128)}, bf16[512,4096]{1,0:T(8,128)(2,1)}, bf16[512,4096]{1,0:T(8,128)(2,1)}, bf16[2048,1024]{1,0:...) custom-call(s32[8]{0:T(128)} %get-tuple-element.251.order_ref, ...), custom_call_target="tpu_custom_call" | custom-call | flops 1048576 | bytes 65536 | tf_op jit(solution)/shard_map/mlp/pallas_call | solution.py:202
  258.2 20.7 %attention.4 = (bf16[1024,128]{1,0:T(8,128)(2,1)}, bf16[1024,128]{1,0:T(8,128)(2,1)}, bf16[2048,256]{1,0:T(8,128)(2,1)}, bf16[512,256]{1,0:T(8,128)(2,1)}) custom-call(f32[4,8]{1,0:T(4,128)} %add_select_fusion.kind_ref, s32[4]{0:T(128)} %compare_select_fusion.3.owner_ref, f32[8,1024]{1,0:T(8,128)} %get-tuple-element.242.cos_ref, ...), custom_call_target="tpu_custom_call" | custom-call | flops 1048576 | bytes 65536 | tf_op jit(solution)/shard_map/attention/pallas_call | solution.py:654
  279.0 9.7 %add_parts.9 = (bf16[2,256,1024]{2,1,0:T(8,128)(2,1)}, bf16[2,256,1024]{2,1,0:T(8,128)(2,1)}, bf16[2,256,1024]{2,1,0:T(8,128)(2,1)}, bf16[2,256,1024]{2,1,0:T(8,...) custom-call(bf16[2,2,2,256,1024]{4,3,2,1,0:T(8,128)(2,1)} %bitcast.7, ...), custom_call_target="tpu_custom_call" | custom-call | flops 1 | bytes 65536 | tf_op jit(solution)/shard_map/add_parts/pallas_call | solution.py:686
  292.8 56.8 %attention.5 = (bf16[1024,384]{1,0:T(8,128)(2,1)}, bf16[1024,384]{1,0:T(8,128)(2,1)}, bf16[2048,768]{1,0:T(8,128)(2,1)}, bf16[512,768]{1,0:T(8,128)(2,1)}) custom-call(f32[4,8]{1,0:T(4,128)} %add_select_fusion.kind_ref, s32[4]{0:T(128)} %compare_select_fusion.3.owner_ref, f32[8,1024]{1,0:T(8,128)} %get-tuple-element.242.cos_ref, ...), custom_call_target="tpu_custom_call" | custom-call | flops 1048576 | bytes 65536 | tf_op jit(solution)/shard_map/attention/pallas_call | solution.py:654
  351.3 6.7 %add_parts.10 = (bf16[256,1024]{1,0:T(8,128)(2,1)}, bf16[256,1024]{1,0:T(8,128)(2,1)}, bf16[256,1024]{1,0:T(8,128)(2,1)}, bf16[256,1024]{1,0:T(8,128)(2,1)}, bf1...) custom-call(bf16[2,256,1024]{2,1,0:T(8,128)(2,1)} %get-tuple-element.142., ...), custom_call_target="tpu_custom_call" | custom-call | flops 1 | bytes 65536 | tf_op jit(solution)/shard_map/add_parts/pallas_call | solution.py:686
  362.2 7.7 %join.1 = bf16[1024,1024]{1,0:T(8,128)(2,1)} custom-call(bf16[1024,1024]{1,0:T(8,128)(2,1)} %bitcast.69, bf16[1024,4096]{1,0:T(8,128)(2,1)} %all-gather.6.cloned.1.call-done.w_ref.wq_ref.wk_ref.wv_ref, f32[1024,1024]{1,0:T(8,128)} %get-tuple-element.130.mlp_ref, f32[1,1024]{1,0:T(1,128)} %bitcast.104, bf16[1024,512]{1,0:T(8,128)(2,1)} %get-tuple-element.121.refs_0_, ...), custom_call_target="tpu_custom_call" | custom-call | flops 12884901888 | bytes 1048576 | tf_op jit(solution)/shard_map/join/pallas_call | solution.py:478
  369.8 23.4 %first_tail.1 = (bf16[512,3072]{1,0:T(8,128)(2,1)}, bf16[512,3072]{1,0:T(8,128)(2,1)}, f32[1024,1024]{1,0:T(8,128)}, f32[1,2048]{1,0:T(1,128)}) custom-call(s32[4]{0:T(128)} %copy-done.35, s32[8]{0:T(128)} %get-tuple-element.251.order_ref, bf16[1024,1024]{1,0:T(8,128)(2,1)} %bitcast.73, bf16[1024,1024]{1,0:T(8,128)(2,1)} %get-tuple-element.155.h_ref, ...), custom_call_target="tpu_custom_call" | custom-call | flops 25769803776 | bytes 1048576 | tf_op jit(solution)/shard_map/first_tail/pallas_call | solution.py:382
  393.4 4.4 add_parts.11
  400.9 5.2 %add_parts.12 = (bf16[2,64,3072]{2,1,0:T(8,128)(2,1)}, bf16[2,64,3072]{2,1,0:T(8,128)(2,1)}, bf16[2,64,3072]{2,1,0:T(8,128)(2,1)}, bf16[2,64,3072]{2,1,0:T(8,128)(2,1)}) custom-call(bf16[2,2,2,64,3072]{4,3,2,1,0:T(8,128)(2,1)} %bitcast.76, bf16[2,2,2,64,3072]{4,3,2,1,0:T(8,128)(2,1)} %bitcast.77), custom_call_target="tpu_custom_call" | custom-call | flops 1 | bytes 65536 | tf_op jit(solution)/shard_map/add_parts/pallas_call | solution.py:686
  409.6 16.1 %last_tail.1 = (f32[1024,1024]{1,0:T(8,128)}, bf16[512,1024]{1,0:T(8,128)(2,1)}, bf16[512,1024]{1,0:T(8,128)(2,1)}, f32[1,1024]{1,0:T(1,128)}, f32[1,1024]{1,0:T(1,128)}, /*index=5*/f32[1,1024]{1,0:T(1,128)}) custom-call(s32[4]{0:T(128)} %copy-done.35, bf16[1024,1024]{1,0:T(8,128)(2,1)} %get-tuple-element.155.h_ref, f32[1,1024]{1,0:T(1,128)} %bitcast.96, ...), custom_call_target="tpu_custom_call" | custom-call | flops 12884901888 | bytes 1048576 | tf_op jit(solution)/shard_map/last_tail/pallas_call | solution.py:445
  432.0 4.0 add_parts.13
  438.5 2.7 add_parts.15
  445.2 13.3 %collective-permute-done.25.refs_5_ = bf16[2,64,128]{2,1,0:T(8,128)(2,1)S(1)} collective-permute-done((bf16[2,64,128]{2,1,0:T(8,128)(2,1)}, bf16[2,64,128]{2,1,0:T(8,128)(2,1)S(1)}, u32[]{:S(2)}, u32[]{:S(2)}) %collective-permute-start.25) | collective-permute-done | bytes 32800 | tf_op jit(solution)/shard_map/ppermute | solution.py:702
  459.0 3.6 collective-permute-done.26.refs_7_
  463.4 2.0 add_parts.16
  470.5 3.6 add_parts.14
  474.8 1.9 add_parts.17
  476.7 2.3 pad_maximum_fusion
  479.0 1.8 convert_element_type.272
  480.8 1.8 convert_element_type.271
  482.6 23.2 %reduce-scatter.13.cloned.1.call-done = bf16[32,4224]{1,0:T(8,128)(2,1)} async-done(((bf16[128,4224]{1,0:T(8,128)(2,1)}), bf16[32,4224]{1,0:T(8,128)(2,1)}) %reduce-scatter.13.cloned.1.call-update) | async-done | bytes 270352 | tf_op jit(solution)/shard_map/reduce_scatter | solution.py:749
  (229 shorter events, 54.9 us)
Async XLA Ops:
  7.2 61.9 %all-gather.6.cloned.1.call-start = ((), (), s32[]{:S(2)}) async-start(), calls=%async_computation.6 | async-start | bytes 9437184 | tf_op jit(solution)/shard_map/all_gather | solution.py:786
  9.7 172.8 %all-gather.10.cloned.1.call-start = ((), (), s32[]{:S(2)}) async-start(), calls=%async_computation.8 | async-start | bytes 9437184 | tf_op jit(solution)/shard_map/all_gather | solution.py:804
  9.9 28.3 %collective-permute-start.3 = (bf16[512,1024]{1,0:T(8,128)(2,1)S(1)}, bf16[512,1024]{1,0:T(8,128)(2,1)S(1)}, u32[]{:S(2)}, u32[]{:S(2)}) collective-permute-start(bf16[512,1024]{1,0:T(8,128)(2,1)S(1)} %slice_bitcast_fusion), channel_id=1, source_target_pairs={{0,1},{1,2},{2,3},{3,0},{4,5},{5,6},{6,7},{7,4},{8,9},{9,10},{10,1... | collective-permute-start | bytes 3145736 | tf_op jit(solution)/shard_map/ppermute | solution.py:775
  38.1 144.4 %all-gather.8.cloned.1.call-start = ((), (), s32[]{:S(2)}) async-start(), calls=%async_computation.7 | async-start | bytes 9437184 | tf_op jit(solution)/shard_map/all_gather | solution.py:803
  38.9 330.9 %reduce-scatter.7.cloned.1.call-start = ((), (), s32[]{:S(2)}) async-start(), calls=%async_computation.9 | async-start | bytes 5242880 | tf_op jit(solution)/shard_map/reduce_scatter | solution.py:819
  38.9 26.2 %collective-permute-start.4 = (bf16[512,1024]{1,0:T(8,128)(2,1)S(1)}, bf16[512,1024]{1,0:T(8,128)(2,1)S(1)}, u32[]{:S(2)}, u32[]{:S(2)}) collective-permute-start(bf16[512,1024]{1,0:T(8,128)(2,1)S(1)} %collective-permute-done.3.refs_0_), channel_id=1, source_target_pairs={{0,1},{1,2},{2,3},{3,0},{4,5},{5,6},{6,7},{7,4},{8,9},{9,10},{10,1... | collective-permute-start | bytes 3145736 | tf_op jit(solution)/shard_map/ppermute | solution.py:775
  39.1 28.2 %collective-permute-start.2 = (s32[2]{0:T(128)S(1)}, s32[2]{0:T(128)S(1)}, u32[]{:S(2)}, u32[]{:S(2)}) collective-permute-start(s32[2]{0:T(128)S(1)} %bitcast.110), channel_id=1, source_target_pairs={{0,3},{1,0},{2,1},{3,2},{4,7},{5,4},{6,5},{7,6},{8,11},{9,8},{10,9... | collective-permute-start | bytes 32 | tf_op jit(solution)/shard_map/ppermute | solution.py:778
  43.0 24.4 %collective-permute-start.1 = (s32[2]{0:T(128)S(1)}, s32[2]{0:T(128)S(1)}, u32[]{:S(2)}, u32[]{:S(2)}) collective-permute-start(s32[2]{0:T(128)S(1)} %bitcast.111), channel_id=1, source_target_pairs={{0,2},{1,3},{2,0},{3,1},{4,6},{5,7},{6,4},{7,5},{8,10},{9,11},{10,... | collective-permute-start | bytes 32 | tf_op jit(solution)/shard_map/ppermute | solution.py:778
  43.0 24.5 %collective-permute-start = (s32[2]{0:T(128)S(1)}, s32[2]{0:T(128)S(1)}, u32[]{:S(2)}, u32[]{:S(2)}) collective-permute-start(s32[2]{0:T(128)S(1)} %bitcast.112), channel_id=1, source_target_pairs={{0,1},{1,2},{2,3},{3,0},{4,5},{5,6},{6,7},{7,4},{8,9},{9,10},{10,1... | collective-permute-start | bytes 32 | tf_op jit(solution)/shard_map/ppermute | solution.py:778
  65.2 25.7 %collective-permute-start.5 = (bf16[512,1024]{1,0:T(8,128)(2,1)S(1)}, bf16[512,1024]{1,0:T(8,128)(2,1)S(1)}, u32[]{:S(2)}, u32[]{:S(2)}) collective-permute-start(bf16[512,1024]{1,0:T(8,128)(2,1)S(1)} %collective-permute-done.4.refs_1_), channel_id=1, source_target_pairs={{0,1},{1,2},{2,3},{3,0},{4,5},{5,6},{6,7},{7,4},{8,9},{9,10},{10,1... | collective-permute-start | bytes 3145736 | tf_op jit(solution)/shard_map/ppermute | solution.py:775
  181.8 226.9 %reduce-scatter.9.cloned.1.call-start = ((), (), s32[]{:S(2)}) async-start(), calls=%async_computation.10 | async-start | bytes 1310720 | tf_op jit(solution)/shard_map/reduce_scatter | solution.py:819
  257.6 21.3 %collective-permute-start.6 = (bf16[2048,1024]{1,0:T(8,128)(2,1)}, bf16[2048,1024]{1,0:T(8,128)(2,1)}, u32[]{:S(2)}, u32[]{:S(2)}) collective-permute-start(bf16[2048,1024]{1,0:T(8,128)(2,1)} %get-tuple-element.126), channel_id=1, source_target_pairs={{0,4},{4,0},{8,12},{12,8},{16,20},{20,16},{24,28},{28,24},{1,5},{5... | collective-permute-start | bytes 12582920 | tf_op jit(solution)/shard_map/ppermute | solution.py:702
  257.7 21.3 %collective-permute-start.7 = (bf16[512,4096]{1,0:T(8,128)(2,1)}, bf16[512,4096]{1,0:T(8,128)(2,1)}, u32[]{:S(2)}, u32[]{:S(2)}) collective-permute-start(bf16[512,4096]{1,0:T(8,128)(2,1)} %get-tuple-element.128), channel_id=1, source_target_pairs={{0,4},{4,0},{8,12},{12,8},{16,20},{20,16},{24,28},{28,24},{1,5},{5... | collective-permute-start | bytes 12582920 | tf_op jit(solution)/shard_map/ppermute | solution.py:702
  278.9 130.7 %reduce-scatter.11.cloned.1.call-start = ((), (), s32[]{:S(2)}) async-start(), calls=%async_computation.11 | async-start | bytes 3932160 | tf_op jit(solution)/shard_map/reduce_scatter | solution.py:819
  288.7 61.0 %collective-permute-start.8 = (bf16[2,256,1024]{2,1,0:T(8,128)(2,1)}, bf16[2,256,1024]{2,1,0:T(8,128)(2,1)S(1)}, u32[]{:S(2)}, u32[]{:S(2)}) collective-permute-start(bf16[2,256,1024]{2,1,0:T(8,128)(2,1)} %get-tuple-element.133), channel_id=1, source_target_pairs={{0,8},{4,12},{8,0},{12,4},{16,24},{20,28},{24,16},{28,20},{1,9},{5... | collective-permute-start | bytes 3145736 | tf_op jit(solution)/shard_map/ppermute | solution.py:702
  289.8 59.9 %collective-permute-start.9 = (bf16[2,256,1024]{2,1,0:T(8,128)(2,1)}, bf16[2,256,1024]{2,1,0:T(8,128)(2,1)S(1)}, u32[]{:S(2)}, u32[]{:S(2)}) collective-permute-start(bf16[2,256,1024]{2,1,0:T(8,128)(2,1)} %get-tuple-element.134), channel_id=1, source_target_pairs={{0,16},{4,20},{8,24},{12,28},{16,0},{20,4},{24,8},{28,12},{1,17},{... | collective-permute-start | bytes 3145736 | tf_op jit(solution)/shard_map/ppermute | solution.py:702
  291.4 58.3 %collective-permute-start.10 = (bf16[2,64,4096]{2,1,0:T(8,128)(2,1)}, bf16[2,64,4096]{2,1,0:T(8,128)(2,1)S(1)}, u32[]{:S(2)}, u32[]{:S(2)}) collective-permute-start(bf16[2,64,4096]{2,1,0:T(8,128)(2,1)} %get-tuple-element.136), channel_id=1, source_target_pairs={{0,8},{4,12},{8,0},{12,4},{16,24},{20,28},{24,16},{28,20},{1,9},{5... | collective-permute-start | bytes 3145736 | tf_op jit(solution)/shard_map/ppermute | solution.py:702
  291.9 57.8 %collective-permute-start.11 = (bf16[2,64,4096]{2,1,0:T(8,128)(2,1)}, bf16[2,64,4096]{2,1,0:T(8,128)(2,1)}, u32[]{:S(2)}, u32[]{:S(2)}) collective-permute-start(bf16[2,64,4096]{2,1,0:T(8,128)(2,1)} %get-tuple-element.138), channel_id=1, source_target_pairs={{0,16},{4,20},{8,24},{12,28},{16,0},{20,4},{24,8},{28,12},{1,17},{... | collective-permute-start | bytes 3145736 | tf_op jit(solution)/shard_map/ppermute | solution.py:702
  349.6 129.4 %reduce-scatter.17.cloned.1.call-start = ((), (), s32[]{:S(2)}) async-start(), calls=%async_computation.14 | async-start | bytes 1310720 | tf_op jit(solution)/shard_map/reduce_scatter | solution.py:749
  358.0 35.3 %collective-permute-start.12 = (bf16[256,1024]{1,0:T(8,128)(2,1)}, bf16[256,1024]{1,0:T(8,128)(2,1)}, u32[]{:S(2)}, u32[]{:S(2)}) collective-permute-start(bf16[256,1024]{1,0:T(8,128)(2,1)} %get-tuple-element.146), channel_id=1, source_target_pairs={{0,16},{4,20},{8,24},{12,28},{16,0},{20,4},{24,8},{28,12},{1,17},{... | collective-permute-start | bytes 1572872 | tf_op jit(solution)/shard_map/ppermute | solution.py:702
  359.2 34.2 %collective-permute-start.13 = (bf16[256,1024]{1,0:T(8,128)(2,1)}, bf16[256,1024]{1,0:T(8,128)(2,1)}, u32[]{:S(2)}, u32[]{:S(2)}) collective-permute-start(bf16[256,1024]{1,0:T(8,128)(2,1)} %get-tuple-element.148), channel_id=1, source_target_pairs={{0,8},{4,12},{8,0},{12,4},{16,24},{20,28},{24,16},{28,20},{1,9},{5... | collective-permute-start | bytes 1572872 | tf_op jit(solution)/shard_map/ppermute | solution.py:702
  360.7 32.7 %collective-permute-start.14 = (bf16[64,4096]{1,0:T(8,128)(2,1)}, bf16[64,4096]{1,0:T(8,128)(2,1)}, u32[]{:S(2)}, u32[]{:S(2)}) collective-permute-start(bf16[64,4096]{1,0:T(8,128)(2,1)} %get-tuple-element.150), channel_id=1, source_target_pairs={{0,16},{4,20},{8,24},{12,28},{16,0},{20,4},{24,8},{28,12},{1,17},{... | collective-permute-start | bytes 1572872 | tf_op jit(solution)/shard_map/ppermute | solution.py:702
  361.1 32.3 %collective-permute-start.15 = (bf16[64,4096]{1,0:T(8,128)(2,1)}, bf16[64,4096]{1,0:T(8,128)(2,1)}, u32[]{:S(2)}, u32[]{:S(2)}) collective-permute-start(bf16[64,4096]{1,0:T(8,128)(2,1)} %get-tuple-element.152), channel_id=1, source_target_pairs={{0,8},{4,12},{8,0},{12,4},{16,24},{20,28},{24,16},{28,20},{1,9},{5... | collective-permute-start | bytes 1572872 | tf_op jit(solution)/shard_map/ppermute | solution.py:702
  397.9 82.9 %reduce-scatter.15.cloned.1.call-start = ((), (), s32[]{:S(2)}) async-start(), calls=%async_computation.13 | async-start | bytes 1310720 | tf_op jit(solution)/shard_map/reduce_scatter | solution.py:749
  398.6 107.1 %reduce-scatter.13.cloned.1.call-start = ((), (), s32[]{:S(2)}) async-start(), calls=%async_computation.12 | async-start | bytes 1351680 | tf_op jit(solution)/shard_map/reduce_scatter | solution.py:749
  406.1 24.1 %collective-permute-start.17 = (bf16[2,64,3072]{2,1,0:T(8,128)(2,1)}, bf16[2,64,3072]{2,1,0:T(8,128)(2,1)S(1)}, u32[]{:S(2)}, u32[]{:S(2)}) collective-permute-start(bf16[2,64,3072]{2,1,0:T(8,128)(2,1)} %get-tuple-element.171), channel_id=1, source_target_pairs={{0,8},{4,12},{8,0},{12,4},{16,24},{20,28},{24,16},{28,20},{1,9},{5... | collective-permute-start | bytes 2359304 | tf_op jit(solution)/shard_map/ppermute | solution.py:702
  407.1 23.1 %collective-permute-start.18 = (bf16[2,64,3072]{2,1,0:T(8,128)(2,1)}, bf16[2,64,3072]{2,1,0:T(8,128)(2,1)S(1)}, u32[]{:S(2)}, u32[]{:S(2)}) collective-permute-start(bf16[2,64,3072]{2,1,0:T(8,128)(2,1)} %get-tuple-element.173), channel_id=1, source_target_pairs={{0,16},{4,20},{8,24},{12,28},{16,0},{20,4},{24,8},{28,12},{1,17},{... | collective-permute-start | bytes 2359304 | tf_op jit(solution)/shard_map/ppermute | solution.py:702
  435.9 33.0 %collective-permute-start.19 = (bf16[64,3072]{1,0:T(8,128)(2,1)}, bf16[64,3072]{1,0:T(8,128)(2,1)S(1)}, u32[]{:S(2)}, u32[]{:S(2)}) collective-permute-start(bf16[64,3072]{1,0:T(8,128)(2,1)} %get-tuple-element.186), channel_id=1, source_target_pairs={{0,16},{4,20},{8,24},{12,28},{16,0},{20,4},{24,8},{28,12},{1,17},{... | collective-permute-start | bytes 1179656 | tf_op jit(solution)/shard_map/ppermute | solution.py:702
  441.1 21.4 %collective-permute-start.23 = (bf16[2,64,1024]{2,1,0:T(8,128)(2,1)}, bf16[2,64,1024]{2,1,0:T(8,128)(2,1)S(1)}, u32[]{:S(2)}, u32[]{:S(2)}) collective-permute-start(bf16[2,64,1024]{2,1,0:T(8,128)(2,1)} %get-tuple-element.200), channel_id=1, source_target_pairs={{0,8},{4,12},{8,0},{12,4},{16,24},{20,28},{24,16},{28,20},{1,9},{5... | collective-permute-start | bytes 786440 | tf_op jit(solution)/shard_map/ppermute | solution.py:702
  442.6 19.9 %collective-permute-start.24 = (bf16[2,64,1024]{2,1,0:T(8,128)(2,1)}, bf16[2,64,1024]{2,1,0:T(8,128)(2,1)S(1)}, u32[]{:S(2)}, u32[]{:S(2)}) collective-permute-start(bf16[2,64,1024]{2,1,0:T(8,128)(2,1)} %get-tuple-element.202), channel_id=1, source_target_pairs={{0,16},{4,20},{8,24},{12,28},{16,0},{20,4},{24,8},{28,12},{1,17},{... | collective-permute-start | bytes 786440 | tf_op jit(solution)/shard_map/ppermute | solution.py:702
  443.1 26.4 %collective-permute-start.20 = (bf16[64,3072]{1,0:T(8,128)(2,1)S(1)}, bf16[64,3072]{1,0:T(8,128)(2,1)S(1)}, u32[]{:S(2)}, u32[]{:S(2)}) collective-permute-start(bf16[64,3072]{1,0:T(8,128)(2,1)S(1)} %copy-done.38), channel_id=1, source_target_pairs={{0,8},{4,12},{8,0},{12,4},{16,24},{20,28},{24,16},{28,20},{1,9},{5... | collective-permute-start | bytes 1179656 | tf_op jit(solution)/shard_map/ppermute | solution.py:702
  443.7 14.7 %collective-permute-start.25 = (bf16[2,64,128]{2,1,0:T(8,128)(2,1)}, bf16[2,64,128]{2,1,0:T(8,128)(2,1)S(1)}, u32[]{:S(2)}, u32[]{:S(2)}) collective-permute-start(bf16[2,64,128]{2,1,0:T(8,128)(2,1)} %get-tuple-element.204), channel_id=1, source_target_pairs={{0,8},{4,12},{8,0},{12,4},{16,24},{20,28},{24,16},{28,20},{1,9},{5... | collective-permute-start | bytes 98312 | tf_op jit(solution)/shard_map/ppermute | solution.py:702
  (49 other events, 330.5 us)
Sparse Core Ops, SparseCore 0:
  10.5 57.0 all-gather.5
  69.5 54.4 all-gather.9
  125.8 54.3 all-gather.7
  182.4 76.7 reduce-scatter.6
  279.1 26.6 reduce-scatter.8
  349.7 59.8 reduce-scatter.10
  411.9 27.1 reduce-scatter.16
  441.5 25.8 reduce-scatter.14
  479.1 26.5 reduce-scatter.12
